TPU v7x, 32 devices: a whole 2x2x4 slice. The times are simulated.
32 devices in a mesh: tm: 16 (over z, y, core), rows: 2 (over x).
Axes of the slice: x: 2, y: 2, z: 4, core: 2. Of those that a mesh axis runs over, the one named last changes fastest.
Arguments:
- latents: bfloat16 [128, 4, 32, 512], P('tm', 'rows'), may hold values from -6 to 6
- clip_ids: int32 [128], replicated, may hold values from 0 to 24, never falling along the last dimension, each value on 1 to 9 neighbouring positions
- gain_in: float32 [512], replicated, may hold values from 0.25 to 1.75
- w_space: bfloat16 [3, 3, 512, 512], P(None, None, None, 'tm'), may hold values from -0.09375 to 0.09375
- w_time: bfloat16 [3, 512, 512], replicated, may hold values from -0.15625 to 0.15625
- gain_attn: float32 [512], replicated, may hold values from 0.25 to 1.75
- w_qkv: bfloat16 [512, 1536], replicated, may hold values from -0.25 to 0.25
- w_out: bfloat16 [512, 512], replicated, may hold values from -0.25 to 0.25
Outputs:
- block_out: bfloat16 [128, 4, 32, 512], P('tm', 'rows')
Inputs may be any that keep to these rules, and one draw needn't show every extreme that they name: `clip_ids`: clip numbers never fall along time; each clip has 1 to 9 frames and some clip has exactly 9.
All inputs are finite; a program needn't handle non-finite values.
Results may differ from a plain program's by a relative error of at most 0.0085.
Values may be sent and summed in bfloat16 or wider, within the bound.
No kernel may reach another device: no remote copies, remote signals or barrier semaphores. Data moves between devices by JAX's collectives and lax.ppermute only.
A program may use at most 64 MiB of HBM per device.

v0:
```python
import jax
import jax.numpy as jnp
from jax import lax
from jax.sharding import PartitionSpec as P


def with_halo(cells, sides, width):
    for axis, dim in sides:
        count = lax.axis_size(axis)
        ends = count - 1
        head = lax.slice_in_dim(cells, 0, width, axis=dim)
        tail = lax.slice_in_dim(cells, cells.shape[dim] - width, cells.shape[dim], axis=dim)
        cells = jnp.concatenate(
            [
                lax.ppermute(tail, axis, [(i, (i + 1) % count) for i in range(ends)]),
                cells,
                lax.ppermute(head, axis, [((i + 1) % count, i) for i in range(ends)]),
            ],
            axis=dim,
        )
    return cells


def shifted(array, axis, by):
    length = lax.axis_size(axis)
    pairs = [(i, i + by) for i in range(length) if 0 <= i + by < length]
    return lax.ppermute(array, axis, pairs)


def entering(array, axis, combine, identity):
    length, index = (lax.axis_size(axis), lax.axis_index(axis))
    everything = jax.tree.map(
        lambda part, kind: lax.all_gather(part.astype(kind), axis),
        array,
        (jnp.bfloat16, jnp.bfloat16, jnp.bfloat16),
    )
    start = jax.tree.map(
        lambda part, zero: jnp.broadcast_to(jnp.asarray(zero, part.dtype), part.shape),
        array,
        identity,
    )

    def step(k, before):
        reached = k < index
        new = combine(
            before, jax.tree.map(lambda part, own: part[k].astype(own.dtype), everything, array)
        )
        return jax.tree.map(lambda a, b: jnp.where(reached, a, b), new, before)

    return lax.fori_loop(0, length, step, start)


def rms_scale(values, gain):
    floats = values.astype(jnp.float32)
    scale = lax.rsqrt(jnp.mean(floats * floats, axis=-1, keepdims=True) + 1e-06)
    return (floats * scale * gain).astype(jnp.bfloat16)


def join_clip(earlier, later):
    early_sum, early_num, early_flag = earlier
    late_sum, late_num, late_flag = later
    pick = late_flag > 0
    return (
        jnp.where(pick, late_sum, early_sum + late_sum),
        jnp.where(pick, late_num, early_num + late_num),
        jnp.maximum(early_flag, late_flag),
    )


def attend_frames(tokens, chans):
    query = tokens[:, :, :chans]
    key = tokens[:, :, chans : 2 * chans]
    value = tokens[:, :, 2 * chans :]
    scores = jnp.einsum("fqc,fkc->fqk", query, key, preferred_element_type=jnp.float32) * chans ** (
        -0.5
    )
    probs = jax.nn.softmax(scores, axis=-1).astype(jnp.bfloat16)
    return jnp.einsum("fqk,fkc->fqc", probs, value, preferred_element_type=jnp.float32).astype(
        jnp.bfloat16
    )


def local(latents, clip_ids, gain_in, w_space, w_time, gain_attn, w_qkv, w_out):
    frames, height, width, chans = latents.shape
    groups = lax.axis_size("rows")
    normed = rms_scale(latents, gain_in)
    padded = with_halo(normed, (("rows", 1),), 1)
    padded = jnp.pad(padded, ((0, 0), (0, 0), (1, 1), (0, 0)))
    windows = [
        padded[:, dy : dy + height, dx : dx + width, :].reshape(-1, chans)
        for dy in range(3)
        for dx in range(3)
    ]
    piece = lax.all_gather(w_space, "tm", axis=3, tiled=True)
    total = jnp.zeros((windows[0].shape[0], piece.shape[3]), jnp.float32)
    for dy in range(3):
        for dx in range(3):
            total = total + jnp.dot(
                windows[dy * 3 + dx], piece[dy, dx], preferred_element_type=jnp.float32
            )
    conv = total
    acts = jax.nn.silu(conv).astype(jnp.bfloat16).reshape(frames, height, width, chans)
    earlier = shifted(acts[frames - 2 :], "tm", 1)
    extended = jnp.concatenate([earlier, acts], 0)
    first = lax.axis_index("tm") * frames
    seg_pad = jnp.concatenate([jnp.full((2,), -1, jnp.int32), clip_ids])
    seg_ext = lax.dynamic_slice_in_dim(seg_pad, first, frames + 2)
    segs = seg_ext[2:]
    total = latents.astype(jnp.float32).reshape(-1, chans)
    for back in range(3):
        source = extended[2 - back : 2 - back + frames]
        keep = (seg_ext[2 - back : 2 - back + frames] == segs).astype(jnp.bfloat16)[
            :, None, None, None
        ]
        total = total + jnp.dot(
            (source * keep).reshape(-1, chans), w_time[back], preferred_element_type=jnp.float32
        )
    resid = total.astype(jnp.bfloat16).reshape(frames, height, width, chans)
    floats = resid.astype(jnp.float32)
    sums_local = []
    nums_local = []
    running = floats[0]
    number = jnp.float32(1.0)
    sums_local.append(running)
    nums_local.append(number)
    for index in range(1, frames):
        same = segs[index] == segs[index - 1]
        running = jnp.where(same, running, jnp.float32(0.0)) + floats[index]
        number = jnp.where(same, number, jnp.float32(0.0)) + jnp.float32(1.0)
        sums_local.append(running)
        nums_local.append(number)
    last_num = jnp.reshape(number, (1,))
    flag = jnp.reshape((segs[frames - 1] != seg_ext[1]).astype(jnp.float32), (1,))
    empty = (jnp.zeros_like(running), jnp.zeros((1,), jnp.float32), jnp.zeros((1,), jnp.float32))
    carry_sum, carry_num, carry_flag = entering((running, last_num, flag), "tm", join_clip, empty)
    mixed_list = []
    for index in range(frames):
        cont = segs[index] == seg_ext[1]
        clip_sum = sums_local[index] + jnp.where(cont, carry_sum, jnp.float32(0.0))
        clip_num = nums_local[index] + jnp.where(cont, carry_num[0], jnp.float32(0.0))
        mixed_list.append((floats[index] + clip_sum / clip_num).astype(jnp.bfloat16))
    mixed = jnp.stack(mixed_list, 0)
    attn_in = rms_scale(mixed, gain_attn)
    qkv = jnp.dot(attn_in.reshape(-1, chans), w_qkv, preferred_element_type=jnp.float32).astype(
        jnp.bfloat16
    )
    grouped = qkv.reshape(groups, frames // groups, height, width, 3 * chans)
    block = lax.all_to_all(grouped, "rows", split_axis=0, concat_axis=2, tiled=True)
    count = block.shape[1]
    tokens = block.reshape(count, -1, 3 * chans)
    out = attend_frames(tokens, chans)
    attended = out.reshape(1, count, height * groups, width, chans)
    returned = lax.all_to_all(attended, "rows", split_axis=2, concat_axis=0, tiled=True)
    result = mixed.astype(jnp.float32).reshape(-1, chans) + jnp.dot(
        returned.reshape(-1, chans), w_out, preferred_element_type=jnp.float32
    )
    return result.astype(jnp.bfloat16).reshape(frames, height, width, chans)


def solution(mesh):
    placed = (P("tm", "rows", None, None), P(), P(), P(None, None, None, "tm"), P(), P(), P(), P())
    return jax.shard_map(
        local, mesh=mesh, in_specs=placed, out_specs=P("tm", "rows", None, None), check_vma=False
    )
```

profile of v0, /device:TPU:0, one launch (start us, length us, event | category | flops | bytes accessed | tf_op | source)
XLA Modules:
  0.0 244.3 jit_solution(15914931476498741329)
XLA Ops:
  6.5 0.7 all-gather.4.cloned.1.call-update
  7.3 1.2 multiply_reduce_fusion.1
  8.6 1.2 multiply_convert_fusion.1
  9.9 4.9 %collective-permute-start = (bf16[8,1,32,512]{3,2,1,0:T(8,128)(2,1)S(1)}, bf16[8,1,32,512]{3,2,1,0:T(8,128)(2,1)S(1)}, u32[]{:S(2)}, u32[]{:S(2)}) collective-permute-start(bf16[8,1,32,512]{3,2,1,0:T(8,128)(2,1)S(1)} %get-tuple-element.195), channel_id=1, source_target_pairs={{0,1},{2,3},{4,5},{6,7},{8,9},{10,11},{12,13},{14,15},{16,17},{18,... | collective-permute-start | bytes 786440 | tf_op jit(solution)/shard_map/ppermute | solution.py:15
  14.7 1.3 collective-permute-start.1
  16.1 0.7 fusion.38
  25.7 1.1 pad_maximum_fusion.1
  26.8 0.7 fusion.8
  27.5 1.7 fusion.34
  29.2 36.5 %all-gather.4.cloned.1.call-done = bf16[3,3,512,512]{2,3,1,0:T(8,128)(2,1)} async-done(((bf16[3,3,512,32]{2,3,1,0:T(8,128)(2,1)}), bf16[3,3,512,512]{2,3,1,0:T(8,128)(2,1)}) %all-gather.4.cloned.1.call-update) | async-done | bytes 4718608 | tf_op jit(solution)/shard_map/all_gather | solution.py:94
  65.7 1.8 fusion.23
  67.5 1.7 fusion.22
  69.2 1.6 convolution_add_fusion.10
  74.3 0.6 multiply_convert_fusion
  74.9 2.2 collective-permute-start.2
  79.1 0.8 fusion.35
  81.1 0.7 dynamic-update-slice.1
  81.8 1.4 dynamic-update-slice
  83.2 31.5 %all-reduce.4 = (bf16[16]{0:T(256)(128)(2,1)S(1)}, bf16[16]{0:T(256)(128)(2,1)S(1)}) all-reduce(bf16[16]{0:T(256)(128)(2,1)S(1)} %dynamic-update-slice, bf16[16]{0:T(256)(128)(2,1)S(1)} %dynamic-update-slice.1), channel_id=2, replica_groups=mesh['tm'=16,'rows'=2] {'tm'}, use_global_device_ids=true, to_apply=%add.2 | all-reduce | flops 32 | bytes 128
  124.3 0.7 fusion.36
  125.0 75.8 %while.16 = (s32[]{:T(128)}, f32[2,32,512]{2,1,0:T(8,128)S(1)}, f32[1]{0:T(128)}, s32[]{:T(128)}, bf16[16,1]{0,1:T(2,128)(2,1)S(1)}, /*index=5*/bf16[16,2,32,512...) while((s32[]{:T(128)}, f32[2,32,512]{2,1,0:T(8,128)S(1)}, f32[1]{0:T(128)}, ...), condition=%wide.region_2.3_spmd.clone, body=%wide.region_1.2_spmd.clone.sunk | while | flops 163849 | bytes 327847 | solution.py:50
  126.3 0.7 fusion.60
  128.2 1.5 fusion.61
  129.8 0.6 constant_dynamic-slice_fusion.3
  131.0 0.7 fusion.60
  133.0 1.5 fusion.61
  134.5 0.6 constant_dynamic-slice_fusion.3
  135.8 0.7 fusion.60
  137.7 1.5 fusion.61
  140.5 0.7 fusion.60
  142.4 1.5 fusion.61
  145.2 0.7 fusion.60
  147.2 1.5 fusion.61
  148.7 0.6 constant_dynamic-slice_fusion.3
  150.0 0.7 fusion.60
  151.9 1.5 fusion.61
  153.5 0.6 constant_dynamic-slice_fusion.3
  154.7 0.7 fusion.60
  156.6 1.5 fusion.61
  159.5 0.7 fusion.60
  161.4 1.5 fusion.61
  162.9 0.6 constant_dynamic-slice_fusion.3
  164.2 0.7 fusion.60
  166.1 1.5 fusion.61
  168.9 0.7 fusion.60
  170.9 1.5 fusion.61
  173.7 0.7 fusion.60
  175.6 1.5 fusion.61
  178.4 0.7 fusion.60
  180.3 1.5 fusion.61
  183.1 0.7 fusion.60
  185.1 1.5 fusion.61
  187.9 0.7 fusion.60
  189.8 1.5 fusion.61
  192.6 0.7 fusion.60
  194.6 1.5 fusion.61
  197.4 0.7 fusion.60
  199.3 1.5 fusion.61
  202.0 1.0 convolution_convert_fusion
  203.0 20.9 %all_to_all.30 = bf16[2,4,2,32,1536]{4,3,2,1,0:T(8,128)(2,1)S(1)} all-to-all(bf16[2,4,2,32,1536]{4,3,2,1,0:T(8,128)(2,1)S(1)} %bitcast.174), channel_id=1, replica_groups=mesh['tm'=16,'rows'=2] {'rows'}, dimensions={0} | all-to-all | bytes 3145728 | tf_op jit(solution)/shard_map/all_to_all | solution.py:148
  224.0 1.2 copy-done.7
  225.6 1.4 convolution_convert_fusion.1
  227.1 9.1 %all_to_all.31 = bf16[1,4,4,32,512]{4,3,1,0,2:T(8,128)(2,1)S(1)} all-to-all(bf16[1,4,4,32,512]{4,3,1,0,2:T(8,128)(2,1)S(1)} %copy.18), channel_id=1, replica_groups=mesh['tm'=16,'rows'=2] {'rows'}, dimensions={2} | all-to-all | bytes 1048576 | tf_op jit(solution)/shard_map/all_to_all | solution.py:153
  236.3 1.2 fusion.11
  (86 shorter events, 15.3 us)
Async XLA Ops:
  6.5 195.4 %copy-start = (bf16[512,1536]{1,0:T(8,128)(2,1)S(1)}, bf16[512,1536]{1,0:T(8,128)(2,1)}, u32[]{:S(2)}) copy-start(bf16[512,1536]{1,0:T(8,128)(2,1)} %param.16) | copy-start | bytes 4718596
  6.5 9.5 %copy-start.14 = (s32[128]{0:T(128)S(1)}, s32[128]{0:T(128)}, u32[]{:S(2)}) copy-start(s32[128]{0:T(128)} %param.11) | copy-start | bytes 1540
  6.5 59.2 %all-gather.4.cloned.1.call-start = ((), (), s32[]{:S(2)}) async-start(), calls=%async_computation.2 | async-start | bytes 5013504 | tf_op jit(solution)/shard_map/all_gather | solution.py:94
  7.3 117.8 %all-gather.6.cloned.1.call-start = ((), (), s32[]{:S(2)}) async-start(), calls=%async_computation.3 | async-start | bytes 1114112 | tf_op jit(solution)/shard_map/all_gather | solution.py:33
  9.9 15.8 %collective-permute-start = (bf16[8,1,32,512]{3,2,1,0:T(8,128)(2,1)S(1)}, bf16[8,1,32,512]{3,2,1,0:T(8,128)(2,1)S(1)}, u32[]{:S(2)}, u32[]{:S(2)}) collective-permute-start(bf16[8,1,32,512]{3,2,1,0:T(8,128)(2,1)S(1)} %get-tuple-element.195), channel_id=1, source_target_pairs={{0,1},{2,3},{4,5},{6,7},{8,9},{10,11},{12,13},{14,15},{16,17},{18,... | collective-permute-start | bytes 786440 | tf_op jit(solution)/shard_map/ppermute | solution.py:15
  14.7 11.0 %collective-permute-start.1 = (bf16[8,1,32,512]{3,2,1,0:T(8,128)(2,1)S(1)}, bf16[8,1,32,512]{3,2,1,0:T(8,128)(2,1)S(1)}, u32[]{:S(2)}, u32[]{:S(2)}) collective-permute-start(bf16[8,1,32,512]{3,2,1,0:T(8,128)(2,1)S(1)} %get-tuple-element.196), channel_id=1, source_target_pairs={{1,0},{3,2},{5,4},{7,6},{9,8},{11,10},{13,12},{15,14},{17,16},{19,... | collective-permute-start | bytes 786440 | tf_op jit(solution)/shard_map/ppermute | solution.py:17
  65.7 1.8 copy-start.5
  65.7 3.4 %copy-start.6 = (bf16[8,2,32,512]{3,2,1,0:T(8,128)(2,1)S(1)}, bf16[8,2,32,512]{3,2,1,0:T(8,128)(2,1)}, u32[]{:S(2)}) copy-start(bf16[8,2,32,512]{3,2,1,0:T(8,128)(2,1)} %get-tuple-element.194) | copy-start | bytes 1572868
  67.5 3.3 %copy-start.2 = (bf16[3,3,512,512]{2,3,1,0:T(8,128)(2,1)S(1)}, bf16[3,3,512,512]{2,3,1,0:T(8,128)(2,1)}, u32[]{:S(2)}) copy-start(bf16[3,3,512,512]{2,3,1,0:T(8,128)(2,1)} %all-gather.4.cloned.1.call-done) | copy-start | bytes 14155780
  69.1 1.6 copy-start.4
  70.7 1.0 copy-start.3
  73.2 1.0 copy-start.10
  74.3 2.8 %copy-start.1 = (bf16[8,2,32,512]{3,2,1,0:T(8,128)(2,1)S(1)}, bf16[8,2,32,512]{3,2,1,0:T(8,128)(2,1)}, u32[]{:S(2)}) copy-start(bf16[8,2,32,512]{3,2,1,0:T(8,128)(2,1)} %param.10) | copy-start | bytes 1572868
  74.3 2.8 %copy-start.8 = (bf16[3,512,512]{2,1,0:T(8,128)(2,1)S(1)}, bf16[3,512,512]{2,1,0:T(8,128)(2,1)}, u32[]{:S(2)}) copy-start(bf16[3,512,512]{2,1,0:T(8,128)(2,1)} %param.14) | copy-start | bytes 4718596
  74.9 3.1 %collective-permute-start.2 = (bf16[2,2,32,512]{3,2,1,0:T(8,128)(2,1)S(1)}, bf16[2,2,32,512]{3,2,1,0:T(8,128)(2,1)S(1)}, u32[]{:S(2)}, u32[]{:S(2)}) collective-permute-start(bf16[2,2,32,512]{3,2,1,0:T(8,128)(2,1)S(1)} %bitcast.187), channel_id=1, source_target_pairs={{0,2},{2,4},{4,6},{6,8},{8,10},{10,12},{12,14},{14,16},{16,18},{18... | collective-permute-start | bytes 393224 | tf_op jit(solution)/shard_map/ppermute | solution.py:27
  79.1 1.4 copy-start.15
  125.0 76.0 %copy-start.12 = (f32[64,512]{1,0:T(8,128)S(1)}, f32[64,512]{1,0:T(8,128)}, u32[]{:S(2)}) copy-start(f32[64,512]{1,0:T(8,128)} %get-tuple-element.188) | copy-start | bytes 393220
  125.0 76.1 %copy-start.11 = (f32[64,512]{1,0:T(8,128)S(1)}, f32[64,512]{1,0:T(8,128)}, u32[]{:S(2)}) copy-start(f32[64,512]{1,0:T(8,128)} %get-tuple-element.186) | copy-start | bytes 393220
  201.1 0.7 copy-start.13
  224.0 1.2 copy-start.7
  227.0 9.2 %copy-start.9 = (bf16[512,512]{1,0:T(8,128)(2,1)S(1)}, bf16[512,512]{1,0:T(8,128)(2,1)}, u32[]{:S(2)}) copy-start(bf16[512,512]{1,0:T(8,128)(2,1)} %param.17) | copy-start | bytes 1572868
Sparse Core Ops, SparseCore 0:
  9.5 56.0 all-gather.3
  80.0 40.4 all-gather.5
where the time goes:
time: 246 us; the launch traced here: 244 us
  blocking collectives  61.5 us (25%)
  other arithmetic  41.5 us (17%)
  waiting for transfers between devices  37.7 us (15%)
  between operations  32.4 us (13%)
  loops' own time  31.1 us (13%)
  local copies, waits for them, and re-layouts  18.6 us (8%)
  matrix products  13.2 us (5%)
  starting transfers between devices  8.35 us (3%)
    all_gather x1, waiting for transfers between devices, local(): piece = lax.all_gather(w_space, 'tm', axis=3, tiled=True)  36.5 us
    unnamed x1, blocking collectives  31.5 us
    another operation x1, loops' own time, entering(): return lax.fori_loop(0, length, step, start)  31.1 us
    select_n x16, other arithmetic, step(): return jax.tree.map(lambda a, b: jnp.where(reached, a, b), new, before)  24.5 us
    all_to_all x1, blocking collectives, local(): lax.all_to_all(grouped, 'rows', split_axis=0, concat_axis=2, tiled=True)  20.9 us
    gt x16, other arithmetic, join_clip(): pick = late_flag > 0  10.4 us
    dynamic_slice x16, local copies, waits for them, and re-layouts, step(): part[k].astype(own.dtype)  9.82 us
    all_to_all x1, blocking collectives, local(): lax.all_to_all(attended, 'rows', split_axis=2, concat_axis=0, tiled=True)  9.12 us
  transfers between devices with their start and end apart: 5, of which 2 were waited for; matrix products, arithmetic and copies ran while one was open for 5% of the time, Pallas kernels for 0%

commit v1 on v0

v1 whole, which is shorter than its diff:
```python
import functools

import jax
import jax.numpy as jnp
from jax import lax
from jax.experimental import pallas as pl
from jax.experimental.pallas import tpu as pltpu
from jax.sharding import PartitionSpec as P

LONGEST = 9
VMEM = pl.BlockSpec(memory_space=pltpu.VMEM)
SMEM = pl.BlockSpec(memory_space=pltpu.SMEM)
PARAMS = pltpu.CompilerParams(vmem_limit_bytes=60 << 20)
F32 = jnp.float32
BF16 = jnp.bfloat16


def dot(a, b):
    return jnp.dot(a, b, preferred_element_type=F32)


def dot_t(a, b):
    return lax.dot_general(a, b, (((1,), (1,)), ((), ())), preferred_element_type=F32)


def spot_of(device, count):
    z, y = device // 4, (device // 2) % 2
    return z + y * (count // 2 - 1 - 2 * z)


def device_at(spot, core, count):
    y = spot // (count // 4)
    return (spot + y * (count // 2 - 1 - 2 * spot)) * 4 + y * 2 + core


def ring_pairs(count):
    ring = count // 2
    pairs = []
    for spot in range(ring):
        pairs.append((device_at(spot, 0, count), device_at((spot + 1) % ring, 0, count)))
        pairs.append((device_at(spot, 1, count), device_at((spot - 1) % ring, 1, count)))
    return pairs


def gather_ring(own, count):
    ring = ring_pairs(count)
    cores = [(i, i ^ 1) for i in range(count)]
    last = count // 4
    twin = lax.ppermute(own, "tm", cores)
    found = [(own, (0, 0, 0)), (twin, (0, 0, 1))]
    straight, crossed = own, twin
    for step in range(1, last + 1):
        straight = lax.ppermute(straight, "tm", ring)
        found.append((straight, (step, 0, 0)))
        found.append((lax.ppermute(straight, "tm", cores), (step, 1, 1)))
        if step < last:
            crossed = lax.ppermute(crossed, "tm", ring)
            found.append((crossed, (step, 0, 1)))
            found.append((lax.ppermute(crossed, "tm", cores), (step, 1, 0)))
    return found


def shard_owner(tag, device, count):
    step, swapped, flip = tag
    core = device % 2
    ring = count // 2
    away = (1 - 2 * core) * ((1 - 2 * swapped) * step)
    spot = (spot_of(device, count) - away + ring) % ring
    return device_at(spot, (core + flip) % 2, count)


def prepare_kernel(tags, *refs):
    *parts, gain_ref, time_ref, wide_ref, lat_ref, head_ref, tail_ref = refs
    frames, rows, width, chans = parts[0].shape
    groups = len(parts)
    mine = lax.axis_index("rows")
    gain = gain_ref[...]
    column = lax.broadcasted_iota(jnp.int32, (rows * width, 1), 0) % width
    edge = jnp.zeros((width, 3 * chans), BF16)
    for frame in range(frames):
        wide_ref[frame, 0] = edge
        wide_ref[frame, groups * rows + 1] = edge
    for at, part in enumerate(parts):
        first = at * rows
        if groups == 2:
            first = (mine if at == 0 else 1 - mine) * rows
        for frame in range(frames):
            raw = part[frame]
            lat_ref[frame, pl.ds(first, rows)] = raw
            x = raw.reshape(rows * width, chans).astype(F32)
            y = x * lax.rsqrt(jnp.mean(x * x, axis=-1, keepdims=True) + 1e-06) * gain
            before = jnp.where(column == 0, 0.0, pltpu.roll(y, 1, 0))
            after = jnp.where(column == width - 1, 0.0, pltpu.roll(y, rows * width - 1, 0))
            for dx, v in enumerate((before, y, after)):
                wide_ref[frame, pl.ds(first + 1, rows), :, dx * chans : (dx + 1) * chans] = v.astype(
                    BF16
                ).reshape(rows, width, chans)
    block = chans // len(tags)
    device = lax.axis_index("tm")
    for slot, tag in enumerate(tags):
        owner = tag
        if isinstance(tag, tuple):
            owner = shard_owner(tag, device, len(tags))
        source = pl.ds(pl.multiple_of(owner * block, block), block)
        to_ref, at = head_ref, slot * block
        if at >= head_ref.shape[1]:
            to_ref, at = tail_ref, at - head_ref.shape[1]
        for back in range(3):
            to_ref[back, at : at + block] = time_ref[back, source]


def convolve(wide_ref, shards):
    frames, height, width, wide = wide_ref.shape
    height -= 2
    total = None
    for dy in range(3):
        weights = jnp.concatenate(
            [jnp.concatenate([shard[dy, dx] for dx in range(3)], axis=-1) for shard in shards], axis=0
        )
        lhs = wide_ref[:, dy : dy + height].reshape(frames * height * width, wide)
        part = dot_t(lhs, weights)
        total = part if total is None else total + part
    acts = (total * jax.nn.sigmoid(total)).astype(BF16)
    return acts.reshape(frames, height * width, -1)


def keep(flag, values):
    return jnp.where(flag, values, jnp.zeros_like(values))


def temporal(acts, clips, weights, frames):
    first = lax.axis_index("tm") * frames
    spots, width = acts[0].shape
    lines = []
    for t in range(frames):
        line = [acts[t]]
        for back in (1, 2):
            if t < back:
                line.append(jnp.zeros((spots, width), BF16))
            else:
                line.append(keep(clips[first + t - back] == clips[first + t], acts[t - back]))
        lines.append(jnp.concatenate(line, axis=-1))
    lhs = jnp.concatenate(lines, axis=0)
    rhs = jnp.concatenate([weights[k] for k in range(3)], axis=0)
    return dot(lhs, rhs)


def packet_sums(acts, clips, weights, frames, lat=None):
    first = lax.axis_index("tm") * frames
    end = clips.shape[0] - 1
    next0 = clips[jnp.minimum(first + frames, end)]
    next1 = clips[jnp.minimum(first + frames + 1, end)]
    spots, width = acts[0].shape
    sums = [jnp.zeros((spots, width), F32) for _ in range(3)]
    base = None if lat is None else jnp.zeros(lat[0].shape, F32)
    for t in range(frames):
        inside = clips[first + t] == next0
        if lat is not None:
            base = base + keep(inside, lat[t].astype(F32))
        for back in range(min(3, t + 1)):
            both = jnp.logical_and(inside, clips[first + t - back] == next0)
            sums[back] = sums[back] + keep(both, acts[t - back].astype(F32))
    sums = [s.astype(BF16) for s in sums]
    last0 = keep(clips[first + frames - 1] == next0, acts[frames - 1])
    prev0 = keep(clips[first + frames - 2] == next0, acts[frames - 2])
    last1 = keep(clips[first + frames - 1] == next1, acts[frames - 1])
    by0 = dot(sums[0], weights[0])
    by1 = dot(jnp.concatenate([last0, sums[1]], axis=0), weights[1])
    by2 = dot(jnp.concatenate([prev0, last1, sums[2]], axis=0), weights[2])
    total = by0 + by1[spots:] + by2[2 * spots :]
    if base is not None:
        total = total + base
    return by1[:spots] + by2[:spots], by2[spots : 2 * spots], total


def early_kernel(wide_ref, lat_ref, clips, weights, *refs):
    *shards, rest_ref, packet_ref = refs
    frames = wide_ref.shape[0]
    acts = convolve(wide_ref, shards)
    acts = [acts[t] for t in range(frames)]
    lat = [lat_ref[t].reshape(acts[0].shape[0], -1) for t in range(frames)]
    for i, part in enumerate(packet_sums(acts, clips, weights, frames, lat)):
        packet_ref[i] = part
    rest = temporal(acts, clips, weights, frames).reshape(rest_ref.shape)
    for t in range(frames):
        rest_ref[t] = rest[t] + lat[t].astype(F32)


def late_kernel(wide_ref, clips, weights, early_ref, *refs):
    *shards, acts_ref, packet_ref = refs
    frames = wide_ref.shape[0]
    acts = convolve(wide_ref, shards)
    acts_ref[...] = acts
    acts = [acts[t] for t in range(frames)]
    for i, part in enumerate(packet_sums(acts, clips, weights, frames)):
        packet_ref[i] = (early_ref[i] + part).astype(BF16)


def rest_kernel(acts_ref, clips, weights, early_ref, rest_ref):
    frames = acts_ref.shape[0]
    part = temporal([acts_ref[t] for t in range(frames)], clips, weights, frames)
    rest_ref[...] = early_ref[...] + part.reshape(rest_ref.shape)


def attend_kernel(rest_ref, packet_ref, clips, gain_ref, qkv_ref, proj_ref, out_ref, mixed_ref, normed_ref):
    frames, rows, width, chans = out_ref.shape
    height = mixed_ref.shape[1]
    spots = height * width
    own = rows * width
    first = lax.axis_index("tm") * frames
    mine = pl.ds(lax.axis_index("rows") * rows, rows)
    gain = gain_ref[...]

    number = jnp.int32(1)
    for back in range(1, LONGEST):
        at = first - back
        hit = jnp.logical_and(at >= 0, clips[jnp.maximum(at, 0)] == clips[first])
        number = number + hit.astype(jnp.int32)
    running = packet_ref[2].astype(F32)
    for t in range(frames):
        resid = rest_ref[t]
        if t < 2:
            resid = resid + packet_ref[t].astype(F32)
        if t > 0:
            same = clips[first + t] == clips[first + t - 1]
            running = keep(same, running)
            number = jnp.where(same, number + 1, 1)
        running = running + resid
        mixed = (resid + running / jnp.full((1, chans), number.astype(F32))).astype(BF16)
        mixed_ref[t] = mixed.reshape(height, width, chans)
        x = mixed.astype(F32)
        y = x * lax.rsqrt(jnp.mean(x * x, axis=-1, keepdims=True) + 1e-06) * gain
        normed_ref[t] = y.astype(BF16).reshape(height, width, chans)

    query = dot(normed_ref[:, mine].reshape(frames * own, chans), qkv_ref[:, :chans]).astype(BF16)
    both = dot(normed_ref[...].reshape(frames * spots, chans), qkv_ref[:, chans:]).astype(BF16)
    attended = []
    for t in range(frames):
        key = both[t * spots : (t + 1) * spots, :chans]
        value = both[t * spots : (t + 1) * spots, chans:]
        scores = dot_t(query[t * own : (t + 1) * own], key) * chans ** (-0.5)
        weights = jnp.exp(scores - jnp.max(scores, axis=-1, keepdims=True))
        probs = (weights / jnp.sum(weights, axis=-1, keepdims=True)).astype(BF16)
        attended.append(dot(probs, value).astype(BF16))
    result = dot(jnp.concatenate(attended, axis=0), proj_ref[...])
    result = result + mixed_ref[:, mine].reshape(frames * own, chans).astype(F32)
    out_ref[...] = result.astype(BF16).reshape(frames, rows, width, chans)


def local(latents, clip_ids, gain_in, w_space, w_time, gain_attn, w_qkv, w_out):
    frames, rows, width, chans = latents.shape
    groups, count = lax.axis_size("rows"), lax.axis_size("tm")
    height = groups * rows
    spots = height * width
    shape = jax.ShapeDtypeStruct
    assert frames + 1 >= LONGEST

    if groups == 2:
        parts = [latents, lax.ppermute(latents, "rows", [(0, 1), (1, 0)])]
    else:
        everything = lax.all_gather(latents, "rows")
        parts = [everything[i] for i in range(groups)]

    shard = jnp.transpose(w_space, (0, 1, 3, 2))
    if shard.shape[2] % 16 == 0 and count % 8 == 0:
        found = gather_ring(shard, count)
        cut = len(found) // 2
    else:
        whole = lax.all_gather(shard, "tm", axis=2, tiled=True)
        half = chans // 2
        found = [(whole[:, :, :half], 0), (whole[:, :, half:], 1)]
        cut = 1
    shards = [pair[0] for pair in found]
    tags = [pair[1] for pair in found]
    split = cut * (chans // len(tags))

    wide, lat, head, tail = pl.pallas_call(
        functools.partial(prepare_kernel, tags),
        out_shape=(
            shape((frames, height + 2, width, 3 * chans), BF16),
            shape((frames, height, width, chans), BF16),
            shape((3, split, chans), BF16),
            shape((3, chans - split, chans), BF16),
        ),
        in_specs=[VMEM] * (len(parts) + 2),
        out_specs=(VMEM, VMEM, VMEM, VMEM),
        compiler_params=PARAMS,
        name="prepare",
    )(*parts, gain_in.reshape(1, chans), w_time)

    rest, packet = pl.pallas_call(
        early_kernel,
        out_shape=(shape((frames, spots, chans), F32), shape((3, spots, chans), F32)),
        in_specs=[VMEM, VMEM, SMEM, VMEM] + [VMEM] * cut,
        out_specs=(VMEM, VMEM),
        compiler_params=PARAMS,
        name="early",
    )(wide, lat, clip_ids, head, *shards[:cut])
    acts, packet = pl.pallas_call(
        late_kernel,
        out_shape=(shape((frames, spots, chans - split), BF16), shape((3, spots, chans), BF16)),
        in_specs=[VMEM, SMEM, VMEM, VMEM] + [VMEM] * (len(tags) - cut),
        out_specs=(VMEM, VMEM),
        compiler_params=PARAMS,
        name="late",
    )(wide, clip_ids, tail, packet, *shards[cut:])
    packet = lax.ppermute(packet, "tm", [(i, i + 1) for i in range(count - 1)])
    rest = pl.pallas_call(
        rest_kernel,
        out_shape=shape((frames, spots, chans), F32),
        in_specs=[VMEM, SMEM, VMEM, VMEM],
        out_specs=VMEM,
        compiler_params=PARAMS,
        name="rest",
    )(acts, clip_ids, tail, rest)
    return pl.pallas_call(
        attend_kernel,
        out_shape=shape((frames, rows, width, chans), BF16),
        in_specs=[VMEM, VMEM, SMEM, VMEM, VMEM, VMEM],
        out_specs=VMEM,
        scratch_shapes=[
            pltpu.VMEM((frames, height, width, chans), BF16),
            pltpu.VMEM((frames, height, width, chans), BF16),
        ],
        compiler_params=PARAMS,
        name="attend",
    )(rest, packet, clip_ids, gain_attn.reshape(1, chans), w_qkv, w_out)


def solution(mesh):
    placed = (P("tm", "rows", None, None), P(), P(), P(None, None, None, "tm"), P(), P(), P(), P())
    return jax.shard_map(
        local, mesh=mesh, in_specs=placed, out_specs=P("tm", "rows", None, None), check_vma=False
    )
```

time: 246 us -> 73.3 us (0.30)
  the two profiles are of different devices: /device:TPU:0 before, /device:TPU:8 now
where the time goes in v1:
time: 73.3 us; the launch traced here: 72.5 us
  Pallas kernels  36.9 us (50%)
  waiting for transfers between devices  17.4 us (24%)
  starting transfers between devices  16.6 us (23%)
  local copies, waits for them, and re-layouts  1.55 us (2%)
    pallas_call x1, Pallas kernels, local(): pl.pallas_call(early_kernel, out_shape=(shape((frames, spots, chans), F32...  10.6 us
    pallas_call x1, Pallas kernels, local(): pl.pallas_call(attend_kernel, out_shape=shape((frames, rows, width, chans...  8.48 us
    pallas_call x1, Pallas kernels, local(): pl.pallas_call(late_kernel, out_shape=(shape((frames, spots, chans - spli...  7.54 us
    ppermute x4, waiting for transfers between devices, gather_ring(): straight = lax.ppermute(straight, 'tm', ring)  7.11 us
    ppermute x4, starting transfers between devices, gather_ring(): straight = lax.ppermute(straight, 'tm', ring)  6.31 us
    pallas_call x1, Pallas kernels, local(): pl.pallas_call(functools.partial(prepare_kernel, tags), out_shape=(shape(...  5.91 us
    ppermute x1, waiting for transfers between devices, local(): parts = [latents, lax.ppermute(latents, 'rows', [(0, 1), (1, 0)])]  4.99 us
    ppermute x3, starting transfers between devices, gather_ring(): crossed = lax.ppermute(crossed, 'tm', ring)  4.73 us
  transfers between devices with their start and end apart: 17, of which 7 were waited for; matrix products, arithmetic and copies ran while one was open for 0% of the time, Pallas kernels for 29%

profile of v1, /device:TPU:8, one launch (start us, length us, event | category | flops | bytes accessed | tf_op | source)
XLA Modules:
  0.0 72.5 jit_solution(18007782628789496011)
XLA Ops:
  0.0 0.0 collective-permute-start.1
  0.0 1.6 %collective-permute-start.2 = (bf16[3,3,32,512]{3,2,1,0:T(8,128)(2,1)}, bf16[3,3,32,512]{3,2,1,0:T(8,128)(2,1)S(1)}, u32[]{:S(2)}, u32[]{:S(2)}) collective-permute-start(bf16[3,3,32,512]{3,2,1,0:T(8,128)(2,1)} %bitcast.4), channel_id=1, source_target_pairs={{0,8},{2,6},{8,16},{10,2},{16,24},{18,10},{24,28},{26,18},{28,20},... | collective-permute-start | bytes 884744 | tf_op jit(solution)/shard_map/ppermute | solution.py:53
  1.6 0.2 collective-permute-done.1.refs_1_
  1.8 1.6 %collective-permute-start.4 = (bf16[3,3,32,512]{3,2,1,0:T(8,128)(2,1)S(1)}, bf16[3,3,32,512]{3,2,1,0:T(8,128)(2,1)S(1)}, u32[]{:S(2)}, u32[]{:S(2)}) collective-permute-start(bf16[3,3,32,512]{3,2,1,0:T(8,128)(2,1)S(1)} %collective-permute-done.1.refs_1_), channel_id=1, source_target_pairs={{0,8},{2,6},{8,16},{10,2},{16,24},{18,10},{24,28},{26,18},{28,20},... | collective-permute-start | bytes 884744 | tf_op jit(solution)/shard_map/ppermute | solution.py:57
  3.4 3.6 %collective-permute-done.2.refs_2_ = bf16[3,3,32,512]{3,2,1,0:T(8,128)(2,1)S(1)} collective-permute-done((bf16[3,3,32,512]{3,2,1,0:T(8,128)(2,1)}, bf16[3,3,32,512]{3,2,1,0:T(8,128)(2,1)S(1)}, u32[]{:S(2)}, u32[]{:S(2)}) %collective-permute-start.2) | collective-permute-done | bytes 294944 | tf_op jit(solution)/shard_map/ppermute | solution.py:53
  6.9 0.0 copy-start.4
  6.9 1.6 %collective-permute-start.6 = (bf16[3,3,32,512]{3,2,1,0:T(8,128)(2,1)S(1)}, bf16[3,3,32,512]{3,2,1,0:T(8,128)(2,1)S(1)}, u32[]{:S(2)}, u32[]{:S(2)}) collective-permute-start(bf16[3,3,32,512]{3,2,1,0:T(8,128)(2,1)S(1)} %collective-permute-done.2.refs_2_), channel_id=1, source_target_pairs={{0,8},{2,6},{8,16},{10,2},{16,24},{18,10},{24,28},{26,18},{28,20},... | collective-permute-start | bytes 884744 | tf_op jit(solution)/shard_map/ppermute | solution.py:53
  8.5 1.6 %collective-permute-done.4.refs_4_ = bf16[3,3,32,512]{3,2,1,0:T(8,128)(2,1)S(1)} collective-permute-done((bf16[3,3,32,512]{3,2,1,0:T(8,128)(2,1)S(1)}, bf16[3,3,32,512]{3,2,1,0:T(8,128)(2,1)S(1)}, u32[]{:S(2)}, u32[]{:S(2)}) %collective-permute-start.4) | collective-permute-done | bytes 294944 | tf_op jit(solution)/shard_map/ppermute | solution.py:57
  10.1 0.0 copy-start.6
  10.1 1.6 %collective-permute-start.8 = (bf16[3,3,32,512]{3,2,1,0:T(8,128)(2,1)S(1)}, bf16[3,3,32,512]{3,2,1,0:T(8,128)(2,1)S(1)}, u32[]{:S(2)}, u32[]{:S(2)}) collective-permute-start(bf16[3,3,32,512]{3,2,1,0:T(8,128)(2,1)S(1)} %collective-permute-done.4.refs_4_), channel_id=1, source_target_pairs={{0,8},{2,6},{8,16},{10,2},{16,24},{18,10},{24,28},{26,18},{28,20},... | collective-permute-start | bytes 884744 | tf_op jit(solution)/shard_map/ppermute | solution.py:57
  11.7 2.0 %collective-permute-done.6.refs_6_ = bf16[3,3,32,512]{3,2,1,0:T(8,128)(2,1)S(1)} collective-permute-done((bf16[3,3,32,512]{3,2,1,0:T(8,128)(2,1)S(1)}, bf16[3,3,32,512]{3,2,1,0:T(8,128)(2,1)S(1)}, u32[]{:S(2)}, u32[]{:S(2)}) %collective-permute-start.6) | collective-permute-done | bytes 294944 | tf_op jit(solution)/shard_map/ppermute | solution.py:53
  13.7 0.0 copy-start.7
  13.7 1.6 %collective-permute-start.10 = (bf16[3,3,32,512]{3,2,1,0:T(8,128)(2,1)S(1)}, bf16[3,3,32,512]{3,2,1,0:T(8,128)(2,1)S(1)}, u32[]{:S(2)}, u32[]{:S(2)}) collective-permute-start(bf16[3,3,32,512]{3,2,1,0:T(8,128)(2,1)S(1)} %collective-permute-done.6.refs_6_), channel_id=1, source_target_pairs={{0,8},{2,6},{8,16},{10,2},{16,24},{18,10},{24,28},{26,18},{28,20},... | collective-permute-start | bytes 884744 | tf_op jit(solution)/shard_map/ppermute | solution.py:53
  15.2 1.5 %collective-permute-start = (bf16[8,2,32,512]{3,2,1,0:T(8,128)(2,1)}, bf16[8,2,32,512]{3,2,1,0:T(8,128)(2,1)S(1)}, u32[]{:S(2)}, u32[]{:S(2)}) collective-permute-start(bf16[8,2,32,512]{3,2,1,0:T(8,128)(2,1)} %refs_0_.1), channel_id=1, source_target_pairs={{0,1},{1,0},{2,3},{3,2},{4,5},{5,4},{6,7},{7,6},{8,9},{9,8},{10,11... | collective-permute-start | bytes 1572872 | tf_op jit(solution)/shard_map/ppermute | solution.py:259
  16.7 0.0 collective-permute-start.3
  16.7 0.5 collective-permute-start.5
  17.2 0.0 collective-permute-done.8.refs_0_
  17.2 0.0 copy-start.3
  17.3 1.6 %collective-permute-start.12 = (bf16[3,3,32,512]{3,2,1,0:T(8,128)(2,1)S(1)}, bf16[3,3,32,512]{3,2,1,0:T(8,128)(2,1)S(1)}, u32[]{:S(2)}, u32[]{:S(2)}) collective-permute-start(bf16[3,3,32,512]{3,2,1,0:T(8,128)(2,1)S(1)} %collective-permute-done.8.refs_0_), channel_id=1, source_target_pairs={{0,8},{2,6},{8,16},{10,2},{16,24},{18,10},{24,28},{26,18},{28,20},... | collective-permute-start | bytes 884744 | tf_op jit(solution)/shard_map/ppermute | solution.py:57
  18.8 1.6 %collective-permute-done.10.refs_2_ = bf16[3,3,32,512]{3,2,1,0:T(8,128)(2,1)S(1)} collective-permute-done((bf16[3,3,32,512]{3,2,1,0:T(8,128)(2,1)S(1)}, bf16[3,3,32,512]{3,2,1,0:T(8,128)(2,1)S(1)}, u32[]{:S(2)}, u32[]{:S(2)}) %collective-permute-start.10) | collective-permute-done | bytes 294944 | tf_op jit(solution)/shard_map/ppermute | solution.py:53
  20.4 0.0 copy-start.5
  20.4 1.6 %collective-permute-start.14 = (bf16[3,3,32,512]{3,2,1,0:T(8,128)(2,1)S(1)}, bf16[3,3,32,512]{3,2,1,0:T(8,128)(2,1)S(1)}, u32[]{:S(2)}, u32[]{:S(2)}) collective-permute-start(bf16[3,3,32,512]{3,2,1,0:T(8,128)(2,1)S(1)} %collective-permute-done.10.refs_2_), channel_id=1, source_target_pairs={{0,8},{2,6},{8,16},{10,2},{16,24},{18,10},{24,28},{26,18},{28,20},... | collective-permute-start | bytes 884744 | tf_op jit(solution)/shard_map/ppermute | solution.py:53
  22.0 5.0 %collective-permute-done.refs_1_ = bf16[8,2,32,512]{3,2,1,0:T(8,128)(2,1)S(1)} collective-permute-done((bf16[8,2,32,512]{3,2,1,0:T(8,128)(2,1)}, bf16[8,2,32,512]{3,2,1,0:T(8,128)(2,1)S(1)}, u32[]{:S(2)}, u32[]{:S(2)}) %collective-permute-start) | collective-permute-done | bytes 524320 | tf_op jit(solution)/shard_map/ppermute | solution.py:259
  27.0 0.0 copy-start
  27.0 0.0 collective-permute-start.7
  27.0 0.0 collective-permute-done.3.refs_3_
  27.0 0.0 copy-start.10
  27.0 0.5 collective-permute-start.9
  27.5 0.0 collective-permute-done.5.refs_5_
  27.5 0.0 copy-start.11
  27.5 0.1 collective-permute-start.11
  27.6 0.0 collective-permute-done.12.refs_4_
  27.6 0.0 copy-start.8
  27.6 0.4 collective-permute-start.13
  28.0 0.0 collective-permute-done.14.refs_6_
  28.0 0.1 collective-permute-start.15
  28.1 0.0 copy-done
  28.1 5.9 %prepare.1 = (bf16[8,6,32,1536]{3,2,1,0:T(8,128)(2,1)}, bf16[8,4,32,512]{3,2,1,0:T(8,128)(2,1)}, bf16[3,256,512]{2,1,0:T(8,128)(2,1)}, bf16[3,256,512]{2,1,0:T(8,128)(2,1)}) custom-call(bf16[8,2,32,512]{3,2,1,0:T(8,128)(2,1)} %refs_0_.1, bf16[8,2,32,512]{3,2,1,0:T(8,128)(2,1)} %copy-done, f32[1,512]{1,0:T(1,128)} %bitcast.7, bf16[3,512,512]{2,1,0:T(8,128)(2,1)} %refs_3_.1), custom_call_target="tpu_custom_call" | custom-call | tf_op jit(solution)/shard_map/prepare/pallas_call | solution.py:277
  34.0 0.0 collective-permute-done.7.refs_7_
  34.0 0.0 copy-done.2
  34.0 0.0 copy-done.4
  34.0 0.0 copy-done.6
  34.0 0.0 copy-done.7
  34.0 0.0 copy-done.10
  34.0 0.0 copy-done.11
  34.1 10.6 %early.1 = (f32[8,128,512]{2,1,0:T(8,128)}, f32[3,128,512]{2,1,0:T(8,128)}) custom-call(bf16[8,6,32,1536]{3,2,1,0:T(8,128)(2,1)} %get-tuple-element.13.wide_ref, bf16[8,4,32,512]{3,2,1,0:T(8,128)(2,1)} %get-tuple-element.15.lat_ref, s32[128]{0:T(128)} %clips.7, bf16[3,256,512]{2,1,0:T(8,128)(2,1)} %get-tuple-element.16.weights, ...), custom_call_target="tpu_custom_call" | custom-call | tf_op jit(solution)/shard_map/early/pallas_call | solution.py:291
  44.7 0.0 copy-done.8
  44.7 0.0 copy-done.9
  44.7 0.0 collective-permute-done.9.refs_1_
  44.7 0.0 copy-start.12
  44.7 0.0 collective-permute-done.11.refs_3_
  44.7 0.0 copy-start.13
  44.7 0.0 collective-permute-done.13.refs_5_
  44.7 0.0 collective-permute-done.15.refs_7_
  44.7 0.0 copy-done.3
  44.7 0.0 copy-done.5
  44.7 0.6 copy-done.12
  45.4 0.1 copy-done.13
  45.5 7.5 %late.1 = (bf16[8,128,256]{2,1,0:T(8,128)(2,1)}, bf16[3,128,512]{2,1,0:T(8,128)(2,1)}) custom-call(bf16[8,6,32,1536]{3,2,1,0:T(8,128)(2,1)} %get-tuple-element.13.wide_ref, s32[128]{0:T(128)} %clips.7, bf16[3,256,512]{2,1,0:T(8,128)(2,1)} %get-tuple-element.14.weights, f32[3,128,512]{2,1,0:T(8,128)} %get-tuple-element.17.early_ref, ...), custom_call_target="tpu_custom_call" | custom-call | tf_op jit(solution)/shard_map/late/pallas_call | solution.py:299
  53.0 2.5 %collective-permute-start.16 = (bf16[3,128,512]{2,1,0:T(8,128)(2,1)}, bf16[3,128,512]{2,1,0:T(8,128)(2,1)S(1)}, u32[]{:S(2)}, u32[]{:S(2)}) collective-permute-start(bf16[3,128,512]{2,1,0:T(8,128)(2,1)} %get-tuple-element.20), channel_id=1, source_target_pairs={{0,2},{2,4},{4,6},{6,8},{8,10},{10,12},{12,14},{14,16},{16,18},{18... | collective-permute-start | bytes 1179656 | tf_op jit(solution)/shard_map/ppermute | solution.py:307
  55.5 4.3 %rest.1.rest_ref = f32[8,128,512]{2,1,0:T(8,128)} custom-call(bf16[8,128,256]{2,1,0:T(8,128)(2,1)} %get-tuple-element.18.acts_ref, s32[128]{0:T(128)} %clips.7, bf16[3,256,512]{2,1,0:T(8,128)(2,1)} %get-tuple-element.14.weights, f32[8,128,512]{2,1,0:T(8,128)} %get-tuple-element.19.early_ref), custom_call_target="tpu_custom_call" | custom-call | tf_op jit(solution)/shard_map/rest/pallas_call | solution.py:308
  59.9 3.4 %collective-permute-done.16.packet_ref = bf16[3,128,512]{2,1,0:T(8,128)(2,1)S(1)} collective-permute-done((bf16[3,128,512]{2,1,0:T(8,128)(2,1)}, bf16[3,128,512]{2,1,0:T(8,128)(2,1)S(1)}, u32[]{:S(2)}, u32[]{:S(2)}) %collective-permute-start.16) | collective-permute-done | bytes 393248 | tf_op jit(solution)/shard_map/ppermute | solution.py:307
  63.3 0.8 %copy-done.1 = bf16[3,128,512]{2,1,0:T(8,128)(2,1)} copy-done((bf16[3,128,512]{2,1,0:T(8,128)(2,1)}, bf16[3,128,512]{2,1,0:T(8,128)(2,1)S(1)}, u32[]{:S(2)}) %copy-start.1) | copy-done | bytes 393240
  64.1 8.5 %attend.1 = bf16[8,2,32,512]{3,2,1,0:T(8,128)(2,1)} custom-call(f32[8,128,512]{2,1,0:T(8,128)} %rest.1.rest_ref, bf16[3,128,512]{2,1,0:T(8,128)(2,1)} %copy-done.1, s32[128]{0:T(128)} %clips.7, f32[1,512]{1,0:T(1,128)} %bitcast.6, bf16[512,1536]{1,0:T(8,128)(2,1)} %qkv_ref.1, bf16[512,512]{1,0:T(8,128)(2,1)} %proj_ref.1), custom_call_target="tpu_custom_call" | custom-call | tf_op jit(solution)/shard_map/attend/pallas_call | solution.py:316
  (3 shorter events, 0.0 us)
Async XLA Ops:
  0.0 1.8 %collective-permute-start.1 = (bf16[3,3,32,512]{3,2,1,0:T(8,128)(2,1)}, bf16[3,3,32,512]{3,2,1,0:T(8,128)(2,1)S(1)}, u32[]{:S(2)}, u32[]{:S(2)}) collective-permute-start(bf16[3,3,32,512]{3,2,1,0:T(8,128)(2,1)} %bitcast.3), channel_id=1, source_target_pairs={{0,2},{2,0},{4,6},{6,4},{8,10},{10,8},{12,14},{14,12},{16,18},{18,... | collective-permute-start | bytes 884744 | tf_op jit(solution)/shard_map/ppermute | solution.py:49
  0.0 6.9 %collective-permute-start.2 = (bf16[3,3,32,512]{3,2,1,0:T(8,128)(2,1)}, bf16[3,3,32,512]{3,2,1,0:T(8,128)(2,1)S(1)}, u32[]{:S(2)}, u32[]{:S(2)}) collective-permute-start(bf16[3,3,32,512]{3,2,1,0:T(8,128)(2,1)} %bitcast.4), channel_id=1, source_target_pairs={{0,8},{2,6},{8,16},{10,2},{16,24},{18,10},{24,28},{26,18},{28,20},... | collective-permute-start | bytes 884744 | tf_op jit(solution)/shard_map/ppermute | solution.py:53
  1.8 32.2 %copy-start.2 = (bf16[3,3,32,512]{3,2,1,0:T(8,128)(2,1)}, bf16[3,3,32,512]{3,2,1,0:T(8,128)(2,1)S(1)}, u32[]{:S(2)}) copy-start(bf16[3,3,32,512]{3,2,1,0:T(8,128)(2,1)S(1)} %collective-permute-done.1.refs_1_) | copy-start | bytes 884740
  1.8 8.3 %collective-permute-start.4 = (bf16[3,3,32,512]{3,2,1,0:T(8,128)(2,1)S(1)}, bf16[3,3,32,512]{3,2,1,0:T(8,128)(2,1)S(1)}, u32[]{:S(2)}, u32[]{:S(2)}) collective-permute-start(bf16[3,3,32,512]{3,2,1,0:T(8,128)(2,1)S(1)} %collective-permute-done.1.refs_1_), channel_id=1, source_target_pairs={{0,8},{2,6},{8,16},{10,2},{16,24},{18,10},{24,28},{26,18},{28,20},... | collective-permute-start | bytes 884744 | tf_op jit(solution)/shard_map/ppermute | solution.py:57
  6.9 27.1 %copy-start.4 = (bf16[3,3,32,512]{3,2,1,0:T(8,128)(2,1)}, bf16[3,3,32,512]{3,2,1,0:T(8,128)(2,1)S(1)}, u32[]{:S(2)}) copy-start(bf16[3,3,32,512]{3,2,1,0:T(8,128)(2,1)S(1)} %collective-permute-done.2.refs_2_) | copy-start | bytes 884740
  6.9 6.7 %collective-permute-start.6 = (bf16[3,3,32,512]{3,2,1,0:T(8,128)(2,1)S(1)}, bf16[3,3,32,512]{3,2,1,0:T(8,128)(2,1)S(1)}, u32[]{:S(2)}, u32[]{:S(2)}) collective-permute-start(bf16[3,3,32,512]{3,2,1,0:T(8,128)(2,1)S(1)} %collective-permute-done.2.refs_2_), channel_id=1, source_target_pairs={{0,8},{2,6},{8,16},{10,2},{16,24},{18,10},{24,28},{26,18},{28,20},... | collective-permute-start | bytes 884744 | tf_op jit(solution)/shard_map/ppermute | solution.py:53
  10.1 23.9 %copy-start.6 = (bf16[3,3,32,512]{3,2,1,0:T(8,128)(2,1)}, bf16[3,3,32,512]{3,2,1,0:T(8,128)(2,1)S(1)}, u32[]{:S(2)}) copy-start(bf16[3,3,32,512]{3,2,1,0:T(8,128)(2,1)S(1)} %collective-permute-done.4.refs_4_) | copy-start | bytes 884740
  10.1 7.1 %collective-permute-start.8 = (bf16[3,3,32,512]{3,2,1,0:T(8,128)(2,1)S(1)}, bf16[3,3,32,512]{3,2,1,0:T(8,128)(2,1)S(1)}, u32[]{:S(2)}, u32[]{:S(2)}) collective-permute-start(bf16[3,3,32,512]{3,2,1,0:T(8,128)(2,1)S(1)} %collective-permute-done.4.refs_4_), channel_id=1, source_target_pairs={{0,8},{2,6},{8,16},{10,2},{16,24},{18,10},{24,28},{26,18},{28,20},... | collective-permute-start | bytes 884744 | tf_op jit(solution)/shard_map/ppermute | solution.py:57
  13.7 20.4 %copy-start.7 = (bf16[3,3,32,512]{3,2,1,0:T(8,128)(2,1)}, bf16[3,3,32,512]{3,2,1,0:T(8,128)(2,1)S(1)}, u32[]{:S(2)}) copy-start(bf16[3,3,32,512]{3,2,1,0:T(8,128)(2,1)S(1)} %collective-permute-done.6.refs_6_) | copy-start | bytes 884740
  13.7 6.7 %collective-permute-start.10 = (bf16[3,3,32,512]{3,2,1,0:T(8,128)(2,1)S(1)}, bf16[3,3,32,512]{3,2,1,0:T(8,128)(2,1)S(1)}, u32[]{:S(2)}, u32[]{:S(2)}) collective-permute-start(bf16[3,3,32,512]{3,2,1,0:T(8,128)(2,1)S(1)} %collective-permute-done.6.refs_6_), channel_id=1, source_target_pairs={{0,8},{2,6},{8,16},{10,2},{16,24},{18,10},{24,28},{26,18},{28,20},... | collective-permute-start | bytes 884744 | tf_op jit(solution)/shard_map/ppermute | solution.py:53
  15.2 11.7 %collective-permute-start = (bf16[8,2,32,512]{3,2,1,0:T(8,128)(2,1)}, bf16[8,2,32,512]{3,2,1,0:T(8,128)(2,1)S(1)}, u32[]{:S(2)}, u32[]{:S(2)}) collective-permute-start(bf16[8,2,32,512]{3,2,1,0:T(8,128)(2,1)} %refs_0_.1), channel_id=1, source_target_pairs={{0,1},{1,0},{2,3},{3,2},{4,5},{5,4},{6,7},{7,6},{8,9},{9,8},{10,11... | collective-permute-start | bytes 1572872 | tf_op jit(solution)/shard_map/ppermute | solution.py:259
  16.7 10.2 %collective-permute-start.3 = (bf16[3,3,32,512]{3,2,1,0:T(8,128)(2,1)S(1)}, bf16[3,3,32,512]{3,2,1,0:T(8,128)(2,1)S(1)}, u32[]{:S(2)}, u32[]{:S(2)}) collective-permute-start(bf16[3,3,32,512]{3,2,1,0:T(8,128)(2,1)S(1)} %collective-permute-done.2.refs_2_), channel_id=1, source_target_pairs={{0,2},{2,0},{4,6},{6,4},{8,10},{10,8},{12,14},{14,12},{16,18},{18,... | collective-permute-start | bytes 884744 | tf_op jit(solution)/shard_map/ppermute | solution.py:55
  16.7 10.7 %collective-permute-start.5 = (bf16[3,3,32,512]{3,2,1,0:T(8,128)(2,1)S(1)}, bf16[3,3,32,512]{3,2,1,0:T(8,128)(2,1)S(1)}, u32[]{:S(2)}, u32[]{:S(2)}) collective-permute-start(bf16[3,3,32,512]{3,2,1,0:T(8,128)(2,1)S(1)} %collective-permute-done.4.refs_4_), channel_id=1, source_target_pairs={{0,2},{2,0},{4,6},{6,4},{8,10},{10,8},{12,14},{14,12},{16,18},{18,... | collective-permute-start | bytes 884744 | tf_op jit(solution)/shard_map/ppermute | solution.py:59
  17.2 27.5 %copy-start.3 = (bf16[3,3,32,512]{3,2,1,0:T(8,128)(2,1)}, bf16[3,3,32,512]{3,2,1,0:T(8,128)(2,1)S(1)}, u32[]{:S(2)}) copy-start(bf16[3,3,32,512]{3,2,1,0:T(8,128)(2,1)S(1)} %collective-permute-done.8.refs_0_) | copy-start | bytes 884740
  17.3 10.3 %collective-permute-start.12 = (bf16[3,3,32,512]{3,2,1,0:T(8,128)(2,1)S(1)}, bf16[3,3,32,512]{3,2,1,0:T(8,128)(2,1)S(1)}, u32[]{:S(2)}, u32[]{:S(2)}) collective-permute-start(bf16[3,3,32,512]{3,2,1,0:T(8,128)(2,1)S(1)} %collective-permute-done.8.refs_0_), channel_id=1, source_target_pairs={{0,8},{2,6},{8,16},{10,2},{16,24},{18,10},{24,28},{26,18},{28,20},... | collective-permute-start | bytes 884744 | tf_op jit(solution)/shard_map/ppermute | solution.py:57
  20.4 24.4 %copy-start.5 = (bf16[3,3,32,512]{3,2,1,0:T(8,128)(2,1)}, bf16[3,3,32,512]{3,2,1,0:T(8,128)(2,1)S(1)}, u32[]{:S(2)}) copy-start(bf16[3,3,32,512]{3,2,1,0:T(8,128)(2,1)S(1)} %collective-permute-done.10.refs_2_) | copy-start | bytes 884740
  20.4 7.6 %collective-permute-start.14 = (bf16[3,3,32,512]{3,2,1,0:T(8,128)(2,1)S(1)}, bf16[3,3,32,512]{3,2,1,0:T(8,128)(2,1)S(1)}, u32[]{:S(2)}, u32[]{:S(2)}) collective-permute-start(bf16[3,3,32,512]{3,2,1,0:T(8,128)(2,1)S(1)} %collective-permute-done.10.refs_2_), channel_id=1, source_target_pairs={{0,8},{2,6},{8,16},{10,2},{16,24},{18,10},{24,28},{26,18},{28,20},... | collective-permute-start | bytes 884744 | tf_op jit(solution)/shard_map/ppermute | solution.py:53
  27.0 1.1 %copy-start = (bf16[8,2,32,512]{3,2,1,0:T(8,128)(2,1)}, bf16[8,2,32,512]{3,2,1,0:T(8,128)(2,1)S(1)}, u32[]{:S(2)}) copy-start(bf16[8,2,32,512]{3,2,1,0:T(8,128)(2,1)S(1)} %collective-permute-done.refs_1_) | copy-start | bytes 1572868
  27.0 7.0 %collective-permute-start.7 = (bf16[3,3,32,512]{3,2,1,0:T(8,128)(2,1)S(1)}, bf16[3,3,32,512]{3,2,1,0:T(8,128)(2,1)}, u32[]{:S(2)}, u32[]{:S(2)}) collective-permute-start(bf16[3,3,32,512]{3,2,1,0:T(8,128)(2,1)S(1)} %collective-permute-done.6.refs_6_), channel_id=1, source_target_pairs={{0,2},{2,0},{4,6},{6,4},{8,10},{10,8},{12,14},{14,12},{16,18},{18,... | collective-permute-start | bytes 884744 | tf_op jit(solution)/shard_map/ppermute | solution.py:55
  27.0 7.1 %copy-start.10 = (bf16[3,3,32,512]{3,2,1,0:T(8,128)(2,1)}, bf16[3,3,32,512]{3,2,1,0:T(8,128)(2,1)S(1)}, u32[]{:S(2)}) copy-start(bf16[3,3,32,512]{3,2,1,0:T(8,128)(2,1)S(1)} %collective-permute-done.3.refs_3_) | copy-start | bytes 884740
  27.0 17.7 %collective-permute-start.9 = (bf16[3,3,32,512]{3,2,1,0:T(8,128)(2,1)S(1)}, bf16[3,3,32,512]{3,2,1,0:T(8,128)(2,1)S(1)}, u32[]{:S(2)}, u32[]{:S(2)}) collective-permute-start(bf16[3,3,32,512]{3,2,1,0:T(8,128)(2,1)S(1)} %collective-permute-done.8.refs_0_), channel_id=1, source_target_pairs={{0,2},{2,0},{4,6},{6,4},{8,10},{10,8},{12,14},{14,12},{16,18},{18,... | collective-permute-start | bytes 884744 | tf_op jit(solution)/shard_map/ppermute | solution.py:59
  27.5 6.6 %copy-start.11 = (bf16[3,3,32,512]{3,2,1,0:T(8,128)(2,1)}, bf16[3,3,32,512]{3,2,1,0:T(8,128)(2,1)S(1)}, u32[]{:S(2)}) copy-start(bf16[3,3,32,512]{3,2,1,0:T(8,128)(2,1)S(1)} %collective-permute-done.5.refs_5_) | copy-start | bytes 884740
  27.5 17.2 %collective-permute-start.11 = (bf16[3,3,32,512]{3,2,1,0:T(8,128)(2,1)S(1)}, bf16[3,3,32,512]{3,2,1,0:T(8,128)(2,1)S(1)}, u32[]{:S(2)}, u32[]{:S(2)}) collective-permute-start(bf16[3,3,32,512]{3,2,1,0:T(8,128)(2,1)S(1)} %collective-permute-done.10.refs_2_), channel_id=1, source_target_pairs={{0,2},{2,0},{4,6},{6,4},{8,10},{10,8},{12,14},{14,12},{16,18},{18,... | collective-permute-start | bytes 884744 | tf_op jit(solution)/shard_map/ppermute | solution.py:55
  27.6 17.1 %copy-start.8 = (bf16[3,3,32,512]{3,2,1,0:T(8,128)(2,1)}, bf16[3,3,32,512]{3,2,1,0:T(8,128)(2,1)S(1)}, u32[]{:S(2)}) copy-start(bf16[3,3,32,512]{3,2,1,0:T(8,128)(2,1)S(1)} %collective-permute-done.12.refs_4_) | copy-start | bytes 884740
  27.6 17.1 %collective-permute-start.13 = (bf16[3,3,32,512]{3,2,1,0:T(8,128)(2,1)S(1)}, bf16[3,3,32,512]{3,2,1,0:T(8,128)(2,1)}, u32[]{:S(2)}, u32[]{:S(2)}) collective-permute-start(bf16[3,3,32,512]{3,2,1,0:T(8,128)(2,1)S(1)} %collective-permute-done.12.refs_4_), channel_id=1, source_target_pairs={{0,2},{2,0},{4,6},{6,4},{8,10},{10,8},{12,14},{14,12},{16,18},{18,... | collective-permute-start | bytes 884744 | tf_op jit(solution)/shard_map/ppermute | solution.py:59
  28.0 16.7 %copy-start.9 = (bf16[3,3,32,512]{3,2,1,0:T(8,128)(2,1)}, bf16[3,3,32,512]{3,2,1,0:T(8,128)(2,1)S(1)}, u32[]{:S(2)}) copy-start(bf16[3,3,32,512]{3,2,1,0:T(8,128)(2,1)S(1)} %collective-permute-done.14.refs_6_) | copy-start | bytes 884740
  28.0 16.7 %collective-permute-start.15 = (bf16[3,3,32,512]{3,2,1,0:T(8,128)(2,1)S(1)}, bf16[3,3,32,512]{3,2,1,0:T(8,128)(2,1)}, u32[]{:S(2)}, u32[]{:S(2)}) collective-permute-start(bf16[3,3,32,512]{3,2,1,0:T(8,128)(2,1)S(1)} %collective-permute-done.14.refs_6_), channel_id=1, source_target_pairs={{0,2},{2,0},{4,6},{6,4},{8,10},{10,8},{12,14},{14,12},{16,18},{18,... | collective-permute-start | bytes 884744 | tf_op jit(solution)/shard_map/ppermute | solution.py:55
  44.7 0.7 copy-start.12
  44.7 0.8 %copy-start.13 = (bf16[3,3,32,512]{3,2,1,0:T(8,128)(2,1)}, bf16[3,3,32,512]{3,2,1,0:T(8,128)(2,1)S(1)}, u32[]{:S(2)}) copy-start(bf16[3,3,32,512]{3,2,1,0:T(8,128)(2,1)S(1)} %collective-permute-done.11.refs_3_) | copy-start | bytes 884740
  53.0 10.3 %collective-permute-start.16 = (bf16[3,128,512]{2,1,0:T(8,128)(2,1)}, bf16[3,128,512]{2,1,0:T(8,128)(2,1)S(1)}, u32[]{:S(2)}, u32[]{:S(2)}) collective-permute-start(bf16[3,128,512]{2,1,0:T(8,128)(2,1)} %get-tuple-element.20), channel_id=1, source_target_pairs={{0,2},{2,4},{4,6},{6,8},{8,10},{10,12},{12,14},{14,16},{16,18},{18... | collective-permute-start | bytes 1179656 | tf_op jit(solution)/shard_map/ppermute | solution.py:307
  63.3 0.8 %copy-start.1 = (bf16[3,128,512]{2,1,0:T(8,128)(2,1)}, bf16[3,128,512]{2,1,0:T(8,128)(2,1)S(1)}, u32[]{:S(2)}) copy-start(bf16[3,128,512]{2,1,0:T(8,128)(2,1)S(1)} %collective-permute-done.16.packet_ref) | copy-start | bytes 1179652

commit v2 on v1

--- a/solution.py
+++ b/solution.py
@@ -10,7 +10,6 @@
 LONGEST = 9
 VMEM = pl.BlockSpec(memory_space=pltpu.VMEM)
 SMEM = pl.BlockSpec(memory_space=pltpu.SMEM)
-PARAMS = pltpu.CompilerParams(vmem_limit_bytes=60 << 20)
 F32 = jnp.float32
 BF16 = jnp.bfloat16
 
@@ -253,6 +252,7 @@
     height = groups * rows
     spots = height * width
     shape = jax.ShapeDtypeStruct
+    params = pltpu.CompilerParams(vmem_limit_bytes=(28 if frames * spots <= 1024 else 60) << 20)
     assert frames + 1 >= LONGEST
 
     if groups == 2:
@@ -284,7 +284,7 @@
         ),
         in_specs=[VMEM] * (len(parts) + 2),
         out_specs=(VMEM, VMEM, VMEM, VMEM),
-        compiler_params=PARAMS,
+        compiler_params=params,
         name="prepare",
     )(*parts, gain_in.reshape(1, chans), w_time)
 
@@ -293,7 +293,7 @@
         out_shape=(shape((frames, spots, chans), F32), shape((3, spots, chans), F32)),
         in_specs=[VMEM, VMEM, SMEM, VMEM] + [VMEM] * cut,
         out_specs=(VMEM, VMEM),
-        compiler_params=PARAMS,
+        compiler_params=params,
         name="early",
     )(wide, lat, clip_ids, head, *shards[:cut])
     acts, packet = pl.pallas_call(
@@ -301,7 +301,7 @@
         out_shape=(shape((frames, spots, chans - split), BF16), shape((3, spots, chans), BF16)),
         in_specs=[VMEM, SMEM, VMEM, VMEM] + [VMEM] * (len(tags) - cut),
         out_specs=(VMEM, VMEM),
-        compiler_params=PARAMS,
+        compiler_params=params,
         name="late",
     )(wide, clip_ids, tail, packet, *shards[cut:])
     packet = lax.ppermute(packet, "tm", [(i, i + 1) for i in range(count - 1)])
@@ -310,7 +310,7 @@
         out_shape=shape((frames, spots, chans), F32),
         in_specs=[VMEM, SMEM, VMEM, VMEM],
         out_specs=VMEM,
-        compiler_params=PARAMS,
+        compiler_params=params,
         name="rest",
     )(acts, clip_ids, tail, rest)
     return pl.pallas_call(
@@ -322,7 +322,7 @@
             pltpu.VMEM((frames, height, width, chans), BF16),
             pltpu.VMEM((frames, height, width, chans), BF16),
         ],
-        compiler_params=PARAMS,
+        compiler_params=params,
         name="attend",
     )(rest, packet, clip_ids, gain_attn.reshape(1, chans), w_qkv, w_out)
 

time: 73.3 us -> 60.2 us (0.82)
  Pallas kernels: 36.9 us -> 19.7 us
  waiting for transfers between devices: 17.4 us -> 20.1 us
  local copies, waits for them, and re-layouts: 1.55 us -> 3.16 us
    pallas_call x1, Pallas kernels: 5.91 us -> 1.09 us  [local(): pl.pallas_call(functools.partial(prepare_kernel, tags), out_shape=(shape(...]
    pallas_call x1, Pallas kernels: 10.6 us -> 6.33 us  [local(): pl.pallas_call(early_kernel, out_shape=(shape((frames, spots, chans), F32...]
    pallas_call x1, Pallas kernels: 7.54 us -> 3.98 us  [local(): pl.pallas_call(late_kernel, out_shape=(shape((frames, spots, chans - spli...]
    pallas_call x1, Pallas kernels: 4.34 us -> 1.52 us  [local(): pl.pallas_call(rest_kernel, out_shape=shape((frames, spots, chans), F32),...]
    ppermute x1, waiting for transfers between devices: 3.44 us -> 6.19 us  [local(): packet = lax.ppermute(packet, 'tm', [(i, i + 1) for i in range(count - 1)])]
    pallas_call x1, Pallas kernels: 8.48 us -> 6.77 us  [local(): pl.pallas_call(attend_kernel, out_shape=shape((frames, rows, width, chans...]
    unnamed x28 -> x16, local copies, waits for them, and re-layouts: 1.55 us -> 3.16 us
  transfers between devices with their start and end apart: 17 -> 17, of which waited for: 7 -> 7; matrix products, arithmetic and copies ran while one was open for 0% -> 0% of each run, Pallas kernels for 29% -> 15%
where the time goes in v2:
time: 60.2 us; the launch traced here: 59.6 us
  waiting for transfers between devices  20.1 us (33%)
  Pallas kernels  19.7 us (33%)
  starting transfers between devices  16.5 us (27%)
  local copies, waits for them, and re-layouts  3.16 us (5%)
    ppermute x4, waiting for transfers between devices, gather_ring(): straight = lax.ppermute(straight, 'tm', ring)  7.17 us
    pallas_call x1, Pallas kernels, local(): pl.pallas_call(attend_kernel, out_shape=shape((frames, rows, width, chans...  6.77 us
    ppermute x4, starting transfers between devices, gather_ring(): straight = lax.ppermute(straight, 'tm', ring)  6.36 us
    pallas_call x1, Pallas kernels, local(): pl.pallas_call(early_kernel, out_shape=(shape((frames, spots, chans), F32...  6.33 us
    ppermute x1, waiting for transfers between devices, local(): packet = lax.ppermute(packet, 'tm', [(i, i + 1) for i in range(count - 1)])  6.19 us
    ppermute x1, waiting for transfers between devices, local(): parts = [latents, lax.ppermute(latents, 'rows', [(0, 1), (1, 0)])]  4.94 us
    ppermute x3, starting transfers between devices, gather_ring(): crossed = lax.ppermute(crossed, 'tm', ring)  4.73 us
    pallas_call x1, Pallas kernels, local(): pl.pallas_call(late_kernel, out_shape=(shape((frames, spots, chans - spli...  3.98 us
  transfers between devices with their start and end apart: 17, of which 7 were waited for; matrix products, arithmetic and copies ran while one was open for 0% of the time, Pallas kernels for 15%

profile of v2, /device:TPU:8, one launch (start us, length us, event | category | flops | bytes accessed | tf_op | source)
XLA Modules:
  0.0 59.6 jit_solution(5359997676580348537)
XLA Ops:
  0.0 0.0 copy-start.5
  0.0 0.0 collective-permute-start.1
  0.0 1.6 %collective-permute-start.2 = (bf16[3,3,32,512]{3,2,1,0:T(8,128)(2,1)}, bf16[3,3,32,512]{3,2,1,0:T(8,128)(2,1)S(1)}, u32[]{:S(2)}, u32[]{:S(2)}) collective-permute-start(bf16[3,3,32,512]{3,2,1,0:T(8,128)(2,1)} %bitcast.4), channel_id=1, source_target_pairs={{0,8},{2,6},{8,16},{10,2},{16,24},{18,10},{24,28},{26,18},{28,20},... | collective-permute-start | bytes 884744 | tf_op jit(solution)/shard_map/ppermute | solution.py:52
  1.6 0.2 collective-permute-done.1.refs_1_
  1.8 1.6 %collective-permute-start.4 = (bf16[3,3,32,512]{3,2,1,0:T(8,128)(2,1)S(1)}, bf16[3,3,32,512]{3,2,1,0:T(8,128)(2,1)S(1)}, u32[]{:S(2)}, u32[]{:S(2)}) collective-permute-start(bf16[3,3,32,512]{3,2,1,0:T(8,128)(2,1)S(1)} %collective-permute-done.1.refs_1_), channel_id=1, source_target_pairs={{0,8},{2,6},{8,16},{10,2},{16,24},{18,10},{24,28},{26,18},{28,20},... | collective-permute-start | bytes 884744 | tf_op jit(solution)/shard_map/ppermute | solution.py:56
  3.4 3.6 %collective-permute-done.2.refs_2_ = bf16[3,3,32,512]{3,2,1,0:T(8,128)(2,1)S(1)} collective-permute-done((bf16[3,3,32,512]{3,2,1,0:T(8,128)(2,1)}, bf16[3,3,32,512]{3,2,1,0:T(8,128)(2,1)S(1)}, u32[]{:S(2)}, u32[]{:S(2)}) %collective-permute-start.2) | collective-permute-done | bytes 294944 | tf_op jit(solution)/shard_map/ppermute | solution.py:52
  7.0 1.6 %collective-permute-start.6 = (bf16[3,3,32,512]{3,2,1,0:T(8,128)(2,1)S(1)}, bf16[3,3,32,512]{3,2,1,0:T(8,128)(2,1)S(1)}, u32[]{:S(2)}, u32[]{:S(2)}) collective-permute-start(bf16[3,3,32,512]{3,2,1,0:T(8,128)(2,1)S(1)} %collective-permute-done.2.refs_2_), channel_id=1, source_target_pairs={{0,8},{2,6},{8,16},{10,2},{16,24},{18,10},{24,28},{26,18},{28,20},... | collective-permute-start | bytes 884744 | tf_op jit(solution)/shard_map/ppermute | solution.py:52
  8.6 1.6 %collective-permute-done.4.refs_4_ = bf16[3,3,32,512]{3,2,1,0:T(8,128)(2,1)S(1)} collective-permute-done((bf16[3,3,32,512]{3,2,1,0:T(8,128)(2,1)S(1)}, bf16[3,3,32,512]{3,2,1,0:T(8,128)(2,1)S(1)}, u32[]{:S(2)}, u32[]{:S(2)}) %collective-permute-start.4) | collective-permute-done | bytes 294944 | tf_op jit(solution)/shard_map/ppermute | solution.py:56
  10.1 1.6 %collective-permute-start.8 = (bf16[3,3,32,512]{3,2,1,0:T(8,128)(2,1)S(1)}, bf16[3,3,32,512]{3,2,1,0:T(8,128)(2,1)S(1)}, u32[]{:S(2)}, u32[]{:S(2)}) collective-permute-start(bf16[3,3,32,512]{3,2,1,0:T(8,128)(2,1)S(1)} %collective-permute-done.4.refs_4_), channel_id=1, source_target_pairs={{0,8},{2,6},{8,16},{10,2},{16,24},{18,10},{24,28},{26,18},{28,20},... | collective-permute-start | bytes 884744 | tf_op jit(solution)/shard_map/ppermute | solution.py:56
  11.7 2.0 %collective-permute-done.6.refs_6_ = bf16[3,3,32,512]{3,2,1,0:T(8,128)(2,1)S(1)} collective-permute-done((bf16[3,3,32,512]{3,2,1,0:T(8,128)(2,1)S(1)}, bf16[3,3,32,512]{3,2,1,0:T(8,128)(2,1)S(1)}, u32[]{:S(2)}, u32[]{:S(2)}) %collective-permute-start.6) | collective-permute-done | bytes 294944 | tf_op jit(solution)/shard_map/ppermute | solution.py:52
  13.7 1.6 %collective-permute-start.10 = (bf16[3,3,32,512]{3,2,1,0:T(8,128)(2,1)S(1)}, bf16[3,3,32,512]{3,2,1,0:T(8,128)(2,1)S(1)}, u32[]{:S(2)}, u32[]{:S(2)}) collective-permute-start(bf16[3,3,32,512]{3,2,1,0:T(8,128)(2,1)S(1)} %collective-permute-done.6.refs_6_), channel_id=1, source_target_pairs={{0,8},{2,6},{8,16},{10,2},{16,24},{18,10},{24,28},{26,18},{28,20},... | collective-permute-start | bytes 884744 | tf_op jit(solution)/shard_map/ppermute | solution.py:52
  15.3 1.5 %collective-permute-start = (bf16[8,2,32,512]{3,2,1,0:T(8,128)(2,1)}, bf16[8,2,32,512]{3,2,1,0:T(8,128)(2,1)S(1)}, u32[]{:S(2)}, u32[]{:S(2)}) collective-permute-start(bf16[8,2,32,512]{3,2,1,0:T(8,128)(2,1)} %refs_0_.1), channel_id=1, source_target_pairs={{0,1},{1,0},{2,3},{3,2},{4,5},{5,4},{6,7},{7,6},{8,9},{9,8},{10,11... | collective-permute-start | bytes 1572872 | tf_op jit(solution)/shard_map/ppermute | solution.py:259
  16.8 0.0 collective-permute-start.3
  16.8 0.5 collective-permute-start.5
  17.3 0.0 collective-permute-done.8.refs_0_
  17.3 1.6 %collective-permute-start.12 = (bf16[3,3,32,512]{3,2,1,0:T(8,128)(2,1)S(1)}, bf16[3,3,32,512]{3,2,1,0:T(8,128)(2,1)S(1)}, u32[]{:S(2)}, u32[]{:S(2)}) collective-permute-start(bf16[3,3,32,512]{3,2,1,0:T(8,128)(2,1)S(1)} %collective-permute-done.8.refs_0_), channel_id=1, source_target_pairs={{0,8},{2,6},{8,16},{10,2},{16,24},{18,10},{24,28},{26,18},{28,20},... | collective-permute-start | bytes 884744 | tf_op jit(solution)/shard_map/ppermute | solution.py:56
  18.9 1.6 %collective-permute-done.10.refs_2_ = bf16[3,3,32,512]{3,2,1,0:T(8,128)(2,1)S(1)} collective-permute-done((bf16[3,3,32,512]{3,2,1,0:T(8,128)(2,1)S(1)}, bf16[3,3,32,512]{3,2,1,0:T(8,128)(2,1)S(1)}, u32[]{:S(2)}, u32[]{:S(2)}) %collective-permute-start.10) | collective-permute-done | bytes 294944 | tf_op jit(solution)/shard_map/ppermute | solution.py:52
  20.4 1.6 %collective-permute-start.14 = (bf16[3,3,32,512]{3,2,1,0:T(8,128)(2,1)S(1)}, bf16[3,3,32,512]{3,2,1,0:T(8,128)(2,1)S(1)}, u32[]{:S(2)}, u32[]{:S(2)}) collective-permute-start(bf16[3,3,32,512]{3,2,1,0:T(8,128)(2,1)S(1)} %collective-permute-done.10.refs_2_), channel_id=1, source_target_pairs={{0,8},{2,6},{8,16},{10,2},{16,24},{18,10},{24,28},{26,18},{28,20},... | collective-permute-start | bytes 884744 | tf_op jit(solution)/shard_map/ppermute | solution.py:52
  22.0 4.9 %collective-permute-done.refs_1_ = bf16[8,2,32,512]{3,2,1,0:T(8,128)(2,1)S(1)} collective-permute-done((bf16[8,2,32,512]{3,2,1,0:T(8,128)(2,1)}, bf16[8,2,32,512]{3,2,1,0:T(8,128)(2,1)S(1)}, u32[]{:S(2)}, u32[]{:S(2)}) %collective-permute-start) | collective-permute-done | bytes 524320 | tf_op jit(solution)/shard_map/ppermute | solution.py:259
  27.0 0.0 collective-permute-start.7
  27.0 0.0 collective-permute-done.3.refs_3_
  27.0 0.5 collective-permute-start.9
  27.5 0.0 collective-permute-done.5.refs_5_
  27.5 0.1 collective-permute-start.11
  27.5 0.0 collective-permute-done.12.refs_4_
  27.5 0.4 collective-permute-start.13
  28.0 0.0 collective-permute-done.14.refs_6_
  28.0 0.1 collective-permute-start.15
  28.1 0.0 copy-start
  28.1 1.4 %copy-done = bf16[3,512,512]{2,1,0:T(8,128)(2,1)S(1)} copy-done((bf16[3,512,512]{2,1,0:T(8,128)(2,1)S(1)}, bf16[3,512,512]{2,1,0:T(8,128)(2,1)}, u32[]{:S(2)}) %copy-start) | copy-done | bytes 1572888
  29.5 0.0 copy-start.3
  29.5 1.0 %copy-done.3 = bf16[8,2,32,512]{3,2,1,0:T(8,128)(2,1)S(1)} copy-done((bf16[8,2,32,512]{3,2,1,0:T(8,128)(2,1)S(1)}, bf16[8,2,32,512]{3,2,1,0:T(8,128)(2,1)}, u32[]{:S(2)}) %copy-start.3) | copy-done | bytes 524312
  30.5 0.0 copy-start.7
  30.5 0.7 %copy-done.7 = f32[512]{0:T(512)S(1)} copy-done((f32[512]{0:T(512)S(1)}, f32[512]{0:T(512)}, u32[]{:S(2)}) %copy-start.7) | copy-done | bytes 2072
  31.2 0.0 copy-start.4
  31.2 1.1 %prepare.1 = (bf16[8,6,32,1536]{3,2,1,0:T(8,128)(2,1)S(1)}, bf16[8,4,32,512]{3,2,1,0:T(8,128)(2,1)S(1)}, bf16[3,256,512]{2,1,0:T(8,128)(2,1)S(1)}, bf16[3,256,512]{2,1,0:T(8,128)(2,1)S(1)}) custom-call(bf16[8,2,32,512]{3,2,1,0:T(8,128)(2,1)S(1)} %copy-done.3, bf16[8,2,32,512]{3,2,1,0:T(8,128)(2,1)S(1)} %collective-permute-done.refs_1_, ...), custom_call_target="tpu_custom_call" | custom-call | tf_op jit(solution)/shard_map/prepare/pallas_call | solution.py:277
  32.3 0.0 collective-permute-done.7.refs_7_
  32.3 0.0 copy-done.5
  32.3 0.0 copy-done.4
  32.3 6.3 %early.1 = (f32[8,128,512]{2,1,0:T(8,128)S(1)}, f32[3,128,512]{2,1,0:T(8,128)S(1)}) custom-call(bf16[8,6,32,1536]{3,2,1,0:T(8,128)(2,1)S(1)} %get-tuple-element.13.wide_ref, bf16[8,4,32,512]{3,2,1,0:T(8,128)(2,1)S(1)} %get-tuple-element.15.lat_ref, s32[128]{0:T(128)S(1)} %copy-done.5, bf16[3,256,512]{2,1,0:T(8,128)(2,1)S(1)} %get-tuple-element.16.weights, ...), custom_call_target="tpu_custom_call" | custom-call | tf_op jit(solution)/shard_map/early/pallas_call | solution.py:291
  38.7 0.0 collective-permute-done.9.refs_1_
  38.7 0.0 collective-permute-done.11.refs_3_
  38.7 0.0 collective-permute-done.13.refs_5_
  38.7 0.0 collective-permute-done.15.refs_7_
  38.7 4.0 %late.1 = (bf16[8,128,256]{2,1,0:T(8,128)(2,1)S(1)}, bf16[3,128,512]{2,1,0:T(8,128)(2,1)S(1)}) custom-call(bf16[8,6,32,1536]{3,2,1,0:T(8,128)(2,1)S(1)} %get-tuple-element.13.wide_ref, s32[128]{0:T(128)S(1)} %copy-done.5, bf16[3,256,512]{2,1,0:T(8,128)(2,1)S(1)} %get-tuple-element.14.weights, f32[3,128,512]{2,1,0:T(8,128)S(1)} %get-tuple-element.17.early_ref, ...), custom_call_target="tpu_custom_call" | custom-call | tf_op jit(solution)/shard_map/late/pallas_call | solution.py:299
  42.7 2.4 %collective-permute-start.16 = (bf16[3,128,512]{2,1,0:T(8,128)(2,1)S(1)}, bf16[3,128,512]{2,1,0:T(8,128)(2,1)S(1)}, u32[]{:S(2)}, u32[]{:S(2)}) collective-permute-start(bf16[3,128,512]{2,1,0:T(8,128)(2,1)S(1)} %get-tuple-element.20), channel_id=1, source_target_pairs={{0,2},{2,4},{4,6},{6,8},{8,10},{10,12},{12,14},{14,16},{16,18},{18... | collective-permute-start | bytes 1179656 | tf_op jit(solution)/shard_map/ppermute | solution.py:307
  45.0 0.0 copy-start.1
  45.1 0.0 copy-start.2
  45.1 0.0 copy-start.6
  45.1 1.5 %rest.1.rest_ref = f32[8,128,512]{2,1,0:T(8,128)S(1)} custom-call(bf16[8,128,256]{2,1,0:T(8,128)(2,1)S(1)} %get-tuple-element.18.acts_ref, s32[128]{0:T(128)S(1)} %copy-done.5, bf16[3,256,512]{2,1,0:T(8,128)(2,1)S(1)} %get-tuple-element.14.weights, f32[8,128,512]{2,1,0:T(8,128)S(1)} %get-tuple-element.19.early_ref), custom_call_target="tpu_custom_call" | custom-call | tf_op jit(solution)/shard_map/rest/pallas_call | solution.py:308
  46.6 6.2 %collective-permute-done.16.packet_ref = bf16[3,128,512]{2,1,0:T(8,128)(2,1)S(1)} collective-permute-done((bf16[3,128,512]{2,1,0:T(8,128)(2,1)S(1)}, bf16[3,128,512]{2,1,0:T(8,128)(2,1)S(1)}, u32[]{:S(2)}, u32[]{:S(2)}) %collective-permute-start.16) | collective-permute-done | bytes 393248 | tf_op jit(solution)/shard_map/ppermute | solution.py:307
  52.8 0.0 copy-done.1
  52.8 0.0 copy-done.2
  52.8 0.0 copy-done.6
  52.8 6.8 %attend.1 = bf16[8,2,32,512]{3,2,1,0:T(8,128)(2,1)} custom-call(f32[8,128,512]{2,1,0:T(8,128)S(1)} %rest.1.rest_ref, bf16[3,128,512]{2,1,0:T(8,128)(2,1)S(1)} %collective-permute-done.16.packet_ref, s32[128]{0:T(128)S(1)} %copy-done.5, f32[1,512]{1,0:T(1,128)S(1)} %bitcast.6, bf16[512,1536]{1,0:T(8,128)(2,1)S(1)} %copy-done.1, bf16[512,512]{1,0:T(8,128)(2,1)S(1)} %copy-done.2), custom_call_target="tpu_custom_call" | custom-call | tf_op jit(solution)/shard_map/attend/pallas_call | solution.py:316
Async XLA Ops:
  0.0 32.3 %copy-start.5 = (s32[128]{0:T(128)S(1)}, s32[128]{0:T(128)}, u32[]{:S(2)}) copy-start(s32[128]{0:T(128)} %clips.7) | copy-start | bytes 1540
  0.0 1.8 %collective-permute-start.1 = (bf16[3,3,32,512]{3,2,1,0:T(8,128)(2,1)}, bf16[3,3,32,512]{3,2,1,0:T(8,128)(2,1)S(1)}, u32[]{:S(2)}, u32[]{:S(2)}) collective-permute-start(bf16[3,3,32,512]{3,2,1,0:T(8,128)(2,1)} %bitcast.3), channel_id=1, source_target_pairs={{0,2},{2,0},{4,6},{6,4},{8,10},{10,8},{12,14},{14,12},{16,18},{18,... | collective-permute-start | bytes 884744 | tf_op jit(solution)/shard_map/ppermute | solution.py:48
  0.0 7.0 %collective-permute-start.2 = (bf16[3,3,32,512]{3,2,1,0:T(8,128)(2,1)}, bf16[3,3,32,512]{3,2,1,0:T(8,128)(2,1)S(1)}, u32[]{:S(2)}, u32[]{:S(2)}) collective-permute-start(bf16[3,3,32,512]{3,2,1,0:T(8,128)(2,1)} %bitcast.4), channel_id=1, source_target_pairs={{0,8},{2,6},{8,16},{10,2},{16,24},{18,10},{24,28},{26,18},{28,20},... | collective-permute-start | bytes 884744 | tf_op jit(solution)/shard_map/ppermute | solution.py:52
  1.8 8.4 %collective-permute-start.4 = (bf16[3,3,32,512]{3,2,1,0:T(8,128)(2,1)S(1)}, bf16[3,3,32,512]{3,2,1,0:T(8,128)(2,1)S(1)}, u32[]{:S(2)}, u32[]{:S(2)}) collective-permute-start(bf16[3,3,32,512]{3,2,1,0:T(8,128)(2,1)S(1)} %collective-permute-done.1.refs_1_), channel_id=1, source_target_pairs={{0,8},{2,6},{8,16},{10,2},{16,24},{18,10},{24,28},{26,18},{28,20},... | collective-permute-start | bytes 884744 | tf_op jit(solution)/shard_map/ppermute | solution.py:56
  7.0 6.7 %collective-permute-start.6 = (bf16[3,3,32,512]{3,2,1,0:T(8,128)(2,1)S(1)}, bf16[3,3,32,512]{3,2,1,0:T(8,128)(2,1)S(1)}, u32[]{:S(2)}, u32[]{:S(2)}) collective-permute-start(bf16[3,3,32,512]{3,2,1,0:T(8,128)(2,1)S(1)} %collective-permute-done.2.refs_2_), channel_id=1, source_target_pairs={{0,8},{2,6},{8,16},{10,2},{16,24},{18,10},{24,28},{26,18},{28,20},... | collective-permute-start | bytes 884744 | tf_op jit(solution)/shard_map/ppermute | solution.py:52
  10.1 7.1 %collective-permute-start.8 = (bf16[3,3,32,512]{3,2,1,0:T(8,128)(2,1)S(1)}, bf16[3,3,32,512]{3,2,1,0:T(8,128)(2,1)S(1)}, u32[]{:S(2)}, u32[]{:S(2)}) collective-permute-start(bf16[3,3,32,512]{3,2,1,0:T(8,128)(2,1)S(1)} %collective-permute-done.4.refs_4_), channel_id=1, source_target_pairs={{0,8},{2,6},{8,16},{10,2},{16,24},{18,10},{24,28},{26,18},{28,20},... | collective-permute-start | bytes 884744 | tf_op jit(solution)/shard_map/ppermute | solution.py:56
  13.7 6.7 %collective-permute-start.10 = (bf16[3,3,32,512]{3,2,1,0:T(8,128)(2,1)S(1)}, bf16[3,3,32,512]{3,2,1,0:T(8,128)(2,1)S(1)}, u32[]{:S(2)}, u32[]{:S(2)}) collective-permute-start(bf16[3,3,32,512]{3,2,1,0:T(8,128)(2,1)S(1)} %collective-permute-done.6.refs_6_), channel_id=1, source_target_pairs={{0,8},{2,6},{8,16},{10,2},{16,24},{18,10},{24,28},{26,18},{28,20},... | collective-permute-start | bytes 884744 | tf_op jit(solution)/shard_map/ppermute | solution.py:52
  15.3 11.7 %collective-permute-start = (bf16[8,2,32,512]{3,2,1,0:T(8,128)(2,1)}, bf16[8,2,32,512]{3,2,1,0:T(8,128)(2,1)S(1)}, u32[]{:S(2)}, u32[]{:S(2)}) collective-permute-start(bf16[8,2,32,512]{3,2,1,0:T(8,128)(2,1)} %refs_0_.1), channel_id=1, source_target_pairs={{0,1},{1,0},{2,3},{3,2},{4,5},{5,4},{6,7},{7,6},{8,9},{9,8},{10,11... | collective-permute-start | bytes 1572872 | tf_op jit(solution)/shard_map/ppermute | solution.py:259
  16.8 10.2 %collective-permute-start.3 = (bf16[3,3,32,512]{3,2,1,0:T(8,128)(2,1)S(1)}, bf16[3,3,32,512]{3,2,1,0:T(8,128)(2,1)S(1)}, u32[]{:S(2)}, u32[]{:S(2)}) collective-permute-start(bf16[3,3,32,512]{3,2,1,0:T(8,128)(2,1)S(1)} %collective-permute-done.2.refs_2_), channel_id=1, source_target_pairs={{0,2},{2,0},{4,6},{6,4},{8,10},{10,8},{12,14},{14,12},{16,18},{18,... | collective-permute-start | bytes 884744 | tf_op jit(solution)/shard_map/ppermute | solution.py:54
  16.8 10.7 %collective-permute-start.5 = (bf16[3,3,32,512]{3,2,1,0:T(8,128)(2,1)S(1)}, bf16[3,3,32,512]{3,2,1,0:T(8,128)(2,1)S(1)}, u32[]{:S(2)}, u32[]{:S(2)}) collective-permute-start(bf16[3,3,32,512]{3,2,1,0:T(8,128)(2,1)S(1)} %collective-permute-done.4.refs_4_), channel_id=1, source_target_pairs={{0,2},{2,0},{4,6},{6,4},{8,10},{10,8},{12,14},{14,12},{16,18},{18,... | collective-permute-start | bytes 884744 | tf_op jit(solution)/shard_map/ppermute | solution.py:58
  17.3 10.3 %collective-permute-start.12 = (bf16[3,3,32,512]{3,2,1,0:T(8,128)(2,1)S(1)}, bf16[3,3,32,512]{3,2,1,0:T(8,128)(2,1)S(1)}, u32[]{:S(2)}, u32[]{:S(2)}) collective-permute-start(bf16[3,3,32,512]{3,2,1,0:T(8,128)(2,1)S(1)} %collective-permute-done.8.refs_0_), channel_id=1, source_target_pairs={{0,8},{2,6},{8,16},{10,2},{16,24},{18,10},{24,28},{26,18},{28,20},... | collective-permute-start | bytes 884744 | tf_op jit(solution)/shard_map/ppermute | solution.py:56
  20.4 7.6 %collective-permute-start.14 = (bf16[3,3,32,512]{3,2,1,0:T(8,128)(2,1)S(1)}, bf16[3,3,32,512]{3,2,1,0:T(8,128)(2,1)S(1)}, u32[]{:S(2)}, u32[]{:S(2)}) collective-permute-start(bf16[3,3,32,512]{3,2,1,0:T(8,128)(2,1)S(1)} %collective-permute-done.10.refs_2_), channel_id=1, source_target_pairs={{0,8},{2,6},{8,16},{10,2},{16,24},{18,10},{24,28},{26,18},{28,20},... | collective-permute-start | bytes 884744 | tf_op jit(solution)/shard_map/ppermute | solution.py:52
  27.0 5.3 %collective-permute-start.7 = (bf16[3,3,32,512]{3,2,1,0:T(8,128)(2,1)S(1)}, bf16[3,3,32,512]{3,2,1,0:T(8,128)(2,1)S(1)}, u32[]{:S(2)}, u32[]{:S(2)}) collective-permute-start(bf16[3,3,32,512]{3,2,1,0:T(8,128)(2,1)S(1)} %collective-permute-done.6.refs_6_), channel_id=1, source_target_pairs={{0,2},{2,0},{4,6},{6,4},{8,10},{10,8},{12,14},{14,12},{16,18},{18,... | collective-permute-start | bytes 884744 | tf_op jit(solution)/shard_map/ppermute | solution.py:54
  27.0 11.7 %collective-permute-start.9 = (bf16[3,3,32,512]{3,2,1,0:T(8,128)(2,1)S(1)}, bf16[3,3,32,512]{3,2,1,0:T(8,128)(2,1)S(1)}, u32[]{:S(2)}, u32[]{:S(2)}) collective-permute-start(bf16[3,3,32,512]{3,2,1,0:T(8,128)(2,1)S(1)} %collective-permute-done.8.refs_0_), channel_id=1, source_target_pairs={{0,2},{2,0},{4,6},{6,4},{8,10},{10,8},{12,14},{14,12},{16,18},{18,... | collective-permute-start | bytes 884744 | tf_op jit(solution)/shard_map/ppermute | solution.py:58
  27.5 11.2 %collective-permute-start.11 = (bf16[3,3,32,512]{3,2,1,0:T(8,128)(2,1)S(1)}, bf16[3,3,32,512]{3,2,1,0:T(8,128)(2,1)S(1)}, u32[]{:S(2)}, u32[]{:S(2)}) collective-permute-start(bf16[3,3,32,512]{3,2,1,0:T(8,128)(2,1)S(1)} %collective-permute-done.10.refs_2_), channel_id=1, source_target_pairs={{0,2},{2,0},{4,6},{6,4},{8,10},{10,8},{12,14},{14,12},{16,18},{18,... | collective-permute-start | bytes 884744 | tf_op jit(solution)/shard_map/ppermute | solution.py:54
  27.5 11.1 %collective-permute-start.13 = (bf16[3,3,32,512]{3,2,1,0:T(8,128)(2,1)S(1)}, bf16[3,3,32,512]{3,2,1,0:T(8,128)(2,1)S(1)}, u32[]{:S(2)}, u32[]{:S(2)}) collective-permute-start(bf16[3,3,32,512]{3,2,1,0:T(8,128)(2,1)S(1)} %collective-permute-done.12.refs_4_), channel_id=1, source_target_pairs={{0,2},{2,0},{4,6},{6,4},{8,10},{10,8},{12,14},{14,12},{16,18},{18,... | collective-permute-start | bytes 884744 | tf_op jit(solution)/shard_map/ppermute | solution.py:58
  28.0 10.7 %collective-permute-start.15 = (bf16[3,3,32,512]{3,2,1,0:T(8,128)(2,1)S(1)}, bf16[3,3,32,512]{3,2,1,0:T(8,128)(2,1)S(1)}, u32[]{:S(2)}, u32[]{:S(2)}) collective-permute-start(bf16[3,3,32,512]{3,2,1,0:T(8,128)(2,1)S(1)} %collective-permute-done.14.refs_6_), channel_id=1, source_target_pairs={{0,2},{2,0},{4,6},{6,4},{8,10},{10,8},{12,14},{14,12},{16,18},{18,... | collective-permute-start | bytes 884744 | tf_op jit(solution)/shard_map/ppermute | solution.py:54
  28.1 1.4 %copy-start = (bf16[3,512,512]{2,1,0:T(8,128)(2,1)S(1)}, bf16[3,512,512]{2,1,0:T(8,128)(2,1)}, u32[]{:S(2)}) copy-start(bf16[3,512,512]{2,1,0:T(8,128)(2,1)} %refs_3_.1) | copy-start | bytes 4718596
  29.5 1.0 %copy-start.3 = (bf16[8,2,32,512]{3,2,1,0:T(8,128)(2,1)S(1)}, bf16[8,2,32,512]{3,2,1,0:T(8,128)(2,1)}, u32[]{:S(2)}) copy-start(bf16[8,2,32,512]{3,2,1,0:T(8,128)(2,1)} %refs_0_.1) | copy-start | bytes 1572868
  30.5 0.7 %copy-start.7 = (f32[512]{0:T(512)S(1)}, f32[512]{0:T(512)}, u32[]{:S(2)}) copy-start(f32[512]{0:T(512)} %param.10) | copy-start | bytes 6148
  31.2 1.1 %copy-start.4 = (bf16[3,3,512,32]{2,3,1,0:T(8,128)(2,1)S(1)}, bf16[3,3,512,32]{2,3,1,0:T(8,128)(2,1)}, u32[]{:S(2)}) copy-start(bf16[3,3,512,32]{2,3,1,0:T(8,128)(2,1)} %param.11) | copy-start | bytes 884740
  42.7 10.1 %collective-permute-start.16 = (bf16[3,128,512]{2,1,0:T(8,128)(2,1)S(1)}, bf16[3,128,512]{2,1,0:T(8,128)(2,1)S(1)}, u32[]{:S(2)}, u32[]{:S(2)}) collective-permute-start(bf16[3,128,512]{2,1,0:T(8,128)(2,1)S(1)} %get-tuple-element.20), channel_id=1, source_target_pairs={{0,2},{2,4},{4,6},{6,8},{8,10},{10,12},{12,14},{14,16},{16,18},{18... | collective-permute-start | bytes 1179656 | tf_op jit(solution)/shard_map/ppermute | solution.py:307
  45.0 7.8 %copy-start.1 = (bf16[512,1536]{1,0:T(8,128)(2,1)S(1)}, bf16[512,1536]{1,0:T(8,128)(2,1)}, u32[]{:S(2)}) copy-start(bf16[512,1536]{1,0:T(8,128)(2,1)} %qkv_ref.1) | copy-start | bytes 4718596
  45.1 7.7 %copy-start.2 = (bf16[512,512]{1,0:T(8,128)(2,1)S(1)}, bf16[512,512]{1,0:T(8,128)(2,1)}, u32[]{:S(2)}) copy-start(bf16[512,512]{1,0:T(8,128)(2,1)} %proj_ref.1) | copy-start | bytes 1572868
  45.1 7.7 %copy-start.6 = (f32[512]{0:T(512)S(1)}, f32[512]{0:T(512)}, u32[]{:S(2)}) copy-start(f32[512]{0:T(512)} %param.13) | copy-start | bytes 6148

commit v3 on v2

--- a/solution.py
+++ b/solution.py
@@ -41,21 +41,30 @@
     return pairs
 
 
-def gather_ring(own, count):
+def ring_tags(count):
+    tags = [(0, 0, 0), (0, 0, 1)]
+    for step in range(1, count // 4 + 1):
+        tags += [(step, 0, 0), (step, 1, 1)]
+        if step < count // 4:
+            tags += [(step, 0, 1), (step, 1, 0)]
+    return tags
+
+
+def gather_ring(own, count, gates):
     ring = ring_pairs(count)
     cores = [(i, i ^ 1) for i in range(count)]
     last = count // 4
     twin = lax.ppermute(own, "tm", cores)
-    found = [(own, (0, 0, 0)), (twin, (0, 0, 1))]
-    straight, crossed = own, twin
+    found = [own, twin]
+    streams = [own, twin]
     for step in range(1, last + 1):
-        straight = lax.ppermute(straight, "tm", ring)
-        found.append((straight, (step, 0, 0)))
-        found.append((lax.ppermute(straight, "tm", cores), (step, 1, 1)))
-        if step < last:
-            crossed = lax.ppermute(crossed, "tm", ring)
-            found.append((crossed, (step, 0, 1)))
-            found.append((lax.ppermute(crossed, "tm", cores), (step, 1, 0)))
+        for stream in range(2 if step < last else 1):
+            gate = gates.get((stream, step))
+            if gate is not None:
+                streams[stream] = lax.optimization_barrier((streams[stream], gate(found)))[0]
+            streams[stream] = lax.ppermute(streams[stream], "tm", ring)
+            found.append(streams[stream])
+            found.append(lax.ppermute(streams[stream], "tm", cores))
     return found
 
 
@@ -68,8 +77,8 @@
     return device_at(spot, (core + flip) % 2, count)
 
 
-def prepare_kernel(tags, *refs):
-    *parts, gain_ref, time_ref, wide_ref, lat_ref, head_ref, tail_ref = refs
+def prepare_kernel(*refs):
+    *parts, gain_ref, wide_ref, lat_ref = refs
     frames, rows, width, chans = parts[0].shape
     groups = len(parts)
     mine = lax.axis_index("rows")
@@ -94,7 +103,10 @@
                 wide_ref[frame, pl.ds(first + 1, rows), :, dx * chans : (dx + 1) * chans] = v.astype(
                     BF16
                 ).reshape(rows, width, chans)
-    block = chans // len(tags)
+
+
+def order_kernel(tags, time_ref, head_ref, tail_ref):
+    block = time_ref.shape[1] // len(tags)
     device = lax.axis_index("tm")
     for slot, tag in enumerate(tags):
         owner = tag
@@ -172,12 +184,15 @@
     return by1[:spots] + by2[:spots], by2[spots : 2 * spots], total
 
 
-def early_kernel(wide_ref, lat_ref, clips, weights, *refs):
-    *shards, rest_ref, packet_ref = refs
-    frames = wide_ref.shape[0]
-    acts = convolve(wide_ref, shards)
-    acts = [acts[t] for t in range(frames)]
-    lat = [lat_ref[t].reshape(acts[0].shape[0], -1) for t in range(frames)]
+def early_kernel(wide_ref, *refs):
+    *shards, acts_ref = refs
+    acts_ref[...] = convolve(wide_ref, shards)
+
+
+def first_kernel(lat0_ref, lat1_ref, acts0_ref, acts1_ref, clips, weights, rest_ref, packet_ref):
+    acts = [ref[t] for ref in (acts0_ref, acts1_ref) for t in range(ref.shape[0])]
+    lat = [ref[t].reshape(acts[0].shape[0], -1) for ref in (lat0_ref, lat1_ref) for t in range(ref.shape[0])]
+    frames = len(acts)
     for i, part in enumerate(packet_sums(acts, clips, weights, frames, lat)):
         packet_ref[i] = part
     rest = temporal(acts, clips, weights, frames).reshape(rest_ref.shape)
@@ -185,12 +200,12 @@
         rest_ref[t] = rest[t] + lat[t].astype(F32)
 
 
-def late_kernel(wide_ref, clips, weights, early_ref, *refs):
+def late_kernel(wide0_ref, wide1_ref, clips, weights, early_ref, *refs):
     *shards, acts_ref, packet_ref = refs
-    frames = wide_ref.shape[0]
-    acts = convolve(wide_ref, shards)
-    acts_ref[...] = acts
-    acts = [acts[t] for t in range(frames)]
+    half, frames = wide0_ref.shape[0], acts_ref.shape[0]
+    acts_ref[:half] = convolve(wide0_ref, shards)
+    acts_ref[half:] = convolve(wide1_ref, shards)
+    acts = [acts_ref[t] for t in range(frames)]
     for i, part in enumerate(packet_sums(acts, clips, weights, frames)):
         packet_ref[i] = (early_ref[i] + part).astype(BF16)
 
@@ -255,55 +270,92 @@
     params = pltpu.CompilerParams(vmem_limit_bytes=(28 if frames * spots <= 1024 else 60) << 20)
     assert frames + 1 >= LONGEST
 
+    half = frames // 2
+    halves = [latents[:half], latents[half:]]
     if groups == 2:
-        parts = [latents, lax.ppermute(latents, "rows", [(0, 1), (1, 0)])]
+        swap = [(0, 1), (1, 0)]
+        others = [lax.ppermute(part, "rows", swap) for part in halves]
+        parts = [[own, other] for own, other in zip(halves, others)]
     else:
-        everything = lax.all_gather(latents, "rows")
-        parts = [everything[i] for i in range(groups)]
+        everything = [lax.all_gather(part, "rows") for part in halves]
+        parts = [[part[i] for i in range(groups)] for part in everything]
 
     shard = jnp.transpose(w_space, (0, 1, 3, 2))
-    if shard.shape[2] % 16 == 0 and count % 8 == 0:
-        found = gather_ring(shard, count)
-        cut = len(found) // 2
+    ringed = shard.shape[2] % 16 == 0 and count % 8 == 0
+    tags = ring_tags(count) if ringed else [0, 1]
+    cut = len(tags) // 2
+    split = cut * (chans // len(tags))
+
+    gain = gain_in.reshape(1, chans)
+    prepared = [
+        pl.pallas_call(
+            prepare_kernel,
+            out_shape=(
+                shape((half, height + 2, width, 3 * chans), BF16),
+                shape((half, height, width, chans), BF16),
+            ),
+            in_specs=[VMEM] * (groups + 1),
+            out_specs=(VMEM, VMEM),
+            compiler_params=params,
+            name="prepare",
+        )(*part, gain)
+        for part in parts
+    ]
+    wides = [pair[0] for pair in prepared]
+    lats = [pair[1] for pair in prepared]
+    head, tail = pl.pallas_call(
+        functools.partial(order_kernel, tags),
+        out_shape=(shape((3, split, chans), BF16), shape((3, chans - split, chans), BF16)),
+        in_specs=[VMEM],
+        out_specs=(VMEM, VMEM),
+        compiler_params=params,
+        name="order",
+    )(w_time)
+
+    acts = [None, None]
+
+    def early(which, shards):
+        acts[which] = pl.pallas_call(
+            early_kernel,
+            out_shape=shape((half, spots, split), BF16),
+            in_specs=[VMEM] * (1 + cut),
+            out_specs=VMEM,
+            compiler_params=params,
+            name="early",
+        )(wides[which], *shards[:cut])
+        return acts[which]
+
+    if ringed:
+        last = count // 4
+        gates = {
+            (1, 2): lambda found: parts[0][1],
+            (0, last - 1): lambda found: parts[1][1],
+            (1, last - 1): functools.partial(early, 0),
+            (0, last): functools.partial(early, 1),
+        }
+        shards = gather_ring(shard, count, gates)
     else:
         whole = lax.all_gather(shard, "tm", axis=2, tiled=True)
-        half = chans // 2
-        found = [(whole[:, :, :half], 0), (whole[:, :, half:], 1)]
-        cut = 1
-    shards = [pair[0] for pair in found]
-    tags = [pair[1] for pair in found]
-    split = cut * (chans // len(tags))
-
-    wide, lat, head, tail = pl.pallas_call(
-        functools.partial(prepare_kernel, tags),
-        out_shape=(
-            shape((frames, height + 2, width, 3 * chans), BF16),
-            shape((frames, height, width, chans), BF16),
-            shape((3, split, chans), BF16),
-            shape((3, chans - split, chans), BF16),
-        ),
-        in_specs=[VMEM] * (len(parts) + 2),
-        out_specs=(VMEM, VMEM, VMEM, VMEM),
-        compiler_params=params,
-        name="prepare",
-    )(*parts, gain_in.reshape(1, chans), w_time)
+        shards = [whole[:, :, :split], whole[:, :, split:]]
+        early(0, shards)
+        early(1, shards)
 
     rest, packet = pl.pallas_call(
-        early_kernel,
+        first_kernel,
         out_shape=(shape((frames, spots, chans), F32), shape((3, spots, chans), F32)),
-        in_specs=[VMEM, VMEM, SMEM, VMEM] + [VMEM] * cut,
+        in_specs=[VMEM] * 4 + [SMEM, VMEM],
         out_specs=(VMEM, VMEM),
         compiler_params=params,
-        name="early",
-    )(wide, lat, clip_ids, head, *shards[:cut])
+        name="first",
+    )(*lats, *acts, clip_ids, head)
     acts, packet = pl.pallas_call(
         late_kernel,
         out_shape=(shape((frames, spots, chans - split), BF16), shape((3, spots, chans), BF16)),
-        in_specs=[VMEM, SMEM, VMEM, VMEM] + [VMEM] * (len(tags) - cut),
+        in_specs=[VMEM, VMEM, SMEM, VMEM, VMEM] + [VMEM] * (len(tags) - cut),
         out_specs=(VMEM, VMEM),
         compiler_params=params,
         name="late",
-    )(wide, clip_ids, tail, packet, *shards[cut:])
+    )(*wides, clip_ids, tail, packet, *shards[cut:])
     packet = lax.ppermute(packet, "tm", [(i, i + 1) for i in range(count - 1)])
     rest = pl.pallas_call(
         rest_kernel,

time: 60.2 us -> 59.1 us (0.982)
  Pallas kernels: 19.7 us -> 17.7 us
  waiting for transfers between devices: 20.1 us -> 22.1 us
  local copies, waits for them, and re-layouts: 3.16 us -> 1.78 us
    unnamed x16 -> x14, local copies, waits for them, and re-layouts: 3.16 us -> 0.71 us
    ppermute x15 -> x16, waiting for transfers between devices: 13.7 us -> 15.9 us  [the longest x7 9.8 us: gather_ring(): streams[stream] = lax.ppermute(streams[stream], 'tm', ring)]
    pallas_call x2 -> x6, Pallas kernels: 7.42 us -> 5.87 us  [the longest x2 2.85 us: early(): pl.pallas_call(early_kernel, out_shape=shape((half, spots, split), BF16),...]
    slice x0 -> x1, local copies, waits for them, and re-layouts: none -> 1.07 us  [local(): halves = [latents[:half], latents[half:]]]
    ppermute x15 -> x16, starting transfers between devices: 14.2 us -> 14.6 us  [the longest x7 11.5 us: gather_ring(): streams[stream] = lax.ppermute(streams[stream], 'tm', ring)]
  transfers between devices with their start and end apart: 17 -> 18, of which waited for: 7 -> 8; matrix products, arithmetic and copies ran while one was open for 0% -> 2% of each run, Pallas kernels for 15% -> 13%
where the time goes in v3:
time: 59.1 us; the launch traced here: 58.9 us
  waiting for transfers between devices  22.1 us (37%)
  Pallas kernels  17.7 us (30%)
  starting transfers between devices  17 us (29%)
  local copies, waits for them, and re-layouts  1.78 us (3%)
    ppermute x7, starting transfers between devices, gather_ring(): streams[stream] = lax.ppermute(streams[stream], 'tm', ring)  11.5 us
    ppermute x7, waiting for transfers between devices, gather_ring(): streams[stream] = lax.ppermute(streams[stream], 'tm', ring)  9.8 us
    pallas_call x1, Pallas kernels, local(): pl.pallas_call(attend_kernel, out_shape=shape((frames, rows, width, chans...  6.78 us
    ppermute x2, waiting for transfers between devices, local(): others = [lax.ppermute(part, 'rows', swap) for part in halves]  6.11 us
    ppermute x1, waiting for transfers between devices, local(): packet = lax.ppermute(packet, 'tm', [(i, i + 1) for i in range(count - 1)])  6.05 us
    pallas_call x1, Pallas kernels, local(): pl.pallas_call(late_kernel, out_shape=(shape((frames, spots, chans - spli...  3.58 us
    pallas_call x2, Pallas kernels, early(): pl.pallas_call(early_kernel, out_shape=shape((half, spots, split), BF16),...  2.85 us
    ppermute x1, starting transfers between devices, local(): packet = lax.ppermute(packet, 'tm', [(i, i + 1) for i in range(count - 1)])  2.39 us
  transfers between devices with their start and end apart: 18, of which 8 were waited for; matrix products, arithmetic and copies ran while one was open for 2% of the time, Pallas kernels for 13%

profile of v3, /device:TPU:8, one launch (start us, length us, event | category | flops | bytes accessed | tf_op | source)
XLA Modules:
  0.0 58.9 jit_solution(4749735917831891672)
XLA Ops:
  0.0 0.0 copy-start.2
  0.0 0.0 collective-permute-start.2
  0.0 1.6 %collective-permute-start.3 = (bf16[3,3,32,512]{3,2,1,0:T(8,128)(2,1)}, bf16[3,3,32,512]{3,2,1,0:T(8,128)(2,1)S(1)}, u32[]{:S(2)}, u32[]{:S(2)}) collective-permute-start(bf16[3,3,32,512]{3,2,1,0:T(8,128)(2,1)} %bitcast.4), channel_id=1, source_target_pairs={{0,8},{2,6},{8,16},{10,2},{16,24},{18,10},{24,28},{26,18},{28,20},... | collective-permute-start | bytes 884744 | tf_op jit(solution)/shard_map/ppermute | solution.py:65
  1.6 0.2 collective-permute-done.2.refs_1_
  1.8 1.6 %collective-permute-start.5 = (bf16[3,3,32,512]{3,2,1,0:T(8,128)(2,1)S(1)}, bf16[3,3,32,512]{3,2,1,0:T(8,128)(2,1)S(1)}, u32[]{:S(2)}, u32[]{:S(2)}) collective-permute-start(bf16[3,3,32,512]{3,2,1,0:T(8,128)(2,1)S(1)} %collective-permute-done.2.refs_1_), channel_id=1, source_target_pairs={{0,8},{2,6},{8,16},{10,2},{16,24},{18,10},{24,28},{26,18},{28,20},... | collective-permute-start | bytes 884744 | tf_op jit(solution)/shard_map/ppermute | solution.py:65
  3.4 3.6 %collective-permute-done.3.refs_2_ = bf16[3,3,32,512]{3,2,1,0:T(8,128)(2,1)S(1)} collective-permute-done((bf16[3,3,32,512]{3,2,1,0:T(8,128)(2,1)}, bf16[3,3,32,512]{3,2,1,0:T(8,128)(2,1)S(1)}, u32[]{:S(2)}, u32[]{:S(2)}) %collective-permute-start.3) | collective-permute-done | bytes 294944 | tf_op jit(solution)/shard_map/ppermute | solution.py:65
  7.0 1.6 %collective-permute-start.7 = (bf16[3,3,32,512]{3,2,1,0:T(8,128)(2,1)S(1)}, bf16[3,3,32,512]{3,2,1,0:T(8,128)(2,1)S(1)}, u32[]{:S(2)}, u32[]{:S(2)}) collective-permute-start(bf16[3,3,32,512]{3,2,1,0:T(8,128)(2,1)S(1)} %collective-permute-done.3.refs_2_), channel_id=1, source_target_pairs={{0,8},{2,6},{8,16},{10,2},{16,24},{18,10},{24,28},{26,18},{28,20},... | collective-permute-start | bytes 884744 | tf_op jit(solution)/shard_map/ppermute | solution.py:65
  8.6 1.1 %fusion = (bf16[4,2,32,512]{3,2,1,0:T(8,128)(2,1)S(1)}, bf16[4,2,32,512]{3,2,1,0:T(8,128)(2,1)S(1)}) fusion(bf16[8,2,32,512]{3,2,1,0:T(8,128)(2,1)} %param.8), kind=kLoop, calls=%fused_computation | loop fusion | bytes 1048576 | tf_op jit(solution)/shard_map/slice | solution.py:274
  9.6 1.6 %collective-permute-start = (bf16[4,2,32,512]{3,2,1,0:T(8,128)(2,1)S(1)}, bf16[4,2,32,512]{3,2,1,0:T(8,128)(2,1)S(1)}, u32[]{:S(2)}, u32[]{:S(2)}) collective-permute-start(bf16[4,2,32,512]{3,2,1,0:T(8,128)(2,1)S(1)} %get-tuple-element.34.refs_0_), channel_id=1, source_target_pairs={{0,1},{1,0},{2,3},{3,2},{4,5},{5,4},{6,7},{7,6},{8,9},{9,8},{10,11... | collective-permute-start | bytes 786440 | tf_op jit(solution)/shard_map/ppermute | solution.py:277
  11.2 0.5 collective-permute-start.1
  11.7 0.0 collective-permute-start.4
  11.7 0.0 collective-permute-done.5.refs_4_
  11.7 0.5 collective-permute-start.6
  12.2 1.5 %collective-permute-done.7.refs_6_ = bf16[3,3,32,512]{3,2,1,0:T(8,128)(2,1)S(1)} collective-permute-done((bf16[3,3,32,512]{3,2,1,0:T(8,128)(2,1)S(1)}, bf16[3,3,32,512]{3,2,1,0:T(8,128)(2,1)S(1)}, u32[]{:S(2)}, u32[]{:S(2)}) %collective-permute-start.7) | collective-permute-done | bytes 294944 | tf_op jit(solution)/shard_map/ppermute | solution.py:65
  13.7 0.0 collective-permute-start.8
  13.7 5.0 %collective-permute-done.refs_1_ = bf16[4,2,32,512]{3,2,1,0:T(8,128)(2,1)S(1)} collective-permute-done((bf16[4,2,32,512]{3,2,1,0:T(8,128)(2,1)S(1)}, bf16[4,2,32,512]{3,2,1,0:T(8,128)(2,1)S(1)}, u32[]{:S(2)}, u32[]{:S(2)}) %collective-permute-start) | collective-permute-done | bytes 262176 | tf_op jit(solution)/shard_map/ppermute | solution.py:277
  18.8 1.7 %collective-permute-start.9 = (bf16[3,3,32,512]{3,2,1,0:T(8,128)(2,1)S(1)}, bf16[3,3,32,512]{3,2,1,0:T(8,128)(2,1)S(1)}, u32[]{:S(2)}, u32[]{:S(2)}) collective-permute-start(bf16[3,3,32,512]{3,2,1,0:T(8,128)(2,1)S(1)} %collective-permute-done.5.refs_4_), channel_id=1, source_target_pairs={{0,8},{2,6},{8,16},{10,2},{16,24},{18,10},{24,28},{26,18},{28,20},... | collective-permute-start | bytes 884744 | tf_op jit(solution)/shard_map/ppermute | solution.py:65
  20.5 1.1 %collective-permute-done.1.refs_1_ = bf16[4,2,32,512]{3,2,1,0:T(8,128)(2,1)S(1)} collective-permute-done((bf16[4,2,32,512]{3,2,1,0:T(8,128)(2,1)S(1)}, bf16[4,2,32,512]{3,2,1,0:T(8,128)(2,1)S(1)}, u32[]{:S(2)}, u32[]{:S(2)}) %collective-permute-start.1) | collective-permute-done | bytes 262176 | tf_op jit(solution)/shard_map/ppermute | solution.py:277
  21.6 1.7 %collective-permute-start.11 = (bf16[3,3,32,512]{3,2,1,0:T(8,128)(2,1)S(1)}, bf16[3,3,32,512]{3,2,1,0:T(8,128)(2,1)S(1)}, u32[]{:S(2)}, u32[]{:S(2)}) collective-permute-start(bf16[3,3,32,512]{3,2,1,0:T(8,128)(2,1)S(1)} %collective-permute-done.7.refs_6_), channel_id=1, source_target_pairs={{0,8},{2,6},{8,16},{10,2},{16,24},{18,10},{24,28},{26,18},{28,20},... | collective-permute-start | bytes 884744 | tf_op jit(solution)/shard_map/ppermute | solution.py:65
  23.3 0.0 copy-start.4
  23.3 0.7 %copy-done.4 = f32[512]{0:T(512)S(1)} copy-done((f32[512]{0:T(512)S(1)}, f32[512]{0:T(512)}, u32[]{:S(2)}) %copy-start.4) | copy-done | bytes 2072
  24.0 0.5 prepare.2
  24.5 0.5 prepare.3
  25.0 0.0 collective-permute-done.4.refs_3_
  25.0 0.0 collective-permute-done.6.refs_5_
  25.1 0.0 collective-permute-done.8.refs_7_
  25.1 0.0 copy-done.2
  25.1 1.4 %early.2.acts0_ref = bf16[4,128,256]{2,1,0:T(8,128)(2,1)S(1)} custom-call(bf16[4,6,32,1536]{3,2,1,0:T(8,128)(2,1)S(1)} %get-tuple-element.19.wide_ref.wide0_ref, bf16[3,3,32,512]{3,2,1,0:T(8,128)(2,1)S(1)} %bitcast.5, bf16[3,3,32,512]{3,2,1,0:T(8,128)(2,1)S(1)} %collective-permute-done.2.refs_1_, bf16[3,3,32,512]{3,2,1,0:T(8,128)(2,1)S(1)} %collective-permute-done.3.refs_2_, ...), custom_call_target="tpu_custom_call" | custom-call | tf_op jit(solution)/shard_map/early/pallas_call | solution.py:318
  26.5 0.0 collective-permute-done.9.refs_0_
  26.5 1.6 %collective-permute-start.13 = (bf16[3,3,32,512]{3,2,1,0:T(8,128)(2,1)S(1)}, bf16[3,3,32,512]{3,2,1,0:T(8,128)(2,1)S(1)}, u32[]{:S(2)}, u32[]{:S(2)}) collective-permute-start(bf16[3,3,32,512]{3,2,1,0:T(8,128)(2,1)S(1)} %collective-permute-done.9.refs_0_), channel_id=1, source_target_pairs={{0,8},{2,6},{8,16},{10,2},{16,24},{18,10},{24,28},{26,18},{28,20},... | collective-permute-start | bytes 884744 | tf_op jit(solution)/shard_map/ppermute | solution.py:65
  28.1 0.0 copy-start
  28.1 0.0 copy-start.5
  28.1 1.4 %early.3.acts1_ref = bf16[4,128,256]{2,1,0:T(8,128)(2,1)S(1)} custom-call(bf16[4,6,32,1536]{3,2,1,0:T(8,128)(2,1)S(1)} %get-tuple-element.20.wide_ref.wide1_ref, bf16[3,3,32,512]{3,2,1,0:T(8,128)(2,1)S(1)} %bitcast.6, bf16[3,3,32,512]{3,2,1,0:T(8,128)(2,1)S(1)} %collective-permute-done.2.refs_1_, bf16[3,3,32,512]{3,2,1,0:T(8,128)(2,1)S(1)} %collective-permute-done.3.refs_2_, ...), custom_call_target="tpu_custom_call" | custom-call | tf_op jit(solution)/shard_map/early/pallas_call | solution.py:318
  29.6 0.0 collective-permute-done.11.refs_2_
  29.6 1.6 %collective-permute-start.15 = (bf16[3,3,32,512]{3,2,1,0:T(8,128)(2,1)S(1)}, bf16[3,3,32,512]{3,2,1,0:T(8,128)(2,1)S(1)}, u32[]{:S(2)}, u32[]{:S(2)}) collective-permute-start(bf16[3,3,32,512]{3,2,1,0:T(8,128)(2,1)S(1)} %collective-permute-done.11.refs_2_), channel_id=1, source_target_pairs={{0,8},{2,6},{8,16},{10,2},{16,24},{18,10},{24,28},{26,18},{28,20},... | collective-permute-start | bytes 884744 | tf_op jit(solution)/shard_map/ppermute | solution.py:65
  31.2 0.0 collective-permute-start.10
  31.2 0.5 collective-permute-start.12
  31.7 1.6 %collective-permute-done.13.refs_4_ = bf16[3,3,32,512]{3,2,1,0:T(8,128)(2,1)S(1)} collective-permute-done((bf16[3,3,32,512]{3,2,1,0:T(8,128)(2,1)S(1)}, bf16[3,3,32,512]{3,2,1,0:T(8,128)(2,1)S(1)}, u32[]{:S(2)}, u32[]{:S(2)}) %collective-permute-start.13) | collective-permute-done | bytes 294944 | tf_op jit(solution)/shard_map/ppermute | solution.py:65
  33.3 0.0 collective-permute-start.14
  33.3 3.2 %collective-permute-done.15.refs_6_ = bf16[3,3,32,512]{3,2,1,0:T(8,128)(2,1)S(1)} collective-permute-done((bf16[3,3,32,512]{3,2,1,0:T(8,128)(2,1)S(1)}, bf16[3,3,32,512]{3,2,1,0:T(8,128)(2,1)S(1)}, u32[]{:S(2)}, u32[]{:S(2)}) %collective-permute-start.15) | collective-permute-done | bytes 294944 | tf_op jit(solution)/shard_map/ppermute | solution.py:65
  36.5 0.0 collective-permute-start.16
  36.5 0.0 copy-done
  36.5 0.1 order.1
  36.6 0.0 copy-done.5
  36.6 1.9 %first.1 = (f32[8,128,512]{2,1,0:T(8,128)S(1)}, f32[3,128,512]{2,1,0:T(8,128)S(1)}) custom-call(bf16[4,4,32,512]{3,2,1,0:T(8,128)(2,1)S(1)} %get-tuple-element.22.lat0_ref, bf16[4,4,32,512]{3,2,1,0:T(8,128)(2,1)S(1)} %get-tuple-element.23.lat1_ref, bf16[4,128,256]{2,1,0:T(8,128)(2,1)S(1)} %early.2.acts0_ref, bf16[4,128,256]{2,1,0:T(8,128)(2,1)S(1)} %early.3.acts1_ref, ...), custom_call_target="tpu_custom_call" | custom-call | tf_op jit(solution)/shard_map/first/pallas_call | solution.py:343
  38.5 0.0 collective-permute-done.10.refs_1_
  38.5 0.0 collective-permute-done.12.refs_3_
  38.5 0.0 collective-permute-done.14.refs_5_
  38.5 0.0 collective-permute-done.16.refs_7_
  38.5 3.6 %late.1 = (bf16[8,128,256]{2,1,0:T(8,128)(2,1)S(1)}, bf16[3,128,512]{2,1,0:T(8,128)(2,1)S(1)}) custom-call(bf16[4,6,32,1536]{3,2,1,0:T(8,128)(2,1)S(1)} %get-tuple-element.19.wide_ref.wide0_ref, bf16[4,6,32,1536]{3,2,1,0:T(8,128)(2,1)S(1)} %get-tuple-element.20.wide_ref.wide1_ref, s32[128]{0:T(128)S(1)} %copy-done.5, ...), custom_call_target="tpu_custom_call" | custom-call | tf_op jit(solution)/shard_map/late/pallas_call | solution.py:351
  42.1 2.4 %collective-permute-start.17 = (bf16[3,128,512]{2,1,0:T(8,128)(2,1)S(1)}, bf16[3,128,512]{2,1,0:T(8,128)(2,1)S(1)}, u32[]{:S(2)}, u32[]{:S(2)}) collective-permute-start(bf16[3,128,512]{2,1,0:T(8,128)(2,1)S(1)} %get-tuple-element.32), channel_id=1, source_target_pairs={{0,2},{2,4},{4,6},{6,8},{8,10},{10,12},{12,14},{14,16},{16,18},{18... | collective-permute-start | bytes 1179656 | tf_op jit(solution)/shard_map/ppermute | solution.py:359
  44.5 0.0 copy-start.1
  44.5 0.0 copy-start.3
  44.5 0.0 copy-start.6
  44.5 1.5 %rest.1.rest_ref = f32[8,128,512]{2,1,0:T(8,128)S(1)} custom-call(bf16[8,128,256]{2,1,0:T(8,128)(2,1)S(1)} %get-tuple-element.30.acts_ref, s32[128]{0:T(128)S(1)} %copy-done.5, bf16[3,256,512]{2,1,0:T(8,128)(2,1)S(1)} %get-tuple-element.21.weights, f32[8,128,512]{2,1,0:T(8,128)S(1)} %get-tuple-element.31.early_ref), custom_call_target="tpu_custom_call" | custom-call | tf_op jit(solution)/shard_map/rest/pallas_call | solution.py:360
  46.1 6.0 %collective-permute-done.17.packet_ref = bf16[3,128,512]{2,1,0:T(8,128)(2,1)S(1)} collective-permute-done((bf16[3,128,512]{2,1,0:T(8,128)(2,1)S(1)}, bf16[3,128,512]{2,1,0:T(8,128)(2,1)S(1)}, u32[]{:S(2)}, u32[]{:S(2)}) %collective-permute-start.17) | collective-permute-done | bytes 393248 | tf_op jit(solution)/shard_map/ppermute | solution.py:359
  52.1 0.0 copy-done.1
  52.1 0.0 copy-done.3
  52.1 0.0 copy-done.6
  52.1 6.8 %attend.1 = bf16[8,2,32,512]{3,2,1,0:T(8,128)(2,1)} custom-call(f32[8,128,512]{2,1,0:T(8,128)S(1)} %rest.1.rest_ref, bf16[3,128,512]{2,1,0:T(8,128)(2,1)S(1)} %collective-permute-done.17.packet_ref, s32[128]{0:T(128)S(1)} %copy-done.5, f32[1,512]{1,0:T(1,128)S(1)} %bitcast.9, bf16[512,1536]{1,0:T(8,128)(2,1)S(1)} %copy-done.1, bf16[512,512]{1,0:T(8,128)(2,1)S(1)} %copy-done.3), custom_call_target="tpu_custom_call" | custom-call | tf_op jit(solution)/shard_map/attend/pallas_call | solution.py:368
Async XLA Ops:
  0.0 25.1 %copy-start.2 = (bf16[3,3,512,32]{2,3,1,0:T(8,128)(2,1)S(1)}, bf16[3,3,512,32]{2,3,1,0:T(8,128)(2,1)}, u32[]{:S(2)}) copy-start(bf16[3,3,512,32]{2,3,1,0:T(8,128)(2,1)} %param.11) | copy-start | bytes 884740
  0.0 1.8 %collective-permute-start.2 = (bf16[3,3,32,512]{3,2,1,0:T(8,128)(2,1)}, bf16[3,3,32,512]{3,2,1,0:T(8,128)(2,1)S(1)}, u32[]{:S(2)}, u32[]{:S(2)}) collective-permute-start(bf16[3,3,32,512]{3,2,1,0:T(8,128)(2,1)} %bitcast.3), channel_id=1, source_target_pairs={{0,2},{2,0},{4,6},{6,4},{8,10},{10,8},{12,14},{14,12},{16,18},{18,... | collective-permute-start | bytes 884744 | tf_op jit(solution)/shard_map/ppermute | solution.py:57
  0.0 7.0 %collective-permute-start.3 = (bf16[3,3,32,512]{3,2,1,0:T(8,128)(2,1)}, bf16[3,3,32,512]{3,2,1,0:T(8,128)(2,1)S(1)}, u32[]{:S(2)}, u32[]{:S(2)}) collective-permute-start(bf16[3,3,32,512]{3,2,1,0:T(8,128)(2,1)} %bitcast.4), channel_id=1, source_target_pairs={{0,8},{2,6},{8,16},{10,2},{16,24},{18,10},{24,28},{26,18},{28,20},... | collective-permute-start | bytes 884744 | tf_op jit(solution)/shard_map/ppermute | solution.py:65
  1.8 9.9 %collective-permute-start.5 = (bf16[3,3,32,512]{3,2,1,0:T(8,128)(2,1)S(1)}, bf16[3,3,32,512]{3,2,1,0:T(8,128)(2,1)S(1)}, u32[]{:S(2)}, u32[]{:S(2)}) collective-permute-start(bf16[3,3,32,512]{3,2,1,0:T(8,128)(2,1)S(1)} %collective-permute-done.2.refs_1_), channel_id=1, source_target_pairs={{0,8},{2,6},{8,16},{10,2},{16,24},{18,10},{24,28},{26,18},{28,20},... | collective-permute-start | bytes 884744 | tf_op jit(solution)/shard_map/ppermute | solution.py:65
  7.0 6.7 %collective-permute-start.7 = (bf16[3,3,32,512]{3,2,1,0:T(8,128)(2,1)S(1)}, bf16[3,3,32,512]{3,2,1,0:T(8,128)(2,1)S(1)}, u32[]{:S(2)}, u32[]{:S(2)}) collective-permute-start(bf16[3,3,32,512]{3,2,1,0:T(8,128)(2,1)S(1)} %collective-permute-done.3.refs_2_), channel_id=1, source_target_pairs={{0,8},{2,6},{8,16},{10,2},{16,24},{18,10},{24,28},{26,18},{28,20},... | collective-permute-start | bytes 884744 | tf_op jit(solution)/shard_map/ppermute | solution.py:65
  9.6 9.1 %collective-permute-start = (bf16[4,2,32,512]{3,2,1,0:T(8,128)(2,1)S(1)}, bf16[4,2,32,512]{3,2,1,0:T(8,128)(2,1)S(1)}, u32[]{:S(2)}, u32[]{:S(2)}) collective-permute-start(bf16[4,2,32,512]{3,2,1,0:T(8,128)(2,1)S(1)} %get-tuple-element.34.refs_0_), channel_id=1, source_target_pairs={{0,1},{1,0},{2,3},{3,2},{4,5},{5,4},{6,7},{7,6},{8,9},{9,8},{10,11... | collective-permute-start | bytes 786440 | tf_op jit(solution)/shard_map/ppermute | solution.py:277
  11.2 10.4 %collective-permute-start.1 = (bf16[4,2,32,512]{3,2,1,0:T(8,128)(2,1)S(1)}, bf16[4,2,32,512]{3,2,1,0:T(8,128)(2,1)S(1)}, u32[]{:S(2)}, u32[]{:S(2)}) collective-permute-start(bf16[4,2,32,512]{3,2,1,0:T(8,128)(2,1)S(1)} %get-tuple-element.33.refs_0_), channel_id=1, source_target_pairs={{0,1},{1,0},{2,3},{3,2},{4,5},{5,4},{6,7},{7,6},{8,9},{9,8},{10,11... | collective-permute-start | bytes 786440 | tf_op jit(solution)/shard_map/ppermute | solution.py:277
  11.7 13.3 %collective-permute-start.4 = (bf16[3,3,32,512]{3,2,1,0:T(8,128)(2,1)S(1)}, bf16[3,3,32,512]{3,2,1,0:T(8,128)(2,1)S(1)}, u32[]{:S(2)}, u32[]{:S(2)}) collective-permute-start(bf16[3,3,32,512]{3,2,1,0:T(8,128)(2,1)S(1)} %collective-permute-done.3.refs_2_), channel_id=1, source_target_pairs={{0,2},{2,0},{4,6},{6,4},{8,10},{10,8},{12,14},{14,12},{16,18},{18,... | collective-permute-start | bytes 884744 | tf_op jit(solution)/shard_map/ppermute | solution.py:67
  11.7 13.3 %collective-permute-start.6 = (bf16[3,3,32,512]{3,2,1,0:T(8,128)(2,1)S(1)}, bf16[3,3,32,512]{3,2,1,0:T(8,128)(2,1)S(1)}, u32[]{:S(2)}, u32[]{:S(2)}) collective-permute-start(bf16[3,3,32,512]{3,2,1,0:T(8,128)(2,1)S(1)} %collective-permute-done.5.refs_4_), channel_id=1, source_target_pairs={{0,2},{2,0},{4,6},{6,4},{8,10},{10,8},{12,14},{14,12},{16,18},{18,... | collective-permute-start | bytes 884744 | tf_op jit(solution)/shard_map/ppermute | solution.py:67
  13.7 11.3 %collective-permute-start.8 = (bf16[3,3,32,512]{3,2,1,0:T(8,128)(2,1)S(1)}, bf16[3,3,32,512]{3,2,1,0:T(8,128)(2,1)S(1)}, u32[]{:S(2)}, u32[]{:S(2)}) collective-permute-start(bf16[3,3,32,512]{3,2,1,0:T(8,128)(2,1)S(1)} %collective-permute-done.7.refs_6_), channel_id=1, source_target_pairs={{0,2},{2,0},{4,6},{6,4},{8,10},{10,8},{12,14},{14,12},{16,18},{18,... | collective-permute-start | bytes 884744 | tf_op jit(solution)/shard_map/ppermute | solution.py:67
  18.8 7.7 %collective-permute-start.9 = (bf16[3,3,32,512]{3,2,1,0:T(8,128)(2,1)S(1)}, bf16[3,3,32,512]{3,2,1,0:T(8,128)(2,1)S(1)}, u32[]{:S(2)}, u32[]{:S(2)}) collective-permute-start(bf16[3,3,32,512]{3,2,1,0:T(8,128)(2,1)S(1)} %collective-permute-done.5.refs_4_), channel_id=1, source_target_pairs={{0,8},{2,6},{8,16},{10,2},{16,24},{18,10},{24,28},{26,18},{28,20},... | collective-permute-start | bytes 884744 | tf_op jit(solution)/shard_map/ppermute | solution.py:65
  21.6 8.0 %collective-permute-start.11 = (bf16[3,3,32,512]{3,2,1,0:T(8,128)(2,1)S(1)}, bf16[3,3,32,512]{3,2,1,0:T(8,128)(2,1)S(1)}, u32[]{:S(2)}, u32[]{:S(2)}) collective-permute-start(bf16[3,3,32,512]{3,2,1,0:T(8,128)(2,1)S(1)} %collective-permute-done.7.refs_6_), channel_id=1, source_target_pairs={{0,8},{2,6},{8,16},{10,2},{16,24},{18,10},{24,28},{26,18},{28,20},... | collective-permute-start | bytes 884744 | tf_op jit(solution)/shard_map/ppermute | solution.py:65
  23.3 0.7 %copy-start.4 = (f32[512]{0:T(512)S(1)}, f32[512]{0:T(512)}, u32[]{:S(2)}) copy-start(f32[512]{0:T(512)} %param.10) | copy-start | bytes 6148
  26.5 6.8 %collective-permute-start.13 = (bf16[3,3,32,512]{3,2,1,0:T(8,128)(2,1)S(1)}, bf16[3,3,32,512]{3,2,1,0:T(8,128)(2,1)S(1)}, u32[]{:S(2)}, u32[]{:S(2)}) collective-permute-start(bf16[3,3,32,512]{3,2,1,0:T(8,128)(2,1)S(1)} %collective-permute-done.9.refs_0_), channel_id=1, source_target_pairs={{0,8},{2,6},{8,16},{10,2},{16,24},{18,10},{24,28},{26,18},{28,20},... | collective-permute-start | bytes 884744 | tf_op jit(solution)/shard_map/ppermute | solution.py:65
  28.1 8.3 %copy-start = (bf16[3,512,512]{2,1,0:T(8,128)(2,1)S(1)}, bf16[3,512,512]{2,1,0:T(8,128)(2,1)}, u32[]{:S(2)}) copy-start(bf16[3,512,512]{2,1,0:T(8,128)(2,1)} %time_ref.1) | copy-start | bytes 4718596
  28.1 8.4 %copy-start.5 = (s32[128]{0:T(128)S(1)}, s32[128]{0:T(128)}, u32[]{:S(2)}) copy-start(s32[128]{0:T(128)} %clips.7) | copy-start | bytes 1540
  29.6 6.9 %collective-permute-start.15 = (bf16[3,3,32,512]{3,2,1,0:T(8,128)(2,1)S(1)}, bf16[3,3,32,512]{3,2,1,0:T(8,128)(2,1)S(1)}, u32[]{:S(2)}, u32[]{:S(2)}) collective-permute-start(bf16[3,3,32,512]{3,2,1,0:T(8,128)(2,1)S(1)} %collective-permute-done.11.refs_2_), channel_id=1, source_target_pairs={{0,8},{2,6},{8,16},{10,2},{16,24},{18,10},{24,28},{26,18},{28,20},... | collective-permute-start | bytes 884744 | tf_op jit(solution)/shard_map/ppermute | solution.py:65
  31.2 7.3 %collective-permute-start.10 = (bf16[3,3,32,512]{3,2,1,0:T(8,128)(2,1)S(1)}, bf16[3,3,32,512]{3,2,1,0:T(8,128)(2,1)S(1)}, u32[]{:S(2)}, u32[]{:S(2)}) collective-permute-start(bf16[3,3,32,512]{3,2,1,0:T(8,128)(2,1)S(1)} %collective-permute-done.9.refs_0_), channel_id=1, source_target_pairs={{0,2},{2,0},{4,6},{6,4},{8,10},{10,8},{12,14},{14,12},{16,18},{18,... | collective-permute-start | bytes 884744 | tf_op jit(solution)/shard_map/ppermute | solution.py:67
  31.2 7.3 %collective-permute-start.12 = (bf16[3,3,32,512]{3,2,1,0:T(8,128)(2,1)S(1)}, bf16[3,3,32,512]{3,2,1,0:T(8,128)(2,1)S(1)}, u32[]{:S(2)}, u32[]{:S(2)}) collective-permute-start(bf16[3,3,32,512]{3,2,1,0:T(8,128)(2,1)S(1)} %collective-permute-done.11.refs_2_), channel_id=1, source_target_pairs={{0,2},{2,0},{4,6},{6,4},{8,10},{10,8},{12,14},{14,12},{16,18},{18,... | collective-permute-start | bytes 884744 | tf_op jit(solution)/shard_map/ppermute | solution.py:67
  33.3 5.2 %collective-permute-start.14 = (bf16[3,3,32,512]{3,2,1,0:T(8,128)(2,1)S(1)}, bf16[3,3,32,512]{3,2,1,0:T(8,128)(2,1)S(1)}, u32[]{:S(2)}, u32[]{:S(2)}) collective-permute-start(bf16[3,3,32,512]{3,2,1,0:T(8,128)(2,1)S(1)} %collective-permute-done.13.refs_4_), channel_id=1, source_target_pairs={{0,2},{2,0},{4,6},{6,4},{8,10},{10,8},{12,14},{14,12},{16,18},{18,... | collective-permute-start | bytes 884744 | tf_op jit(solution)/shard_map/ppermute | solution.py:67
  36.5 2.1 %collective-permute-start.16 = (bf16[3,3,32,512]{3,2,1,0:T(8,128)(2,1)S(1)}, bf16[3,3,32,512]{3,2,1,0:T(8,128)(2,1)S(1)}, u32[]{:S(2)}, u32[]{:S(2)}) collective-permute-start(bf16[3,3,32,512]{3,2,1,0:T(8,128)(2,1)S(1)} %collective-permute-done.15.refs_6_), channel_id=1, source_target_pairs={{0,2},{2,0},{4,6},{6,4},{8,10},{10,8},{12,14},{14,12},{16,18},{18,... | collective-permute-start | bytes 884744 | tf_op jit(solution)/shard_map/ppermute | solution.py:67
  42.1 10.0 %collective-permute-start.17 = (bf16[3,128,512]{2,1,0:T(8,128)(2,1)S(1)}, bf16[3,128,512]{2,1,0:T(8,128)(2,1)S(1)}, u32[]{:S(2)}, u32[]{:S(2)}) collective-permute-start(bf16[3,128,512]{2,1,0:T(8,128)(2,1)S(1)} %get-tuple-element.32), channel_id=1, source_target_pairs={{0,2},{2,4},{4,6},{6,8},{8,10},{10,12},{12,14},{14,16},{16,18},{18... | collective-permute-start | bytes 1179656 | tf_op jit(solution)/shard_map/ppermute | solution.py:359
  44.5 7.6 %copy-start.1 = (bf16[512,1536]{1,0:T(8,128)(2,1)S(1)}, bf16[512,1536]{1,0:T(8,128)(2,1)}, u32[]{:S(2)}) copy-start(bf16[512,1536]{1,0:T(8,128)(2,1)} %qkv_ref.1) | copy-start | bytes 4718596
  44.5 7.6 %copy-start.3 = (bf16[512,512]{1,0:T(8,128)(2,1)S(1)}, bf16[512,512]{1,0:T(8,128)(2,1)}, u32[]{:S(2)}) copy-start(bf16[512,512]{1,0:T(8,128)(2,1)} %proj_ref.1) | copy-start | bytes 1572868
  44.5 7.6 %copy-start.6 = (f32[512]{0:T(512)S(1)}, f32[512]{0:T(512)}, u32[]{:S(2)}) copy-start(f32[512]{0:T(512)} %param.13) | copy-start | bytes 6148

commit v4 on v3

--- a/solution.py
+++ b/solution.py
@@ -54,15 +54,17 @@
     ring = ring_pairs(count)
     cores = [(i, i ^ 1) for i in range(count)]
     last = count // 4
-    twin = lax.ppermute(own, "tm", cores)
-    found = [own, twin]
-    streams = [own, twin]
+    found = [own, lax.ppermute(own, "tm", cores)]
+    streams = [own, own]
     for step in range(1, last + 1):
         for stream in range(2 if step < last else 1):
             gate = gates.get((stream, step))
             if gate is not None:
                 streams[stream] = lax.optimization_barrier((streams[stream], gate(found)))[0]
-            streams[stream] = lax.ppermute(streams[stream], "tm", ring)
+            pairs = ring
+            if stream == 1 and step == 1:
+                pairs = [(source ^ 1, target) for source, target in ring]
+            streams[stream] = lax.ppermute(streams[stream], "tm", pairs)
             found.append(streams[stream])
             found.append(lax.ppermute(streams[stream], "tm", cores))
     return found
@@ -270,7 +272,7 @@
     params = pltpu.CompilerParams(vmem_limit_bytes=(28 if frames * spots <= 1024 else 60) << 20)
     assert frames + 1 >= LONGEST
 
-    half = frames // 2
+    half = frames // 2 + 1
     halves = [latents[:half], latents[half:]]
     if groups == 2:
         swap = [(0, 1), (1, 0)]
@@ -291,8 +293,8 @@
         pl.pallas_call(
             prepare_kernel,
             out_shape=(
-                shape((half, height + 2, width, 3 * chans), BF16),
-                shape((half, height, width, chans), BF16),
+                shape((part[0].shape[0], height + 2, width, 3 * chans), BF16),
+                shape((part[0].shape[0], height, width, chans), BF16),
             ),
             in_specs=[VMEM] * (groups + 1),
             out_specs=(VMEM, VMEM),
@@ -317,7 +319,7 @@
     def early(which, shards):
         acts[which] = pl.pallas_call(
             early_kernel,
-            out_shape=shape((half, spots, split), BF16),
+            out_shape=shape((wides[which].shape[0], spots, split), BF16),
             in_specs=[VMEM] * (1 + cut),
             out_specs=VMEM,
             compiler_params=params,
@@ -328,7 +330,7 @@
     if ringed:
         last = count // 4
         gates = {
-            (1, 2): lambda found: parts[0][1],
+            (0, 2): lambda found: parts[0][1],
             (0, last - 1): lambda found: parts[1][1],
             (1, last - 1): functools.partial(early, 0),
             (0, last): functools.partial(early, 1),

time: 59.1 us -> 62 us (1.049)
  waiting for transfers between devices: 22.1 us -> 25.2 us
  starting transfers between devices: 17 us -> 15.6 us
  local copies, waits for them, and re-layouts: 1.78 us -> 2.69 us
    ppermute x8, waiting for transfers between devices: 9.96 us -> 16 us  [the longest x7 16 us: gather_ring(): streams[stream] = lax.ppermute(streams[stream], 'tm', pairs)]
    ppermute x2, waiting for transfers between devices: 6.11 us -> 3.18 us  [local(): others = [lax.ppermute(part, 'rows', swap) for part in halves]]
    ppermute x8, starting transfers between devices: 11.5 us -> 10 us  [the longest x7 10 us: gather_ring(): streams[stream] = lax.ppermute(streams[stream], 'tm', pairs)]
    slice x1 -> x2, local copies, waits for them, and re-layouts: 1.07 us -> 1.98 us  [local(): halves = [latents[:half], latents[half:]]]
  transfers between devices with their start and end apart: 18 -> 18, of which waited for: 8 -> 7; matrix products, arithmetic and copies ran while one was open for 2% -> 2% of each run, Pallas kernels for 13% -> 12%
where the time goes in v4:
time: 62 us; the launch traced here: 61.8 us
  waiting for transfers between devices  25.2 us (41%)
  Pallas kernels  18.1 us (29%)
  starting transfers between devices  15.6 us (25%)
  local copies, waits for them, and re-layouts  2.69 us (4%)
    ppermute x7, waiting for transfers between devices, gather_ring(): streams[stream] = lax.ppermute(streams[stream], 'tm', pairs)  16 us
    ppermute x7, starting transfers between devices, gather_ring(): streams[stream] = lax.ppermute(streams[stream], 'tm', pairs)  10 us
    pallas_call x1, Pallas kernels, local(): pl.pallas_call(attend_kernel, out_shape=shape((frames, rows, width, chans...  6.78 us
    ppermute x1, waiting for transfers between devices, local(): packet = lax.ppermute(packet, 'tm', [(i, i + 1) for i in range(count - 1)])  6.03 us
    pallas_call x1, Pallas kernels, local(): pl.pallas_call(late_kernel, out_shape=(shape((frames, spots, chans - spli...  3.94 us
    ppermute x2, waiting for transfers between devices, local(): others = [lax.ppermute(part, 'rows', swap) for part in halves]  3.18 us
    pallas_call x2, Pallas kernels, early(): pl.pallas_call(early_kernel, out_shape=shape((wides[which].shape[0], spot...  2.84 us
    ppermute x1, starting transfers between devices, local(): packet = lax.ppermute(packet, 'tm', [(i, i + 1) for i in range(count - 1)])  2.4 us
  transfers between devices with their start and end apart: 18, of which 7 were waited for; matrix products, arithmetic and copies ran while one was open for 2% of the time, Pallas kernels for 12%

profile of v4, /device:TPU:8, one launch (start us, length us, event | category | flops | bytes accessed | tf_op | source)
XLA Modules:
  0.0 61.8 jit_solution(16886680161821260899)
XLA Ops:
  0.0 0.0 copy-start.2
  0.0 1.0 %slice.6.refs_0_ = bf16[5,2,32,512]{3,2,1,0:T(8,128)(2,1)S(1)} slice(bf16[8,2,32,512]{3,2,1,0:T(8,128)(2,1)} %param.8), slice={[0:5], [0:2], [0:32], [0:512]} | slice | bytes 655360 | tf_op jit(solution)/shard_map/slice | solution.py:276
  1.0 1.6 %collective-permute-start = (bf16[5,2,32,512]{3,2,1,0:T(8,128)(2,1)S(1)}, bf16[5,2,32,512]{3,2,1,0:T(8,128)(2,1)S(1)}, u32[]{:S(2)}, u32[]{:S(2)}) collective-permute-start(bf16[5,2,32,512]{3,2,1,0:T(8,128)(2,1)S(1)} %slice.6.refs_0_), channel_id=1, source_target_pairs={{0,1},{1,0},{2,3},{3,2},{4,5},{5,4},{6,7},{7,6},{8,9},{9,8},{10,11... | collective-permute-start | bytes 983048 | tf_op jit(solution)/shard_map/ppermute | solution.py:279
  2.6 1.6 %collective-permute-start.3 = (bf16[3,3,32,512]{3,2,1,0:T(8,128)(2,1)}, bf16[3,3,32,512]{3,2,1,0:T(8,128)(2,1)S(1)}, u32[]{:S(2)}, u32[]{:S(2)}) collective-permute-start(bf16[3,3,32,512]{3,2,1,0:T(8,128)(2,1)} %bitcast.3), channel_id=1, source_target_pairs={{0,8},{2,6},{8,16},{10,2},{16,24},{18,10},{24,28},{26,18},{28,20},... | collective-permute-start | bytes 884744 | tf_op jit(solution)/shard_map/ppermute | solution.py:67
  4.2 0.0 collective-permute-start.5
  4.2 7.5 %collective-permute-done.3.refs_2_ = bf16[3,3,32,512]{3,2,1,0:T(8,128)(2,1)S(1)} collective-permute-done((bf16[3,3,32,512]{3,2,1,0:T(8,128)(2,1)}, bf16[3,3,32,512]{3,2,1,0:T(8,128)(2,1)S(1)}, u32[]{:S(2)}, u32[]{:S(2)}) %collective-permute-start.3) | collective-permute-done | bytes 294944 | tf_op jit(solution)/shard_map/ppermute | solution.py:67
  11.7 0.0 collective-permute-done.refs_1_
  11.7 1.6 %collective-permute-start.7 = (bf16[3,3,32,512]{3,2,1,0:T(8,128)(2,1)S(1)}, bf16[3,3,32,512]{3,2,1,0:T(8,128)(2,1)S(1)}, u32[]{:S(2)}, u32[]{:S(2)}) collective-permute-start(bf16[3,3,32,512]{3,2,1,0:T(8,128)(2,1)S(1)} %collective-permute-done.3.refs_2_), channel_id=1, source_target_pairs={{0,8},{2,6},{8,16},{10,2},{16,24},{18,10},{24,28},{26,18},{28,20},... | collective-permute-start | bytes 884744 | tf_op jit(solution)/shard_map/ppermute | solution.py:67
  13.3 0.0 collective-permute-start.2
  13.3 0.9 %slice.7.refs_0_ = bf16[3,2,32,512]{3,2,1,0:T(8,128)(2,1)S(1)} slice(bf16[8,2,32,512]{3,2,1,0:T(8,128)(2,1)} %param.8), slice={[5:8], [0:2], [0:32], [0:512]} | slice | bytes 393216 | tf_op jit(solution)/shard_map/slice | solution.py:276
  14.2 0.6 collective-permute-start.1
  14.8 0.2 collective-permute-start.4
  15.0 0.0 collective-permute-done.5.refs_4_
  15.1 0.3 collective-permute-start.6
  15.3 3.1 %collective-permute-done.7.refs_6_ = bf16[3,3,32,512]{3,2,1,0:T(8,128)(2,1)S(1)} collective-permute-done((bf16[3,3,32,512]{3,2,1,0:T(8,128)(2,1)S(1)}, bf16[3,3,32,512]{3,2,1,0:T(8,128)(2,1)S(1)}, u32[]{:S(2)}, u32[]{:S(2)}) %collective-permute-start.7) | collective-permute-done | bytes 294944 | tf_op jit(solution)/shard_map/ppermute | solution.py:67
  18.4 0.0 collective-permute-start.8
  18.4 3.2 %collective-permute-done.1.refs_1_ = bf16[3,2,32,512]{3,2,1,0:T(8,128)(2,1)S(1)} collective-permute-done((bf16[3,2,32,512]{3,2,1,0:T(8,128)(2,1)S(1)}, bf16[3,2,32,512]{3,2,1,0:T(8,128)(2,1)S(1)}, u32[]{:S(2)}, u32[]{:S(2)}) %collective-permute-start.1) | collective-permute-done | bytes 196640 | tf_op jit(solution)/shard_map/ppermute | solution.py:279
  21.6 1.6 %collective-permute-start.9 = (bf16[3,3,32,512]{3,2,1,0:T(8,128)(2,1)S(1)}, bf16[3,3,32,512]{3,2,1,0:T(8,128)(2,1)S(1)}, u32[]{:S(2)}, u32[]{:S(2)}) collective-permute-start(bf16[3,3,32,512]{3,2,1,0:T(8,128)(2,1)S(1)} %collective-permute-done.5.refs_4_), channel_id=1, source_target_pairs={{0,8},{2,6},{8,16},{10,2},{16,24},{18,10},{24,28},{26,18},{28,20},... | collective-permute-start | bytes 884744 | tf_op jit(solution)/shard_map/ppermute | solution.py:67
  23.2 0.0 collective-permute-done.2.refs_1_
  23.2 2.3 %collective-permute-start.11 = (bf16[3,3,32,512]{3,2,1,0:T(8,128)(2,1)S(1)}, bf16[3,3,32,512]{3,2,1,0:T(8,128)(2,1)S(1)}, u32[]{:S(2)}, u32[]{:S(2)}) collective-permute-start(bf16[3,3,32,512]{3,2,1,0:T(8,128)(2,1)S(1)} %collective-permute-done.7.refs_6_), channel_id=1, source_target_pairs={{0,8},{2,6},{8,16},{10,2},{16,24},{18,10},{24,28},{26,18},{28,20},... | collective-permute-start | bytes 884744 | tf_op jit(solution)/shard_map/ppermute | solution.py:67
  25.6 0.0 copy-start.4
  25.6 0.7 %copy-done.4 = f32[512]{0:T(512)S(1)} copy-done((f32[512]{0:T(512)S(1)}, f32[512]{0:T(512)}, u32[]{:S(2)}) %copy-start.4) | copy-done | bytes 2072
  26.3 0.4 prepare.3
  26.7 0.6 %prepare.2 = (bf16[5,6,32,1536]{3,2,1,0:T(8,128)(2,1)S(1)}, bf16[5,4,32,512]{3,2,1,0:T(8,128)(2,1)S(1)}) custom-call(bf16[5,2,32,512]{3,2,1,0:T(8,128)(2,1)S(1)} %slice.6.refs_0_, bf16[5,2,32,512]{3,2,1,0:T(8,128)(2,1)S(1)} %collective-permute-done.refs_1_, f32[1,512]{1,0:T(1,128)S(1)} %bitcast.9), custom_call_target="tpu_custom_call" | custom-call | tf_op jit(solution)/shard_map/prepare/pallas_call | solution.py:293
  27.3 0.0 collective-permute-done.4.refs_3_
  27.3 0.0 collective-permute-done.6.refs_5_
  27.3 0.0 collective-permute-done.8.refs_7_
  27.3 0.0 copy-done.2
  27.3 1.7 %early.2.acts0_ref = bf16[5,128,256]{2,1,0:T(8,128)(2,1)S(1)} custom-call(bf16[5,6,32,1536]{3,2,1,0:T(8,128)(2,1)S(1)} %get-tuple-element.19.wide_ref.wide0_ref, bf16[3,3,32,512]{3,2,1,0:T(8,128)(2,1)S(1)} %bitcast.6, bf16[3,3,32,512]{3,2,1,0:T(8,128)(2,1)S(1)} %collective-permute-done.2.refs_1_, bf16[3,3,32,512]{3,2,1,0:T(8,128)(2,1)S(1)} %collective-permute-done.3.refs_2_, ...), custom_call_target="tpu_custom_call" | custom-call | tf_op jit(solution)/shard_map/early/pallas_call | solution.py:320
  29.1 0.0 collective-permute-done.9.refs_0_
  29.1 0.9 %collective-permute-start.13 = (bf16[3,3,32,512]{3,2,1,0:T(8,128)(2,1)S(1)}, bf16[3,3,32,512]{3,2,1,0:T(8,128)(2,1)S(1)}, u32[]{:S(2)}, u32[]{:S(2)}) collective-permute-start(bf16[3,3,32,512]{3,2,1,0:T(8,128)(2,1)S(1)} %collective-permute-done.9.refs_0_), channel_id=1, source_target_pairs={{0,8},{2,6},{8,16},{10,2},{16,24},{18,10},{24,28},{26,18},{28,20},... | collective-permute-start | bytes 884744 | tf_op jit(solution)/shard_map/ppermute | solution.py:67
  30.0 0.0 copy-start
  30.0 0.0 copy-start.5
  30.0 1.1 %early.3.acts1_ref = bf16[3,128,256]{2,1,0:T(8,128)(2,1)S(1)} custom-call(bf16[3,6,32,1536]{3,2,1,0:T(8,128)(2,1)S(1)} %get-tuple-element.20.wide_ref.wide1_ref, bf16[3,3,32,512]{3,2,1,0:T(8,128)(2,1)S(1)} %bitcast.7, bf16[3,3,32,512]{3,2,1,0:T(8,128)(2,1)S(1)} %collective-permute-done.2.refs_1_, bf16[3,3,32,512]{3,2,1,0:T(8,128)(2,1)S(1)} %collective-permute-done.3.refs_2_, ...), custom_call_target="tpu_custom_call" | custom-call | tf_op jit(solution)/shard_map/early/pallas_call | solution.py:320
  31.1 0.4 collective-permute-done.11.refs_2_
  31.5 2.0 %collective-permute-start.15 = (bf16[3,3,32,512]{3,2,1,0:T(8,128)(2,1)S(1)}, bf16[3,3,32,512]{3,2,1,0:T(8,128)(2,1)S(1)}, u32[]{:S(2)}, u32[]{:S(2)}) collective-permute-start(bf16[3,3,32,512]{3,2,1,0:T(8,128)(2,1)S(1)} %collective-permute-done.11.refs_2_), channel_id=1, source_target_pairs={{0,8},{2,6},{8,16},{10,2},{16,24},{18,10},{24,28},{26,18},{28,20},... | collective-permute-start | bytes 884744 | tf_op jit(solution)/shard_map/ppermute | solution.py:67
  33.5 0.0 collective-permute-start.10
  33.5 0.5 collective-permute-start.12
  34.0 1.9 %collective-permute-done.13.refs_4_ = bf16[3,3,32,512]{3,2,1,0:T(8,128)(2,1)S(1)} collective-permute-done((bf16[3,3,32,512]{3,2,1,0:T(8,128)(2,1)S(1)}, bf16[3,3,32,512]{3,2,1,0:T(8,128)(2,1)S(1)}, u32[]{:S(2)}, u32[]{:S(2)}) %collective-permute-start.13) | collective-permute-done | bytes 294944 | tf_op jit(solution)/shard_map/ppermute | solution.py:67
  35.9 0.0 collective-permute-start.14
  35.9 3.2 %collective-permute-done.15.refs_6_ = bf16[3,3,32,512]{3,2,1,0:T(8,128)(2,1)S(1)} collective-permute-done((bf16[3,3,32,512]{3,2,1,0:T(8,128)(2,1)S(1)}, bf16[3,3,32,512]{3,2,1,0:T(8,128)(2,1)S(1)}, u32[]{:S(2)}, u32[]{:S(2)}) %collective-permute-start.15) | collective-permute-done | bytes 294944 | tf_op jit(solution)/shard_map/ppermute | solution.py:67
  39.0 0.0 collective-permute-start.16
  39.0 0.0 copy-done
  39.0 0.1 order.1
  39.2 0.0 copy-done.5
  39.2 1.9 %first.1 = (f32[8,128,512]{2,1,0:T(8,128)S(1)}, f32[3,128,512]{2,1,0:T(8,128)S(1)}) custom-call(bf16[5,4,32,512]{3,2,1,0:T(8,128)(2,1)S(1)} %get-tuple-element.22.lat0_ref, bf16[3,4,32,512]{3,2,1,0:T(8,128)(2,1)S(1)} %get-tuple-element.23.lat1_ref, bf16[5,128,256]{2,1,0:T(8,128)(2,1)S(1)} %early.2.acts0_ref, bf16[3,128,256]{2,1,0:T(8,128)(2,1)S(1)} %early.3.acts1_ref, ...), custom_call_target="tpu_custom_call" | custom-call | tf_op jit(solution)/shard_map/first/pallas_call | solution.py:345
  41.0 0.0 collective-permute-done.10.refs_1_
  41.0 0.0 collective-permute-done.12.refs_3_
  41.1 0.0 collective-permute-done.14.refs_5_
  41.1 0.0 collective-permute-done.16.refs_7_
  41.1 3.9 %late.1 = (bf16[8,128,256]{2,1,0:T(8,128)(2,1)S(1)}, bf16[3,128,512]{2,1,0:T(8,128)(2,1)S(1)}) custom-call(bf16[5,6,32,1536]{3,2,1,0:T(8,128)(2,1)S(1)} %get-tuple-element.19.wide_ref.wide0_ref, bf16[3,6,32,1536]{3,2,1,0:T(8,128)(2,1)S(1)} %get-tuple-element.20.wide_ref.wide1_ref, s32[128]{0:T(128)S(1)} %copy-done.5, ...), custom_call_target="tpu_custom_call" | custom-call | tf_op jit(solution)/shard_map/late/pallas_call | solution.py:353
  45.0 2.4 %collective-permute-start.17 = (bf16[3,128,512]{2,1,0:T(8,128)(2,1)S(1)}, bf16[3,128,512]{2,1,0:T(8,128)(2,1)S(1)}, u32[]{:S(2)}, u32[]{:S(2)}) collective-permute-start(bf16[3,128,512]{2,1,0:T(8,128)(2,1)S(1)} %get-tuple-element.32), channel_id=1, source_target_pairs={{0,2},{2,4},{4,6},{6,8},{8,10},{10,12},{12,14},{14,16},{16,18},{18... | collective-permute-start | bytes 1179656 | tf_op jit(solution)/shard_map/ppermute | solution.py:361
  47.4 0.0 copy-start.1
  47.4 0.0 copy-start.3
  47.5 0.0 copy-start.6
  47.5 1.5 %rest.1.rest_ref = f32[8,128,512]{2,1,0:T(8,128)S(1)} custom-call(bf16[8,128,256]{2,1,0:T(8,128)(2,1)S(1)} %get-tuple-element.30.acts_ref, s32[128]{0:T(128)S(1)} %copy-done.5, bf16[3,256,512]{2,1,0:T(8,128)(2,1)S(1)} %get-tuple-element.21.weights, f32[8,128,512]{2,1,0:T(8,128)S(1)} %get-tuple-element.31.early_ref), custom_call_target="tpu_custom_call" | custom-call | tf_op jit(solution)/shard_map/rest/pallas_call | solution.py:362
  49.0 6.0 %collective-permute-done.17.packet_ref = bf16[3,128,512]{2,1,0:T(8,128)(2,1)S(1)} collective-permute-done((bf16[3,128,512]{2,1,0:T(8,128)(2,1)S(1)}, bf16[3,128,512]{2,1,0:T(8,128)(2,1)S(1)}, u32[]{:S(2)}, u32[]{:S(2)}) %collective-permute-start.17) | collective-permute-done | bytes 393248 | tf_op jit(solution)/shard_map/ppermute | solution.py:361
  55.0 0.0 copy-done.1
  55.0 0.0 copy-done.3
  55.0 0.0 copy-done.6
  55.0 6.8 %attend.1 = bf16[8,2,32,512]{3,2,1,0:T(8,128)(2,1)} custom-call(f32[8,128,512]{2,1,0:T(8,128)S(1)} %rest.1.rest_ref, bf16[3,128,512]{2,1,0:T(8,128)(2,1)S(1)} %collective-permute-done.17.packet_ref, s32[128]{0:T(128)S(1)} %copy-done.5, f32[1,512]{1,0:T(1,128)S(1)} %bitcast.10, bf16[512,1536]{1,0:T(8,128)(2,1)S(1)} %copy-done.1, bf16[512,512]{1,0:T(8,128)(2,1)S(1)} %copy-done.3), custom_call_target="tpu_custom_call" | custom-call | tf_op jit(solution)/shard_map/attend/pallas_call | solution.py:370
Async XLA Ops:
  0.0 27.3 %copy-start.2 = (bf16[3,3,512,32]{2,3,1,0:T(8,128)(2,1)S(1)}, bf16[3,3,512,32]{2,3,1,0:T(8,128)(2,1)}, u32[]{:S(2)}) copy-start(bf16[3,3,512,32]{2,3,1,0:T(8,128)(2,1)} %param.11) | copy-start | bytes 884740
  1.0 10.7 %collective-permute-start = (bf16[5,2,32,512]{3,2,1,0:T(8,128)(2,1)S(1)}, bf16[5,2,32,512]{3,2,1,0:T(8,128)(2,1)S(1)}, u32[]{:S(2)}, u32[]{:S(2)}) collective-permute-start(bf16[5,2,32,512]{3,2,1,0:T(8,128)(2,1)S(1)} %slice.6.refs_0_), channel_id=1, source_target_pairs={{0,1},{1,0},{2,3},{3,2},{4,5},{5,4},{6,7},{7,6},{8,9},{9,8},{10,11... | collective-permute-start | bytes 983048 | tf_op jit(solution)/shard_map/ppermute | solution.py:279
  2.6 9.1 %collective-permute-start.3 = (bf16[3,3,32,512]{3,2,1,0:T(8,128)(2,1)}, bf16[3,3,32,512]{3,2,1,0:T(8,128)(2,1)S(1)}, u32[]{:S(2)}, u32[]{:S(2)}) collective-permute-start(bf16[3,3,32,512]{3,2,1,0:T(8,128)(2,1)} %bitcast.3), channel_id=1, source_target_pairs={{0,8},{2,6},{8,16},{10,2},{16,24},{18,10},{24,28},{26,18},{28,20},... | collective-permute-start | bytes 884744 | tf_op jit(solution)/shard_map/ppermute | solution.py:67
  4.2 10.9 %collective-permute-start.5 = (bf16[3,3,32,512]{3,2,1,0:T(8,128)(2,1)}, bf16[3,3,32,512]{3,2,1,0:T(8,128)(2,1)S(1)}, u32[]{:S(2)}, u32[]{:S(2)}) collective-permute-start(bf16[3,3,32,512]{3,2,1,0:T(8,128)(2,1)} %bitcast.4), channel_id=1, source_target_pairs={{2,8},{0,6},{10,16},{8,2},{18,24},{16,10},{26,28},{24,18},{30,20},... | collective-permute-start | bytes 884744 | tf_op jit(solution)/shard_map/ppermute | solution.py:67
  11.7 6.7 %collective-permute-start.7 = (bf16[3,3,32,512]{3,2,1,0:T(8,128)(2,1)S(1)}, bf16[3,3,32,512]{3,2,1,0:T(8,128)(2,1)S(1)}, u32[]{:S(2)}, u32[]{:S(2)}) collective-permute-start(bf16[3,3,32,512]{3,2,1,0:T(8,128)(2,1)S(1)} %collective-permute-done.3.refs_2_), channel_id=1, source_target_pairs={{0,8},{2,6},{8,16},{10,2},{16,24},{18,10},{24,28},{26,18},{28,20},... | collective-permute-start | bytes 884744 | tf_op jit(solution)/shard_map/ppermute | solution.py:67
  13.3 10.0 %collective-permute-start.2 = (bf16[3,3,32,512]{3,2,1,0:T(8,128)(2,1)}, bf16[3,3,32,512]{3,2,1,0:T(8,128)(2,1)S(1)}, u32[]{:S(2)}, u32[]{:S(2)}) collective-permute-start(bf16[3,3,32,512]{3,2,1,0:T(8,128)(2,1)} %bitcast.5), channel_id=1, source_target_pairs={{0,2},{2,0},{4,6},{6,4},{8,10},{10,8},{12,14},{14,12},{16,18},{18,... | collective-permute-start | bytes 884744 | tf_op jit(solution)/shard_map/ppermute | solution.py:57
  14.2 7.4 %collective-permute-start.1 = (bf16[3,2,32,512]{3,2,1,0:T(8,128)(2,1)S(1)}, bf16[3,2,32,512]{3,2,1,0:T(8,128)(2,1)S(1)}, u32[]{:S(2)}, u32[]{:S(2)}) collective-permute-start(bf16[3,2,32,512]{3,2,1,0:T(8,128)(2,1)S(1)} %slice.7.refs_0_), channel_id=1, source_target_pairs={{0,1},{1,0},{2,3},{3,2},{4,5},{5,4},{6,7},{7,6},{8,9},{9,8},{10,11... | collective-permute-start | bytes 589832 | tf_op jit(solution)/shard_map/ppermute | solution.py:279
  14.8 12.5 %collective-permute-start.4 = (bf16[3,3,32,512]{3,2,1,0:T(8,128)(2,1)S(1)}, bf16[3,3,32,512]{3,2,1,0:T(8,128)(2,1)S(1)}, u32[]{:S(2)}, u32[]{:S(2)}) collective-permute-start(bf16[3,3,32,512]{3,2,1,0:T(8,128)(2,1)S(1)} %collective-permute-done.3.refs_2_), channel_id=1, source_target_pairs={{0,2},{2,0},{4,6},{6,4},{8,10},{10,8},{12,14},{14,12},{16,18},{18,... | collective-permute-start | bytes 884744 | tf_op jit(solution)/shard_map/ppermute | solution.py:69
  15.1 12.3 %collective-permute-start.6 = (bf16[3,3,32,512]{3,2,1,0:T(8,128)(2,1)S(1)}, bf16[3,3,32,512]{3,2,1,0:T(8,128)(2,1)S(1)}, u32[]{:S(2)}, u32[]{:S(2)}) collective-permute-start(bf16[3,3,32,512]{3,2,1,0:T(8,128)(2,1)S(1)} %collective-permute-done.5.refs_4_), channel_id=1, source_target_pairs={{0,2},{2,0},{4,6},{6,4},{8,10},{10,8},{12,14},{14,12},{16,18},{18,... | collective-permute-start | bytes 884744 | tf_op jit(solution)/shard_map/ppermute | solution.py:69
  18.4 8.9 %collective-permute-start.8 = (bf16[3,3,32,512]{3,2,1,0:T(8,128)(2,1)S(1)}, bf16[3,3,32,512]{3,2,1,0:T(8,128)(2,1)S(1)}, u32[]{:S(2)}, u32[]{:S(2)}) collective-permute-start(bf16[3,3,32,512]{3,2,1,0:T(8,128)(2,1)S(1)} %collective-permute-done.7.refs_6_), channel_id=1, source_target_pairs={{0,2},{2,0},{4,6},{6,4},{8,10},{10,8},{12,14},{14,12},{16,18},{18,... | collective-permute-start | bytes 884744 | tf_op jit(solution)/shard_map/ppermute | solution.py:69
  21.6 7.5 %collective-permute-start.9 = (bf16[3,3,32,512]{3,2,1,0:T(8,128)(2,1)S(1)}, bf16[3,3,32,512]{3,2,1,0:T(8,128)(2,1)S(1)}, u32[]{:S(2)}, u32[]{:S(2)}) collective-permute-start(bf16[3,3,32,512]{3,2,1,0:T(8,128)(2,1)S(1)} %collective-permute-done.5.refs_4_), channel_id=1, source_target_pairs={{0,8},{2,6},{8,16},{10,2},{16,24},{18,10},{24,28},{26,18},{28,20},... | collective-permute-start | bytes 884744 | tf_op jit(solution)/shard_map/ppermute | solution.py:67
  23.2 8.2 %collective-permute-start.11 = (bf16[3,3,32,512]{3,2,1,0:T(8,128)(2,1)S(1)}, bf16[3,3,32,512]{3,2,1,0:T(8,128)(2,1)S(1)}, u32[]{:S(2)}, u32[]{:S(2)}) collective-permute-start(bf16[3,3,32,512]{3,2,1,0:T(8,128)(2,1)S(1)} %collective-permute-done.7.refs_6_), channel_id=1, source_target_pairs={{0,8},{2,6},{8,16},{10,2},{16,24},{18,10},{24,28},{26,18},{28,20},... | collective-permute-start | bytes 884744 | tf_op jit(solution)/shard_map/ppermute | solution.py:67
  25.6 0.7 %copy-start.4 = (f32[512]{0:T(512)S(1)}, f32[512]{0:T(512)}, u32[]{:S(2)}) copy-start(f32[512]{0:T(512)} %param.10) | copy-start | bytes 6148
  29.1 6.8 %collective-permute-start.13 = (bf16[3,3,32,512]{3,2,1,0:T(8,128)(2,1)S(1)}, bf16[3,3,32,512]{3,2,1,0:T(8,128)(2,1)S(1)}, u32[]{:S(2)}, u32[]{:S(2)}) collective-permute-start(bf16[3,3,32,512]{3,2,1,0:T(8,128)(2,1)S(1)} %collective-permute-done.9.refs_0_), channel_id=1, source_target_pairs={{0,8},{2,6},{8,16},{10,2},{16,24},{18,10},{24,28},{26,18},{28,20},... | collective-permute-start | bytes 884744 | tf_op jit(solution)/shard_map/ppermute | solution.py:67
  30.0 9.1 %copy-start = (bf16[3,512,512]{2,1,0:T(8,128)(2,1)S(1)}, bf16[3,512,512]{2,1,0:T(8,128)(2,1)}, u32[]{:S(2)}) copy-start(bf16[3,512,512]{2,1,0:T(8,128)(2,1)} %time_ref.1) | copy-start | bytes 4718596
  30.0 9.2 %copy-start.5 = (s32[128]{0:T(128)S(1)}, s32[128]{0:T(128)}, u32[]{:S(2)}) copy-start(s32[128]{0:T(128)} %clips.7) | copy-start | bytes 1540
  31.5 7.5 %collective-permute-start.15 = (bf16[3,3,32,512]{3,2,1,0:T(8,128)(2,1)S(1)}, bf16[3,3,32,512]{3,2,1,0:T(8,128)(2,1)S(1)}, u32[]{:S(2)}, u32[]{:S(2)}) collective-permute-start(bf16[3,3,32,512]{3,2,1,0:T(8,128)(2,1)S(1)} %collective-permute-done.11.refs_2_), channel_id=1, source_target_pairs={{0,8},{2,6},{8,16},{10,2},{16,24},{18,10},{24,28},{26,18},{28,20},... | collective-permute-start | bytes 884744 | tf_op jit(solution)/shard_map/ppermute | solution.py:67
  33.5 7.5 %collective-permute-start.10 = (bf16[3,3,32,512]{3,2,1,0:T(8,128)(2,1)S(1)}, bf16[3,3,32,512]{3,2,1,0:T(8,128)(2,1)S(1)}, u32[]{:S(2)}, u32[]{:S(2)}) collective-permute-start(bf16[3,3,32,512]{3,2,1,0:T(8,128)(2,1)S(1)} %collective-permute-done.9.refs_0_), channel_id=1, source_target_pairs={{0,2},{2,0},{4,6},{6,4},{8,10},{10,8},{12,14},{14,12},{16,18},{18,... | collective-permute-start | bytes 884744 | tf_op jit(solution)/shard_map/ppermute | solution.py:69
  33.5 7.5 %collective-permute-start.12 = (bf16[3,3,32,512]{3,2,1,0:T(8,128)(2,1)S(1)}, bf16[3,3,32,512]{3,2,1,0:T(8,128)(2,1)S(1)}, u32[]{:S(2)}, u32[]{:S(2)}) collective-permute-start(bf16[3,3,32,512]{3,2,1,0:T(8,128)(2,1)S(1)} %collective-permute-done.11.refs_2_), channel_id=1, source_target_pairs={{0,2},{2,0},{4,6},{6,4},{8,10},{10,8},{12,14},{14,12},{16,18},{18,... | collective-permute-start | bytes 884744 | tf_op jit(solution)/shard_map/ppermute | solution.py:69
  35.9 5.2 %collective-permute-start.14 = (bf16[3,3,32,512]{3,2,1,0:T(8,128)(2,1)S(1)}, bf16[3,3,32,512]{3,2,1,0:T(8,128)(2,1)S(1)}, u32[]{:S(2)}, u32[]{:S(2)}) collective-permute-start(bf16[3,3,32,512]{3,2,1,0:T(8,128)(2,1)S(1)} %collective-permute-done.13.refs_4_), channel_id=1, source_target_pairs={{0,2},{2,0},{4,6},{6,4},{8,10},{10,8},{12,14},{14,12},{16,18},{18,... | collective-permute-start | bytes 884744 | tf_op jit(solution)/shard_map/ppermute | solution.py:69
  39.0 2.0 %collective-permute-start.16 = (bf16[3,3,32,512]{3,2,1,0:T(8,128)(2,1)S(1)}, bf16[3,3,32,512]{3,2,1,0:T(8,128)(2,1)S(1)}, u32[]{:S(2)}, u32[]{:S(2)}) collective-permute-start(bf16[3,3,32,512]{3,2,1,0:T(8,128)(2,1)S(1)} %collective-permute-done.15.refs_6_), channel_id=1, source_target_pairs={{0,2},{2,0},{4,6},{6,4},{8,10},{10,8},{12,14},{14,12},{16,18},{18,... | collective-permute-start | bytes 884744 | tf_op jit(solution)/shard_map/ppermute | solution.py:69
  45.0 10.0 %collective-permute-start.17 = (bf16[3,128,512]{2,1,0:T(8,128)(2,1)S(1)}, bf16[3,128,512]{2,1,0:T(8,128)(2,1)S(1)}, u32[]{:S(2)}, u32[]{:S(2)}) collective-permute-start(bf16[3,128,512]{2,1,0:T(8,128)(2,1)S(1)} %get-tuple-element.32), channel_id=1, source_target_pairs={{0,2},{2,4},{4,6},{6,8},{8,10},{10,12},{12,14},{14,16},{16,18},{18... | collective-permute-start | bytes 1179656 | tf_op jit(solution)/shard_map/ppermute | solution.py:361
  47.4 7.6 %copy-start.1 = (bf16[512,1536]{1,0:T(8,128)(2,1)S(1)}, bf16[512,1536]{1,0:T(8,128)(2,1)}, u32[]{:S(2)}) copy-start(bf16[512,1536]{1,0:T(8,128)(2,1)} %qkv_ref.1) | copy-start | bytes 4718596
  47.4 7.6 %copy-start.3 = (bf16[512,512]{1,0:T(8,128)(2,1)S(1)}, bf16[512,512]{1,0:T(8,128)(2,1)}, u32[]{:S(2)}) copy-start(bf16[512,512]{1,0:T(8,128)(2,1)} %proj_ref.1) | copy-start | bytes 1572868
  47.5 7.6 %copy-start.6 = (f32[512]{0:T(512)S(1)}, f32[512]{0:T(512)}, u32[]{:S(2)}) copy-start(f32[512]{0:T(512)} %param.13) | copy-start | bytes 6148

commit v5 on v3

--- a/solution.py
+++ b/solution.py
@@ -54,9 +54,8 @@
     ring = ring_pairs(count)
     cores = [(i, i ^ 1) for i in range(count)]
     last = count // 4
-    twin = lax.ppermute(own, "tm", cores)
-    found = [own, twin]
-    streams = [own, twin]
+    found = [own, lax.ppermute(own, "tm", cores)]
+    streams = list(found)
     for step in range(1, last + 1):
         for stream in range(2 if step < last else 1):
             gate = gates.get((stream, step))
@@ -77,9 +76,10 @@
     return device_at(spot, (core + flip) % 2, count)
 
 
-def prepare_kernel(*refs):
+def prepare_kernel(start, *refs):
     *parts, gain_ref, wide_ref, lat_ref = refs
-    frames, rows, width, chans = parts[0].shape
+    _, rows, width, chans = parts[0].shape
+    frames = wide_ref.shape[0]
     groups = len(parts)
     mine = lax.axis_index("rows")
     gain = gain_ref[...]
@@ -93,7 +93,7 @@
         if groups == 2:
             first = (mine if at == 0 else 1 - mine) * rows
         for frame in range(frames):
-            raw = part[frame]
+            raw = part[start + frame]
             lat_ref[frame, pl.ds(first, rows)] = raw
             x = raw.reshape(rows * width, chans).astype(F32)
             y = x * lax.rsqrt(jnp.mean(x * x, axis=-1, keepdims=True) + 1e-06) * gain
@@ -271,14 +271,11 @@
     assert frames + 1 >= LONGEST
 
     half = frames // 2
-    halves = [latents[:half], latents[half:]]
     if groups == 2:
-        swap = [(0, 1), (1, 0)]
-        others = [lax.ppermute(part, "rows", swap) for part in halves]
-        parts = [[own, other] for own, other in zip(halves, others)]
+        parts = [latents, lax.ppermute(latents, "rows", [(0, 1), (1, 0)])]
     else:
-        everything = [lax.all_gather(part, "rows") for part in halves]
-        parts = [[part[i] for i in range(groups)] for part in everything]
+        everything = lax.all_gather(latents, "rows")
+        parts = [everything[i] for i in range(groups)]
 
     shard = jnp.transpose(w_space, (0, 1, 3, 2))
     ringed = shard.shape[2] % 16 == 0 and count % 8 == 0
@@ -289,7 +286,7 @@
     gain = gain_in.reshape(1, chans)
     prepared = [
         pl.pallas_call(
-            prepare_kernel,
+            functools.partial(prepare_kernel, start),
             out_shape=(
                 shape((half, height + 2, width, 3 * chans), BF16),
                 shape((half, height, width, chans), BF16),
@@ -298,8 +295,8 @@
             out_specs=(VMEM, VMEM),
             compiler_params=params,
             name="prepare",
-        )(*part, gain)
-        for part in parts
+        )(*parts, gain)
+        for start in (0, half)
     ]
     wides = [pair[0] for pair in prepared]
     lats = [pair[1] for pair in prepared]
@@ -317,7 +314,7 @@
     def early(which, shards):
         acts[which] = pl.pallas_call(
             early_kernel,
-            out_shape=shape((half, spots, split), BF16),
+            out_shape=shape((wides[which].shape[0], spots, split), BF16),
             in_specs=[VMEM] * (1 + cut),
             out_specs=VMEM,
             compiler_params=params,
@@ -328,8 +325,7 @@
     if ringed:
         last = count // 4
         gates = {
-            (1, 2): lambda found: parts[0][1],
-            (0, last - 1): lambda found: parts[1][1],
+            (1, 2): lambda found: parts[1],
             (1, last - 1): functools.partial(early, 0),
             (0, last): functools.partial(early, 1),
         }

time: 59.1 us -> 54.7 us (0.926)
  waiting for transfers between devices: 22.1 us -> 19.7 us
  starting transfers between devices: 17 us -> 15.1 us
    ppermute x3 -> x2, waiting for transfers between devices: 6.27 us -> 0.89 us  [the longest x1 0.89 us: local(): parts = [latents, lax.ppermute(latents, 'rows', [(0, 1), (1, 0)])]]
    ppermute x7, waiting for transfers between devices: 9.8 us -> 12.8 us  [gather_ring(): streams[stream] = lax.ppermute(streams[stream], 'tm', ring)]
    slice x1 -> x0, local copies, waits for them, and re-layouts: 1.07 us -> none  [local(): halves = [latents[:half], latents[half:]]]
    unnamed x14 -> x16, local copies, waits for them, and re-layouts: 0.71 us -> 1.75 us
    ppermute x7, starting transfers between devices: 11.5 us -> 10.7 us  [gather_ring(): streams[stream] = lax.ppermute(streams[stream], 'tm', ring)]
    ppermute x3 -> x2, starting transfers between devices: 2.09 us -> 1.49 us  [the longest x1 1.49 us: local(): parts = [latents, lax.ppermute(latents, 'rows', [(0, 1), (1, 0)])]]
  transfers between devices with their start and end apart: 18 -> 17, of which waited for: 8 -> 7; matrix products, arithmetic and copies ran while one was open for 2% -> 0% of each run, Pallas kernels for 13% -> 14%
where the time goes in v5:
time: 54.7 us; the launch traced here: 54.5 us
  waiting for transfers between devices  19.7 us (36%)
  Pallas kernels  17.7 us (32%)
  starting transfers between devices  15.1 us (28%)
  local copies, waits for them, and re-layouts  1.75 us (3%)
    ppermute x7, waiting for transfers between devices, gather_ring(): streams[stream] = lax.ppermute(streams[stream], 'tm', ring)  12.8 us
    ppermute x7, starting transfers between devices, gather_ring(): streams[stream] = lax.ppermute(streams[stream], 'tm', ring)  10.7 us
    pallas_call x1, Pallas kernels, local(): pl.pallas_call(attend_kernel, out_shape=shape((frames, rows, width, chans...  6.78 us
    ppermute x1, waiting for transfers between devices, local(): packet = lax.ppermute(packet, 'tm', [(i, i + 1) for i in range(count - 1)])  6.02 us
    pallas_call x1, Pallas kernels, local(): pl.pallas_call(late_kernel, out_shape=(shape((frames, spots, chans - spli...  3.58 us
    pallas_call x2, Pallas kernels, early(): pl.pallas_call(early_kernel, out_shape=shape((wides[which].shape[0], spot...  2.83 us
    ppermute x1, starting transfers between devices, local(): packet = lax.ppermute(packet, 'tm', [(i, i + 1) for i in range(count - 1)])  2.42 us
    pallas_call x1, Pallas kernels, local(): pl.pallas_call(first_kernel, out_shape=(shape((frames, spots, chans), F32...  1.9 us
  transfers between devices with their start and end apart: 17, of which 7 were waited for; matrix products, arithmetic and copies ran while one was open for 0% of the time, Pallas kernels for 14%

profile of v5, /device:TPU:8, one launch (start us, length us, event | category | flops | bytes accessed | tf_op | source)
XLA Modules:
  0.0 54.5 jit_solution(8291755089322341439)
XLA Ops:
  0.0 0.0 collective-permute-start.1
  0.0 1.6 %collective-permute-start.2 = (bf16[3,3,32,512]{3,2,1,0:T(8,128)(2,1)}, bf16[3,3,32,512]{3,2,1,0:T(8,128)(2,1)S(1)}, u32[]{:S(2)}, u32[]{:S(2)}) collective-permute-start(bf16[3,3,32,512]{3,2,1,0:T(8,128)(2,1)} %bitcast.4), channel_id=1, source_target_pairs={{0,8},{2,6},{8,16},{10,2},{16,24},{18,10},{24,28},{26,18},{28,20},... | collective-permute-start | bytes 884744 | tf_op jit(solution)/shard_map/ppermute | solution.py:64
  1.6 1.5 %collective-permute-start = (bf16[8,2,32,512]{3,2,1,0:T(8,128)(2,1)}, bf16[8,2,32,512]{3,2,1,0:T(8,128)(2,1)S(1)}, u32[]{:S(2)}, u32[]{:S(2)}) collective-permute-start(bf16[8,2,32,512]{3,2,1,0:T(8,128)(2,1)} %refs_0_.3), channel_id=1, source_target_pairs={{0,1},{1,0},{2,3},{3,2},{4,5},{5,4},{6,7},{7,6},{8,9},{9,8},{10,11... | collective-permute-start | bytes 1572872 | tf_op jit(solution)/shard_map/ppermute | solution.py:275
  3.1 0.0 collective-permute-done.1.refs_1_
  3.1 1.6 %collective-permute-start.4 = (bf16[3,3,32,512]{3,2,1,0:T(8,128)(2,1)S(1)}, bf16[3,3,32,512]{3,2,1,0:T(8,128)(2,1)S(1)}, u32[]{:S(2)}, u32[]{:S(2)}) collective-permute-start(bf16[3,3,32,512]{3,2,1,0:T(8,128)(2,1)S(1)} %collective-permute-done.1.refs_1_), channel_id=1, source_target_pairs={{0,8},{2,6},{8,16},{10,2},{16,24},{18,10},{24,28},{26,18},{28,20},... | collective-permute-start | bytes 884744 | tf_op jit(solution)/shard_map/ppermute | solution.py:64
  4.7 2.3 %collective-permute-done.2.refs_2_ = bf16[3,3,32,512]{3,2,1,0:T(8,128)(2,1)S(1)} collective-permute-done((bf16[3,3,32,512]{3,2,1,0:T(8,128)(2,1)}, bf16[3,3,32,512]{3,2,1,0:T(8,128)(2,1)S(1)}, u32[]{:S(2)}, u32[]{:S(2)}) %collective-permute-start.2) | collective-permute-done | bytes 294944 | tf_op jit(solution)/shard_map/ppermute | solution.py:64
  6.9 1.6 %collective-permute-start.6 = (bf16[3,3,32,512]{3,2,1,0:T(8,128)(2,1)S(1)}, bf16[3,3,32,512]{3,2,1,0:T(8,128)(2,1)S(1)}, u32[]{:S(2)}, u32[]{:S(2)}) collective-permute-start(bf16[3,3,32,512]{3,2,1,0:T(8,128)(2,1)S(1)} %collective-permute-done.2.refs_2_), channel_id=1, source_target_pairs={{0,8},{2,6},{8,16},{10,2},{16,24},{18,10},{24,28},{26,18},{28,20},... | collective-permute-start | bytes 884744 | tf_op jit(solution)/shard_map/ppermute | solution.py:64
  8.5 0.0 collective-permute-start.3
  8.5 1.6 %collective-permute-done.4.refs_4_ = bf16[3,3,32,512]{3,2,1,0:T(8,128)(2,1)S(1)} collective-permute-done((bf16[3,3,32,512]{3,2,1,0:T(8,128)(2,1)S(1)}, bf16[3,3,32,512]{3,2,1,0:T(8,128)(2,1)S(1)}, u32[]{:S(2)}, u32[]{:S(2)}) %collective-permute-start.4) | collective-permute-done | bytes 294944 | tf_op jit(solution)/shard_map/ppermute | solution.py:64
  10.1 0.0 collective-permute-start.5
  10.1 3.6 %collective-permute-done.6.refs_6_ = bf16[3,3,32,512]{3,2,1,0:T(8,128)(2,1)S(1)} collective-permute-done((bf16[3,3,32,512]{3,2,1,0:T(8,128)(2,1)S(1)}, bf16[3,3,32,512]{3,2,1,0:T(8,128)(2,1)S(1)}, u32[]{:S(2)}, u32[]{:S(2)}) %collective-permute-start.6) | collective-permute-done | bytes 294944 | tf_op jit(solution)/shard_map/ppermute | solution.py:64
  13.7 0.0 collective-permute-start.7
  13.7 0.9 %collective-permute-done.refs_1_ = bf16[8,2,32,512]{3,2,1,0:T(8,128)(2,1)S(1)} collective-permute-done((bf16[8,2,32,512]{3,2,1,0:T(8,128)(2,1)}, bf16[8,2,32,512]{3,2,1,0:T(8,128)(2,1)S(1)}, u32[]{:S(2)}, u32[]{:S(2)}) %collective-permute-start) | collective-permute-done | bytes 524320 | tf_op jit(solution)/shard_map/ppermute | solution.py:275
  14.6 1.7 %collective-permute-start.8 = (bf16[3,3,32,512]{3,2,1,0:T(8,128)(2,1)S(1)}, bf16[3,3,32,512]{3,2,1,0:T(8,128)(2,1)S(1)}, u32[]{:S(2)}, u32[]{:S(2)}) collective-permute-start(bf16[3,3,32,512]{3,2,1,0:T(8,128)(2,1)S(1)} %collective-permute-done.4.refs_4_), channel_id=1, source_target_pairs={{0,8},{2,6},{8,16},{10,2},{16,24},{18,10},{24,28},{26,18},{28,20},... | collective-permute-start | bytes 884744 | tf_op jit(solution)/shard_map/ppermute | solution.py:64
  16.3 1.6 %collective-permute-start.10 = (bf16[3,3,32,512]{3,2,1,0:T(8,128)(2,1)S(1)}, bf16[3,3,32,512]{3,2,1,0:T(8,128)(2,1)S(1)}, u32[]{:S(2)}, u32[]{:S(2)}) collective-permute-start(bf16[3,3,32,512]{3,2,1,0:T(8,128)(2,1)S(1)} %collective-permute-done.6.refs_6_), channel_id=1, source_target_pairs={{0,8},{2,6},{8,16},{10,2},{16,24},{18,10},{24,28},{26,18},{28,20},... | collective-permute-start | bytes 884744 | tf_op jit(solution)/shard_map/ppermute | solution.py:64
  17.9 0.0 copy-start
  17.9 1.0 %copy-done = bf16[8,2,32,512]{3,2,1,0:T(8,128)(2,1)S(1)} copy-done((bf16[8,2,32,512]{3,2,1,0:T(8,128)(2,1)S(1)}, bf16[8,2,32,512]{3,2,1,0:T(8,128)(2,1)}, u32[]{:S(2)}) %copy-start) | copy-done | bytes 524312
  18.9 0.0 copy-start.5
  18.9 0.7 %copy-done.5 = f32[512]{0:T(512)S(1)} copy-done((f32[512]{0:T(512)S(1)}, f32[512]{0:T(512)}, u32[]{:S(2)}) %copy-start.5) | copy-done | bytes 2072
  19.6 0.0 copy-start.3
  19.6 0.5 prepare.2
  20.1 0.5 prepare.3
  20.6 0.0 collective-permute-done.3.refs_3_
  20.7 0.0 collective-permute-done.5.refs_5_
  20.7 0.0 collective-permute-done.7.refs_7_
  20.7 0.0 copy-done.3
  20.7 1.4 %early.2.acts0_ref = bf16[4,128,256]{2,1,0:T(8,128)(2,1)S(1)} custom-call(bf16[4,6,32,1536]{3,2,1,0:T(8,128)(2,1)S(1)} %get-tuple-element.18.wide_ref.wide0_ref, bf16[3,3,32,512]{3,2,1,0:T(8,128)(2,1)S(1)} %bitcast.5, bf16[3,3,32,512]{3,2,1,0:T(8,128)(2,1)S(1)} %collective-permute-done.1.refs_1_, bf16[3,3,32,512]{3,2,1,0:T(8,128)(2,1)S(1)} %collective-permute-done.2.refs_2_, ...), custom_call_target="tpu_custom_call" | custom-call | tf_op jit(solution)/shard_map/early/pallas_call | solution.py:315
  22.1 0.0 collective-permute-done.8.refs_0_
  22.1 1.6 %collective-permute-start.12 = (bf16[3,3,32,512]{3,2,1,0:T(8,128)(2,1)S(1)}, bf16[3,3,32,512]{3,2,1,0:T(8,128)(2,1)S(1)}, u32[]{:S(2)}, u32[]{:S(2)}) collective-permute-start(bf16[3,3,32,512]{3,2,1,0:T(8,128)(2,1)S(1)} %collective-permute-done.8.refs_0_), channel_id=1, source_target_pairs={{0,8},{2,6},{8,16},{10,2},{16,24},{18,10},{24,28},{26,18},{28,20},... | collective-permute-start | bytes 884744 | tf_op jit(solution)/shard_map/ppermute | solution.py:64
  23.7 0.0 copy-start.1
  23.7 0.0 copy-start.6
  23.7 1.4 %early.3.acts1_ref = bf16[4,128,256]{2,1,0:T(8,128)(2,1)S(1)} custom-call(bf16[4,6,32,1536]{3,2,1,0:T(8,128)(2,1)S(1)} %get-tuple-element.19.wide_ref.wide1_ref, bf16[3,3,32,512]{3,2,1,0:T(8,128)(2,1)S(1)} %bitcast.6, bf16[3,3,32,512]{3,2,1,0:T(8,128)(2,1)S(1)} %collective-permute-done.1.refs_1_, bf16[3,3,32,512]{3,2,1,0:T(8,128)(2,1)S(1)} %collective-permute-done.2.refs_2_, ...), custom_call_target="tpu_custom_call" | custom-call | tf_op jit(solution)/shard_map/early/pallas_call | solution.py:315
  25.2 0.0 collective-permute-done.10.refs_2_
  25.2 1.0 %collective-permute-start.14 = (bf16[3,3,32,512]{3,2,1,0:T(8,128)(2,1)S(1)}, bf16[3,3,32,512]{3,2,1,0:T(8,128)(2,1)S(1)}, u32[]{:S(2)}, u32[]{:S(2)}) collective-permute-start(bf16[3,3,32,512]{3,2,1,0:T(8,128)(2,1)S(1)} %collective-permute-done.10.refs_2_), channel_id=1, source_target_pairs={{0,8},{2,6},{8,16},{10,2},{16,24},{18,10},{24,28},{26,18},{28,20},... | collective-permute-start | bytes 884744 | tf_op jit(solution)/shard_map/ppermute | solution.py:64
  26.2 0.0 collective-permute-start.9
  26.2 0.5 collective-permute-start.11
  26.7 2.2 %collective-permute-done.12.refs_4_ = bf16[3,3,32,512]{3,2,1,0:T(8,128)(2,1)S(1)} collective-permute-done((bf16[3,3,32,512]{3,2,1,0:T(8,128)(2,1)S(1)}, bf16[3,3,32,512]{3,2,1,0:T(8,128)(2,1)S(1)}, u32[]{:S(2)}, u32[]{:S(2)}) %collective-permute-start.12) | collective-permute-done | bytes 294944 | tf_op jit(solution)/shard_map/ppermute | solution.py:64
  28.9 0.0 collective-permute-start.13
  28.9 3.2 %collective-permute-done.14.refs_6_ = bf16[3,3,32,512]{3,2,1,0:T(8,128)(2,1)S(1)} collective-permute-done((bf16[3,3,32,512]{3,2,1,0:T(8,128)(2,1)S(1)}, bf16[3,3,32,512]{3,2,1,0:T(8,128)(2,1)S(1)}, u32[]{:S(2)}, u32[]{:S(2)}) %collective-permute-start.14) | collective-permute-done | bytes 294944 | tf_op jit(solution)/shard_map/ppermute | solution.py:64
  32.1 0.0 collective-permute-start.15
  32.1 0.0 copy-done.1
  32.1 0.1 order.1
  32.2 0.0 copy-done.6
  32.2 1.9 %first.1 = (f32[8,128,512]{2,1,0:T(8,128)S(1)}, f32[3,128,512]{2,1,0:T(8,128)S(1)}) custom-call(bf16[4,4,32,512]{3,2,1,0:T(8,128)(2,1)S(1)} %get-tuple-element.21.lat0_ref, bf16[4,4,32,512]{3,2,1,0:T(8,128)(2,1)S(1)} %get-tuple-element.22.lat1_ref, bf16[4,128,256]{2,1,0:T(8,128)(2,1)S(1)} %early.2.acts0_ref, bf16[4,128,256]{2,1,0:T(8,128)(2,1)S(1)} %early.3.acts1_ref, ...), custom_call_target="tpu_custom_call" | custom-call | tf_op jit(solution)/shard_map/first/pallas_call | solution.py:339
  34.1 0.0 collective-permute-done.9.refs_1_
  34.1 0.0 collective-permute-done.11.refs_3_
  34.1 0.0 collective-permute-done.13.refs_5_
  34.1 0.0 collective-permute-done.15.refs_7_
  34.1 3.6 %late.1 = (bf16[8,128,256]{2,1,0:T(8,128)(2,1)S(1)}, bf16[3,128,512]{2,1,0:T(8,128)(2,1)S(1)}) custom-call(bf16[4,6,32,1536]{3,2,1,0:T(8,128)(2,1)S(1)} %get-tuple-element.18.wide_ref.wide0_ref, bf16[4,6,32,1536]{3,2,1,0:T(8,128)(2,1)S(1)} %get-tuple-element.19.wide_ref.wide1_ref, s32[128]{0:T(128)S(1)} %copy-done.6, ...), custom_call_target="tpu_custom_call" | custom-call | tf_op jit(solution)/shard_map/late/pallas_call | solution.py:347
  37.7 2.4 %collective-permute-start.16 = (bf16[3,128,512]{2,1,0:T(8,128)(2,1)S(1)}, bf16[3,128,512]{2,1,0:T(8,128)(2,1)S(1)}, u32[]{:S(2)}, u32[]{:S(2)}) collective-permute-start(bf16[3,128,512]{2,1,0:T(8,128)(2,1)S(1)} %get-tuple-element.30), channel_id=1, source_target_pairs={{0,2},{2,4},{4,6},{6,8},{8,10},{10,12},{12,14},{14,16},{16,18},{18... | collective-permute-start | bytes 1179656 | tf_op jit(solution)/shard_map/ppermute | solution.py:355
  40.2 0.0 copy-start.2
  40.2 0.0 copy-start.4
  40.2 0.0 copy-start.7
  40.2 1.5 %rest.1.rest_ref = f32[8,128,512]{2,1,0:T(8,128)S(1)} custom-call(bf16[8,128,256]{2,1,0:T(8,128)(2,1)S(1)} %get-tuple-element.28.acts_ref, s32[128]{0:T(128)S(1)} %copy-done.6, bf16[3,256,512]{2,1,0:T(8,128)(2,1)S(1)} %get-tuple-element.20.weights, f32[8,128,512]{2,1,0:T(8,128)S(1)} %get-tuple-element.29.early_ref), custom_call_target="tpu_custom_call" | custom-call | tf_op jit(solution)/shard_map/rest/pallas_call | solution.py:356
  41.7 6.0 %collective-permute-done.16.packet_ref = bf16[3,128,512]{2,1,0:T(8,128)(2,1)S(1)} collective-permute-done((bf16[3,128,512]{2,1,0:T(8,128)(2,1)S(1)}, bf16[3,128,512]{2,1,0:T(8,128)(2,1)S(1)}, u32[]{:S(2)}, u32[]{:S(2)}) %collective-permute-start.16) | collective-permute-done | bytes 393248 | tf_op jit(solution)/shard_map/ppermute | solution.py:355
  47.7 0.0 copy-done.2
  47.7 0.0 copy-done.4
  47.7 0.0 copy-done.7
  47.7 6.8 %attend.1 = bf16[8,2,32,512]{3,2,1,0:T(8,128)(2,1)} custom-call(f32[8,128,512]{2,1,0:T(8,128)S(1)} %rest.1.rest_ref, bf16[3,128,512]{2,1,0:T(8,128)(2,1)S(1)} %collective-permute-done.16.packet_ref, s32[128]{0:T(128)S(1)} %copy-done.6, f32[1,512]{1,0:T(1,128)S(1)} %bitcast.9, bf16[512,1536]{1,0:T(8,128)(2,1)S(1)} %copy-done.2, bf16[512,512]{1,0:T(8,128)(2,1)S(1)} %copy-done.4), custom_call_target="tpu_custom_call" | custom-call | tf_op jit(solution)/shard_map/attend/pallas_call | solution.py:364
Async XLA Ops:
  0.0 3.1 %collective-permute-start.1 = (bf16[3,3,32,512]{3,2,1,0:T(8,128)(2,1)}, bf16[3,3,32,512]{3,2,1,0:T(8,128)(2,1)S(1)}, u32[]{:S(2)}, u32[]{:S(2)}) collective-permute-start(bf16[3,3,32,512]{3,2,1,0:T(8,128)(2,1)} %bitcast.3), channel_id=1, source_target_pairs={{0,2},{2,0},{4,6},{6,4},{8,10},{10,8},{12,14},{14,12},{16,18},{18,... | collective-permute-start | bytes 884744 | tf_op jit(solution)/shard_map/ppermute | solution.py:57
  0.0 6.9 %collective-permute-start.2 = (bf16[3,3,32,512]{3,2,1,0:T(8,128)(2,1)}, bf16[3,3,32,512]{3,2,1,0:T(8,128)(2,1)S(1)}, u32[]{:S(2)}, u32[]{:S(2)}) collective-permute-start(bf16[3,3,32,512]{3,2,1,0:T(8,128)(2,1)} %bitcast.4), channel_id=1, source_target_pairs={{0,8},{2,6},{8,16},{10,2},{16,24},{18,10},{24,28},{26,18},{28,20},... | collective-permute-start | bytes 884744 | tf_op jit(solution)/shard_map/ppermute | solution.py:64
  1.6 13.0 %collective-permute-start = (bf16[8,2,32,512]{3,2,1,0:T(8,128)(2,1)}, bf16[8,2,32,512]{3,2,1,0:T(8,128)(2,1)S(1)}, u32[]{:S(2)}, u32[]{:S(2)}) collective-permute-start(bf16[8,2,32,512]{3,2,1,0:T(8,128)(2,1)} %refs_0_.3), channel_id=1, source_target_pairs={{0,1},{1,0},{2,3},{3,2},{4,5},{5,4},{6,7},{7,6},{8,9},{9,8},{10,11... | collective-permute-start | bytes 1572872 | tf_op jit(solution)/shard_map/ppermute | solution.py:275
  3.1 7.0 %collective-permute-start.4 = (bf16[3,3,32,512]{3,2,1,0:T(8,128)(2,1)S(1)}, bf16[3,3,32,512]{3,2,1,0:T(8,128)(2,1)S(1)}, u32[]{:S(2)}, u32[]{:S(2)}) collective-permute-start(bf16[3,3,32,512]{3,2,1,0:T(8,128)(2,1)S(1)} %collective-permute-done.1.refs_1_), channel_id=1, source_target_pairs={{0,8},{2,6},{8,16},{10,2},{16,24},{18,10},{24,28},{26,18},{28,20},... | collective-permute-start | bytes 884744 | tf_op jit(solution)/shard_map/ppermute | solution.py:64
  6.9 6.7 %collective-permute-start.6 = (bf16[3,3,32,512]{3,2,1,0:T(8,128)(2,1)S(1)}, bf16[3,3,32,512]{3,2,1,0:T(8,128)(2,1)S(1)}, u32[]{:S(2)}, u32[]{:S(2)}) collective-permute-start(bf16[3,3,32,512]{3,2,1,0:T(8,128)(2,1)S(1)} %collective-permute-done.2.refs_2_), channel_id=1, source_target_pairs={{0,8},{2,6},{8,16},{10,2},{16,24},{18,10},{24,28},{26,18},{28,20},... | collective-permute-start | bytes 884744 | tf_op jit(solution)/shard_map/ppermute | solution.py:64
  8.5 12.1 %collective-permute-start.3 = (bf16[3,3,32,512]{3,2,1,0:T(8,128)(2,1)S(1)}, bf16[3,3,32,512]{3,2,1,0:T(8,128)(2,1)S(1)}, u32[]{:S(2)}, u32[]{:S(2)}) collective-permute-start(bf16[3,3,32,512]{3,2,1,0:T(8,128)(2,1)S(1)} %collective-permute-done.2.refs_2_), channel_id=1, source_target_pairs={{0,2},{2,0},{4,6},{6,4},{8,10},{10,8},{12,14},{14,12},{16,18},{18,... | collective-permute-start | bytes 884744 | tf_op jit(solution)/shard_map/ppermute | solution.py:66
  10.1 10.6 %collective-permute-start.5 = (bf16[3,3,32,512]{3,2,1,0:T(8,128)(2,1)S(1)}, bf16[3,3,32,512]{3,2,1,0:T(8,128)(2,1)S(1)}, u32[]{:S(2)}, u32[]{:S(2)}) collective-permute-start(bf16[3,3,32,512]{3,2,1,0:T(8,128)(2,1)S(1)} %collective-permute-done.4.refs_4_), channel_id=1, source_target_pairs={{0,2},{2,0},{4,6},{6,4},{8,10},{10,8},{12,14},{14,12},{16,18},{18,... | collective-permute-start | bytes 884744 | tf_op jit(solution)/shard_map/ppermute | solution.py:66
  13.7 7.0 %collective-permute-start.7 = (bf16[3,3,32,512]{3,2,1,0:T(8,128)(2,1)S(1)}, bf16[3,3,32,512]{3,2,1,0:T(8,128)(2,1)S(1)}, u32[]{:S(2)}, u32[]{:S(2)}) collective-permute-start(bf16[3,3,32,512]{3,2,1,0:T(8,128)(2,1)S(1)} %collective-permute-done.6.refs_6_), channel_id=1, source_target_pairs={{0,2},{2,0},{4,6},{6,4},{8,10},{10,8},{12,14},{14,12},{16,18},{18,... | collective-permute-start | bytes 884744 | tf_op jit(solution)/shard_map/ppermute | solution.py:66
  14.6 7.6 %collective-permute-start.8 = (bf16[3,3,32,512]{3,2,1,0:T(8,128)(2,1)S(1)}, bf16[3,3,32,512]{3,2,1,0:T(8,128)(2,1)S(1)}, u32[]{:S(2)}, u32[]{:S(2)}) collective-permute-start(bf16[3,3,32,512]{3,2,1,0:T(8,128)(2,1)S(1)} %collective-permute-done.4.refs_4_), channel_id=1, source_target_pairs={{0,8},{2,6},{8,16},{10,2},{16,24},{18,10},{24,28},{26,18},{28,20},... | collective-permute-start | bytes 884744 | tf_op jit(solution)/shard_map/ppermute | solution.py:64
  16.3 8.9 %collective-permute-start.10 = (bf16[3,3,32,512]{3,2,1,0:T(8,128)(2,1)S(1)}, bf16[3,3,32,512]{3,2,1,0:T(8,128)(2,1)S(1)}, u32[]{:S(2)}, u32[]{:S(2)}) collective-permute-start(bf16[3,3,32,512]{3,2,1,0:T(8,128)(2,1)S(1)} %collective-permute-done.6.refs_6_), channel_id=1, source_target_pairs={{0,8},{2,6},{8,16},{10,2},{16,24},{18,10},{24,28},{26,18},{28,20},... | collective-permute-start | bytes 884744 | tf_op jit(solution)/shard_map/ppermute | solution.py:64
  17.9 1.0 %copy-start = (bf16[8,2,32,512]{3,2,1,0:T(8,128)(2,1)S(1)}, bf16[8,2,32,512]{3,2,1,0:T(8,128)(2,1)}, u32[]{:S(2)}) copy-start(bf16[8,2,32,512]{3,2,1,0:T(8,128)(2,1)} %refs_0_.3) | copy-start | bytes 1572868
  18.9 0.7 %copy-start.5 = (f32[512]{0:T(512)S(1)}, f32[512]{0:T(512)}, u32[]{:S(2)}) copy-start(f32[512]{0:T(512)} %param.10) | copy-start | bytes 6148
  19.6 1.1 %copy-start.3 = (bf16[3,3,512,32]{2,3,1,0:T(8,128)(2,1)S(1)}, bf16[3,3,512,32]{2,3,1,0:T(8,128)(2,1)}, u32[]{:S(2)}) copy-start(bf16[3,3,512,32]{2,3,1,0:T(8,128)(2,1)} %param.11) | copy-start | bytes 884740
  22.1 6.8 %collective-permute-start.12 = (bf16[3,3,32,512]{3,2,1,0:T(8,128)(2,1)S(1)}, bf16[3,3,32,512]{3,2,1,0:T(8,128)(2,1)S(1)}, u32[]{:S(2)}, u32[]{:S(2)}) collective-permute-start(bf16[3,3,32,512]{3,2,1,0:T(8,128)(2,1)S(1)} %collective-permute-done.8.refs_0_), channel_id=1, source_target_pairs={{0,8},{2,6},{8,16},{10,2},{16,24},{18,10},{24,28},{26,18},{28,20},... | collective-permute-start | bytes 884744 | tf_op jit(solution)/shard_map/ppermute | solution.py:64
  23.7 8.3 %copy-start.1 = (bf16[3,512,512]{2,1,0:T(8,128)(2,1)S(1)}, bf16[3,512,512]{2,1,0:T(8,128)(2,1)}, u32[]{:S(2)}) copy-start(bf16[3,512,512]{2,1,0:T(8,128)(2,1)} %time_ref.1) | copy-start | bytes 4718596
  23.7 8.4 %copy-start.6 = (s32[128]{0:T(128)S(1)}, s32[128]{0:T(128)}, u32[]{:S(2)}) copy-start(s32[128]{0:T(128)} %clips.7) | copy-start | bytes 1540
  25.2 6.9 %collective-permute-start.14 = (bf16[3,3,32,512]{3,2,1,0:T(8,128)(2,1)S(1)}, bf16[3,3,32,512]{3,2,1,0:T(8,128)(2,1)S(1)}, u32[]{:S(2)}, u32[]{:S(2)}) collective-permute-start(bf16[3,3,32,512]{3,2,1,0:T(8,128)(2,1)S(1)} %collective-permute-done.10.refs_2_), channel_id=1, source_target_pairs={{0,8},{2,6},{8,16},{10,2},{16,24},{18,10},{24,28},{26,18},{28,20},... | collective-permute-start | bytes 884744 | tf_op jit(solution)/shard_map/ppermute | solution.py:64
  26.2 7.9 %collective-permute-start.9 = (bf16[3,3,32,512]{3,2,1,0:T(8,128)(2,1)S(1)}, bf16[3,3,32,512]{3,2,1,0:T(8,128)(2,1)S(1)}, u32[]{:S(2)}, u32[]{:S(2)}) collective-permute-start(bf16[3,3,32,512]{3,2,1,0:T(8,128)(2,1)S(1)} %collective-permute-done.8.refs_0_), channel_id=1, source_target_pairs={{0,2},{2,0},{4,6},{6,4},{8,10},{10,8},{12,14},{14,12},{16,18},{18,... | collective-permute-start | bytes 884744 | tf_op jit(solution)/shard_map/ppermute | solution.py:66
  26.2 7.9 %collective-permute-start.11 = (bf16[3,3,32,512]{3,2,1,0:T(8,128)(2,1)S(1)}, bf16[3,3,32,512]{3,2,1,0:T(8,128)(2,1)S(1)}, u32[]{:S(2)}, u32[]{:S(2)}) collective-permute-start(bf16[3,3,32,512]{3,2,1,0:T(8,128)(2,1)S(1)} %collective-permute-done.10.refs_2_), channel_id=1, source_target_pairs={{0,2},{2,0},{4,6},{6,4},{8,10},{10,8},{12,14},{14,12},{16,18},{18,... | collective-permute-start | bytes 884744 | tf_op jit(solution)/shard_map/ppermute | solution.py:66
  28.9 5.2 %collective-permute-start.13 = (bf16[3,3,32,512]{3,2,1,0:T(8,128)(2,1)S(1)}, bf16[3,3,32,512]{3,2,1,0:T(8,128)(2,1)S(1)}, u32[]{:S(2)}, u32[]{:S(2)}) collective-permute-start(bf16[3,3,32,512]{3,2,1,0:T(8,128)(2,1)S(1)} %collective-permute-done.12.refs_4_), channel_id=1, source_target_pairs={{0,2},{2,0},{4,6},{6,4},{8,10},{10,8},{12,14},{14,12},{16,18},{18,... | collective-permute-start | bytes 884744 | tf_op jit(solution)/shard_map/ppermute | solution.py:66
  32.1 2.1 %collective-permute-start.15 = (bf16[3,3,32,512]{3,2,1,0:T(8,128)(2,1)S(1)}, bf16[3,3,32,512]{3,2,1,0:T(8,128)(2,1)S(1)}, u32[]{:S(2)}, u32[]{:S(2)}) collective-permute-start(bf16[3,3,32,512]{3,2,1,0:T(8,128)(2,1)S(1)} %collective-permute-done.14.refs_6_), channel_id=1, source_target_pairs={{0,2},{2,0},{4,6},{6,4},{8,10},{10,8},{12,14},{14,12},{16,18},{18,... | collective-permute-start | bytes 884744 | tf_op jit(solution)/shard_map/ppermute | solution.py:66
  37.7 10.0 %collective-permute-start.16 = (bf16[3,128,512]{2,1,0:T(8,128)(2,1)S(1)}, bf16[3,128,512]{2,1,0:T(8,128)(2,1)S(1)}, u32[]{:S(2)}, u32[]{:S(2)}) collective-permute-start(bf16[3,128,512]{2,1,0:T(8,128)(2,1)S(1)} %get-tuple-element.30), channel_id=1, source_target_pairs={{0,2},{2,4},{4,6},{6,8},{8,10},{10,12},{12,14},{14,16},{16,18},{18... | collective-permute-start | bytes 1179656 | tf_op jit(solution)/shard_map/ppermute | solution.py:355
  40.2 7.6 %copy-start.2 = (bf16[512,1536]{1,0:T(8,128)(2,1)S(1)}, bf16[512,1536]{1,0:T(8,128)(2,1)}, u32[]{:S(2)}) copy-start(bf16[512,1536]{1,0:T(8,128)(2,1)} %qkv_ref.1) | copy-start | bytes 4718596
  40.2 7.6 %copy-start.4 = (bf16[512,512]{1,0:T(8,128)(2,1)S(1)}, bf16[512,512]{1,0:T(8,128)(2,1)}, u32[]{:S(2)}) copy-start(bf16[512,512]{1,0:T(8,128)(2,1)} %proj_ref.1) | copy-start | bytes 1572868
  40.2 7.6 %copy-start.7 = (f32[512]{0:T(512)S(1)}, f32[512]{0:T(512)}, u32[]{:S(2)}) copy-start(f32[512]{0:T(512)} %param.13) | copy-start | bytes 6148

commit v6 on v5

--- a/solution.py
+++ b/solution.py
@@ -48,6 +48,12 @@
         if step < count // 4:
             tags += [(step, 0, 1), (step, 1, 0)]
     return tags
+
+
+def after(shard, gate, found):
+    if gate is None:
+        return shard
+    return lax.optimization_barrier((shard, gate(found)))[0]
 
 
 def gather_ring(own, count, gates):
@@ -58,12 +64,10 @@
     streams = list(found)
     for step in range(1, last + 1):
         for stream in range(2 if step < last else 1):
-            gate = gates.get((stream, step))
-            if gate is not None:
-                streams[stream] = lax.optimization_barrier((streams[stream], gate(found)))[0]
-            streams[stream] = lax.ppermute(streams[stream], "tm", ring)
-            found.append(streams[stream])
-            found.append(lax.ppermute(streams[stream], "tm", cores))
+            shard = lax.ppermute(after(streams[stream], gates.get((stream, step, 0)), found), "tm", ring)
+            streams[stream] = shard
+            found.append(shard)
+            found.append(lax.ppermute(after(shard, gates.get((stream, step, 1)), found), "tm", cores))
     return found
 
 
@@ -310,11 +314,12 @@
     )(w_time)
 
     acts = [None, None]
+    first = []
 
     def early(which, shards):
         acts[which] = pl.pallas_call(
             early_kernel,
-            out_shape=shape((wides[which].shape[0], spots, split), BF16),
+            out_shape=shape((half, spots, split), BF16),
             in_specs=[VMEM] * (1 + cut),
             out_specs=VMEM,
             compiler_params=params,
@@ -322,28 +327,37 @@
         )(wides[which], *shards[:cut])
         return acts[which]
 
+    def begin(found):
+        for which in range(2):
+            if acts[which] is None:
+                early(which, found)
+        first.extend(
+            pl.pallas_call(
+                first_kernel,
+                out_shape=(shape((frames, spots, chans), F32), shape((3, spots, chans), F32)),
+                in_specs=[VMEM] * 4 + [SMEM, VMEM],
+                out_specs=(VMEM, VMEM),
+                compiler_params=params,
+                name="first",
+            )(*lats, *acts, clip_ids, head)
+        )
+        return first[1]
+
     if ringed:
         last = count // 4
         gates = {
-            (1, 2): lambda found: parts[1],
-            (1, last - 1): functools.partial(early, 0),
-            (0, last): functools.partial(early, 1),
+            (0, 2, 0): lambda found: tail,
+            (0, last - 1, 0): lambda found: parts[1],
+            (1, last - 1, 0): functools.partial(early, 0),
+            (0, last, 0): functools.partial(early, 1),
         }
         shards = gather_ring(shard, count, gates)
     else:
         whole = lax.all_gather(shard, "tm", axis=2, tiled=True)
         shards = [whole[:, :, :split], whole[:, :, split:]]
-        early(0, shards)
-        early(1, shards)
-
-    rest, packet = pl.pallas_call(
-        first_kernel,
-        out_shape=(shape((frames, spots, chans), F32), shape((3, spots, chans), F32)),
-        in_specs=[VMEM] * 4 + [SMEM, VMEM],
-        out_specs=(VMEM, VMEM),
-        compiler_params=params,
-        name="first",
-    )(*lats, *acts, clip_ids, head)
+    if not first:
+        begin(shards)
+    rest, packet = first
     acts, packet = pl.pallas_call(
         late_kernel,
         out_shape=(shape((frames, spots, chans - split), BF16), shape((3, spots, chans), BF16)),

time: 54.7 us -> 56.7 us (1.037)
  local copies, waits for them, and re-layouts: 1.75 us -> 3.16 us
  waiting for transfers between devices: 19.7 us -> 20.5 us
    ppermute x14, waiting for transfers between devices: 12.8 us -> 14.4 us  [the longest x7 14.4 us: gather_ring(): lax.ppermute(after(streams[stream], gates.get((stream, step, 0)), found),...]
    unnamed x16, local copies, waits for them, and re-layouts: 1.75 us -> 3.16 us
    ppermute x1, waiting for transfers between devices: 0.89 us -> 0.01 us  [local(): parts = [latents, lax.ppermute(latents, 'rows', [(0, 1), (1, 0)])]]
  transfers between devices with their start and end apart: 17 -> 17, of which waited for: 7 -> 6; matrix products, arithmetic and copies ran while one was open for 0% -> 0% of each run, Pallas kernels for 14% -> 13%
where the time goes in v6:
time: 56.7 us; the launch traced here: 56.5 us
  waiting for transfers between devices  20.5 us (36%)
  Pallas kernels  17.8 us (31%)
  starting transfers between devices  14.9 us (26%)
  local copies, waits for them, and re-layouts  3.16 us (6%)
    ppermute x7, waiting for transfers between devices, gather_ring(): lax.ppermute(after(streams[stream], gates.get((stream, step, 0)), found),...  14.4 us
    ppermute x7, starting transfers between devices, gather_ring(): lax.ppermute(after(streams[stream], gates.get((stream, step, 0)), found),...  10.5 us
    pallas_call x1, Pallas kernels, local(): pl.pallas_call(attend_kernel, out_shape=shape((frames, rows, width, chans...  6.78 us
    ppermute x1, waiting for transfers between devices, local(): packet = lax.ppermute(packet, 'tm', [(i, i + 1) for i in range(count - 1)])  6.03 us
    pallas_call x1, Pallas kernels, local(): pl.pallas_call(late_kernel, out_shape=(shape((frames, spots, chans - spli...  3.57 us
    unnamed x16, local copies, waits for them, and re-layouts  3.16 us
    pallas_call x2, Pallas kernels, early(): pl.pallas_call(early_kernel, out_shape=shape((half, spots, split), BF16),...  2.86 us
    ppermute x1, starting transfers between devices, local(): packet = lax.ppermute(packet, 'tm', [(i, i + 1) for i in range(count - 1)])  2.4 us
  transfers between devices with their start and end apart: 17, of which 6 were waited for; matrix products, arithmetic and copies ran while one was open for 0% of the time, Pallas kernels for 13%

profile of v6, /device:TPU:8, one launch (start us, length us, event | category | flops | bytes accessed | tf_op | source)
XLA Modules:
  0.0 56.5 jit_solution(16196815190183510050)
XLA Ops:
  0.0 1.6 %collective-permute-start.2 = (bf16[3,3,32,512]{3,2,1,0:T(8,128)(2,1)}, bf16[3,3,32,512]{3,2,1,0:T(8,128)(2,1)S(1)}, u32[]{:S(2)}, u32[]{:S(2)}) collective-permute-start(bf16[3,3,32,512]{3,2,1,0:T(8,128)(2,1)} %bitcast.3), channel_id=1, source_target_pairs={{0,8},{2,6},{8,16},{10,2},{16,24},{18,10},{24,28},{26,18},{28,20},... | collective-permute-start | bytes 884744 | tf_op jit(solution)/shard_map/ppermute | solution.py:67
  1.6 0.0 collective-permute-start.1
  1.6 1.5 %collective-permute-start = (bf16[8,2,32,512]{3,2,1,0:T(8,128)(2,1)}, bf16[8,2,32,512]{3,2,1,0:T(8,128)(2,1)S(1)}, u32[]{:S(2)}, u32[]{:S(2)}) collective-permute-start(bf16[8,2,32,512]{3,2,1,0:T(8,128)(2,1)} %refs_0_.3), channel_id=1, source_target_pairs={{0,1},{1,0},{2,3},{3,2},{4,5},{5,4},{6,7},{7,6},{8,9},{9,8},{10,11... | collective-permute-start | bytes 1572872 | tf_op jit(solution)/shard_map/ppermute | solution.py:279
  3.1 0.0 copy-start.1
  3.1 1.4 %copy-done.1 = bf16[3,512,512]{2,1,0:T(8,128)(2,1)S(1)} copy-done((bf16[3,512,512]{2,1,0:T(8,128)(2,1)S(1)}, bf16[3,512,512]{2,1,0:T(8,128)(2,1)}, u32[]{:S(2)}) %copy-start.1) | copy-done | bytes 1572888
  4.5 0.0 copy-start.3
  4.5 0.1 order.1
  4.6 2.3 %collective-permute-done.2.refs_2_ = bf16[3,3,32,512]{3,2,1,0:T(8,128)(2,1)S(1)} collective-permute-done((bf16[3,3,32,512]{3,2,1,0:T(8,128)(2,1)}, bf16[3,3,32,512]{3,2,1,0:T(8,128)(2,1)S(1)}, u32[]{:S(2)}, u32[]{:S(2)}) %collective-permute-start.2) | collective-permute-done | bytes 294944 | tf_op jit(solution)/shard_map/ppermute | solution.py:67
  6.9 0.0 collective-permute-done.1.refs_1_
  6.9 1.6 %collective-permute-start.4 = (bf16[3,3,32,512]{3,2,1,0:T(8,128)(2,1)S(1)}, bf16[3,3,32,512]{3,2,1,0:T(8,128)(2,1)S(1)}, u32[]{:S(2)}, u32[]{:S(2)}) collective-permute-start(bf16[3,3,32,512]{3,2,1,0:T(8,128)(2,1)S(1)} %collective-permute-done.1.refs_1_), channel_id=1, source_target_pairs={{0,8},{2,6},{8,16},{10,2},{16,24},{18,10},{24,28},{26,18},{28,20},... | collective-permute-start | bytes 884744 | tf_op jit(solution)/shard_map/ppermute | solution.py:67
  8.5 1.6 %collective-permute-start.6 = (bf16[3,3,32,512]{3,2,1,0:T(8,128)(2,1)S(1)}, bf16[3,3,32,512]{3,2,1,0:T(8,128)(2,1)S(1)}, u32[]{:S(2)}, u32[]{:S(2)}) collective-permute-start(bf16[3,3,32,512]{3,2,1,0:T(8,128)(2,1)S(1)} %collective-permute-done.2.refs_2_), channel_id=1, source_target_pairs={{0,8},{2,6},{8,16},{10,2},{16,24},{18,10},{24,28},{26,18},{28,20},... | collective-permute-start | bytes 884744 | tf_op jit(solution)/shard_map/ppermute | solution.py:67
  10.1 0.0 collective-permute-start.3
  10.1 3.6 %collective-permute-done.4.refs_4_ = bf16[3,3,32,512]{3,2,1,0:T(8,128)(2,1)S(1)} collective-permute-done((bf16[3,3,32,512]{3,2,1,0:T(8,128)(2,1)S(1)}, bf16[3,3,32,512]{3,2,1,0:T(8,128)(2,1)S(1)}, u32[]{:S(2)}, u32[]{:S(2)}) %collective-permute-start.4) | collective-permute-done | bytes 294944 | tf_op jit(solution)/shard_map/ppermute | solution.py:67
  13.7 0.0 collective-permute-start.5
  13.7 3.2 %collective-permute-done.6.refs_6_ = bf16[3,3,32,512]{3,2,1,0:T(8,128)(2,1)S(1)} collective-permute-done((bf16[3,3,32,512]{3,2,1,0:T(8,128)(2,1)S(1)}, bf16[3,3,32,512]{3,2,1,0:T(8,128)(2,1)S(1)}, u32[]{:S(2)}, u32[]{:S(2)}) %collective-permute-start.6) | collective-permute-done | bytes 294944 | tf_op jit(solution)/shard_map/ppermute | solution.py:67
  16.8 0.0 collective-permute-start.7
  16.8 1.6 %collective-permute-start.8 = (bf16[3,3,32,512]{3,2,1,0:T(8,128)(2,1)S(1)}, bf16[3,3,32,512]{3,2,1,0:T(8,128)(2,1)S(1)}, u32[]{:S(2)}, u32[]{:S(2)}) collective-permute-start(bf16[3,3,32,512]{3,2,1,0:T(8,128)(2,1)S(1)} %collective-permute-done.4.refs_4_), channel_id=1, source_target_pairs={{0,8},{2,6},{8,16},{10,2},{16,24},{18,10},{24,28},{26,18},{28,20},... | collective-permute-start | bytes 884744 | tf_op jit(solution)/shard_map/ppermute | solution.py:67
  18.4 0.0 collective-permute-done.refs_1_
  18.4 1.6 %collective-permute-start.10 = (bf16[3,3,32,512]{3,2,1,0:T(8,128)(2,1)S(1)}, bf16[3,3,32,512]{3,2,1,0:T(8,128)(2,1)S(1)}, u32[]{:S(2)}, u32[]{:S(2)}) collective-permute-start(bf16[3,3,32,512]{3,2,1,0:T(8,128)(2,1)S(1)} %collective-permute-done.6.refs_6_), channel_id=1, source_target_pairs={{0,8},{2,6},{8,16},{10,2},{16,24},{18,10},{24,28},{26,18},{28,20},... | collective-permute-start | bytes 884744 | tf_op jit(solution)/shard_map/ppermute | solution.py:67
  20.0 0.0 copy-start
  20.0 1.0 %copy-done = bf16[8,2,32,512]{3,2,1,0:T(8,128)(2,1)S(1)} copy-done((bf16[8,2,32,512]{3,2,1,0:T(8,128)(2,1)S(1)}, bf16[8,2,32,512]{3,2,1,0:T(8,128)(2,1)}, u32[]{:S(2)}) %copy-start) | copy-done | bytes 524312
  21.0 0.0 copy-start.5
  21.0 0.7 %copy-done.5 = f32[512]{0:T(512)S(1)} copy-done((f32[512]{0:T(512)S(1)}, f32[512]{0:T(512)}, u32[]{:S(2)}) %copy-start.5) | copy-done | bytes 2072
  21.7 0.5 prepare.2
  22.2 0.5 prepare.3
  22.7 0.0 collective-permute-done.3.refs_3_
  22.8 0.0 collective-permute-done.5.refs_5_
  22.8 0.0 collective-permute-done.7.refs_7_
  22.8 0.0 copy-done.3
  22.8 1.4 %early.2.acts0_ref = bf16[4,128,256]{2,1,0:T(8,128)(2,1)S(1)} custom-call(bf16[4,6,32,1536]{3,2,1,0:T(8,128)(2,1)S(1)} %get-tuple-element.19.wide_ref.wide0_ref, bf16[3,3,32,512]{3,2,1,0:T(8,128)(2,1)S(1)} %bitcast.5, bf16[3,3,32,512]{3,2,1,0:T(8,128)(2,1)S(1)} %collective-permute-done.1.refs_1_, bf16[3,3,32,512]{3,2,1,0:T(8,128)(2,1)S(1)} %collective-permute-done.2.refs_2_, ...), custom_call_target="tpu_custom_call" | custom-call | tf_op jit(solution)/shard_map/early/pallas_call | solution.py:320
  24.2 0.0 collective-permute-done.8.refs_0_
  24.2 1.6 %collective-permute-start.12 = (bf16[3,3,32,512]{3,2,1,0:T(8,128)(2,1)S(1)}, bf16[3,3,32,512]{3,2,1,0:T(8,128)(2,1)S(1)}, u32[]{:S(2)}, u32[]{:S(2)}) collective-permute-start(bf16[3,3,32,512]{3,2,1,0:T(8,128)(2,1)S(1)} %collective-permute-done.8.refs_0_), channel_id=1, source_target_pairs={{0,8},{2,6},{8,16},{10,2},{16,24},{18,10},{24,28},{26,18},{28,20},... | collective-permute-start | bytes 884744 | tf_op jit(solution)/shard_map/ppermute | solution.py:67
  25.8 0.0 copy-start.6
  25.8 1.4 %early.3.acts1_ref = bf16[4,128,256]{2,1,0:T(8,128)(2,1)S(1)} custom-call(bf16[4,6,32,1536]{3,2,1,0:T(8,128)(2,1)S(1)} %get-tuple-element.20.wide_ref.wide1_ref, bf16[3,3,32,512]{3,2,1,0:T(8,128)(2,1)S(1)} %bitcast.6, bf16[3,3,32,512]{3,2,1,0:T(8,128)(2,1)S(1)} %collective-permute-done.1.refs_1_, bf16[3,3,32,512]{3,2,1,0:T(8,128)(2,1)S(1)} %collective-permute-done.2.refs_2_, ...), custom_call_target="tpu_custom_call" | custom-call | tf_op jit(solution)/shard_map/early/pallas_call | solution.py:320
  27.2 0.0 collective-permute-done.10.refs_2_
  27.3 1.0 %collective-permute-start.14 = (bf16[3,3,32,512]{3,2,1,0:T(8,128)(2,1)S(1)}, bf16[3,3,32,512]{3,2,1,0:T(8,128)(2,1)S(1)}, u32[]{:S(2)}, u32[]{:S(2)}) collective-permute-start(bf16[3,3,32,512]{3,2,1,0:T(8,128)(2,1)S(1)} %collective-permute-done.10.refs_2_), channel_id=1, source_target_pairs={{0,8},{2,6},{8,16},{10,2},{16,24},{18,10},{24,28},{26,18},{28,20},... | collective-permute-start | bytes 884744 | tf_op jit(solution)/shard_map/ppermute | solution.py:67
  28.3 0.0 collective-permute-start.9
  28.3 0.5 collective-permute-start.11
  28.8 2.2 %collective-permute-done.12.refs_4_ = bf16[3,3,32,512]{3,2,1,0:T(8,128)(2,1)S(1)} collective-permute-done((bf16[3,3,32,512]{3,2,1,0:T(8,128)(2,1)S(1)}, bf16[3,3,32,512]{3,2,1,0:T(8,128)(2,1)S(1)}, u32[]{:S(2)}, u32[]{:S(2)}) %collective-permute-start.12) | collective-permute-done | bytes 294944 | tf_op jit(solution)/shard_map/ppermute | solution.py:67
  31.0 0.0 collective-permute-start.13
  31.0 3.2 %collective-permute-done.14.refs_6_ = bf16[3,3,32,512]{3,2,1,0:T(8,128)(2,1)S(1)} collective-permute-done((bf16[3,3,32,512]{3,2,1,0:T(8,128)(2,1)S(1)}, bf16[3,3,32,512]{3,2,1,0:T(8,128)(2,1)S(1)}, u32[]{:S(2)}, u32[]{:S(2)}) %collective-permute-start.14) | collective-permute-done | bytes 294944 | tf_op jit(solution)/shard_map/ppermute | solution.py:67
  34.2 0.0 collective-permute-start.15
  34.2 0.0 copy-done.6
  34.2 1.9 %first.1 = (f32[8,128,512]{2,1,0:T(8,128)S(1)}, f32[3,128,512]{2,1,0:T(8,128)S(1)}) custom-call(bf16[4,4,32,512]{3,2,1,0:T(8,128)(2,1)S(1)} %get-tuple-element.22.lat0_ref, bf16[4,4,32,512]{3,2,1,0:T(8,128)(2,1)S(1)} %get-tuple-element.23.lat1_ref, bf16[4,128,256]{2,1,0:T(8,128)(2,1)S(1)} %early.2.acts0_ref, bf16[4,128,256]{2,1,0:T(8,128)(2,1)S(1)} %early.3.acts1_ref, ...), custom_call_target="tpu_custom_call" | custom-call | tf_op jit(solution)/shard_map/first/pallas_call | solution.py:335
  36.1 0.0 collective-permute-done.9.refs_1_
  36.1 0.0 collective-permute-done.11.refs_3_
  36.1 0.0 collective-permute-done.13.refs_5_
  36.1 0.0 collective-permute-done.15.refs_7_
  36.1 3.6 %late.1 = (bf16[8,128,256]{2,1,0:T(8,128)(2,1)S(1)}, bf16[3,128,512]{2,1,0:T(8,128)(2,1)S(1)}) custom-call(bf16[4,6,32,1536]{3,2,1,0:T(8,128)(2,1)S(1)} %get-tuple-element.19.wide_ref.wide0_ref, bf16[4,6,32,1536]{3,2,1,0:T(8,128)(2,1)S(1)} %get-tuple-element.20.wide_ref.wide1_ref, s32[128]{0:T(128)S(1)} %copy-done.6, ...), custom_call_target="tpu_custom_call" | custom-call | tf_op jit(solution)/shard_map/late/pallas_call | solution.py:361
  39.7 2.4 %collective-permute-start.16 = (bf16[3,128,512]{2,1,0:T(8,128)(2,1)S(1)}, bf16[3,128,512]{2,1,0:T(8,128)(2,1)S(1)}, u32[]{:S(2)}, u32[]{:S(2)}) collective-permute-start(bf16[3,128,512]{2,1,0:T(8,128)(2,1)S(1)} %get-tuple-element.32), channel_id=1, source_target_pairs={{0,2},{2,4},{4,6},{6,8},{8,10},{10,12},{12,14},{14,16},{16,18},{18... | collective-permute-start | bytes 1179656 | tf_op jit(solution)/shard_map/ppermute | solution.py:369
  42.1 0.0 copy-start.2
  42.1 0.0 copy-start.4
  42.1 0.0 copy-start.7
  42.1 1.5 %rest.1.rest_ref = f32[8,128,512]{2,1,0:T(8,128)S(1)} custom-call(bf16[8,128,256]{2,1,0:T(8,128)(2,1)S(1)} %get-tuple-element.30.acts_ref, s32[128]{0:T(128)S(1)} %copy-done.6, bf16[3,256,512]{2,1,0:T(8,128)(2,1)S(1)} %get-tuple-element.21.weights, f32[8,128,512]{2,1,0:T(8,128)S(1)} %get-tuple-element.31.early_ref), custom_call_target="tpu_custom_call" | custom-call | tf_op jit(solution)/shard_map/rest/pallas_call | solution.py:370
  43.7 6.0 %collective-permute-done.16.packet_ref = bf16[3,128,512]{2,1,0:T(8,128)(2,1)S(1)} collective-permute-done((bf16[3,128,512]{2,1,0:T(8,128)(2,1)S(1)}, bf16[3,128,512]{2,1,0:T(8,128)(2,1)S(1)}, u32[]{:S(2)}, u32[]{:S(2)}) %collective-permute-start.16) | collective-permute-done | bytes 393248 | tf_op jit(solution)/shard_map/ppermute | solution.py:369
  49.7 0.0 copy-done.2
  49.7 0.0 copy-done.4
  49.7 0.0 copy-done.7
  49.7 6.8 %attend.1 = bf16[8,2,32,512]{3,2,1,0:T(8,128)(2,1)} custom-call(f32[8,128,512]{2,1,0:T(8,128)S(1)} %rest.1.rest_ref, bf16[3,128,512]{2,1,0:T(8,128)(2,1)S(1)} %collective-permute-done.16.packet_ref, s32[128]{0:T(128)S(1)} %copy-done.6, f32[1,512]{1,0:T(1,128)S(1)} %bitcast.9, bf16[512,1536]{1,0:T(8,128)(2,1)S(1)} %copy-done.2, bf16[512,512]{1,0:T(8,128)(2,1)S(1)} %copy-done.4), custom_call_target="tpu_custom_call" | custom-call | tf_op jit(solution)/shard_map/attend/pallas_call | solution.py:378
Async XLA Ops:
  0.0 6.9 %collective-permute-start.2 = (bf16[3,3,32,512]{3,2,1,0:T(8,128)(2,1)}, bf16[3,3,32,512]{3,2,1,0:T(8,128)(2,1)S(1)}, u32[]{:S(2)}, u32[]{:S(2)}) collective-permute-start(bf16[3,3,32,512]{3,2,1,0:T(8,128)(2,1)} %bitcast.3), channel_id=1, source_target_pairs={{0,8},{2,6},{8,16},{10,2},{16,24},{18,10},{24,28},{26,18},{28,20},... | collective-permute-start | bytes 884744 | tf_op jit(solution)/shard_map/ppermute | solution.py:67
  1.6 5.4 %collective-permute-start.1 = (bf16[3,3,32,512]{3,2,1,0:T(8,128)(2,1)}, bf16[3,3,32,512]{3,2,1,0:T(8,128)(2,1)S(1)}, u32[]{:S(2)}, u32[]{:S(2)}) collective-permute-start(bf16[3,3,32,512]{3,2,1,0:T(8,128)(2,1)} %bitcast.4), channel_id=1, source_target_pairs={{0,2},{2,0},{4,6},{6,4},{8,10},{10,8},{12,14},{14,12},{16,18},{18,... | collective-permute-start | bytes 884744 | tf_op jit(solution)/shard_map/ppermute | solution.py:63
  1.6 16.8 %collective-permute-start = (bf16[8,2,32,512]{3,2,1,0:T(8,128)(2,1)}, bf16[8,2,32,512]{3,2,1,0:T(8,128)(2,1)S(1)}, u32[]{:S(2)}, u32[]{:S(2)}) collective-permute-start(bf16[8,2,32,512]{3,2,1,0:T(8,128)(2,1)} %refs_0_.3), channel_id=1, source_target_pairs={{0,1},{1,0},{2,3},{3,2},{4,5},{5,4},{6,7},{7,6},{8,9},{9,8},{10,11... | collective-permute-start | bytes 1572872 | tf_op jit(solution)/shard_map/ppermute | solution.py:279
  3.1 1.4 %copy-start.1 = (bf16[3,512,512]{2,1,0:T(8,128)(2,1)S(1)}, bf16[3,512,512]{2,1,0:T(8,128)(2,1)}, u32[]{:S(2)}) copy-start(bf16[3,512,512]{2,1,0:T(8,128)(2,1)} %time_ref.1) | copy-start | bytes 4718596
  4.5 18.3 %copy-start.3 = (bf16[3,3,512,32]{2,3,1,0:T(8,128)(2,1)S(1)}, bf16[3,3,512,32]{2,3,1,0:T(8,128)(2,1)}, u32[]{:S(2)}) copy-start(bf16[3,3,512,32]{2,3,1,0:T(8,128)(2,1)} %param.11) | copy-start | bytes 884740
  6.9 6.7 %collective-permute-start.4 = (bf16[3,3,32,512]{3,2,1,0:T(8,128)(2,1)S(1)}, bf16[3,3,32,512]{3,2,1,0:T(8,128)(2,1)S(1)}, u32[]{:S(2)}, u32[]{:S(2)}) collective-permute-start(bf16[3,3,32,512]{3,2,1,0:T(8,128)(2,1)S(1)} %collective-permute-done.1.refs_1_), channel_id=1, source_target_pairs={{0,8},{2,6},{8,16},{10,2},{16,24},{18,10},{24,28},{26,18},{28,20},... | collective-permute-start | bytes 884744 | tf_op jit(solution)/shard_map/ppermute | solution.py:67
  8.5 8.3 %collective-permute-start.6 = (bf16[3,3,32,512]{3,2,1,0:T(8,128)(2,1)S(1)}, bf16[3,3,32,512]{3,2,1,0:T(8,128)(2,1)S(1)}, u32[]{:S(2)}, u32[]{:S(2)}) collective-permute-start(bf16[3,3,32,512]{3,2,1,0:T(8,128)(2,1)S(1)} %collective-permute-done.2.refs_2_), channel_id=1, source_target_pairs={{0,8},{2,6},{8,16},{10,2},{16,24},{18,10},{24,28},{26,18},{28,20},... | collective-permute-start | bytes 884744 | tf_op jit(solution)/shard_map/ppermute | solution.py:67
  10.1 12.7 %collective-permute-start.3 = (bf16[3,3,32,512]{3,2,1,0:T(8,128)(2,1)S(1)}, bf16[3,3,32,512]{3,2,1,0:T(8,128)(2,1)S(1)}, u32[]{:S(2)}, u32[]{:S(2)}) collective-permute-start(bf16[3,3,32,512]{3,2,1,0:T(8,128)(2,1)S(1)} %collective-permute-done.2.refs_2_), channel_id=1, source_target_pairs={{0,2},{2,0},{4,6},{6,4},{8,10},{10,8},{12,14},{14,12},{16,18},{18,... | collective-permute-start | bytes 884744 | tf_op jit(solution)/shard_map/ppermute | solution.py:70
  13.7 9.1 %collective-permute-start.5 = (bf16[3,3,32,512]{3,2,1,0:T(8,128)(2,1)S(1)}, bf16[3,3,32,512]{3,2,1,0:T(8,128)(2,1)S(1)}, u32[]{:S(2)}, u32[]{:S(2)}) collective-permute-start(bf16[3,3,32,512]{3,2,1,0:T(8,128)(2,1)S(1)} %collective-permute-done.4.refs_4_), channel_id=1, source_target_pairs={{0,2},{2,0},{4,6},{6,4},{8,10},{10,8},{12,14},{14,12},{16,18},{18,... | collective-permute-start | bytes 884744 | tf_op jit(solution)/shard_map/ppermute | solution.py:70
  16.8 5.9 %collective-permute-start.7 = (bf16[3,3,32,512]{3,2,1,0:T(8,128)(2,1)S(1)}, bf16[3,3,32,512]{3,2,1,0:T(8,128)(2,1)S(1)}, u32[]{:S(2)}, u32[]{:S(2)}) collective-permute-start(bf16[3,3,32,512]{3,2,1,0:T(8,128)(2,1)S(1)} %collective-permute-done.6.refs_6_), channel_id=1, source_target_pairs={{0,2},{2,0},{4,6},{6,4},{8,10},{10,8},{12,14},{14,12},{16,18},{18,... | collective-permute-start | bytes 884744 | tf_op jit(solution)/shard_map/ppermute | solution.py:70
  16.8 7.4 %collective-permute-start.8 = (bf16[3,3,32,512]{3,2,1,0:T(8,128)(2,1)S(1)}, bf16[3,3,32,512]{3,2,1,0:T(8,128)(2,1)S(1)}, u32[]{:S(2)}, u32[]{:S(2)}) collective-permute-start(bf16[3,3,32,512]{3,2,1,0:T(8,128)(2,1)S(1)} %collective-permute-done.4.refs_4_), channel_id=1, source_target_pairs={{0,8},{2,6},{8,16},{10,2},{16,24},{18,10},{24,28},{26,18},{28,20},... | collective-permute-start | bytes 884744 | tf_op jit(solution)/shard_map/ppermute | solution.py:67
  18.4 8.8 %collective-permute-start.10 = (bf16[3,3,32,512]{3,2,1,0:T(8,128)(2,1)S(1)}, bf16[3,3,32,512]{3,2,1,0:T(8,128)(2,1)S(1)}, u32[]{:S(2)}, u32[]{:S(2)}) collective-permute-start(bf16[3,3,32,512]{3,2,1,0:T(8,128)(2,1)S(1)} %collective-permute-done.6.refs_6_), channel_id=1, source_target_pairs={{0,8},{2,6},{8,16},{10,2},{16,24},{18,10},{24,28},{26,18},{28,20},... | collective-permute-start | bytes 884744 | tf_op jit(solution)/shard_map/ppermute | solution.py:67
  20.0 1.0 %copy-start = (bf16[8,2,32,512]{3,2,1,0:T(8,128)(2,1)S(1)}, bf16[8,2,32,512]{3,2,1,0:T(8,128)(2,1)}, u32[]{:S(2)}) copy-start(bf16[8,2,32,512]{3,2,1,0:T(8,128)(2,1)} %refs_0_.3) | copy-start | bytes 1572868
  21.0 0.7 %copy-start.5 = (f32[512]{0:T(512)S(1)}, f32[512]{0:T(512)}, u32[]{:S(2)}) copy-start(f32[512]{0:T(512)} %param.10) | copy-start | bytes 6148
  24.2 6.8 %collective-permute-start.12 = (bf16[3,3,32,512]{3,2,1,0:T(8,128)(2,1)S(1)}, bf16[3,3,32,512]{3,2,1,0:T(8,128)(2,1)S(1)}, u32[]{:S(2)}, u32[]{:S(2)}) collective-permute-start(bf16[3,3,32,512]{3,2,1,0:T(8,128)(2,1)S(1)} %collective-permute-done.8.refs_0_), channel_id=1, source_target_pairs={{0,8},{2,6},{8,16},{10,2},{16,24},{18,10},{24,28},{26,18},{28,20},... | collective-permute-start | bytes 884744 | tf_op jit(solution)/shard_map/ppermute | solution.py:67
  25.8 8.4 %copy-start.6 = (s32[128]{0:T(128)S(1)}, s32[128]{0:T(128)}, u32[]{:S(2)}) copy-start(s32[128]{0:T(128)} %clips.7) | copy-start | bytes 1540
  27.3 6.9 %collective-permute-start.14 = (bf16[3,3,32,512]{3,2,1,0:T(8,128)(2,1)S(1)}, bf16[3,3,32,512]{3,2,1,0:T(8,128)(2,1)S(1)}, u32[]{:S(2)}, u32[]{:S(2)}) collective-permute-start(bf16[3,3,32,512]{3,2,1,0:T(8,128)(2,1)S(1)} %collective-permute-done.10.refs_2_), channel_id=1, source_target_pairs={{0,8},{2,6},{8,16},{10,2},{16,24},{18,10},{24,28},{26,18},{28,20},... | collective-permute-start | bytes 884744 | tf_op jit(solution)/shard_map/ppermute | solution.py:67
  28.3 7.8 %collective-permute-start.9 = (bf16[3,3,32,512]{3,2,1,0:T(8,128)(2,1)S(1)}, bf16[3,3,32,512]{3,2,1,0:T(8,128)(2,1)S(1)}, u32[]{:S(2)}, u32[]{:S(2)}) collective-permute-start(bf16[3,3,32,512]{3,2,1,0:T(8,128)(2,1)S(1)} %collective-permute-done.8.refs_0_), channel_id=1, source_target_pairs={{0,2},{2,0},{4,6},{6,4},{8,10},{10,8},{12,14},{14,12},{16,18},{18,... | collective-permute-start | bytes 884744 | tf_op jit(solution)/shard_map/ppermute | solution.py:70
  28.3 7.8 %collective-permute-start.11 = (bf16[3,3,32,512]{3,2,1,0:T(8,128)(2,1)S(1)}, bf16[3,3,32,512]{3,2,1,0:T(8,128)(2,1)S(1)}, u32[]{:S(2)}, u32[]{:S(2)}) collective-permute-start(bf16[3,3,32,512]{3,2,1,0:T(8,128)(2,1)S(1)} %collective-permute-done.10.refs_2_), channel_id=1, source_target_pairs={{0,2},{2,0},{4,6},{6,4},{8,10},{10,8},{12,14},{14,12},{16,18},{18,... | collective-permute-start | bytes 884744 | tf_op jit(solution)/shard_map/ppermute | solution.py:70
  31.0 5.1 %collective-permute-start.13 = (bf16[3,3,32,512]{3,2,1,0:T(8,128)(2,1)S(1)}, bf16[3,3,32,512]{3,2,1,0:T(8,128)(2,1)S(1)}, u32[]{:S(2)}, u32[]{:S(2)}) collective-permute-start(bf16[3,3,32,512]{3,2,1,0:T(8,128)(2,1)S(1)} %collective-permute-done.12.refs_4_), channel_id=1, source_target_pairs={{0,2},{2,0},{4,6},{6,4},{8,10},{10,8},{12,14},{14,12},{16,18},{18,... | collective-permute-start | bytes 884744 | tf_op jit(solution)/shard_map/ppermute | solution.py:70
  34.2 1.9 %collective-permute-start.15 = (bf16[3,3,32,512]{3,2,1,0:T(8,128)(2,1)S(1)}, bf16[3,3,32,512]{3,2,1,0:T(8,128)(2,1)S(1)}, u32[]{:S(2)}, u32[]{:S(2)}) collective-permute-start(bf16[3,3,32,512]{3,2,1,0:T(8,128)(2,1)S(1)} %collective-permute-done.14.refs_6_), channel_id=1, source_target_pairs={{0,2},{2,0},{4,6},{6,4},{8,10},{10,8},{12,14},{14,12},{16,18},{18,... | collective-permute-start | bytes 884744 | tf_op jit(solution)/shard_map/ppermute | solution.py:70
  39.7 10.0 %collective-permute-start.16 = (bf16[3,128,512]{2,1,0:T(8,128)(2,1)S(1)}, bf16[3,128,512]{2,1,0:T(8,128)(2,1)S(1)}, u32[]{:S(2)}, u32[]{:S(2)}) collective-permute-start(bf16[3,128,512]{2,1,0:T(8,128)(2,1)S(1)} %get-tuple-element.32), channel_id=1, source_target_pairs={{0,2},{2,4},{4,6},{6,8},{8,10},{10,12},{12,14},{14,16},{16,18},{18... | collective-permute-start | bytes 1179656 | tf_op jit(solution)/shard_map/ppermute | solution.py:369
  42.1 7.6 %copy-start.2 = (bf16[512,1536]{1,0:T(8,128)(2,1)S(1)}, bf16[512,1536]{1,0:T(8,128)(2,1)}, u32[]{:S(2)}) copy-start(bf16[512,1536]{1,0:T(8,128)(2,1)} %qkv_ref.1) | copy-start | bytes 4718596
  42.1 7.6 %copy-start.4 = (bf16[512,512]{1,0:T(8,128)(2,1)S(1)}, bf16[512,512]{1,0:T(8,128)(2,1)}, u32[]{:S(2)}) copy-start(bf16[512,512]{1,0:T(8,128)(2,1)} %proj_ref.1) | copy-start | bytes 1572868
  42.1 7.6 %copy-start.7 = (f32[512]{0:T(512)S(1)}, f32[512]{0:T(512)}, u32[]{:S(2)}) copy-start(f32[512]{0:T(512)} %param.13) | copy-start | bytes 6148

commit v7 on v6

--- a/solution.py
+++ b/solution.py
@@ -80,48 +80,41 @@
     return device_at(spot, (core + flip) % 2, count)
 
 
-def prepare_kernel(start, *refs):
-    *parts, gain_ref, wide_ref, lat_ref = refs
-    _, rows, width, chans = parts[0].shape
+def prepare_kernel(start, at, groups, *refs):
+    part, gain_ref, wide_ref, lat_ref = *refs[:2], *refs[-2:]
+    _, rows, width, chans = part.shape
     frames = wide_ref.shape[0]
-    groups = len(parts)
-    mine = lax.axis_index("rows")
     gain = gain_ref[...]
     column = lax.broadcasted_iota(jnp.int32, (rows * width, 1), 0) % width
     edge = jnp.zeros((width, 3 * chans), BF16)
+    first = at * rows
+    if groups == 2:
+        mine = lax.axis_index("rows")
+        first = (mine if at == 0 else 1 - mine) * rows
     for frame in range(frames):
-        wide_ref[frame, 0] = edge
-        wide_ref[frame, groups * rows + 1] = edge
-    for at, part in enumerate(parts):
-        first = at * rows
-        if groups == 2:
-            first = (mine if at == 0 else 1 - mine) * rows
-        for frame in range(frames):
-            raw = part[start + frame]
-            lat_ref[frame, pl.ds(first, rows)] = raw
-            x = raw.reshape(rows * width, chans).astype(F32)
-            y = x * lax.rsqrt(jnp.mean(x * x, axis=-1, keepdims=True) + 1e-06) * gain
-            before = jnp.where(column == 0, 0.0, pltpu.roll(y, 1, 0))
-            after = jnp.where(column == width - 1, 0.0, pltpu.roll(y, rows * width - 1, 0))
-            for dx, v in enumerate((before, y, after)):
-                wide_ref[frame, pl.ds(first + 1, rows), :, dx * chans : (dx + 1) * chans] = v.astype(
-                    BF16
-                ).reshape(rows, width, chans)
-
-
-def order_kernel(tags, time_ref, head_ref, tail_ref):
-    block = time_ref.shape[1] // len(tags)
+        if at == 0:
+            wide_ref[frame, 0] = edge
+            wide_ref[frame, groups * rows + 1] = edge
+        raw = part[start + frame]
+        lat_ref[frame, pl.ds(first, rows)] = raw
+        x = raw.reshape(rows * width, chans).astype(F32)
+        y = x * lax.rsqrt(jnp.mean(x * x, axis=-1, keepdims=True) + 1e-06) * gain
+        before = jnp.where(column == 0, 0.0, pltpu.roll(y, 1, 0))
+        after = jnp.where(column == width - 1, 0.0, pltpu.roll(y, rows * width - 1, 0))
+        for dx, v in enumerate((before, y, after)):
+            wide_ref[frame, pl.ds(first + 1, rows), :, dx * chans : (dx + 1) * chans] = v.astype(
+                BF16
+            ).reshape(rows, width, chans)
+
+
+def ordered(time_ref, tags, slots):
+    block = time_ref.shape[1] // slots
     device = lax.axis_index("tm")
-    for slot, tag in enumerate(tags):
-        owner = tag
-        if isinstance(tag, tuple):
-            owner = shard_owner(tag, device, len(tags))
-        source = pl.ds(pl.multiple_of(owner * block, block), block)
-        to_ref, at = head_ref, slot * block
-        if at >= head_ref.shape[1]:
-            to_ref, at = tail_ref, at - head_ref.shape[1]
-        for back in range(3):
-            to_ref[back, at : at + block] = time_ref[back, source]
+    rows = []
+    for tag in tags:
+        owner = shard_owner(tag, device, slots) if isinstance(tag, tuple) else tag
+        rows.append(pl.ds(pl.multiple_of(owner * block, block), block))
+    return [jnp.concatenate([time_ref[back, row] for row in rows], axis=0) for back in range(3)]
 
 
 def convolve(wide_ref, shards):
@@ -193,7 +186,8 @@
     acts_ref[...] = convolve(wide_ref, shards)
 
 
-def first_kernel(lat0_ref, lat1_ref, acts0_ref, acts1_ref, clips, weights, rest_ref, packet_ref):
+def first_kernel(tags, slots, lat0_ref, lat1_ref, acts0_ref, acts1_ref, clips, time_ref, rest_ref, packet_ref):
+    weights = ordered(time_ref, tags, slots)
     acts = [ref[t] for ref in (acts0_ref, acts1_ref) for t in range(ref.shape[0])]
     lat = [ref[t].reshape(acts[0].shape[0], -1) for ref in (lat0_ref, lat1_ref) for t in range(ref.shape[0])]
     frames = len(acts)
@@ -204,65 +198,93 @@
         rest_ref[t] = rest[t] + lat[t].astype(F32)
 
 
-def late_kernel(wide0_ref, wide1_ref, clips, weights, early_ref, *refs):
+def late_kernel(tags, slots, wide0_ref, wide1_ref, clips, time_ref, early_ref, *refs):
     *shards, acts_ref, packet_ref = refs
     half, frames = wide0_ref.shape[0], acts_ref.shape[0]
     acts_ref[:half] = convolve(wide0_ref, shards)
     acts_ref[half:] = convolve(wide1_ref, shards)
     acts = [acts_ref[t] for t in range(frames)]
+    weights = ordered(time_ref, tags, slots)
     for i, part in enumerate(packet_sums(acts, clips, weights, frames)):
         packet_ref[i] = (early_ref[i] + part).astype(BF16)
 
 
-def rest_kernel(acts_ref, clips, weights, early_ref, rest_ref):
-    frames = acts_ref.shape[0]
-    part = temporal([acts_ref[t] for t in range(frames)], clips, weights, frames)
-    rest_ref[...] = early_ref[...] + part.reshape(rest_ref.shape)
-
-
-def attend_kernel(rest_ref, packet_ref, clips, gain_ref, qkv_ref, proj_ref, out_ref, mixed_ref, normed_ref):
-    frames, rows, width, chans = out_ref.shape
-    height = mixed_ref.shape[1]
-    spots = height * width
-    own = rows * width
+def places(clips, frames):
     first = lax.axis_index("tm") * frames
-    mine = pl.ds(lax.axis_index("rows") * rows, rows)
-    gain = gain_ref[...]
-
     number = jnp.int32(1)
     for back in range(1, LONGEST):
         at = first - back
         hit = jnp.logical_and(at >= 0, clips[jnp.maximum(at, 0)] == clips[first])
         number = number + hit.astype(jnp.int32)
-    running = packet_ref[2].astype(F32)
-    for t in range(frames):
-        resid = rest_ref[t]
-        if t < 2:
-            resid = resid + packet_ref[t].astype(F32)
-        if t > 0:
-            same = clips[first + t] == clips[first + t - 1]
-            running = keep(same, running)
-            number = jnp.where(same, number + 1, 1)
-        running = running + resid
-        mixed = (resid + running / jnp.full((1, chans), number.astype(F32))).astype(BF16)
-        mixed_ref[t] = mixed.reshape(height, width, chans)
-        x = mixed.astype(F32)
-        y = x * lax.rsqrt(jnp.mean(x * x, axis=-1, keepdims=True) + 1e-06) * gain
-        normed_ref[t] = y.astype(BF16).reshape(height, width, chans)
-
-    query = dot(normed_ref[:, mine].reshape(frames * own, chans), qkv_ref[:, :chans]).astype(BF16)
-    both = dot(normed_ref[...].reshape(frames * spots, chans), qkv_ref[:, chans:]).astype(BF16)
-    attended = []
-    for t in range(frames):
-        key = both[t * spots : (t + 1) * spots, :chans]
-        value = both[t * spots : (t + 1) * spots, chans:]
-        scores = dot_t(query[t * own : (t + 1) * own], key) * chans ** (-0.5)
-        weights = jnp.exp(scores - jnp.max(scores, axis=-1, keepdims=True))
-        probs = (weights / jnp.sum(weights, axis=-1, keepdims=True)).astype(BF16)
-        attended.append(dot(probs, value).astype(BF16))
-    result = dot(jnp.concatenate(attended, axis=0), proj_ref[...])
-    result = result + mixed_ref[:, mine].reshape(frames * own, chans).astype(F32)
-    out_ref[...] = result.astype(BF16).reshape(frames, rows, width, chans)
+    found = [(None, clips[first] == clips[first], number)]
+    for t in range(1, frames):
+        same = clips[first + t] == clips[first + t - 1]
+        number = jnp.where(same, number + 1, 1)
+        found.append((same, clips[first + t] == clips[first], number))
+    return found
+
+
+def share(number, chans):
+    return 1.0 / jnp.full((1, chans), number.astype(F32))
+
+
+def rest_kernel(tags, slots, acts_ref, clips, time_ref, early_ref, base_ref):
+    frames, spots, chans = base_ref.shape
+    weights = ordered(time_ref, tags, slots)
+    part = temporal([acts_ref[t] for t in range(frames)], clips, weights, frames)
+    running = None
+    for t, (same, _, number) in enumerate(places(clips, frames)):
+        resid = early_ref[t] + part[t * spots : (t + 1) * spots]
+        running = resid if t == 0 else keep(same, running) + resid
+        base_ref[t] = resid + running * share(number, chans)
+
+
+def attend_kernel(base_ref, packet_ref, clips, gain_ref, qkv_ref, proj_ref, out_ref, mixed_ref, normed_ref):
+    frames, rows, width, chans = out_ref.shape
+    height = mixed_ref.shape[1]
+    spots = height * width
+    own = rows * width
+    mine = pl.ds(lax.axis_index("rows") * rows, rows)
+    gain = gain_ref[...]
+    place = places(clips, frames)
+    step = frames // 2
+    joint = 2 if spots <= 128 and step % 2 == 0 else 1
+    blocked = (
+        lax.broadcasted_iota(jnp.int32, (joint * own, joint * spots), 0) // own
+        != lax.broadcasted_iota(jnp.int32, (joint * own, joint * spots), 1) // spots
+    )
+
+    terms = [packet_ref[0].astype(F32), packet_ref[1].astype(F32)]
+    carried = packet_ref[2].astype(F32) + terms[0]
+    for start in range(0, frames, step):
+        for t in range(start, start + step):
+            if t == 1:
+                carried = carried + terms[1]
+            _, among, number = place[t]
+            mixed = base_ref[t] + carried * keep(among, share(number, chans))
+            if t < 2:
+                mixed = mixed + terms[t]
+            mixed = mixed.astype(BF16)
+            mixed_ref[t] = mixed.reshape(height, width, chans)
+            x = mixed.astype(F32)
+            y = x * lax.rsqrt(jnp.mean(x * x, axis=-1, keepdims=True) + 1e-06) * gain
+            normed_ref[t] = y.astype(BF16).reshape(height, width, chans)
+        span = slice(start, start + step)
+        query = dot(normed_ref[span, mine].reshape(step * own, chans), qkv_ref[:, :chans]).astype(BF16)
+        both = dot(normed_ref[span].reshape(step * spots, chans), qkv_ref[:, chans:]).astype(BF16)
+        attended = []
+        for t in range(0, step, joint):
+            key = both[t * spots : (t + joint) * spots, :chans]
+            value = both[t * spots : (t + joint) * spots, chans:]
+            scores = dot_t(query[t * own : (t + joint) * own], key) * chans ** (-0.5)
+            if joint > 1:
+                scores = jnp.where(blocked, -jnp.inf, scores)
+            weights = jnp.exp(scores - jnp.max(scores, axis=-1, keepdims=True))
+            probs = (weights / jnp.sum(weights, axis=-1, keepdims=True)).astype(BF16)
+            attended.append(dot(probs, value).astype(BF16))
+        result = dot(jnp.concatenate(attended, axis=0), proj_ref[...])
+        result = result + mixed_ref[span, mine].reshape(step * own, chans).astype(F32)
+        out_ref[span] = result.astype(BF16).reshape(step, rows, width, chans)
 
 
 def local(latents, clip_ids, gain_in, w_space, w_time, gain_attn, w_qkv, w_out):
@@ -288,31 +310,28 @@
     split = cut * (chans // len(tags))
 
     gain = gain_in.reshape(1, chans)
-    prepared = [
-        pl.pallas_call(
-            functools.partial(prepare_kernel, start),
-            out_shape=(
-                shape((half, height + 2, width, 3 * chans), BF16),
-                shape((half, height, width, chans), BF16),
-            ),
-            in_specs=[VMEM] * (groups + 1),
-            out_specs=(VMEM, VMEM),
-            compiler_params=params,
-            name="prepare",
-        )(*parts, gain)
-        for start in (0, half)
-    ]
+    prepared = []
+    own = []
+    for start in (0, half):
+        pair = ()
+        for at, part in enumerate(parts):
+            pair = pl.pallas_call(
+                functools.partial(prepare_kernel, start, at, groups),
+                out_shape=(
+                    shape((half, height + 2, width, 3 * chans), BF16),
+                    shape((half, height, width, chans), BF16),
+                ),
+                in_specs=[VMEM] * (2 + len(pair)),
+                out_specs=(VMEM, VMEM),
+                input_output_aliases={2: 0, 3: 1} if pair else {},
+                compiler_params=params,
+                name="prepare",
+            )(part, gain, *pair)
+            if at == 0:
+                own.append(pair)
+        prepared.append(pair)
     wides = [pair[0] for pair in prepared]
     lats = [pair[1] for pair in prepared]
-    head, tail = pl.pallas_call(
-        functools.partial(order_kernel, tags),
-        out_shape=(shape((3, split, chans), BF16), shape((3, chans - split, chans), BF16)),
-        in_specs=[VMEM],
-        out_specs=(VMEM, VMEM),
-        compiler_params=params,
-        name="order",
-    )(w_time)
-
     acts = [None, None]
     first = []
 
@@ -333,23 +352,25 @@
                 early(which, found)
         first.extend(
             pl.pallas_call(
-                first_kernel,
+                functools.partial(first_kernel, tags[:cut], len(tags)),
                 out_shape=(shape((frames, spots, chans), F32), shape((3, spots, chans), F32)),
                 in_specs=[VMEM] * 4 + [SMEM, VMEM],
                 out_specs=(VMEM, VMEM),
                 compiler_params=params,
                 name="first",
-            )(*lats, *acts, clip_ids, head)
+            )(*lats, *acts, clip_ids, w_time)
         )
         return first[1]
 
     if ringed:
         last = count // 4
         gates = {
-            (0, 2, 0): lambda found: tail,
-            (0, last - 1, 0): lambda found: parts[1],
+            (1, 1, 1): lambda found: own,
+            (1, last - 2, 1): lambda found: parts[1],
             (1, last - 1, 0): functools.partial(early, 0),
+            (1, last - 1, 1): lambda found: found[9],
             (0, last, 0): functools.partial(early, 1),
+            (0, last, 1): begin,
         }
         shards = gather_ring(shard, count, gates)
     else:
@@ -359,22 +380,22 @@
         begin(shards)
     rest, packet = first
     acts, packet = pl.pallas_call(
-        late_kernel,
+        functools.partial(late_kernel, tags[cut:], len(tags)),
         out_shape=(shape((frames, spots, chans - split), BF16), shape((3, spots, chans), BF16)),
         in_specs=[VMEM, VMEM, SMEM, VMEM, VMEM] + [VMEM] * (len(tags) - cut),
         out_specs=(VMEM, VMEM),
         compiler_params=params,
         name="late",
-    )(*wides, clip_ids, tail, packet, *shards[cut:])
+    )(*wides, clip_ids, w_time, packet, *shards[cut:])
     packet = lax.ppermute(packet, "tm", [(i, i + 1) for i in range(count - 1)])
     rest = pl.pallas_call(
-        rest_kernel,
+        functools.partial(rest_kernel, tags[cut:], len(tags)),
         out_shape=shape((frames, spots, chans), F32),
         in_specs=[VMEM, SMEM, VMEM, VMEM],
         out_specs=VMEM,
         compiler_params=params,
         name="rest",
-    )(acts, clip_ids, tail, rest)
+    )(acts, clip_ids, w_time, rest)
     return pl.pallas_call(
         attend_kernel,
         out_shape=shape((frames, rows, width, chans), BF16),

time: 56.7 us -> 49.6 us (0.87)
  waiting for transfers between devices: 20.5 us -> 15.8 us
  Pallas kernels: 17.8 us -> 16.3 us
  local copies, waits for them, and re-layouts: 3.16 us -> 1.75 us
    ppermute x7, waiting for transfers between devices: 14.4 us -> 7.1 us  [gather_ring(): lax.ppermute(after(streams[stream], gates.get((stream, step, 0)), found),...]
    pallas_call x1, Pallas kernels: 6.78 us -> 5.11 us  [local(): pl.pallas_call(attend_kernel, out_shape=shape((frames, rows, width, chans...]
    ppermute x7, waiting for transfers between devices: 0.02 us -> 1.59 us  [gather_ring(): lax.ppermute(after(shard, gates.get((stream, step, 1)), found), 'tm', cores)]
    unnamed x16, local copies, waits for them, and re-layouts: 3.16 us -> 1.75 us
    ppermute x1, waiting for transfers between devices: 0.01 us -> 0.89 us  [local(): parts = [latents, lax.ppermute(latents, 'rows', [(0, 1), (1, 0)])]]
    ppermute x7, starting transfers between devices: 10.5 us -> 11.3 us  [gather_ring(): lax.ppermute(after(streams[stream], gates.get((stream, step, 0)), found),...]
    pallas_call x6 -> x7, Pallas kernels: 8.12 us -> 8.38 us  [the longest x1 3.58 us: local(): pl.pallas_call(functools.partial(late_kernel, tags[cut:], len(tags)), out...]
  transfers between devices with their start and end apart: 17 -> 17, of which waited for: 6 -> 8; matrix products, arithmetic and copies ran while one was open for 0% -> 0% of each run, Pallas kernels for 13% -> 15%
where the time goes in v7:
time: 49.6 us; the launch traced here: 49.4 us
  Pallas kernels  16.3 us (33%)
  waiting for transfers between devices  15.8 us (32%)
  starting transfers between devices  15.4 us (31%)
  local copies, waits for them, and re-layouts  1.75 us (4%)
    ppermute x7, starting transfers between devices, gather_ring(): lax.ppermute(after(streams[stream], gates.get((stream, step, 0)), found),...  11.3 us
    ppermute x7, waiting for transfers between devices, gather_ring(): lax.ppermute(after(streams[stream], gates.get((stream, step, 0)), found),...  7.1 us
    ppermute x1, waiting for transfers between devices, local(): packet = lax.ppermute(packet, 'tm', [(i, i + 1) for i in range(count - 1)])  6.2 us
    pallas_call x1, Pallas kernels, local(): pl.pallas_call(attend_kernel, out_shape=shape((frames, rows, width, chans...  5.11 us
    pallas_call x1, Pallas kernels, local(): pl.pallas_call(functools.partial(late_kernel, tags[cut:], len(tags)), out...  3.58 us
    pallas_call x2, Pallas kernels, early(): pl.pallas_call(early_kernel, out_shape=shape((half, spots, split), BF16),...  2.84 us
    ppermute x1, starting transfers between devices, local(): packet = lax.ppermute(packet, 'tm', [(i, i + 1) for i in range(count - 1)])  2.03 us
    pallas_call x1, Pallas kernels, begin(): pl.pallas_call(functools.partial(first_kernel, tags[:cut], len(tags)), ou...  1.93 us
  transfers between devices with their start and end apart: 17, of which 8 were waited for; matrix products, arithmetic and copies ran while one was open for 0% of the time, Pallas kernels for 15%

profile of v7, /device:TPU:8, one launch (start us, length us, event | category | flops | bytes accessed | tf_op | source)
XLA Modules:
  0.0 49.4 jit_solution(7645590450171802582)
XLA Ops:
  0.0 0.0 collective-permute-start.1
  0.0 1.6 %collective-permute-start.2 = (bf16[3,3,32,512]{3,2,1,0:T(8,128)(2,1)}, bf16[3,3,32,512]{3,2,1,0:T(8,128)(2,1)S(1)}, u32[]{:S(2)}, u32[]{:S(2)}) collective-permute-start(bf16[3,3,32,512]{3,2,1,0:T(8,128)(2,1)} %bitcast.4), channel_id=1, source_target_pairs={{0,8},{2,6},{8,16},{10,2},{16,24},{18,10},{24,28},{26,18},{28,20},... | collective-permute-start | bytes 884744 | tf_op jit(solution)/shard_map/ppermute | solution.py:67
  1.6 1.5 %collective-permute-start = (bf16[8,2,32,512]{3,2,1,0:T(8,128)(2,1)}, bf16[8,2,32,512]{3,2,1,0:T(8,128)(2,1)S(1)}, u32[]{:S(2)}, u32[]{:S(2)}) collective-permute-start(bf16[8,2,32,512]{3,2,1,0:T(8,128)(2,1)} %refs_0_.3), channel_id=1, source_target_pairs={{0,1},{1,0},{2,3},{3,2},{4,5},{5,4},{6,7},{7,6},{8,9},{9,8},{10,11... | collective-permute-start | bytes 1572872 | tf_op jit(solution)/shard_map/ppermute | solution.py:301
  3.1 0.0 collective-permute-done.1.refs_1_
  3.1 1.6 %collective-permute-start.4 = (bf16[3,3,32,512]{3,2,1,0:T(8,128)(2,1)S(1)}, bf16[3,3,32,512]{3,2,1,0:T(8,128)(2,1)S(1)}, u32[]{:S(2)}, u32[]{:S(2)}) collective-permute-start(bf16[3,3,32,512]{3,2,1,0:T(8,128)(2,1)S(1)} %collective-permute-done.1.refs_1_), channel_id=1, source_target_pairs={{0,8},{2,6},{8,16},{10,2},{16,24},{18,10},{24,28},{26,18},{28,20},... | collective-permute-start | bytes 884744 | tf_op jit(solution)/shard_map/ppermute | solution.py:67
  4.7 2.3 %collective-permute-done.2.refs_2_ = bf16[3,3,32,512]{3,2,1,0:T(8,128)(2,1)S(1)} collective-permute-done((bf16[3,3,32,512]{3,2,1,0:T(8,128)(2,1)}, bf16[3,3,32,512]{3,2,1,0:T(8,128)(2,1)S(1)}, u32[]{:S(2)}, u32[]{:S(2)}) %collective-permute-start.2) | collective-permute-done | bytes 294944 | tf_op jit(solution)/shard_map/ppermute | solution.py:67
  6.9 1.6 %collective-permute-start.6 = (bf16[3,3,32,512]{3,2,1,0:T(8,128)(2,1)S(1)}, bf16[3,3,32,512]{3,2,1,0:T(8,128)(2,1)S(1)}, u32[]{:S(2)}, u32[]{:S(2)}) collective-permute-start(bf16[3,3,32,512]{3,2,1,0:T(8,128)(2,1)S(1)} %collective-permute-done.2.refs_2_), channel_id=1, source_target_pairs={{0,8},{2,6},{8,16},{10,2},{16,24},{18,10},{24,28},{26,18},{28,20},... | collective-permute-start | bytes 884744 | tf_op jit(solution)/shard_map/ppermute | solution.py:67
  8.5 0.0 copy-start.1
  8.5 1.0 %copy-done.1 = bf16[8,2,32,512]{3,2,1,0:T(8,128)(2,1)S(1)} copy-done((bf16[8,2,32,512]{3,2,1,0:T(8,128)(2,1)S(1)}, bf16[8,2,32,512]{3,2,1,0:T(8,128)(2,1)}, u32[]{:S(2)}) %copy-start.1) | copy-done | bytes 524312
  9.6 0.0 copy-start.5
  9.6 0.7 %copy-done.5 = f32[512]{0:T(512)S(1)} copy-done((f32[512]{0:T(512)S(1)}, f32[512]{0:T(512)}, u32[]{:S(2)}) %copy-start.5) | copy-done | bytes 2072
  10.2 0.3 prepare.4
  10.6 0.3 prepare.6
  10.9 0.1 collective-permute-start.3
  11.0 0.0 collective-permute-done.4.refs_4_
  11.0 1.6 %collective-permute-start.8 = (bf16[3,3,32,512]{3,2,1,0:T(8,128)(2,1)S(1)}, bf16[3,3,32,512]{3,2,1,0:T(8,128)(2,1)S(1)}, u32[]{:S(2)}, u32[]{:S(2)}) collective-permute-start(bf16[3,3,32,512]{3,2,1,0:T(8,128)(2,1)S(1)} %collective-permute-done.4.refs_4_), channel_id=1, source_target_pairs={{0,8},{2,6},{8,16},{10,2},{16,24},{18,10},{24,28},{26,18},{28,20},... | collective-permute-start | bytes 884744 | tf_op jit(solution)/shard_map/ppermute | solution.py:67
  12.6 0.0 collective-permute-start.5
  12.6 1.1 %collective-permute-done.6.refs_6_ = bf16[3,3,32,512]{3,2,1,0:T(8,128)(2,1)S(1)} collective-permute-done((bf16[3,3,32,512]{3,2,1,0:T(8,128)(2,1)S(1)}, bf16[3,3,32,512]{3,2,1,0:T(8,128)(2,1)S(1)}, u32[]{:S(2)}, u32[]{:S(2)}) %collective-permute-start.6) | collective-permute-done | bytes 294944 | tf_op jit(solution)/shard_map/ppermute | solution.py:67
  13.7 0.0 collective-permute-start.7
  13.7 0.9 %collective-permute-done.refs_0_ = bf16[8,2,32,512]{3,2,1,0:T(8,128)(2,1)S(1)} collective-permute-done((bf16[8,2,32,512]{3,2,1,0:T(8,128)(2,1)}, bf16[8,2,32,512]{3,2,1,0:T(8,128)(2,1)S(1)}, u32[]{:S(2)}, u32[]{:S(2)}) %collective-permute-start) | collective-permute-done | bytes 524320 | tf_op jit(solution)/shard_map/ppermute | solution.py:301
  14.6 1.7 %collective-permute-start.10 = (bf16[3,3,32,512]{3,2,1,0:T(8,128)(2,1)S(1)}, bf16[3,3,32,512]{3,2,1,0:T(8,128)(2,1)S(1)}, u32[]{:S(2)}, u32[]{:S(2)}) collective-permute-start(bf16[3,3,32,512]{3,2,1,0:T(8,128)(2,1)S(1)} %collective-permute-done.6.refs_6_), channel_id=1, source_target_pairs={{0,8},{2,6},{8,16},{10,2},{16,24},{18,10},{24,28},{26,18},{28,20},... | collective-permute-start | bytes 884744 | tf_op jit(solution)/shard_map/ppermute | solution.py:67
  16.3 0.3 prepare.5
  16.6 0.0 copy-start.3
  16.6 0.3 prepare.7
  16.8 0.9 %collective-permute-done.8.refs_0_ = bf16[3,3,32,512]{3,2,1,0:T(8,128)(2,1)S(1)} collective-permute-done((bf16[3,3,32,512]{3,2,1,0:T(8,128)(2,1)S(1)}, bf16[3,3,32,512]{3,2,1,0:T(8,128)(2,1)S(1)}, u32[]{:S(2)}, u32[]{:S(2)}) %collective-permute-start.8) | collective-permute-done | bytes 294944 | tf_op jit(solution)/shard_map/ppermute | solution.py:67
  17.7 0.0 collective-permute-start.9
  17.7 0.0 collective-permute-done.3.refs_3_
  17.7 0.0 collective-permute-done.5.refs_5_
  17.8 0.0 collective-permute-done.7.refs_7_
  17.8 0.0 copy-done.3
  17.8 1.4 %early.2.acts0_ref = bf16[4,128,256]{2,1,0:T(8,128)(2,1)S(1)} custom-call(bf16[4,6,32,1536]{3,2,1,0:T(8,128)(2,1)S(1)} %get-tuple-element.25.wide_ref.wide0_ref, bf16[3,3,32,512]{3,2,1,0:T(8,128)(2,1)S(1)} %bitcast.5, bf16[3,3,32,512]{3,2,1,0:T(8,128)(2,1)S(1)} %collective-permute-done.1.refs_1_, bf16[3,3,32,512]{3,2,1,0:T(8,128)(2,1)S(1)} %collective-permute-done.2.refs_2_, ...), custom_call_target="tpu_custom_call" | custom-call | tf_op jit(solution)/shard_map/early/pallas_call | solution.py:339
  19.2 1.6 %collective-permute-start.12 = (bf16[3,3,32,512]{3,2,1,0:T(8,128)(2,1)S(1)}, bf16[3,3,32,512]{3,2,1,0:T(8,128)(2,1)S(1)}, u32[]{:S(2)}, u32[]{:S(2)}) collective-permute-start(bf16[3,3,32,512]{3,2,1,0:T(8,128)(2,1)S(1)} %collective-permute-done.8.refs_0_), channel_id=1, source_target_pairs={{0,8},{2,6},{8,16},{10,2},{16,24},{18,10},{24,28},{26,18},{28,20},... | collective-permute-start | bytes 884744 | tf_op jit(solution)/shard_map/ppermute | solution.py:67
  20.8 0.0 copy-start
  20.8 0.0 copy-start.6
  20.8 1.4 %early.3.acts1_ref = bf16[4,128,256]{2,1,0:T(8,128)(2,1)S(1)} custom-call(bf16[4,6,32,1536]{3,2,1,0:T(8,128)(2,1)S(1)} %get-tuple-element.28.wide_ref.wide1_ref, bf16[3,3,32,512]{3,2,1,0:T(8,128)(2,1)S(1)} %bitcast.6, bf16[3,3,32,512]{3,2,1,0:T(8,128)(2,1)S(1)} %collective-permute-done.1.refs_1_, bf16[3,3,32,512]{3,2,1,0:T(8,128)(2,1)S(1)} %collective-permute-done.2.refs_2_, ...), custom_call_target="tpu_custom_call" | custom-call | tf_op jit(solution)/shard_map/early/pallas_call | solution.py:339
  22.3 0.0 collective-permute-done.10.refs_2_
  22.3 1.6 %collective-permute-start.14 = (bf16[3,3,32,512]{3,2,1,0:T(8,128)(2,1)S(1)}, bf16[3,3,32,512]{3,2,1,0:T(8,128)(2,1)S(1)}, u32[]{:S(2)}, u32[]{:S(2)}) collective-permute-start(bf16[3,3,32,512]{3,2,1,0:T(8,128)(2,1)S(1)} %collective-permute-done.10.refs_2_), channel_id=1, source_target_pairs={{0,8},{2,6},{8,16},{10,2},{16,24},{18,10},{24,28},{26,18},{28,20},... | collective-permute-start | bytes 884744 | tf_op jit(solution)/shard_map/ppermute | solution.py:67
  23.8 0.0 copy-done
  23.8 0.0 copy-done.6
  23.8 1.9 %first.1 = (f32[8,128,512]{2,1,0:T(8,128)S(1)}, f32[3,128,512]{2,1,0:T(8,128)S(1)}) custom-call(bf16[4,4,32,512]{3,2,1,0:T(8,128)(2,1)S(1)} %get-tuple-element.29.lat0_ref, bf16[4,4,32,512]{3,2,1,0:T(8,128)(2,1)S(1)} %get-tuple-element.30.lat1_ref, bf16[4,128,256]{2,1,0:T(8,128)(2,1)S(1)} %early.2.acts0_ref, bf16[4,128,256]{2,1,0:T(8,128)(2,1)S(1)} %early.3.acts1_ref, ...), custom_call_target="tpu_custom_call" | custom-call | tf_op jit(solution)/shard_map/first/pallas_call | solution.py:354
  25.8 0.1 collective-permute-start.11
  25.9 0.0 collective-permute-done.9.refs_1_
  25.9 0.1 collective-permute-done.12.refs_4_
  26.0 0.4 collective-permute-start.13
  26.4 2.8 %collective-permute-done.14.refs_6_ = bf16[3,3,32,512]{3,2,1,0:T(8,128)(2,1)S(1)} collective-permute-done((bf16[3,3,32,512]{3,2,1,0:T(8,128)(2,1)S(1)}, bf16[3,3,32,512]{3,2,1,0:T(8,128)(2,1)S(1)}, u32[]{:S(2)}, u32[]{:S(2)}) %collective-permute-start.14) | collective-permute-done | bytes 294944 | tf_op jit(solution)/shard_map/ppermute | solution.py:67
  29.1 0.0 collective-permute-start.15
  29.1 0.0 collective-permute-done.11.refs_3_
  29.1 0.0 collective-permute-done.13.refs_5_
  29.1 1.6 %collective-permute-done.15.refs_7_ = bf16[3,3,32,512]{3,2,1,0:T(8,128)(2,1)S(1)} collective-permute-done((bf16[3,3,32,512]{3,2,1,0:T(8,128)(2,1)S(1)}, bf16[3,3,32,512]{3,2,1,0:T(8,128)(2,1)S(1)}, u32[]{:S(2)}, u32[]{:S(2)}) %collective-permute-start.15) | collective-permute-done | bytes 294944 | tf_op jit(solution)/shard_map/ppermute | solution.py:70
  30.7 3.6 %late.1 = (bf16[8,128,256]{2,1,0:T(8,128)(2,1)S(1)}, bf16[3,128,512]{2,1,0:T(8,128)(2,1)S(1)}) custom-call(bf16[4,6,32,1536]{3,2,1,0:T(8,128)(2,1)S(1)} %get-tuple-element.25.wide_ref.wide0_ref, bf16[4,6,32,1536]{3,2,1,0:T(8,128)(2,1)S(1)} %get-tuple-element.28.wide_ref.wide1_ref, s32[128]{0:T(128)S(1)} %copy-done.6, bf16[3,512,512]{2,1,0:T(8,128)(2,1)S(1)} %copy-done, ...), custom_call_target="tpu_custom_call" | custom-call | tf_op jit(solution)/shard_map/late/pallas_call | solution.py:382
  34.3 2.0 %collective-permute-start.16 = (bf16[3,128,512]{2,1,0:T(8,128)(2,1)S(1)}, bf16[3,128,512]{2,1,0:T(8,128)(2,1)S(1)}, u32[]{:S(2)}, u32[]{:S(2)}) collective-permute-start(bf16[3,128,512]{2,1,0:T(8,128)(2,1)S(1)} %get-tuple-element.40), channel_id=1, source_target_pairs={{0,2},{2,4},{4,6},{6,8},{8,10},{10,12},{12,14},{14,16},{16,18},{18... | collective-permute-start | bytes 1179656 | tf_op jit(solution)/shard_map/ppermute | solution.py:390
  36.3 0.0 copy-start.2
  36.3 0.0 copy-start.4
  36.4 0.0 copy-start.7
  36.4 1.7 %rest.1.base_ref = f32[8,128,512]{2,1,0:T(8,128)S(1)} custom-call(bf16[8,128,256]{2,1,0:T(8,128)(2,1)S(1)} %get-tuple-element.38.acts_ref, s32[128]{0:T(128)S(1)} %copy-done.6, bf16[3,512,512]{2,1,0:T(8,128)(2,1)S(1)} %copy-done, f32[8,128,512]{2,1,0:T(8,128)S(1)} %get-tuple-element.39.early_ref), custom_call_target="tpu_custom_call" | custom-call | tf_op jit(solution)/shard_map/rest/pallas_call | solution.py:391
  38.1 6.2 %collective-permute-done.16.packet_ref = bf16[3,128,512]{2,1,0:T(8,128)(2,1)S(1)} collective-permute-done((bf16[3,128,512]{2,1,0:T(8,128)(2,1)S(1)}, bf16[3,128,512]{2,1,0:T(8,128)(2,1)S(1)}, u32[]{:S(2)}, u32[]{:S(2)}) %collective-permute-start.16) | collective-permute-done | bytes 393248 | tf_op jit(solution)/shard_map/ppermute | solution.py:390
  44.3 0.0 copy-done.2
  44.3 0.0 copy-done.4
  44.3 0.0 copy-done.7
  44.3 5.1 %attend.1 = bf16[8,2,32,512]{3,2,1,0:T(8,128)(2,1)} custom-call(f32[8,128,512]{2,1,0:T(8,128)S(1)} %rest.1.base_ref, bf16[3,128,512]{2,1,0:T(8,128)(2,1)S(1)} %collective-permute-done.16.packet_ref, s32[128]{0:T(128)S(1)} %copy-done.6, f32[1,512]{1,0:T(1,128)S(1)} %bitcast.11, bf16[512,1536]{1,0:T(8,128)(2,1)S(1)} %copy-done.2, bf16[512,512]{1,0:T(8,128)(2,1)S(1)} %copy-done.4), custom_call_target="tpu_custom_call" | custom-call | tf_op jit(solution)/shard_map/attend/pallas_call | solution.py:399
Async XLA Ops:
  0.0 3.1 %collective-permute-start.1 = (bf16[3,3,32,512]{3,2,1,0:T(8,128)(2,1)}, bf16[3,3,32,512]{3,2,1,0:T(8,128)(2,1)S(1)}, u32[]{:S(2)}, u32[]{:S(2)}) collective-permute-start(bf16[3,3,32,512]{3,2,1,0:T(8,128)(2,1)} %bitcast.3), channel_id=1, source_target_pairs={{0,2},{2,0},{4,6},{6,4},{8,10},{10,8},{12,14},{14,12},{16,18},{18,... | collective-permute-start | bytes 884744 | tf_op jit(solution)/shard_map/ppermute | solution.py:63
  0.0 6.9 %collective-permute-start.2 = (bf16[3,3,32,512]{3,2,1,0:T(8,128)(2,1)}, bf16[3,3,32,512]{3,2,1,0:T(8,128)(2,1)S(1)}, u32[]{:S(2)}, u32[]{:S(2)}) collective-permute-start(bf16[3,3,32,512]{3,2,1,0:T(8,128)(2,1)} %bitcast.4), channel_id=1, source_target_pairs={{0,8},{2,6},{8,16},{10,2},{16,24},{18,10},{24,28},{26,18},{28,20},... | collective-permute-start | bytes 884744 | tf_op jit(solution)/shard_map/ppermute | solution.py:67
  1.6 13.0 %collective-permute-start = (bf16[8,2,32,512]{3,2,1,0:T(8,128)(2,1)}, bf16[8,2,32,512]{3,2,1,0:T(8,128)(2,1)S(1)}, u32[]{:S(2)}, u32[]{:S(2)}) collective-permute-start(bf16[8,2,32,512]{3,2,1,0:T(8,128)(2,1)} %refs_0_.3), channel_id=1, source_target_pairs={{0,1},{1,0},{2,3},{3,2},{4,5},{5,4},{6,7},{7,6},{8,9},{9,8},{10,11... | collective-permute-start | bytes 1572872 | tf_op jit(solution)/shard_map/ppermute | solution.py:301
  3.1 7.9 %collective-permute-start.4 = (bf16[3,3,32,512]{3,2,1,0:T(8,128)(2,1)S(1)}, bf16[3,3,32,512]{3,2,1,0:T(8,128)(2,1)S(1)}, u32[]{:S(2)}, u32[]{:S(2)}) collective-permute-start(bf16[3,3,32,512]{3,2,1,0:T(8,128)(2,1)S(1)} %collective-permute-done.1.refs_1_), channel_id=1, source_target_pairs={{0,8},{2,6},{8,16},{10,2},{16,24},{18,10},{24,28},{26,18},{28,20},... | collective-permute-start | bytes 884744 | tf_op jit(solution)/shard_map/ppermute | solution.py:67
  6.9 6.7 %collective-permute-start.6 = (bf16[3,3,32,512]{3,2,1,0:T(8,128)(2,1)S(1)}, bf16[3,3,32,512]{3,2,1,0:T(8,128)(2,1)S(1)}, u32[]{:S(2)}, u32[]{:S(2)}) collective-permute-start(bf16[3,3,32,512]{3,2,1,0:T(8,128)(2,1)S(1)} %collective-permute-done.2.refs_2_), channel_id=1, source_target_pairs={{0,8},{2,6},{8,16},{10,2},{16,24},{18,10},{24,28},{26,18},{28,20},... | collective-permute-start | bytes 884744 | tf_op jit(solution)/shard_map/ppermute | solution.py:67
  8.5 1.0 %copy-start.1 = (bf16[8,2,32,512]{3,2,1,0:T(8,128)(2,1)S(1)}, bf16[8,2,32,512]{3,2,1,0:T(8,128)(2,1)}, u32[]{:S(2)}) copy-start(bf16[8,2,32,512]{3,2,1,0:T(8,128)(2,1)} %refs_0_.3) | copy-start | bytes 1572868
  9.6 0.7 %copy-start.5 = (f32[512]{0:T(512)S(1)}, f32[512]{0:T(512)}, u32[]{:S(2)}) copy-start(f32[512]{0:T(512)} %param.10) | copy-start | bytes 6148
  10.9 6.9 %collective-permute-start.3 = (bf16[3,3,32,512]{3,2,1,0:T(8,128)(2,1)S(1)}, bf16[3,3,32,512]{3,2,1,0:T(8,128)(2,1)S(1)}, u32[]{:S(2)}, u32[]{:S(2)}) collective-permute-start(bf16[3,3,32,512]{3,2,1,0:T(8,128)(2,1)S(1)} %collective-permute-done.2.refs_2_), channel_id=1, source_target_pairs={{0,2},{2,0},{4,6},{6,4},{8,10},{10,8},{12,14},{14,12},{16,18},{18,... | collective-permute-start | bytes 884744 | tf_op jit(solution)/shard_map/ppermute | solution.py:70
  11.0 6.8 %collective-permute-start.8 = (bf16[3,3,32,512]{3,2,1,0:T(8,128)(2,1)S(1)}, bf16[3,3,32,512]{3,2,1,0:T(8,128)(2,1)S(1)}, u32[]{:S(2)}, u32[]{:S(2)}) collective-permute-start(bf16[3,3,32,512]{3,2,1,0:T(8,128)(2,1)S(1)} %collective-permute-done.4.refs_4_), channel_id=1, source_target_pairs={{0,8},{2,6},{8,16},{10,2},{16,24},{18,10},{24,28},{26,18},{28,20},... | collective-permute-start | bytes 884744 | tf_op jit(solution)/shard_map/ppermute | solution.py:67
  12.6 5.2 %collective-permute-start.5 = (bf16[3,3,32,512]{3,2,1,0:T(8,128)(2,1)S(1)}, bf16[3,3,32,512]{3,2,1,0:T(8,128)(2,1)S(1)}, u32[]{:S(2)}, u32[]{:S(2)}) collective-permute-start(bf16[3,3,32,512]{3,2,1,0:T(8,128)(2,1)S(1)} %collective-permute-done.4.refs_4_), channel_id=1, source_target_pairs={{0,2},{2,0},{4,6},{6,4},{8,10},{10,8},{12,14},{14,12},{16,18},{18,... | collective-permute-start | bytes 884744 | tf_op jit(solution)/shard_map/ppermute | solution.py:70
  13.7 4.1 %collective-permute-start.7 = (bf16[3,3,32,512]{3,2,1,0:T(8,128)(2,1)S(1)}, bf16[3,3,32,512]{3,2,1,0:T(8,128)(2,1)S(1)}, u32[]{:S(2)}, u32[]{:S(2)}) collective-permute-start(bf16[3,3,32,512]{3,2,1,0:T(8,128)(2,1)S(1)} %collective-permute-done.6.refs_6_), channel_id=1, source_target_pairs={{0,2},{2,0},{4,6},{6,4},{8,10},{10,8},{12,14},{14,12},{16,18},{18,... | collective-permute-start | bytes 884744 | tf_op jit(solution)/shard_map/ppermute | solution.py:70
  14.6 7.7 %collective-permute-start.10 = (bf16[3,3,32,512]{3,2,1,0:T(8,128)(2,1)S(1)}, bf16[3,3,32,512]{3,2,1,0:T(8,128)(2,1)S(1)}, u32[]{:S(2)}, u32[]{:S(2)}) collective-permute-start(bf16[3,3,32,512]{3,2,1,0:T(8,128)(2,1)S(1)} %collective-permute-done.6.refs_6_), channel_id=1, source_target_pairs={{0,8},{2,6},{8,16},{10,2},{16,24},{18,10},{24,28},{26,18},{28,20},... | collective-permute-start | bytes 884744 | tf_op jit(solution)/shard_map/ppermute | solution.py:67
  16.6 1.2 %copy-start.3 = (bf16[3,3,512,32]{2,3,1,0:T(8,128)(2,1)S(1)}, bf16[3,3,512,32]{2,3,1,0:T(8,128)(2,1)}, u32[]{:S(2)}) copy-start(bf16[3,3,512,32]{2,3,1,0:T(8,128)(2,1)} %param.11) | copy-start | bytes 884740
  17.7 8.1 %collective-permute-start.9 = (bf16[3,3,32,512]{3,2,1,0:T(8,128)(2,1)S(1)}, bf16[3,3,32,512]{3,2,1,0:T(8,128)(2,1)S(1)}, u32[]{:S(2)}, u32[]{:S(2)}) collective-permute-start(bf16[3,3,32,512]{3,2,1,0:T(8,128)(2,1)S(1)} %collective-permute-done.8.refs_0_), channel_id=1, source_target_pairs={{0,2},{2,0},{4,6},{6,4},{8,10},{10,8},{12,14},{14,12},{16,18},{18,... | collective-permute-start | bytes 884744 | tf_op jit(solution)/shard_map/ppermute | solution.py:70
  19.2 6.8 %collective-permute-start.12 = (bf16[3,3,32,512]{3,2,1,0:T(8,128)(2,1)S(1)}, bf16[3,3,32,512]{3,2,1,0:T(8,128)(2,1)S(1)}, u32[]{:S(2)}, u32[]{:S(2)}) collective-permute-start(bf16[3,3,32,512]{3,2,1,0:T(8,128)(2,1)S(1)} %collective-permute-done.8.refs_0_), channel_id=1, source_target_pairs={{0,8},{2,6},{8,16},{10,2},{16,24},{18,10},{24,28},{26,18},{28,20},... | collective-permute-start | bytes 884744 | tf_op jit(solution)/shard_map/ppermute | solution.py:67
  20.8 3.0 %copy-start = (bf16[3,512,512]{2,1,0:T(8,128)(2,1)S(1)}, bf16[3,512,512]{2,1,0:T(8,128)(2,1)}, u32[]{:S(2)}) copy-start(bf16[3,512,512]{2,1,0:T(8,128)(2,1)} %time_ref.5) | copy-start | bytes 4718596
  20.8 3.0 %copy-start.6 = (s32[128]{0:T(128)S(1)}, s32[128]{0:T(128)}, u32[]{:S(2)}) copy-start(s32[128]{0:T(128)} %clips.7) | copy-start | bytes 1540
  22.3 6.9 %collective-permute-start.14 = (bf16[3,3,32,512]{3,2,1,0:T(8,128)(2,1)S(1)}, bf16[3,3,32,512]{3,2,1,0:T(8,128)(2,1)S(1)}, u32[]{:S(2)}, u32[]{:S(2)}) collective-permute-start(bf16[3,3,32,512]{3,2,1,0:T(8,128)(2,1)S(1)} %collective-permute-done.10.refs_2_), channel_id=1, source_target_pairs={{0,8},{2,6},{8,16},{10,2},{16,24},{18,10},{24,28},{26,18},{28,20},... | collective-permute-start | bytes 884744 | tf_op jit(solution)/shard_map/ppermute | solution.py:67
  25.8 3.4 %collective-permute-start.11 = (bf16[3,3,32,512]{3,2,1,0:T(8,128)(2,1)S(1)}, bf16[3,3,32,512]{3,2,1,0:T(8,128)(2,1)S(1)}, u32[]{:S(2)}, u32[]{:S(2)}) collective-permute-start(bf16[3,3,32,512]{3,2,1,0:T(8,128)(2,1)S(1)} %collective-permute-done.10.refs_2_), channel_id=1, source_target_pairs={{0,2},{2,0},{4,6},{6,4},{8,10},{10,8},{12,14},{14,12},{16,18},{18,... | collective-permute-start | bytes 884744 | tf_op jit(solution)/shard_map/ppermute | solution.py:70
  26.0 3.2 %collective-permute-start.13 = (bf16[3,3,32,512]{3,2,1,0:T(8,128)(2,1)S(1)}, bf16[3,3,32,512]{3,2,1,0:T(8,128)(2,1)S(1)}, u32[]{:S(2)}, u32[]{:S(2)}) collective-permute-start(bf16[3,3,32,512]{3,2,1,0:T(8,128)(2,1)S(1)} %collective-permute-done.12.refs_4_), channel_id=1, source_target_pairs={{0,2},{2,0},{4,6},{6,4},{8,10},{10,8},{12,14},{14,12},{16,18},{18,... | collective-permute-start | bytes 884744 | tf_op jit(solution)/shard_map/ppermute | solution.py:70
  29.1 1.6 %collective-permute-start.15 = (bf16[3,3,32,512]{3,2,1,0:T(8,128)(2,1)S(1)}, bf16[3,3,32,512]{3,2,1,0:T(8,128)(2,1)S(1)}, u32[]{:S(2)}, u32[]{:S(2)}) collective-permute-start(bf16[3,3,32,512]{3,2,1,0:T(8,128)(2,1)S(1)} %collective-permute-done.14.refs_6_), channel_id=1, source_target_pairs={{0,2},{2,0},{4,6},{6,4},{8,10},{10,8},{12,14},{14,12},{16,18},{18,... | collective-permute-start | bytes 884744 | tf_op jit(solution)/shard_map/ppermute | solution.py:70
  34.3 10.0 %collective-permute-start.16 = (bf16[3,128,512]{2,1,0:T(8,128)(2,1)S(1)}, bf16[3,128,512]{2,1,0:T(8,128)(2,1)S(1)}, u32[]{:S(2)}, u32[]{:S(2)}) collective-permute-start(bf16[3,128,512]{2,1,0:T(8,128)(2,1)S(1)} %get-tuple-element.40), channel_id=1, source_target_pairs={{0,2},{2,4},{4,6},{6,8},{8,10},{10,12},{12,14},{14,16},{16,18},{18... | collective-permute-start | bytes 1179656 | tf_op jit(solution)/shard_map/ppermute | solution.py:390
  36.3 8.0 %copy-start.2 = (bf16[512,1536]{1,0:T(8,128)(2,1)S(1)}, bf16[512,1536]{1,0:T(8,128)(2,1)}, u32[]{:S(2)}) copy-start(bf16[512,1536]{1,0:T(8,128)(2,1)} %qkv_ref.1) | copy-start | bytes 4718596
  36.3 8.0 %copy-start.4 = (bf16[512,512]{1,0:T(8,128)(2,1)S(1)}, bf16[512,512]{1,0:T(8,128)(2,1)}, u32[]{:S(2)}) copy-start(bf16[512,512]{1,0:T(8,128)(2,1)} %proj_ref.1) | copy-start | bytes 1572868
  36.4 7.9 %copy-start.7 = (f32[512]{0:T(512)S(1)}, f32[512]{0:T(512)}, u32[]{:S(2)}) copy-start(f32[512]{0:T(512)} %param.13) | copy-start | bytes 6148

commit v8 on v7

--- a/solution.py
+++ b/solution.py
@@ -280,7 +280,7 @@
             if joint > 1:
                 scores = jnp.where(blocked, -jnp.inf, scores)
             weights = jnp.exp(scores - jnp.max(scores, axis=-1, keepdims=True))
-            probs = (weights / jnp.sum(weights, axis=-1, keepdims=True)).astype(BF16)
+            probs = (weights * (1.0 / jnp.sum(weights, axis=-1, keepdims=True))).astype(BF16)
             attended.append(dot(probs, value).astype(BF16))
         result = dot(jnp.concatenate(attended, axis=0), proj_ref[...])
         result = result + mixed_ref[span, mine].reshape(step * own, chans).astype(F32)
@@ -310,32 +310,35 @@
     split = cut * (chans // len(tags))
 
     gain = gain_in.reshape(1, chans)
-    prepared = []
-    own = []
-    for start in (0, half):
-        pair = ()
-        for at, part in enumerate(parts):
-            pair = pl.pallas_call(
-                functools.partial(prepare_kernel, start, at, groups),
-                out_shape=(
-                    shape((half, height + 2, width, 3 * chans), BF16),
-                    shape((half, height, width, chans), BF16),
-                ),
-                in_specs=[VMEM] * (2 + len(pair)),
-                out_specs=(VMEM, VMEM),
-                input_output_aliases={2: 0, 3: 1} if pair else {},
-                compiler_params=params,
-                name="prepare",
-            )(part, gain, *pair)
-            if at == 0:
-                own.append(pair)
-        prepared.append(pair)
-    wides = [pair[0] for pair in prepared]
-    lats = [pair[1] for pair in prepared]
+    def prepare(start, at, part, pair=()):
+        return pl.pallas_call(
+            functools.partial(prepare_kernel, start, at, groups),
+            out_shape=(
+                shape((half, height + 2, width, 3 * chans), BF16),
+                shape((half, height, width, chans), BF16),
+            ),
+            in_specs=[VMEM] * (2 + len(pair)),
+            out_specs=(VMEM, VMEM),
+            input_output_aliases={2: 0, 3: 1} if pair else {},
+            compiler_params=params,
+            name="prepare",
+        )(part, gain, *pair)
+
+    own = [prepare(start, 0, parts[0]) for start in (0, half)]
+    wides, lats = [None, None], [None, None]
+
+    def prepare_rest(which):
+        pair = own[which]
+        for at in range(1, groups):
+            part = parts[at]
+            pair = prepare(which * half, at, part, pair)
+        wides[which], lats[which] = pair
+
     acts = [None, None]
     first = []
 
     def early(which, shards):
+        prepare_rest(which)
         acts[which] = pl.pallas_call(
             early_kernel,
             out_shape=shape((half, spots, split), BF16),
@@ -367,7 +370,7 @@
         gates = {
             (1, 1, 1): lambda found: own,
             (1, last - 2, 1): lambda found: parts[1],
-            (1, last - 1, 0): functools.partial(early, 0),
+            (0, last - 1, 1): functools.partial(early, 0),
             (1, last - 1, 1): lambda found: found[9],
             (0, last, 0): functools.partial(early, 1),
             (0, last, 1): begin,

time: 49.6 us -> 48.7 us (0.982)
  waiting for transfers between devices: 15.8 us -> 14.3 us
    ppermute x7, waiting for transfers between devices: 7.1 us -> 5.69 us  [gather_ring(): lax.ppermute(after(streams[stream], gates.get((stream, step, 0)), found),...]
  transfers between devices with their start and end apart: 17 -> 17, of which waited for: 8 -> 9; matrix products, arithmetic and copies ran while one was open for 0% -> 0% of each run, Pallas kernels for 15% -> 16%
where the time goes in v8:
time: 48.7 us; the launch traced here: 48.3 us
  Pallas kernels  16.3 us (33%)
  starting transfers between devices  15.7 us (32%)
  waiting for transfers between devices  14.3 us (29%)
  local copies, waits for them, and re-layouts  1.76 us (4%)
    ppermute x7, starting transfers between devices, gather_ring(): lax.ppermute(after(streams[stream], gates.get((stream, step, 0)), found),...  11.4 us
    ppermute x1, waiting for transfers between devices, local(): packet = lax.ppermute(packet, 'tm', [(i, i + 1) for i in range(count - 1)])  6.16 us
    ppermute x7, waiting for transfers between devices, gather_ring(): lax.ppermute(after(streams[stream], gates.get((stream, step, 0)), found),...  5.69 us
    pallas_call x1, Pallas kernels, local(): pl.pallas_call(attend_kernel, out_shape=shape((frames, rows, width, chans...  5.11 us
    pallas_call x1, Pallas kernels, local(): pl.pallas_call(functools.partial(late_kernel, tags[cut:], len(tags)), out...  3.56 us
    pallas_call x2, Pallas kernels, early(): pl.pallas_call(early_kernel, out_shape=shape((half, spots, split), BF16),...  2.84 us
    ppermute x1, starting transfers between devices, local(): packet = lax.ppermute(packet, 'tm', [(i, i + 1) for i in range(count - 1)])  2.06 us
    pallas_call x1, Pallas kernels, begin(): pl.pallas_call(functools.partial(first_kernel, tags[:cut], len(tags)), ou...  1.94 us
  transfers between devices with their start and end apart: 17, of which 9 were waited for; matrix products, arithmetic and copies ran while one was open for 0% of the time, Pallas kernels for 16%

profile of v8, /device:TPU:8, one launch (start us, length us, event | category | flops | bytes accessed | tf_op | source)
XLA Modules:
  0.0 48.3 jit_solution(8681620251783542729)
XLA Ops:
  0.0 0.0 collective-permute-start.1
  0.0 1.6 %collective-permute-start.2 = (bf16[3,3,32,512]{3,2,1,0:T(8,128)(2,1)}, bf16[3,3,32,512]{3,2,1,0:T(8,128)(2,1)S(1)}, u32[]{:S(2)}, u32[]{:S(2)}) collective-permute-start(bf16[3,3,32,512]{3,2,1,0:T(8,128)(2,1)} %bitcast.4), channel_id=1, source_target_pairs={{0,8},{2,6},{8,16},{10,2},{16,24},{18,10},{24,28},{26,18},{28,20},... | collective-permute-start | bytes 884744 | tf_op jit(solution)/shard_map/ppermute | solution.py:67
  1.6 1.5 %collective-permute-start = (bf16[8,2,32,512]{3,2,1,0:T(8,128)(2,1)}, bf16[8,2,32,512]{3,2,1,0:T(8,128)(2,1)S(1)}, u32[]{:S(2)}, u32[]{:S(2)}) collective-permute-start(bf16[8,2,32,512]{3,2,1,0:T(8,128)(2,1)} %refs_0_.3), channel_id=1, source_target_pairs={{0,1},{1,0},{2,3},{3,2},{4,5},{5,4},{6,7},{7,6},{8,9},{9,8},{10,11... | collective-permute-start | bytes 1572872 | tf_op jit(solution)/shard_map/ppermute | solution.py:301
  3.1 0.0 collective-permute-done.1.refs_1_
  3.1 1.6 %collective-permute-start.4 = (bf16[3,3,32,512]{3,2,1,0:T(8,128)(2,1)S(1)}, bf16[3,3,32,512]{3,2,1,0:T(8,128)(2,1)S(1)}, u32[]{:S(2)}, u32[]{:S(2)}) collective-permute-start(bf16[3,3,32,512]{3,2,1,0:T(8,128)(2,1)S(1)} %collective-permute-done.1.refs_1_), channel_id=1, source_target_pairs={{0,8},{2,6},{8,16},{10,2},{16,24},{18,10},{24,28},{26,18},{28,20},... | collective-permute-start | bytes 884744 | tf_op jit(solution)/shard_map/ppermute | solution.py:67
  4.7 2.3 %collective-permute-done.2.refs_2_ = bf16[3,3,32,512]{3,2,1,0:T(8,128)(2,1)S(1)} collective-permute-done((bf16[3,3,32,512]{3,2,1,0:T(8,128)(2,1)}, bf16[3,3,32,512]{3,2,1,0:T(8,128)(2,1)S(1)}, u32[]{:S(2)}, u32[]{:S(2)}) %collective-permute-start.2) | collective-permute-done | bytes 294944 | tf_op jit(solution)/shard_map/ppermute | solution.py:67
  6.9 1.6 %collective-permute-start.6 = (bf16[3,3,32,512]{3,2,1,0:T(8,128)(2,1)S(1)}, bf16[3,3,32,512]{3,2,1,0:T(8,128)(2,1)S(1)}, u32[]{:S(2)}, u32[]{:S(2)}) collective-permute-start(bf16[3,3,32,512]{3,2,1,0:T(8,128)(2,1)S(1)} %collective-permute-done.2.refs_2_), channel_id=1, source_target_pairs={{0,8},{2,6},{8,16},{10,2},{16,24},{18,10},{24,28},{26,18},{28,20},... | collective-permute-start | bytes 884744 | tf_op jit(solution)/shard_map/ppermute | solution.py:67
  8.5 0.0 copy-start.1
  8.5 1.0 %copy-done.1 = bf16[8,2,32,512]{3,2,1,0:T(8,128)(2,1)S(1)} copy-done((bf16[8,2,32,512]{3,2,1,0:T(8,128)(2,1)S(1)}, bf16[8,2,32,512]{3,2,1,0:T(8,128)(2,1)}, u32[]{:S(2)}) %copy-start.1) | copy-done | bytes 524312
  9.6 0.0 copy-start.5
  9.6 0.7 %copy-done.5 = f32[512]{0:T(512)S(1)} copy-done((f32[512]{0:T(512)S(1)}, f32[512]{0:T(512)}, u32[]{:S(2)}) %copy-start.5) | copy-done | bytes 2072
  10.2 0.0 copy-start.3
  10.2 0.3 prepare.4
  10.6 0.3 prepare.6
  10.9 0.1 collective-permute-start.3
  11.0 0.0 collective-permute-done.4.refs_4_
  11.0 1.6 %collective-permute-start.8 = (bf16[3,3,32,512]{3,2,1,0:T(8,128)(2,1)S(1)}, bf16[3,3,32,512]{3,2,1,0:T(8,128)(2,1)S(1)}, u32[]{:S(2)}, u32[]{:S(2)}) collective-permute-start(bf16[3,3,32,512]{3,2,1,0:T(8,128)(2,1)S(1)} %collective-permute-done.4.refs_4_), channel_id=1, source_target_pairs={{0,8},{2,6},{8,16},{10,2},{16,24},{18,10},{24,28},{26,18},{28,20},... | collective-permute-start | bytes 884744 | tf_op jit(solution)/shard_map/ppermute | solution.py:67
  12.6 0.0 collective-permute-start.5
  12.6 1.1 %collective-permute-done.6.refs_6_ = bf16[3,3,32,512]{3,2,1,0:T(8,128)(2,1)S(1)} collective-permute-done((bf16[3,3,32,512]{3,2,1,0:T(8,128)(2,1)S(1)}, bf16[3,3,32,512]{3,2,1,0:T(8,128)(2,1)S(1)}, u32[]{:S(2)}, u32[]{:S(2)}) %collective-permute-start.6) | collective-permute-done | bytes 294944 | tf_op jit(solution)/shard_map/ppermute | solution.py:67
  13.7 0.0 collective-permute-start.7
  13.7 0.9 %collective-permute-done.refs_0_ = bf16[8,2,32,512]{3,2,1,0:T(8,128)(2,1)S(1)} collective-permute-done((bf16[8,2,32,512]{3,2,1,0:T(8,128)(2,1)}, bf16[8,2,32,512]{3,2,1,0:T(8,128)(2,1)S(1)}, u32[]{:S(2)}, u32[]{:S(2)}) %collective-permute-start) | collective-permute-done | bytes 524320 | tf_op jit(solution)/shard_map/ppermute | solution.py:301
  14.6 1.7 %collective-permute-start.10 = (bf16[3,3,32,512]{3,2,1,0:T(8,128)(2,1)S(1)}, bf16[3,3,32,512]{3,2,1,0:T(8,128)(2,1)S(1)}, u32[]{:S(2)}, u32[]{:S(2)}) collective-permute-start(bf16[3,3,32,512]{3,2,1,0:T(8,128)(2,1)S(1)} %collective-permute-done.6.refs_6_), channel_id=1, source_target_pairs={{0,8},{2,6},{8,16},{10,2},{16,24},{18,10},{24,28},{26,18},{28,20},... | collective-permute-start | bytes 884744 | tf_op jit(solution)/shard_map/ppermute | solution.py:67
  16.3 0.3 prepare.7
  16.6 1.2 %collective-permute-done.8.refs_0_ = bf16[3,3,32,512]{3,2,1,0:T(8,128)(2,1)S(1)} collective-permute-done((bf16[3,3,32,512]{3,2,1,0:T(8,128)(2,1)S(1)}, bf16[3,3,32,512]{3,2,1,0:T(8,128)(2,1)S(1)}, u32[]{:S(2)}, u32[]{:S(2)}) %collective-permute-start.8) | collective-permute-done | bytes 294944 | tf_op jit(solution)/shard_map/ppermute | solution.py:67
  17.7 0.0 collective-permute-start.9
  17.7 0.0 collective-permute-done.3.refs_3_
  17.8 1.6 %collective-permute-start.12 = (bf16[3,3,32,512]{3,2,1,0:T(8,128)(2,1)S(1)}, bf16[3,3,32,512]{3,2,1,0:T(8,128)(2,1)S(1)}, u32[]{:S(2)}, u32[]{:S(2)}) collective-permute-start(bf16[3,3,32,512]{3,2,1,0:T(8,128)(2,1)S(1)} %collective-permute-done.8.refs_0_), channel_id=1, source_target_pairs={{0,8},{2,6},{8,16},{10,2},{16,24},{18,10},{24,28},{26,18},{28,20},... | collective-permute-start | bytes 884744 | tf_op jit(solution)/shard_map/ppermute | solution.py:67
  19.3 0.0 collective-permute-done.5.refs_5_
  19.3 0.0 collective-permute-done.7.refs_7_
  19.3 0.0 copy-done.3
  19.3 1.4 %early.3.acts1_ref = bf16[4,128,256]{2,1,0:T(8,128)(2,1)S(1)} custom-call(bf16[4,6,32,1536]{3,2,1,0:T(8,128)(2,1)S(1)} %get-tuple-element.28.wide_ref.wide1_ref, bf16[3,3,32,512]{3,2,1,0:T(8,128)(2,1)S(1)} %bitcast.5, bf16[3,3,32,512]{3,2,1,0:T(8,128)(2,1)S(1)} %collective-permute-done.1.refs_1_, bf16[3,3,32,512]{3,2,1,0:T(8,128)(2,1)S(1)} %collective-permute-done.2.refs_2_, ...), custom_call_target="tpu_custom_call" | custom-call | tf_op jit(solution)/shard_map/early/pallas_call | solution.py:342
  20.8 0.5 %collective-permute-done.10.refs_2_ = bf16[3,3,32,512]{3,2,1,0:T(8,128)(2,1)S(1)} collective-permute-done((bf16[3,3,32,512]{3,2,1,0:T(8,128)(2,1)S(1)}, bf16[3,3,32,512]{3,2,1,0:T(8,128)(2,1)S(1)}, u32[]{:S(2)}, u32[]{:S(2)}) %collective-permute-start.10) | collective-permute-done | bytes 294944 | tf_op jit(solution)/shard_map/ppermute | solution.py:67
  21.3 1.7 %collective-permute-start.14 = (bf16[3,3,32,512]{3,2,1,0:T(8,128)(2,1)S(1)}, bf16[3,3,32,512]{3,2,1,0:T(8,128)(2,1)S(1)}, u32[]{:S(2)}, u32[]{:S(2)}) collective-permute-start(bf16[3,3,32,512]{3,2,1,0:T(8,128)(2,1)S(1)} %collective-permute-done.10.refs_2_), channel_id=1, source_target_pairs={{0,8},{2,6},{8,16},{10,2},{16,24},{18,10},{24,28},{26,18},{28,20},... | collective-permute-start | bytes 884744 | tf_op jit(solution)/shard_map/ppermute | solution.py:67
  23.0 0.3 prepare.5
  23.3 0.0 copy-start
  23.3 0.0 copy-start.6
  23.3 1.4 %early.2.acts0_ref = bf16[4,128,256]{2,1,0:T(8,128)(2,1)S(1)} custom-call(bf16[4,6,32,1536]{3,2,1,0:T(8,128)(2,1)S(1)} %get-tuple-element.25.wide_ref.wide0_ref, bf16[3,3,32,512]{3,2,1,0:T(8,128)(2,1)S(1)} %bitcast.6, bf16[3,3,32,512]{3,2,1,0:T(8,128)(2,1)S(1)} %collective-permute-done.1.refs_1_, bf16[3,3,32,512]{3,2,1,0:T(8,128)(2,1)S(1)} %collective-permute-done.2.refs_2_, ...), custom_call_target="tpu_custom_call" | custom-call | tf_op jit(solution)/shard_map/early/pallas_call | solution.py:342
  24.7 0.1 collective-permute-start.11
  24.8 0.0 copy-done
  24.8 0.0 copy-done.6
  24.8 1.9 %first.1 = (f32[8,128,512]{2,1,0:T(8,128)S(1)}, f32[3,128,512]{2,1,0:T(8,128)S(1)}) custom-call(bf16[4,4,32,512]{3,2,1,0:T(8,128)(2,1)S(1)} %get-tuple-element.29.lat0_ref, bf16[4,4,32,512]{3,2,1,0:T(8,128)(2,1)S(1)} %get-tuple-element.30.lat1_ref, bf16[4,128,256]{2,1,0:T(8,128)(2,1)S(1)} %early.2.acts0_ref, bf16[4,128,256]{2,1,0:T(8,128)(2,1)S(1)} %early.3.acts1_ref, ...), custom_call_target="tpu_custom_call" | custom-call | tf_op jit(solution)/shard_map/first/pallas_call | solution.py:357
  26.8 0.0 collective-permute-done.9.refs_1_
  26.8 0.0 collective-permute-done.12.refs_4_
  26.8 0.5 %collective-permute-start.13 = (bf16[3,3,32,512]{3,2,1,0:T(8,128)(2,1)S(1)}, bf16[3,3,32,512]{3,2,1,0:T(8,128)(2,1)S(1)}, u32[]{:S(2)}, u32[]{:S(2)}) collective-permute-start(bf16[3,3,32,512]{3,2,1,0:T(8,128)(2,1)S(1)} %collective-permute-done.12.refs_4_), channel_id=1, source_target_pairs={{0,2},{2,0},{4,6},{6,4},{8,10},{10,8},{12,14},{14,12},{16,18},{18,... | collective-permute-start | bytes 884744 | tf_op jit(solution)/shard_map/ppermute | solution.py:70
  27.3 0.7 %collective-permute-done.14.refs_6_ = bf16[3,3,32,512]{3,2,1,0:T(8,128)(2,1)S(1)} collective-permute-done((bf16[3,3,32,512]{3,2,1,0:T(8,128)(2,1)S(1)}, bf16[3,3,32,512]{3,2,1,0:T(8,128)(2,1)S(1)}, u32[]{:S(2)}, u32[]{:S(2)}) %collective-permute-start.14) | collective-permute-done | bytes 294944 | tf_op jit(solution)/shard_map/ppermute | solution.py:67
  28.0 0.0 collective-permute-start.15
  28.0 0.0 collective-permute-done.11.refs_3_
  28.0 0.5 %collective-permute-done.13.refs_5_ = bf16[3,3,32,512]{3,2,1,0:T(8,128)(2,1)S(1)} collective-permute-done((bf16[3,3,32,512]{3,2,1,0:T(8,128)(2,1)S(1)}, bf16[3,3,32,512]{3,2,1,0:T(8,128)(2,1)S(1)}, u32[]{:S(2)}, u32[]{:S(2)}) %collective-permute-start.13) | collective-permute-done | bytes 294944 | tf_op jit(solution)/shard_map/ppermute | solution.py:70
  28.6 1.0 %collective-permute-done.15.refs_7_ = bf16[3,3,32,512]{3,2,1,0:T(8,128)(2,1)S(1)} collective-permute-done((bf16[3,3,32,512]{3,2,1,0:T(8,128)(2,1)S(1)}, bf16[3,3,32,512]{3,2,1,0:T(8,128)(2,1)S(1)}, u32[]{:S(2)}, u32[]{:S(2)}) %collective-permute-start.15) | collective-permute-done | bytes 294944 | tf_op jit(solution)/shard_map/ppermute | solution.py:70
  29.6 3.6 %late.1 = (bf16[8,128,256]{2,1,0:T(8,128)(2,1)S(1)}, bf16[3,128,512]{2,1,0:T(8,128)(2,1)S(1)}) custom-call(bf16[4,6,32,1536]{3,2,1,0:T(8,128)(2,1)S(1)} %get-tuple-element.25.wide_ref.wide0_ref, bf16[4,6,32,1536]{3,2,1,0:T(8,128)(2,1)S(1)} %get-tuple-element.28.wide_ref.wide1_ref, s32[128]{0:T(128)S(1)} %copy-done.6, bf16[3,512,512]{2,1,0:T(8,128)(2,1)S(1)} %copy-done, ...), custom_call_target="tpu_custom_call" | custom-call | tf_op jit(solution)/shard_map/late/pallas_call | solution.py:385
  33.2 2.1 %collective-permute-start.16 = (bf16[3,128,512]{2,1,0:T(8,128)(2,1)S(1)}, bf16[3,128,512]{2,1,0:T(8,128)(2,1)S(1)}, u32[]{:S(2)}, u32[]{:S(2)}) collective-permute-start(bf16[3,128,512]{2,1,0:T(8,128)(2,1)S(1)} %get-tuple-element.40), channel_id=1, source_target_pairs={{0,2},{2,4},{4,6},{6,8},{8,10},{10,12},{12,14},{14,16},{16,18},{18... | collective-permute-start | bytes 1179656 | tf_op jit(solution)/shard_map/ppermute | solution.py:393
  35.2 0.0 copy-start.2
  35.2 0.0 copy-start.4
  35.2 0.0 copy-start.7
  35.3 1.7 %rest.1.base_ref = f32[8,128,512]{2,1,0:T(8,128)S(1)} custom-call(bf16[8,128,256]{2,1,0:T(8,128)(2,1)S(1)} %get-tuple-element.38.acts_ref, s32[128]{0:T(128)S(1)} %copy-done.6, bf16[3,512,512]{2,1,0:T(8,128)(2,1)S(1)} %copy-done, f32[8,128,512]{2,1,0:T(8,128)S(1)} %get-tuple-element.39.early_ref), custom_call_target="tpu_custom_call" | custom-call | tf_op jit(solution)/shard_map/rest/pallas_call | solution.py:394
  37.0 6.2 %collective-permute-done.16.packet_ref = bf16[3,128,512]{2,1,0:T(8,128)(2,1)S(1)} collective-permute-done((bf16[3,128,512]{2,1,0:T(8,128)(2,1)S(1)}, bf16[3,128,512]{2,1,0:T(8,128)(2,1)S(1)}, u32[]{:S(2)}, u32[]{:S(2)}) %collective-permute-start.16) | collective-permute-done | bytes 393248 | tf_op jit(solution)/shard_map/ppermute | solution.py:393
  43.2 0.0 copy-done.2
  43.2 0.0 copy-done.4
  43.2 0.0 copy-done.7
  43.2 5.1 %attend.1 = bf16[8,2,32,512]{3,2,1,0:T(8,128)(2,1)} custom-call(f32[8,128,512]{2,1,0:T(8,128)S(1)} %rest.1.base_ref, bf16[3,128,512]{2,1,0:T(8,128)(2,1)S(1)} %collective-permute-done.16.packet_ref, s32[128]{0:T(128)S(1)} %copy-done.6, f32[1,512]{1,0:T(1,128)S(1)} %bitcast.11, bf16[512,1536]{1,0:T(8,128)(2,1)S(1)} %copy-done.2, bf16[512,512]{1,0:T(8,128)(2,1)S(1)} %copy-done.4), custom_call_target="tpu_custom_call" | custom-call | tf_op jit(solution)/shard_map/attend/pallas_call | solution.py:402
Async XLA Ops:
  0.0 3.1 %collective-permute-start.1 = (bf16[3,3,32,512]{3,2,1,0:T(8,128)(2,1)}, bf16[3,3,32,512]{3,2,1,0:T(8,128)(2,1)S(1)}, u32[]{:S(2)}, u32[]{:S(2)}) collective-permute-start(bf16[3,3,32,512]{3,2,1,0:T(8,128)(2,1)} %bitcast.3), channel_id=1, source_target_pairs={{0,2},{2,0},{4,6},{6,4},{8,10},{10,8},{12,14},{14,12},{16,18},{18,... | collective-permute-start | bytes 884744 | tf_op jit(solution)/shard_map/ppermute | solution.py:63
  0.0 6.9 %collective-permute-start.2 = (bf16[3,3,32,512]{3,2,1,0:T(8,128)(2,1)}, bf16[3,3,32,512]{3,2,1,0:T(8,128)(2,1)S(1)}, u32[]{:S(2)}, u32[]{:S(2)}) collective-permute-start(bf16[3,3,32,512]{3,2,1,0:T(8,128)(2,1)} %bitcast.4), channel_id=1, source_target_pairs={{0,8},{2,6},{8,16},{10,2},{16,24},{18,10},{24,28},{26,18},{28,20},... | collective-permute-start | bytes 884744 | tf_op jit(solution)/shard_map/ppermute | solution.py:67
  1.6 13.0 %collective-permute-start = (bf16[8,2,32,512]{3,2,1,0:T(8,128)(2,1)}, bf16[8,2,32,512]{3,2,1,0:T(8,128)(2,1)S(1)}, u32[]{:S(2)}, u32[]{:S(2)}) collective-permute-start(bf16[8,2,32,512]{3,2,1,0:T(8,128)(2,1)} %refs_0_.3), channel_id=1, source_target_pairs={{0,1},{1,0},{2,3},{3,2},{4,5},{5,4},{6,7},{7,6},{8,9},{9,8},{10,11... | collective-permute-start | bytes 1572872 | tf_op jit(solution)/shard_map/ppermute | solution.py:301
  3.1 7.9 %collective-permute-start.4 = (bf16[3,3,32,512]{3,2,1,0:T(8,128)(2,1)S(1)}, bf16[3,3,32,512]{3,2,1,0:T(8,128)(2,1)S(1)}, u32[]{:S(2)}, u32[]{:S(2)}) collective-permute-start(bf16[3,3,32,512]{3,2,1,0:T(8,128)(2,1)S(1)} %collective-permute-done.1.refs_1_), channel_id=1, source_target_pairs={{0,8},{2,6},{8,16},{10,2},{16,24},{18,10},{24,28},{26,18},{28,20},... | collective-permute-start | bytes 884744 | tf_op jit(solution)/shard_map/ppermute | solution.py:67
  6.9 6.7 %collective-permute-start.6 = (bf16[3,3,32,512]{3,2,1,0:T(8,128)(2,1)S(1)}, bf16[3,3,32,512]{3,2,1,0:T(8,128)(2,1)S(1)}, u32[]{:S(2)}, u32[]{:S(2)}) collective-permute-start(bf16[3,3,32,512]{3,2,1,0:T(8,128)(2,1)S(1)} %collective-permute-done.2.refs_2_), channel_id=1, source_target_pairs={{0,8},{2,6},{8,16},{10,2},{16,24},{18,10},{24,28},{26,18},{28,20},... | collective-permute-start | bytes 884744 | tf_op jit(solution)/shard_map/ppermute | solution.py:67
  8.5 1.0 %copy-start.1 = (bf16[8,2,32,512]{3,2,1,0:T(8,128)(2,1)S(1)}, bf16[8,2,32,512]{3,2,1,0:T(8,128)(2,1)}, u32[]{:S(2)}) copy-start(bf16[8,2,32,512]{3,2,1,0:T(8,128)(2,1)} %refs_0_.3) | copy-start | bytes 1572868
  9.6 0.7 %copy-start.5 = (f32[512]{0:T(512)S(1)}, f32[512]{0:T(512)}, u32[]{:S(2)}) copy-start(f32[512]{0:T(512)} %param.10) | copy-start | bytes 6148
  10.2 9.1 %copy-start.3 = (bf16[3,3,512,32]{2,3,1,0:T(8,128)(2,1)S(1)}, bf16[3,3,512,32]{2,3,1,0:T(8,128)(2,1)}, u32[]{:S(2)}) copy-start(bf16[3,3,512,32]{2,3,1,0:T(8,128)(2,1)} %param.11) | copy-start | bytes 884740
  10.9 6.9 %collective-permute-start.3 = (bf16[3,3,32,512]{3,2,1,0:T(8,128)(2,1)S(1)}, bf16[3,3,32,512]{3,2,1,0:T(8,128)(2,1)S(1)}, u32[]{:S(2)}, u32[]{:S(2)}) collective-permute-start(bf16[3,3,32,512]{3,2,1,0:T(8,128)(2,1)S(1)} %collective-permute-done.2.refs_2_), channel_id=1, source_target_pairs={{0,2},{2,0},{4,6},{6,4},{8,10},{10,8},{12,14},{14,12},{16,18},{18,... | collective-permute-start | bytes 884744 | tf_op jit(solution)/shard_map/ppermute | solution.py:70
  11.0 6.8 %collective-permute-start.8 = (bf16[3,3,32,512]{3,2,1,0:T(8,128)(2,1)S(1)}, bf16[3,3,32,512]{3,2,1,0:T(8,128)(2,1)S(1)}, u32[]{:S(2)}, u32[]{:S(2)}) collective-permute-start(bf16[3,3,32,512]{3,2,1,0:T(8,128)(2,1)S(1)} %collective-permute-done.4.refs_4_), channel_id=1, source_target_pairs={{0,8},{2,6},{8,16},{10,2},{16,24},{18,10},{24,28},{26,18},{28,20},... | collective-permute-start | bytes 884744 | tf_op jit(solution)/shard_map/ppermute | solution.py:67
  12.6 6.7 %collective-permute-start.5 = (bf16[3,3,32,512]{3,2,1,0:T(8,128)(2,1)S(1)}, bf16[3,3,32,512]{3,2,1,0:T(8,128)(2,1)S(1)}, u32[]{:S(2)}, u32[]{:S(2)}) collective-permute-start(bf16[3,3,32,512]{3,2,1,0:T(8,128)(2,1)S(1)} %collective-permute-done.4.refs_4_), channel_id=1, source_target_pairs={{0,2},{2,0},{4,6},{6,4},{8,10},{10,8},{12,14},{14,12},{16,18},{18,... | collective-permute-start | bytes 884744 | tf_op jit(solution)/shard_map/ppermute | solution.py:70
  13.7 5.7 %collective-permute-start.7 = (bf16[3,3,32,512]{3,2,1,0:T(8,128)(2,1)S(1)}, bf16[3,3,32,512]{3,2,1,0:T(8,128)(2,1)S(1)}, u32[]{:S(2)}, u32[]{:S(2)}) collective-permute-start(bf16[3,3,32,512]{3,2,1,0:T(8,128)(2,1)S(1)} %collective-permute-done.6.refs_6_), channel_id=1, source_target_pairs={{0,2},{2,0},{4,6},{6,4},{8,10},{10,8},{12,14},{14,12},{16,18},{18,... | collective-permute-start | bytes 884744 | tf_op jit(solution)/shard_map/ppermute | solution.py:70
  14.6 6.7 %collective-permute-start.10 = (bf16[3,3,32,512]{3,2,1,0:T(8,128)(2,1)S(1)}, bf16[3,3,32,512]{3,2,1,0:T(8,128)(2,1)S(1)}, u32[]{:S(2)}, u32[]{:S(2)}) collective-permute-start(bf16[3,3,32,512]{3,2,1,0:T(8,128)(2,1)S(1)} %collective-permute-done.6.refs_6_), channel_id=1, source_target_pairs={{0,8},{2,6},{8,16},{10,2},{16,24},{18,10},{24,28},{26,18},{28,20},... | collective-permute-start | bytes 884744 | tf_op jit(solution)/shard_map/ppermute | solution.py:67
  17.7 9.0 %collective-permute-start.9 = (bf16[3,3,32,512]{3,2,1,0:T(8,128)(2,1)S(1)}, bf16[3,3,32,512]{3,2,1,0:T(8,128)(2,1)S(1)}, u32[]{:S(2)}, u32[]{:S(2)}) collective-permute-start(bf16[3,3,32,512]{3,2,1,0:T(8,128)(2,1)S(1)} %collective-permute-done.8.refs_0_), channel_id=1, source_target_pairs={{0,2},{2,0},{4,6},{6,4},{8,10},{10,8},{12,14},{14,12},{16,18},{18,... | collective-permute-start | bytes 884744 | tf_op jit(solution)/shard_map/ppermute | solution.py:70
  17.8 9.0 %collective-permute-start.12 = (bf16[3,3,32,512]{3,2,1,0:T(8,128)(2,1)S(1)}, bf16[3,3,32,512]{3,2,1,0:T(8,128)(2,1)S(1)}, u32[]{:S(2)}, u32[]{:S(2)}) collective-permute-start(bf16[3,3,32,512]{3,2,1,0:T(8,128)(2,1)S(1)} %collective-permute-done.8.refs_0_), channel_id=1, source_target_pairs={{0,8},{2,6},{8,16},{10,2},{16,24},{18,10},{24,28},{26,18},{28,20},... | collective-permute-start | bytes 884744 | tf_op jit(solution)/shard_map/ppermute | solution.py:67
  21.3 6.7 %collective-permute-start.14 = (bf16[3,3,32,512]{3,2,1,0:T(8,128)(2,1)S(1)}, bf16[3,3,32,512]{3,2,1,0:T(8,128)(2,1)S(1)}, u32[]{:S(2)}, u32[]{:S(2)}) collective-permute-start(bf16[3,3,32,512]{3,2,1,0:T(8,128)(2,1)S(1)} %collective-permute-done.10.refs_2_), channel_id=1, source_target_pairs={{0,8},{2,6},{8,16},{10,2},{16,24},{18,10},{24,28},{26,18},{28,20},... | collective-permute-start | bytes 884744 | tf_op jit(solution)/shard_map/ppermute | solution.py:67
  23.3 1.5 %copy-start = (bf16[3,512,512]{2,1,0:T(8,128)(2,1)S(1)}, bf16[3,512,512]{2,1,0:T(8,128)(2,1)}, u32[]{:S(2)}) copy-start(bf16[3,512,512]{2,1,0:T(8,128)(2,1)} %time_ref.5) | copy-start | bytes 4718596
  23.3 1.5 %copy-start.6 = (s32[128]{0:T(128)S(1)}, s32[128]{0:T(128)}, u32[]{:S(2)}) copy-start(s32[128]{0:T(128)} %clips.7) | copy-start | bytes 1540
  24.7 3.3 %collective-permute-start.11 = (bf16[3,3,32,512]{3,2,1,0:T(8,128)(2,1)S(1)}, bf16[3,3,32,512]{3,2,1,0:T(8,128)(2,1)S(1)}, u32[]{:S(2)}, u32[]{:S(2)}) collective-permute-start(bf16[3,3,32,512]{3,2,1,0:T(8,128)(2,1)S(1)} %collective-permute-done.10.refs_2_), channel_id=1, source_target_pairs={{0,2},{2,0},{4,6},{6,4},{8,10},{10,8},{12,14},{14,12},{16,18},{18,... | collective-permute-start | bytes 884744 | tf_op jit(solution)/shard_map/ppermute | solution.py:70
  26.8 1.8 %collective-permute-start.13 = (bf16[3,3,32,512]{3,2,1,0:T(8,128)(2,1)S(1)}, bf16[3,3,32,512]{3,2,1,0:T(8,128)(2,1)S(1)}, u32[]{:S(2)}, u32[]{:S(2)}) collective-permute-start(bf16[3,3,32,512]{3,2,1,0:T(8,128)(2,1)S(1)} %collective-permute-done.12.refs_4_), channel_id=1, source_target_pairs={{0,2},{2,0},{4,6},{6,4},{8,10},{10,8},{12,14},{14,12},{16,18},{18,... | collective-permute-start | bytes 884744 | tf_op jit(solution)/shard_map/ppermute | solution.py:70
  28.0 1.6 %collective-permute-start.15 = (bf16[3,3,32,512]{3,2,1,0:T(8,128)(2,1)S(1)}, bf16[3,3,32,512]{3,2,1,0:T(8,128)(2,1)S(1)}, u32[]{:S(2)}, u32[]{:S(2)}) collective-permute-start(bf16[3,3,32,512]{3,2,1,0:T(8,128)(2,1)S(1)} %collective-permute-done.14.refs_6_), channel_id=1, source_target_pairs={{0,2},{2,0},{4,6},{6,4},{8,10},{10,8},{12,14},{14,12},{16,18},{18,... | collective-permute-start | bytes 884744 | tf_op jit(solution)/shard_map/ppermute | solution.py:70
  33.2 10.0 %collective-permute-start.16 = (bf16[3,128,512]{2,1,0:T(8,128)(2,1)S(1)}, bf16[3,128,512]{2,1,0:T(8,128)(2,1)S(1)}, u32[]{:S(2)}, u32[]{:S(2)}) collective-permute-start(bf16[3,128,512]{2,1,0:T(8,128)(2,1)S(1)} %get-tuple-element.40), channel_id=1, source_target_pairs={{0,2},{2,4},{4,6},{6,8},{8,10},{10,12},{12,14},{14,16},{16,18},{18... | collective-permute-start | bytes 1179656 | tf_op jit(solution)/shard_map/ppermute | solution.py:393
  35.2 7.9 %copy-start.2 = (bf16[512,1536]{1,0:T(8,128)(2,1)S(1)}, bf16[512,1536]{1,0:T(8,128)(2,1)}, u32[]{:S(2)}) copy-start(bf16[512,1536]{1,0:T(8,128)(2,1)} %qkv_ref.1) | copy-start | bytes 4718596
  35.2 7.9 %copy-start.4 = (bf16[512,512]{1,0:T(8,128)(2,1)S(1)}, bf16[512,512]{1,0:T(8,128)(2,1)}, u32[]{:S(2)}) copy-start(bf16[512,512]{1,0:T(8,128)(2,1)} %proj_ref.1) | copy-start | bytes 1572868
  35.2 7.9 %copy-start.7 = (f32[512]{0:T(512)S(1)}, f32[512]{0:T(512)}, u32[]{:S(2)}) copy-start(f32[512]{0:T(512)} %param.13) | copy-start | bytes 6148

commit v9 on v8

--- a/solution.py
+++ b/solution.py
@@ -80,31 +80,46 @@
     return device_at(spot, (core + flip) % 2, count)
 
 
-def prepare_kernel(start, at, groups, *refs):
-    part, gain_ref, wide_ref, lat_ref = *refs[:2], *refs[-2:]
-    _, rows, width, chans = part.shape
-    frames = wide_ref.shape[0]
+def normed_rows(raw, gain):
+    rows, width, chans = raw.shape
+    column = lax.broadcasted_iota(jnp.int32, (rows * width, 1), 0) % width
+    x = raw.reshape(rows * width, chans).astype(F32)
+    y = x * lax.rsqrt(jnp.mean(x * x, axis=-1, keepdims=True) + 1e-06) * gain
+    before = jnp.where(column == 0, 0.0, pltpu.roll(y, 1, 0))
+    after = jnp.where(column == width - 1, 0.0, pltpu.roll(y, rows * width - 1, 0))
+    return [v.astype(BF16).reshape(rows, width, chans) for v in (before, y, after)]
+
+
+def prepare_kernel(start, part_ref, gain_ref, band_ref):
+    chans = part_ref.shape[-1]
     gain = gain_ref[...]
-    column = lax.broadcasted_iota(jnp.int32, (rows * width, 1), 0) % width
-    edge = jnp.zeros((width, 3 * chans), BF16)
-    first = at * rows
-    if groups == 2:
-        mine = lax.axis_index("rows")
-        first = (mine if at == 0 else 1 - mine) * rows
-    for frame in range(frames):
-        if at == 0:
-            wide_ref[frame, 0] = edge
-            wide_ref[frame, groups * rows + 1] = edge
-        raw = part[start + frame]
-        lat_ref[frame, pl.ds(first, rows)] = raw
-        x = raw.reshape(rows * width, chans).astype(F32)
-        y = x * lax.rsqrt(jnp.mean(x * x, axis=-1, keepdims=True) + 1e-06) * gain
-        before = jnp.where(column == 0, 0.0, pltpu.roll(y, 1, 0))
-        after = jnp.where(column == width - 1, 0.0, pltpu.roll(y, rows * width - 1, 0))
-        for dx, v in enumerate((before, y, after)):
-            wide_ref[frame, pl.ds(first + 1, rows), :, dx * chans : (dx + 1) * chans] = v.astype(
-                BF16
-            ).reshape(rows, width, chans)
+    for frame in range(band_ref.shape[0]):
+        for dx, v in enumerate(normed_rows(part_ref[start + frame], gain)):
+            band_ref[frame, :, :, dx * chans : (dx + 1) * chans] = v
+
+
+def join_kernel(start, *refs):
+    band_ref, *parts, gain_ref, wide_ref, lat_ref = refs
+    frames, rows, width, wide = band_ref.shape
+    chans = wide // 3
+    groups = len(parts)
+    mine = lax.axis_index("rows")
+    gain = gain_ref[...]
+    edge = jnp.zeros((width, wide), BF16)
+    for at, part in enumerate(parts):
+        first = at * rows
+        if groups == 2:
+            first = (mine if at == 0 else 1 - mine) * rows
+        for frame in range(frames):
+            raw = part[start + frame]
+            lat_ref[frame, pl.ds(first, rows)] = raw
+            if at == 0:
+                wide_ref[frame, 0] = edge
+                wide_ref[frame, groups * rows + 1] = edge
+                wide_ref[frame, pl.ds(first + 1, rows)] = band_ref[frame]
+                continue
+            for dx, v in enumerate(normed_rows(raw, gain)):
+                wide_ref[frame, pl.ds(first + 1, rows), :, dx * chans : (dx + 1) * chans] = v
 
 
 def ordered(time_ref, tags, slots):
@@ -310,35 +325,37 @@
     split = cut * (chans // len(tags))
 
     gain = gain_in.reshape(1, chans)
-    def prepare(start, at, part, pair=()):
-        return pl.pallas_call(
-            functools.partial(prepare_kernel, start, at, groups),
+    own = [
+        pl.pallas_call(
+            functools.partial(prepare_kernel, start),
+            out_shape=shape((half, rows, width, 3 * chans), BF16),
+            in_specs=[VMEM, VMEM],
+            out_specs=VMEM,
+            compiler_params=params,
+            name="prepare",
+        )(parts[0], gain)
+        for start in (0, half)
+    ]
+    wides, lats = [None, None], [None, None]
+
+    def join(which):
+        wides[which], lats[which] = pl.pallas_call(
+            functools.partial(join_kernel, which * half),
             out_shape=(
                 shape((half, height + 2, width, 3 * chans), BF16),
                 shape((half, height, width, chans), BF16),
             ),
-            in_specs=[VMEM] * (2 + len(pair)),
+            in_specs=[VMEM] * (groups + 2),
             out_specs=(VMEM, VMEM),
-            input_output_aliases={2: 0, 3: 1} if pair else {},
             compiler_params=params,
-            name="prepare",
-        )(part, gain, *pair)
-
-    own = [prepare(start, 0, parts[0]) for start in (0, half)]
-    wides, lats = [None, None], [None, None]
-
-    def prepare_rest(which):
-        pair = own[which]
-        for at in range(1, groups):
-            part = parts[at]
-            pair = prepare(which * half, at, part, pair)
-        wides[which], lats[which] = pair
+            name="join",
+        )(own[which], *parts, gain)
 
     acts = [None, None]
     first = []
 
     def early(which, shards):
-        prepare_rest(which)
+        join(which)
         acts[which] = pl.pallas_call(
             early_kernel,
             out_shape=shape((half, spots, split), BF16),

time: 48.7 us -> 50.8 us (1.043)
  waiting for transfers between devices: 14.3 us -> 16.5 us
    ppermute x7, waiting for transfers between devices: 5.69 us -> 8.72 us  [gather_ring(): lax.ppermute(after(streams[stream], gates.get((stream, step, 0)), found),...]
    ppermute x1, waiting for transfers between devices: 0.89 us -> 0.01 us  [local(): parts = [latents, lax.ppermute(latents, 'rows', [(0, 1), (1, 0)])]]
    unnamed x16 -> x18, local copies, waits for them, and re-layouts: 1.76 us -> 1.76 us
  transfers between devices with their start and end apart: 17 -> 17, of which waited for: 9 -> 8; matrix products, arithmetic and copies ran while one was open for 0% -> 0% of each run, Pallas kernels for 16% -> 15%
where the time goes in v9:
time: 50.8 us; the launch traced here: 50.6 us
  waiting for transfers between devices  16.5 us (32%)
  Pallas kernels  16.4 us (32%)
  starting transfers between devices  15.8 us (31%)
  local copies, waits for them, and re-layouts  1.76 us (3%)
    ppermute x7, starting transfers between devices, gather_ring(): lax.ppermute(after(streams[stream], gates.get((stream, step, 0)), found),...  11.1 us
    ppermute x7, waiting for transfers between devices, gather_ring(): lax.ppermute(after(streams[stream], gates.get((stream, step, 0)), found),...  8.72 us
    ppermute x1, waiting for transfers between devices, local(): packet = lax.ppermute(packet, 'tm', [(i, i + 1) for i in range(count - 1)])  6.17 us
    pallas_call x1, Pallas kernels, local(): pl.pallas_call(attend_kernel, out_shape=shape((frames, rows, width, chans...  5.12 us
    pallas_call x1, Pallas kernels, local(): pl.pallas_call(functools.partial(late_kernel, tags[cut:], len(tags)), out...  3.57 us
    pallas_call x2, Pallas kernels, early(): pl.pallas_call(early_kernel, out_shape=shape((half, spots, split), BF16),...  2.84 us
    ppermute x1, starting transfers between devices, local(): packet = lax.ppermute(packet, 'tm', [(i, i + 1) for i in range(count - 1)])  2.05 us
    pallas_call x1, Pallas kernels, begin(): pl.pallas_call(functools.partial(first_kernel, tags[:cut], len(tags)), ou...  1.93 us
  transfers between devices with their start and end apart: 17, of which 8 were waited for; matrix products, arithmetic and copies ran while one was open for 0% of the time, Pallas kernels for 15%

profile of v9, /device:TPU:8, one launch (start us, length us, event | category | flops | bytes accessed | tf_op | source)
XLA Modules:
  0.0 50.6 jit_solution(14573023068535387469)
XLA Ops:
  0.0 0.0 copy-start.6
  0.0 0.0 collective-permute-start.1
  0.0 1.6 %collective-permute-start.2 = (bf16[3,3,32,512]{3,2,1,0:T(8,128)(2,1)}, bf16[3,3,32,512]{3,2,1,0:T(8,128)(2,1)S(1)}, u32[]{:S(2)}, u32[]{:S(2)}) collective-permute-start(bf16[3,3,32,512]{3,2,1,0:T(8,128)(2,1)} %bitcast.4), channel_id=1, source_target_pairs={{0,8},{2,6},{8,16},{10,2},{16,24},{18,10},{24,28},{26,18},{28,20},... | collective-permute-start | bytes 884744 | tf_op jit(solution)/shard_map/ppermute | solution.py:67
  1.6 1.5 %collective-permute-start = (bf16[8,2,32,512]{3,2,1,0:T(8,128)(2,1)}, bf16[8,2,32,512]{3,2,1,0:T(8,128)(2,1)S(1)}, u32[]{:S(2)}, u32[]{:S(2)}) collective-permute-start(bf16[8,2,32,512]{3,2,1,0:T(8,128)(2,1)} %refs_1_.3), channel_id=1, source_target_pairs={{0,1},{1,0},{2,3},{3,2},{4,5},{5,4},{6,7},{7,6},{8,9},{9,8},{10,11... | collective-permute-start | bytes 1572872 | tf_op jit(solution)/shard_map/ppermute | solution.py:316
  3.1 0.0 collective-permute-done.1.refs_1_
  3.1 1.6 %collective-permute-start.4 = (bf16[3,3,32,512]{3,2,1,0:T(8,128)(2,1)S(1)}, bf16[3,3,32,512]{3,2,1,0:T(8,128)(2,1)S(1)}, u32[]{:S(2)}, u32[]{:S(2)}) collective-permute-start(bf16[3,3,32,512]{3,2,1,0:T(8,128)(2,1)S(1)} %collective-permute-done.1.refs_1_), channel_id=1, source_target_pairs={{0,8},{2,6},{8,16},{10,2},{16,24},{18,10},{24,28},{26,18},{28,20},... | collective-permute-start | bytes 884744 | tf_op jit(solution)/shard_map/ppermute | solution.py:67
  4.7 2.3 %collective-permute-done.2.refs_2_ = bf16[3,3,32,512]{3,2,1,0:T(8,128)(2,1)S(1)} collective-permute-done((bf16[3,3,32,512]{3,2,1,0:T(8,128)(2,1)}, bf16[3,3,32,512]{3,2,1,0:T(8,128)(2,1)S(1)}, u32[]{:S(2)}, u32[]{:S(2)}) %collective-permute-start.2) | collective-permute-done | bytes 294944 | tf_op jit(solution)/shard_map/ppermute | solution.py:67
  7.0 1.6 %collective-permute-start.6 = (bf16[3,3,32,512]{3,2,1,0:T(8,128)(2,1)S(1)}, bf16[3,3,32,512]{3,2,1,0:T(8,128)(2,1)S(1)}, u32[]{:S(2)}, u32[]{:S(2)}) collective-permute-start(bf16[3,3,32,512]{3,2,1,0:T(8,128)(2,1)S(1)} %collective-permute-done.2.refs_2_), channel_id=1, source_target_pairs={{0,8},{2,6},{8,16},{10,2},{16,24},{18,10},{24,28},{26,18},{28,20},... | collective-permute-start | bytes 884744 | tf_op jit(solution)/shard_map/ppermute | solution.py:67
  8.6 0.0 copy-start.1
  8.6 1.0 %copy-done.1 = bf16[8,2,32,512]{3,2,1,0:T(8,128)(2,1)S(1)} copy-done((bf16[8,2,32,512]{3,2,1,0:T(8,128)(2,1)S(1)}, bf16[8,2,32,512]{3,2,1,0:T(8,128)(2,1)}, u32[]{:S(2)}) %copy-start.1) | copy-done | bytes 524312
  9.6 0.0 copy-start.5
  9.6 0.7 %copy-done.5 = f32[512]{0:T(512)S(1)} copy-done((f32[512]{0:T(512)S(1)}, f32[512]{0:T(512)}, u32[]{:S(2)}) %copy-start.5) | copy-done | bytes 2072
  10.3 0.0 copy-start.3
  10.3 0.3 prepare.2.refs_0_
  10.6 0.3 prepare.3.refs_0_
  10.8 0.1 collective-permute-start.3
  10.9 0.0 collective-permute-done.4.refs_4_
  10.9 0.5 collective-permute-start.5
  11.4 2.3 %collective-permute-done.6.refs_6_ = bf16[3,3,32,512]{3,2,1,0:T(8,128)(2,1)S(1)} collective-permute-done((bf16[3,3,32,512]{3,2,1,0:T(8,128)(2,1)S(1)}, bf16[3,3,32,512]{3,2,1,0:T(8,128)(2,1)S(1)}, u32[]{:S(2)}, u32[]{:S(2)}) %collective-permute-start.6) | collective-permute-done | bytes 294944 | tf_op jit(solution)/shard_map/ppermute | solution.py:67
  13.7 0.0 collective-permute-start.7
  13.7 1.6 %collective-permute-start.10 = (bf16[3,3,32,512]{3,2,1,0:T(8,128)(2,1)S(1)}, bf16[3,3,32,512]{3,2,1,0:T(8,128)(2,1)S(1)}, u32[]{:S(2)}, u32[]{:S(2)}) collective-permute-start(bf16[3,3,32,512]{3,2,1,0:T(8,128)(2,1)S(1)} %collective-permute-done.6.refs_6_), channel_id=1, source_target_pairs={{0,8},{2,6},{8,16},{10,2},{16,24},{18,10},{24,28},{26,18},{28,20},... | collective-permute-start | bytes 884744 | tf_op jit(solution)/shard_map/ppermute | solution.py:67
  15.3 0.0 collective-permute-done.refs_2_
  15.3 1.6 %collective-permute-start.8 = (bf16[3,3,32,512]{3,2,1,0:T(8,128)(2,1)S(1)}, bf16[3,3,32,512]{3,2,1,0:T(8,128)(2,1)S(1)}, u32[]{:S(2)}, u32[]{:S(2)}) collective-permute-start(bf16[3,3,32,512]{3,2,1,0:T(8,128)(2,1)S(1)} %collective-permute-done.4.refs_4_), channel_id=1, source_target_pairs={{0,8},{2,6},{8,16},{10,2},{16,24},{18,10},{24,28},{26,18},{28,20},... | collective-permute-start | bytes 884744 | tf_op jit(solution)/shard_map/ppermute | solution.py:67
  16.9 0.0 copy-done.6
  16.9 0.3 join.3
  17.2 0.0 collective-permute-done.3.refs_3_
  17.2 0.0 collective-permute-done.5.refs_5_
  17.2 0.0 collective-permute-done.7.refs_7_
  17.2 0.0 copy-done.3
  17.2 1.4 %early.3.acts1_ref = bf16[4,128,256]{2,1,0:T(8,128)(2,1)S(1)} custom-call(bf16[4,6,32,1536]{3,2,1,0:T(8,128)(2,1)S(1)} %get-tuple-element.20.wide_ref.wide1_ref, bf16[3,3,32,512]{3,2,1,0:T(8,128)(2,1)S(1)} %bitcast.5, bf16[3,3,32,512]{3,2,1,0:T(8,128)(2,1)S(1)} %collective-permute-done.1.refs_1_, bf16[3,3,32,512]{3,2,1,0:T(8,128)(2,1)S(1)} %collective-permute-done.2.refs_2_, ...), custom_call_target="tpu_custom_call" | custom-call | tf_op jit(solution)/shard_map/early/pallas_call | solution.py:359
  18.7 1.8 %collective-permute-done.10.refs_2_ = bf16[3,3,32,512]{3,2,1,0:T(8,128)(2,1)S(1)} collective-permute-done((bf16[3,3,32,512]{3,2,1,0:T(8,128)(2,1)S(1)}, bf16[3,3,32,512]{3,2,1,0:T(8,128)(2,1)S(1)}, u32[]{:S(2)}, u32[]{:S(2)}) %collective-permute-start.10) | collective-permute-done | bytes 294944 | tf_op jit(solution)/shard_map/ppermute | solution.py:67
  20.4 1.6 %collective-permute-start.14 = (bf16[3,3,32,512]{3,2,1,0:T(8,128)(2,1)S(1)}, bf16[3,3,32,512]{3,2,1,0:T(8,128)(2,1)S(1)}, u32[]{:S(2)}, u32[]{:S(2)}) collective-permute-start(bf16[3,3,32,512]{3,2,1,0:T(8,128)(2,1)S(1)} %collective-permute-done.10.refs_2_), channel_id=1, source_target_pairs={{0,8},{2,6},{8,16},{10,2},{16,24},{18,10},{24,28},{26,18},{28,20},... | collective-permute-start | bytes 884744 | tf_op jit(solution)/shard_map/ppermute | solution.py:67
  22.0 1.6 %collective-permute-done.8.refs_0_ = bf16[3,3,32,512]{3,2,1,0:T(8,128)(2,1)S(1)} collective-permute-done((bf16[3,3,32,512]{3,2,1,0:T(8,128)(2,1)S(1)}, bf16[3,3,32,512]{3,2,1,0:T(8,128)(2,1)S(1)}, u32[]{:S(2)}, u32[]{:S(2)}) %collective-permute-start.8) | collective-permute-done | bytes 294944 | tf_op jit(solution)/shard_map/ppermute | solution.py:67
  23.6 0.0 collective-permute-start.9
  23.6 1.6 %collective-permute-start.12 = (bf16[3,3,32,512]{3,2,1,0:T(8,128)(2,1)S(1)}, bf16[3,3,32,512]{3,2,1,0:T(8,128)(2,1)S(1)}, u32[]{:S(2)}, u32[]{:S(2)}) collective-permute-start(bf16[3,3,32,512]{3,2,1,0:T(8,128)(2,1)S(1)} %collective-permute-done.8.refs_0_), channel_id=1, source_target_pairs={{0,8},{2,6},{8,16},{10,2},{16,24},{18,10},{24,28},{26,18},{28,20},... | collective-permute-start | bytes 884744 | tf_op jit(solution)/shard_map/ppermute | solution.py:67
  25.2 0.3 join.2
  25.5 0.0 copy-start
  25.5 0.0 copy-start.7
  25.5 1.4 %early.2.acts0_ref = bf16[4,128,256]{2,1,0:T(8,128)(2,1)S(1)} custom-call(bf16[4,6,32,1536]{3,2,1,0:T(8,128)(2,1)S(1)} %get-tuple-element.19.wide_ref.wide0_ref, bf16[3,3,32,512]{3,2,1,0:T(8,128)(2,1)S(1)} %bitcast.6, bf16[3,3,32,512]{3,2,1,0:T(8,128)(2,1)S(1)} %collective-permute-done.1.refs_1_, bf16[3,3,32,512]{3,2,1,0:T(8,128)(2,1)S(1)} %collective-permute-done.2.refs_2_, ...), custom_call_target="tpu_custom_call" | custom-call | tf_op jit(solution)/shard_map/early/pallas_call | solution.py:359
  27.0 0.1 collective-permute-start.11
  27.0 0.0 copy-done
  27.0 0.0 copy-done.7
  27.1 1.9 %first.1 = (f32[8,128,512]{2,1,0:T(8,128)S(1)}, f32[3,128,512]{2,1,0:T(8,128)S(1)}) custom-call(bf16[4,4,32,512]{3,2,1,0:T(8,128)(2,1)S(1)} %get-tuple-element.21.lat0_ref, bf16[4,4,32,512]{3,2,1,0:T(8,128)(2,1)S(1)} %get-tuple-element.22.lat1_ref, bf16[4,128,256]{2,1,0:T(8,128)(2,1)S(1)} %early.2.acts0_ref, bf16[4,128,256]{2,1,0:T(8,128)(2,1)S(1)} %early.3.acts1_ref, ...), custom_call_target="tpu_custom_call" | custom-call | tf_op jit(solution)/shard_map/first/pallas_call | solution.py:374
  29.0 0.0 collective-permute-done.14.refs_6_
  29.0 0.5 %collective-permute-start.15 = (bf16[3,3,32,512]{3,2,1,0:T(8,128)(2,1)S(1)}, bf16[3,3,32,512]{3,2,1,0:T(8,128)(2,1)S(1)}, u32[]{:S(2)}, u32[]{:S(2)}) collective-permute-start(bf16[3,3,32,512]{3,2,1,0:T(8,128)(2,1)S(1)} %collective-permute-done.14.refs_6_), channel_id=1, source_target_pairs={{0,2},{2,0},{4,6},{6,4},{8,10},{10,8},{12,14},{14,12},{16,18},{18,... | collective-permute-start | bytes 884744 | tf_op jit(solution)/shard_map/ppermute | solution.py:70
  29.5 0.0 collective-permute-done.9.refs_1_
  29.5 0.8 %collective-permute-done.12.refs_4_ = bf16[3,3,32,512]{3,2,1,0:T(8,128)(2,1)S(1)} collective-permute-done((bf16[3,3,32,512]{3,2,1,0:T(8,128)(2,1)S(1)}, bf16[3,3,32,512]{3,2,1,0:T(8,128)(2,1)S(1)}, u32[]{:S(2)}, u32[]{:S(2)}) %collective-permute-start.12) | collective-permute-done | bytes 294944 | tf_op jit(solution)/shard_map/ppermute | solution.py:67
  30.3 0.0 collective-permute-start.13
  30.3 0.0 collective-permute-done.11.refs_3_
  30.3 0.4 collective-permute-done.15.refs_7_
  30.7 1.2 %collective-permute-done.13.refs_5_ = bf16[3,3,32,512]{3,2,1,0:T(8,128)(2,1)S(1)} collective-permute-done((bf16[3,3,32,512]{3,2,1,0:T(8,128)(2,1)S(1)}, bf16[3,3,32,512]{3,2,1,0:T(8,128)(2,1)S(1)}, u32[]{:S(2)}, u32[]{:S(2)}) %collective-permute-start.13) | collective-permute-done | bytes 294944 | tf_op jit(solution)/shard_map/ppermute | solution.py:70
  31.9 3.6 %late.1 = (bf16[8,128,256]{2,1,0:T(8,128)(2,1)S(1)}, bf16[3,128,512]{2,1,0:T(8,128)(2,1)S(1)}) custom-call(bf16[4,6,32,1536]{3,2,1,0:T(8,128)(2,1)S(1)} %get-tuple-element.19.wide_ref.wide0_ref, bf16[4,6,32,1536]{3,2,1,0:T(8,128)(2,1)S(1)} %get-tuple-element.20.wide_ref.wide1_ref, s32[128]{0:T(128)S(1)} %copy-done.7, bf16[3,512,512]{2,1,0:T(8,128)(2,1)S(1)} %copy-done, ...), custom_call_target="tpu_custom_call" | custom-call | tf_op jit(solution)/shard_map/late/pallas_call | solution.py:402
  35.5 2.0 %collective-permute-start.16 = (bf16[3,128,512]{2,1,0:T(8,128)(2,1)S(1)}, bf16[3,128,512]{2,1,0:T(8,128)(2,1)S(1)}, u32[]{:S(2)}, u32[]{:S(2)}) collective-permute-start(bf16[3,128,512]{2,1,0:T(8,128)(2,1)S(1)} %get-tuple-element.32), channel_id=1, source_target_pairs={{0,2},{2,4},{4,6},{6,8},{8,10},{10,12},{12,14},{14,16},{16,18},{18... | collective-permute-start | bytes 1179656 | tf_op jit(solution)/shard_map/ppermute | solution.py:410
  37.5 0.0 copy-start.2
  37.6 0.0 copy-start.4
  37.6 0.0 copy-start.8
  37.6 1.7 %rest.1.base_ref = f32[8,128,512]{2,1,0:T(8,128)S(1)} custom-call(bf16[8,128,256]{2,1,0:T(8,128)(2,1)S(1)} %get-tuple-element.30.acts_ref, s32[128]{0:T(128)S(1)} %copy-done.7, bf16[3,512,512]{2,1,0:T(8,128)(2,1)S(1)} %copy-done, f32[8,128,512]{2,1,0:T(8,128)S(1)} %get-tuple-element.31.early_ref), custom_call_target="tpu_custom_call" | custom-call | tf_op jit(solution)/shard_map/rest/pallas_call | solution.py:411
  39.3 6.2 %collective-permute-done.16.packet_ref = bf16[3,128,512]{2,1,0:T(8,128)(2,1)S(1)} collective-permute-done((bf16[3,128,512]{2,1,0:T(8,128)(2,1)S(1)}, bf16[3,128,512]{2,1,0:T(8,128)(2,1)S(1)}, u32[]{:S(2)}, u32[]{:S(2)}) %collective-permute-start.16) | collective-permute-done | bytes 393248 | tf_op jit(solution)/shard_map/ppermute | solution.py:410
  45.5 0.0 copy-done.2
  45.5 0.0 copy-done.4
  45.5 0.0 copy-done.8
  45.5 5.1 %attend.1 = bf16[8,2,32,512]{3,2,1,0:T(8,128)(2,1)} custom-call(f32[8,128,512]{2,1,0:T(8,128)S(1)} %rest.1.base_ref, bf16[3,128,512]{2,1,0:T(8,128)(2,1)S(1)} %collective-permute-done.16.packet_ref, s32[128]{0:T(128)S(1)} %copy-done.7, f32[1,512]{1,0:T(1,128)S(1)} %bitcast.11, bf16[512,1536]{1,0:T(8,128)(2,1)S(1)} %copy-done.2, bf16[512,512]{1,0:T(8,128)(2,1)S(1)} %copy-done.4), custom_call_target="tpu_custom_call" | custom-call | tf_op jit(solution)/shard_map/attend/pallas_call | solution.py:419
Async XLA Ops:
  0.0 16.9 %copy-start.6 = (f32[512]{0:T(512)S(1)}, f32[512]{0:T(512)}, u32[]{:S(2)}) copy-start(f32[512]{0:T(512)} %param.10) | copy-start | bytes 6148
  0.0 3.1 %collective-permute-start.1 = (bf16[3,3,32,512]{3,2,1,0:T(8,128)(2,1)}, bf16[3,3,32,512]{3,2,1,0:T(8,128)(2,1)S(1)}, u32[]{:S(2)}, u32[]{:S(2)}) collective-permute-start(bf16[3,3,32,512]{3,2,1,0:T(8,128)(2,1)} %bitcast.3), channel_id=1, source_target_pairs={{0,2},{2,0},{4,6},{6,4},{8,10},{10,8},{12,14},{14,12},{16,18},{18,... | collective-permute-start | bytes 884744 | tf_op jit(solution)/shard_map/ppermute | solution.py:63
  0.0 7.0 %collective-permute-start.2 = (bf16[3,3,32,512]{3,2,1,0:T(8,128)(2,1)}, bf16[3,3,32,512]{3,2,1,0:T(8,128)(2,1)S(1)}, u32[]{:S(2)}, u32[]{:S(2)}) collective-permute-start(bf16[3,3,32,512]{3,2,1,0:T(8,128)(2,1)} %bitcast.4), channel_id=1, source_target_pairs={{0,8},{2,6},{8,16},{10,2},{16,24},{18,10},{24,28},{26,18},{28,20},... | collective-permute-start | bytes 884744 | tf_op jit(solution)/shard_map/ppermute | solution.py:67
  1.6 13.7 %collective-permute-start = (bf16[8,2,32,512]{3,2,1,0:T(8,128)(2,1)}, bf16[8,2,32,512]{3,2,1,0:T(8,128)(2,1)S(1)}, u32[]{:S(2)}, u32[]{:S(2)}) collective-permute-start(bf16[8,2,32,512]{3,2,1,0:T(8,128)(2,1)} %refs_1_.3), channel_id=1, source_target_pairs={{0,1},{1,0},{2,3},{3,2},{4,5},{5,4},{6,7},{7,6},{8,9},{9,8},{10,11... | collective-permute-start | bytes 1572872 | tf_op jit(solution)/shard_map/ppermute | solution.py:316
  3.1 7.8 %collective-permute-start.4 = (bf16[3,3,32,512]{3,2,1,0:T(8,128)(2,1)S(1)}, bf16[3,3,32,512]{3,2,1,0:T(8,128)(2,1)S(1)}, u32[]{:S(2)}, u32[]{:S(2)}) collective-permute-start(bf16[3,3,32,512]{3,2,1,0:T(8,128)(2,1)S(1)} %collective-permute-done.1.refs_1_), channel_id=1, source_target_pairs={{0,8},{2,6},{8,16},{10,2},{16,24},{18,10},{24,28},{26,18},{28,20},... | collective-permute-start | bytes 884744 | tf_op jit(solution)/shard_map/ppermute | solution.py:67
  7.0 6.7 %collective-permute-start.6 = (bf16[3,3,32,512]{3,2,1,0:T(8,128)(2,1)S(1)}, bf16[3,3,32,512]{3,2,1,0:T(8,128)(2,1)S(1)}, u32[]{:S(2)}, u32[]{:S(2)}) collective-permute-start(bf16[3,3,32,512]{3,2,1,0:T(8,128)(2,1)S(1)} %collective-permute-done.2.refs_2_), channel_id=1, source_target_pairs={{0,8},{2,6},{8,16},{10,2},{16,24},{18,10},{24,28},{26,18},{28,20},... | collective-permute-start | bytes 884744 | tf_op jit(solution)/shard_map/ppermute | solution.py:67
  8.6 1.0 %copy-start.1 = (bf16[8,2,32,512]{3,2,1,0:T(8,128)(2,1)S(1)}, bf16[8,2,32,512]{3,2,1,0:T(8,128)(2,1)}, u32[]{:S(2)}) copy-start(bf16[8,2,32,512]{3,2,1,0:T(8,128)(2,1)} %refs_1_.3) | copy-start | bytes 1572868
  9.6 0.7 %copy-start.5 = (f32[512]{0:T(512)S(1)}, f32[512]{0:T(512)}, u32[]{:S(2)}) copy-start(f32[512]{0:T(512)} %param.10) | copy-start | bytes 6148
  10.3 7.0 %copy-start.3 = (bf16[3,3,512,32]{2,3,1,0:T(8,128)(2,1)S(1)}, bf16[3,3,512,32]{2,3,1,0:T(8,128)(2,1)}, u32[]{:S(2)}) copy-start(bf16[3,3,512,32]{2,3,1,0:T(8,128)(2,1)} %param.11) | copy-start | bytes 884740
  10.8 6.4 %collective-permute-start.3 = (bf16[3,3,32,512]{3,2,1,0:T(8,128)(2,1)S(1)}, bf16[3,3,32,512]{3,2,1,0:T(8,128)(2,1)S(1)}, u32[]{:S(2)}, u32[]{:S(2)}) collective-permute-start(bf16[3,3,32,512]{3,2,1,0:T(8,128)(2,1)S(1)} %collective-permute-done.2.refs_2_), channel_id=1, source_target_pairs={{0,2},{2,0},{4,6},{6,4},{8,10},{10,8},{12,14},{14,12},{16,18},{18,... | collective-permute-start | bytes 884744 | tf_op jit(solution)/shard_map/ppermute | solution.py:70
  10.9 6.3 %collective-permute-start.5 = (bf16[3,3,32,512]{3,2,1,0:T(8,128)(2,1)S(1)}, bf16[3,3,32,512]{3,2,1,0:T(8,128)(2,1)S(1)}, u32[]{:S(2)}, u32[]{:S(2)}) collective-permute-start(bf16[3,3,32,512]{3,2,1,0:T(8,128)(2,1)S(1)} %collective-permute-done.4.refs_4_), channel_id=1, source_target_pairs={{0,2},{2,0},{4,6},{6,4},{8,10},{10,8},{12,14},{14,12},{16,18},{18,... | collective-permute-start | bytes 884744 | tf_op jit(solution)/shard_map/ppermute | solution.py:70
  13.7 3.5 %collective-permute-start.7 = (bf16[3,3,32,512]{3,2,1,0:T(8,128)(2,1)S(1)}, bf16[3,3,32,512]{3,2,1,0:T(8,128)(2,1)S(1)}, u32[]{:S(2)}, u32[]{:S(2)}) collective-permute-start(bf16[3,3,32,512]{3,2,1,0:T(8,128)(2,1)S(1)} %collective-permute-done.6.refs_6_), channel_id=1, source_target_pairs={{0,2},{2,0},{4,6},{6,4},{8,10},{10,8},{12,14},{14,12},{16,18},{18,... | collective-permute-start | bytes 884744 | tf_op jit(solution)/shard_map/ppermute | solution.py:70
  13.7 6.7 %collective-permute-start.10 = (bf16[3,3,32,512]{3,2,1,0:T(8,128)(2,1)S(1)}, bf16[3,3,32,512]{3,2,1,0:T(8,128)(2,1)S(1)}, u32[]{:S(2)}, u32[]{:S(2)}) collective-permute-start(bf16[3,3,32,512]{3,2,1,0:T(8,128)(2,1)S(1)} %collective-permute-done.6.refs_6_), channel_id=1, source_target_pairs={{0,8},{2,6},{8,16},{10,2},{16,24},{18,10},{24,28},{26,18},{28,20},... | collective-permute-start | bytes 884744 | tf_op jit(solution)/shard_map/ppermute | solution.py:67
  15.3 8.3 %collective-permute-start.8 = (bf16[3,3,32,512]{3,2,1,0:T(8,128)(2,1)S(1)}, bf16[3,3,32,512]{3,2,1,0:T(8,128)(2,1)S(1)}, u32[]{:S(2)}, u32[]{:S(2)}) collective-permute-start(bf16[3,3,32,512]{3,2,1,0:T(8,128)(2,1)S(1)} %collective-permute-done.4.refs_4_), channel_id=1, source_target_pairs={{0,8},{2,6},{8,16},{10,2},{16,24},{18,10},{24,28},{26,18},{28,20},... | collective-permute-start | bytes 884744 | tf_op jit(solution)/shard_map/ppermute | solution.py:67
  20.4 8.6 %collective-permute-start.14 = (bf16[3,3,32,512]{3,2,1,0:T(8,128)(2,1)S(1)}, bf16[3,3,32,512]{3,2,1,0:T(8,128)(2,1)S(1)}, u32[]{:S(2)}, u32[]{:S(2)}) collective-permute-start(bf16[3,3,32,512]{3,2,1,0:T(8,128)(2,1)S(1)} %collective-permute-done.10.refs_2_), channel_id=1, source_target_pairs={{0,8},{2,6},{8,16},{10,2},{16,24},{18,10},{24,28},{26,18},{28,20},... | collective-permute-start | bytes 884744 | tf_op jit(solution)/shard_map/ppermute | solution.py:67
  23.6 5.9 %collective-permute-start.9 = (bf16[3,3,32,512]{3,2,1,0:T(8,128)(2,1)S(1)}, bf16[3,3,32,512]{3,2,1,0:T(8,128)(2,1)S(1)}, u32[]{:S(2)}, u32[]{:S(2)}) collective-permute-start(bf16[3,3,32,512]{3,2,1,0:T(8,128)(2,1)S(1)} %collective-permute-done.8.refs_0_), channel_id=1, source_target_pairs={{0,2},{2,0},{4,6},{6,4},{8,10},{10,8},{12,14},{14,12},{16,18},{18,... | collective-permute-start | bytes 884744 | tf_op jit(solution)/shard_map/ppermute | solution.py:70
  23.6 6.7 %collective-permute-start.12 = (bf16[3,3,32,512]{3,2,1,0:T(8,128)(2,1)S(1)}, bf16[3,3,32,512]{3,2,1,0:T(8,128)(2,1)S(1)}, u32[]{:S(2)}, u32[]{:S(2)}) collective-permute-start(bf16[3,3,32,512]{3,2,1,0:T(8,128)(2,1)S(1)} %collective-permute-done.8.refs_0_), channel_id=1, source_target_pairs={{0,8},{2,6},{8,16},{10,2},{16,24},{18,10},{24,28},{26,18},{28,20},... | collective-permute-start | bytes 884744 | tf_op jit(solution)/shard_map/ppermute | solution.py:67
  25.5 1.5 %copy-start = (bf16[3,512,512]{2,1,0:T(8,128)(2,1)S(1)}, bf16[3,512,512]{2,1,0:T(8,128)(2,1)}, u32[]{:S(2)}) copy-start(bf16[3,512,512]{2,1,0:T(8,128)(2,1)} %time_ref.5) | copy-start | bytes 4718596
  25.5 1.5 %copy-start.7 = (s32[128]{0:T(128)S(1)}, s32[128]{0:T(128)}, u32[]{:S(2)}) copy-start(s32[128]{0:T(128)} %clips.7) | copy-start | bytes 1540
  27.0 3.4 %collective-permute-start.11 = (bf16[3,3,32,512]{3,2,1,0:T(8,128)(2,1)S(1)}, bf16[3,3,32,512]{3,2,1,0:T(8,128)(2,1)S(1)}, u32[]{:S(2)}, u32[]{:S(2)}) collective-permute-start(bf16[3,3,32,512]{3,2,1,0:T(8,128)(2,1)S(1)} %collective-permute-done.10.refs_2_), channel_id=1, source_target_pairs={{0,2},{2,0},{4,6},{6,4},{8,10},{10,8},{12,14},{14,12},{16,18},{18,... | collective-permute-start | bytes 884744 | tf_op jit(solution)/shard_map/ppermute | solution.py:70
  29.0 1.8 %collective-permute-start.15 = (bf16[3,3,32,512]{3,2,1,0:T(8,128)(2,1)S(1)}, bf16[3,3,32,512]{3,2,1,0:T(8,128)(2,1)S(1)}, u32[]{:S(2)}, u32[]{:S(2)}) collective-permute-start(bf16[3,3,32,512]{3,2,1,0:T(8,128)(2,1)S(1)} %collective-permute-done.14.refs_6_), channel_id=1, source_target_pairs={{0,2},{2,0},{4,6},{6,4},{8,10},{10,8},{12,14},{14,12},{16,18},{18,... | collective-permute-start | bytes 884744 | tf_op jit(solution)/shard_map/ppermute | solution.py:70
  30.3 1.6 %collective-permute-start.13 = (bf16[3,3,32,512]{3,2,1,0:T(8,128)(2,1)S(1)}, bf16[3,3,32,512]{3,2,1,0:T(8,128)(2,1)S(1)}, u32[]{:S(2)}, u32[]{:S(2)}) collective-permute-start(bf16[3,3,32,512]{3,2,1,0:T(8,128)(2,1)S(1)} %collective-permute-done.12.refs_4_), channel_id=1, source_target_pairs={{0,2},{2,0},{4,6},{6,4},{8,10},{10,8},{12,14},{14,12},{16,18},{18,... | collective-permute-start | bytes 884744 | tf_op jit(solution)/shard_map/ppermute | solution.py:70
  35.5 10.0 %collective-permute-start.16 = (bf16[3,128,512]{2,1,0:T(8,128)(2,1)S(1)}, bf16[3,128,512]{2,1,0:T(8,128)(2,1)S(1)}, u32[]{:S(2)}, u32[]{:S(2)}) collective-permute-start(bf16[3,128,512]{2,1,0:T(8,128)(2,1)S(1)} %get-tuple-element.32), channel_id=1, source_target_pairs={{0,2},{2,4},{4,6},{6,8},{8,10},{10,12},{12,14},{14,16},{16,18},{18... | collective-permute-start | bytes 1179656 | tf_op jit(solution)/shard_map/ppermute | solution.py:410
  37.5 7.9 %copy-start.2 = (bf16[512,1536]{1,0:T(8,128)(2,1)S(1)}, bf16[512,1536]{1,0:T(8,128)(2,1)}, u32[]{:S(2)}) copy-start(bf16[512,1536]{1,0:T(8,128)(2,1)} %qkv_ref.1) | copy-start | bytes 4718596
  37.6 7.9 %copy-start.4 = (bf16[512,512]{1,0:T(8,128)(2,1)S(1)}, bf16[512,512]{1,0:T(8,128)(2,1)}, u32[]{:S(2)}) copy-start(bf16[512,512]{1,0:T(8,128)(2,1)} %proj_ref.1) | copy-start | bytes 1572868
  37.6 7.9 %copy-start.8 = (f32[512]{0:T(512)S(1)}, f32[512]{0:T(512)}, u32[]{:S(2)}) copy-start(f32[512]{0:T(512)} %param.13) | copy-start | bytes 6148

commit v10 on v9

--- a/solution.py
+++ b/solution.py
@@ -386,11 +386,9 @@
         last = count // 4
         gates = {
             (1, 1, 1): lambda found: own,
-            (1, last - 2, 1): lambda found: parts[1],
             (0, last - 1, 1): functools.partial(early, 0),
             (1, last - 1, 1): lambda found: found[9],
             (0, last, 0): functools.partial(early, 1),
-            (0, last, 1): begin,
         }
         shards = gather_ring(shard, count, gates)
     else:

time: 50.8 us -> 49.6 us (0.976)
  waiting for transfers between devices: 16.5 us -> 15.3 us
    ppermute x7, waiting for transfers between devices: 1.59 us -> 0.02 us  [gather_ring(): lax.ppermute(after(shard, gates.get((stream, step, 1)), found), 'tm', cores)]
    ppermute x1, waiting for transfers between devices: 0.01 us -> 0.84 us  [local(): parts = [latents, lax.ppermute(latents, 'rows', [(0, 1), (1, 0)])]]
    ppermute x7, waiting for transfers between devices: 8.72 us -> 8.16 us  [gather_ring(): lax.ppermute(after(streams[stream], gates.get((stream, step, 0)), found),...]
    ppermute x7, starting transfers between devices: 1.18 us -> 0.66 us  [gather_ring(): lax.ppermute(after(shard, gates.get((stream, step, 1)), found), 'tm', cores)]
  transfers between devices with their start and end apart: 17 -> 17, of which waited for: 8 -> 7; matrix products, arithmetic and copies ran while one was open for 0% -> 0% of each run, Pallas kernels for 15% -> 16%
where the time goes in v10:
time: 49.6 us; the launch traced here: 49.2 us
  Pallas kernels  16.4 us (33%)
  starting transfers between devices  15.5 us (31%)
  waiting for transfers between devices  15.3 us (31%)
  local copies, waits for them, and re-layouts  1.76 us (4%)
    ppermute x7, starting transfers between devices, gather_ring(): lax.ppermute(after(streams[stream], gates.get((stream, step, 0)), found),...  11.5 us
    ppermute x7, waiting for transfers between devices, gather_ring(): lax.ppermute(after(streams[stream], gates.get((stream, step, 0)), found),...  8.16 us
    ppermute x1, waiting for transfers between devices, local(): packet = lax.ppermute(packet, 'tm', [(i, i + 1) for i in range(count - 1)])  6.3 us
    pallas_call x1, Pallas kernels, local(): pl.pallas_call(attend_kernel, out_shape=shape((frames, rows, width, chans...  5.12 us
    pallas_call x1, Pallas kernels, local(): pl.pallas_call(functools.partial(late_kernel, tags[cut:], len(tags)), out...  3.59 us
    pallas_call x2, Pallas kernels, early(): pl.pallas_call(early_kernel, out_shape=shape((half, spots, split), BF16),...  2.84 us
    ppermute x1, starting transfers between devices, local(): packet = lax.ppermute(packet, 'tm', [(i, i + 1) for i in range(count - 1)])  1.92 us
    pallas_call x1, Pallas kernels, begin(): pl.pallas_call(functools.partial(first_kernel, tags[:cut], len(tags)), ou...  1.92 us
  transfers between devices with their start and end apart: 17, of which 7 were waited for; matrix products, arithmetic and copies ran while one was open for 0% of the time, Pallas kernels for 16%

profile of v10, /device:TPU:8, one launch (start us, length us, event | category | flops | bytes accessed | tf_op | source)
XLA Modules:
  0.0 49.2 jit_solution(1623463596126633986)
XLA Ops:
  0.0 0.0 copy-start.6
  0.0 0.0 collective-permute-start.1
  0.0 1.6 %collective-permute-start.2 = (bf16[3,3,32,512]{3,2,1,0:T(8,128)(2,1)}, bf16[3,3,32,512]{3,2,1,0:T(8,128)(2,1)S(1)}, u32[]{:S(2)}, u32[]{:S(2)}) collective-permute-start(bf16[3,3,32,512]{3,2,1,0:T(8,128)(2,1)} %bitcast.4), channel_id=1, source_target_pairs={{0,8},{2,6},{8,16},{10,2},{16,24},{18,10},{24,28},{26,18},{28,20},... | collective-permute-start | bytes 884744 | tf_op jit(solution)/shard_map/ppermute | solution.py:67
  1.6 1.5 %collective-permute-start = (bf16[8,2,32,512]{3,2,1,0:T(8,128)(2,1)}, bf16[8,2,32,512]{3,2,1,0:T(8,128)(2,1)S(1)}, u32[]{:S(2)}, u32[]{:S(2)}) collective-permute-start(bf16[8,2,32,512]{3,2,1,0:T(8,128)(2,1)} %refs_1_.3), channel_id=1, source_target_pairs={{0,1},{1,0},{2,3},{3,2},{4,5},{5,4},{6,7},{7,6},{8,9},{9,8},{10,11... | collective-permute-start | bytes 1572872 | tf_op jit(solution)/shard_map/ppermute | solution.py:316
  3.1 0.0 collective-permute-done.1.refs_1_
  3.1 1.6 %collective-permute-start.4 = (bf16[3,3,32,512]{3,2,1,0:T(8,128)(2,1)S(1)}, bf16[3,3,32,512]{3,2,1,0:T(8,128)(2,1)S(1)}, u32[]{:S(2)}, u32[]{:S(2)}) collective-permute-start(bf16[3,3,32,512]{3,2,1,0:T(8,128)(2,1)S(1)} %collective-permute-done.1.refs_1_), channel_id=1, source_target_pairs={{0,8},{2,6},{8,16},{10,2},{16,24},{18,10},{24,28},{26,18},{28,20},... | collective-permute-start | bytes 884744 | tf_op jit(solution)/shard_map/ppermute | solution.py:67
  4.7 2.3 %collective-permute-done.2.refs_2_ = bf16[3,3,32,512]{3,2,1,0:T(8,128)(2,1)S(1)} collective-permute-done((bf16[3,3,32,512]{3,2,1,0:T(8,128)(2,1)}, bf16[3,3,32,512]{3,2,1,0:T(8,128)(2,1)S(1)}, u32[]{:S(2)}, u32[]{:S(2)}) %collective-permute-start.2) | collective-permute-done | bytes 294944 | tf_op jit(solution)/shard_map/ppermute | solution.py:67
  7.0 1.6 %collective-permute-start.6 = (bf16[3,3,32,512]{3,2,1,0:T(8,128)(2,1)S(1)}, bf16[3,3,32,512]{3,2,1,0:T(8,128)(2,1)S(1)}, u32[]{:S(2)}, u32[]{:S(2)}) collective-permute-start(bf16[3,3,32,512]{3,2,1,0:T(8,128)(2,1)S(1)} %collective-permute-done.2.refs_2_), channel_id=1, source_target_pairs={{0,8},{2,6},{8,16},{10,2},{16,24},{18,10},{24,28},{26,18},{28,20},... | collective-permute-start | bytes 884744 | tf_op jit(solution)/shard_map/ppermute | solution.py:67
  8.6 0.0 copy-start.1
  8.6 1.0 %copy-done.1 = bf16[8,2,32,512]{3,2,1,0:T(8,128)(2,1)S(1)} copy-done((bf16[8,2,32,512]{3,2,1,0:T(8,128)(2,1)S(1)}, bf16[8,2,32,512]{3,2,1,0:T(8,128)(2,1)}, u32[]{:S(2)}) %copy-start.1) | copy-done | bytes 524312
  9.6 0.0 copy-start.5
  9.6 0.7 %copy-done.5 = f32[512]{0:T(512)S(1)} copy-done((f32[512]{0:T(512)S(1)}, f32[512]{0:T(512)}, u32[]{:S(2)}) %copy-start.5) | copy-done | bytes 2072
  10.3 0.0 copy-start.3
  10.3 0.3 prepare.2.refs_0_
  10.6 0.3 prepare.3.refs_0_
  10.8 0.1 collective-permute-start.3
  10.9 0.0 collective-permute-done.4.refs_4_
  10.9 1.6 %collective-permute-start.8 = (bf16[3,3,32,512]{3,2,1,0:T(8,128)(2,1)S(1)}, bf16[3,3,32,512]{3,2,1,0:T(8,128)(2,1)S(1)}, u32[]{:S(2)}, u32[]{:S(2)}) collective-permute-start(bf16[3,3,32,512]{3,2,1,0:T(8,128)(2,1)S(1)} %collective-permute-done.4.refs_4_), channel_id=1, source_target_pairs={{0,8},{2,6},{8,16},{10,2},{16,24},{18,10},{24,28},{26,18},{28,20},... | collective-permute-start | bytes 884744 | tf_op jit(solution)/shard_map/ppermute | solution.py:67
  12.5 0.0 collective-permute-start.5
  12.5 1.2 %collective-permute-done.6.refs_6_ = bf16[3,3,32,512]{3,2,1,0:T(8,128)(2,1)S(1)} collective-permute-done((bf16[3,3,32,512]{3,2,1,0:T(8,128)(2,1)S(1)}, bf16[3,3,32,512]{3,2,1,0:T(8,128)(2,1)S(1)}, u32[]{:S(2)}, u32[]{:S(2)}) %collective-permute-start.6) | collective-permute-done | bytes 294944 | tf_op jit(solution)/shard_map/ppermute | solution.py:67
  13.7 0.0 collective-permute-start.7
  13.7 0.8 %collective-permute-done.refs_2_ = bf16[8,2,32,512]{3,2,1,0:T(8,128)(2,1)S(1)} collective-permute-done((bf16[8,2,32,512]{3,2,1,0:T(8,128)(2,1)}, bf16[8,2,32,512]{3,2,1,0:T(8,128)(2,1)S(1)}, u32[]{:S(2)}, u32[]{:S(2)}) %collective-permute-start) | collective-permute-done | bytes 524320 | tf_op jit(solution)/shard_map/ppermute | solution.py:316
  14.6 1.7 %collective-permute-start.10 = (bf16[3,3,32,512]{3,2,1,0:T(8,128)(2,1)S(1)}, bf16[3,3,32,512]{3,2,1,0:T(8,128)(2,1)S(1)}, u32[]{:S(2)}, u32[]{:S(2)}) collective-permute-start(bf16[3,3,32,512]{3,2,1,0:T(8,128)(2,1)S(1)} %collective-permute-done.6.refs_6_), channel_id=1, source_target_pairs={{0,8},{2,6},{8,16},{10,2},{16,24},{18,10},{24,28},{26,18},{28,20},... | collective-permute-start | bytes 884744 | tf_op jit(solution)/shard_map/ppermute | solution.py:67
  16.3 0.0 copy-done.6
  16.3 0.3 join.3
  16.6 1.1 %collective-permute-done.8.refs_0_ = bf16[3,3,32,512]{3,2,1,0:T(8,128)(2,1)S(1)} collective-permute-done((bf16[3,3,32,512]{3,2,1,0:T(8,128)(2,1)S(1)}, bf16[3,3,32,512]{3,2,1,0:T(8,128)(2,1)S(1)}, u32[]{:S(2)}, u32[]{:S(2)}) %collective-permute-start.8) | collective-permute-done | bytes 294944 | tf_op jit(solution)/shard_map/ppermute | solution.py:67
  17.7 1.6 %collective-permute-start.12 = (bf16[3,3,32,512]{3,2,1,0:T(8,128)(2,1)S(1)}, bf16[3,3,32,512]{3,2,1,0:T(8,128)(2,1)S(1)}, u32[]{:S(2)}, u32[]{:S(2)}) collective-permute-start(bf16[3,3,32,512]{3,2,1,0:T(8,128)(2,1)S(1)} %collective-permute-done.8.refs_0_), channel_id=1, source_target_pairs={{0,8},{2,6},{8,16},{10,2},{16,24},{18,10},{24,28},{26,18},{28,20},... | collective-permute-start | bytes 884744 | tf_op jit(solution)/shard_map/ppermute | solution.py:67
  19.3 0.0 collective-permute-done.3.refs_3_
  19.3 0.0 collective-permute-start.9
  19.3 0.0 collective-permute-done.5.refs_5_
  19.3 0.0 collective-permute-done.7.refs_7_
  19.3 0.0 copy-done.3
  19.3 1.4 %early.3.acts1_ref = bf16[4,128,256]{2,1,0:T(8,128)(2,1)S(1)} custom-call(bf16[4,6,32,1536]{3,2,1,0:T(8,128)(2,1)S(1)} %get-tuple-element.18.wide_ref.wide1_ref, bf16[3,3,32,512]{3,2,1,0:T(8,128)(2,1)S(1)} %bitcast.5, bf16[3,3,32,512]{3,2,1,0:T(8,128)(2,1)S(1)} %collective-permute-done.1.refs_1_, bf16[3,3,32,512]{3,2,1,0:T(8,128)(2,1)S(1)} %collective-permute-done.2.refs_2_, ...), custom_call_target="tpu_custom_call" | custom-call | tf_op jit(solution)/shard_map/early/pallas_call | solution.py:359
  20.7 0.6 %collective-permute-done.10.refs_2_ = bf16[3,3,32,512]{3,2,1,0:T(8,128)(2,1)S(1)} collective-permute-done((bf16[3,3,32,512]{3,2,1,0:T(8,128)(2,1)S(1)}, bf16[3,3,32,512]{3,2,1,0:T(8,128)(2,1)S(1)}, u32[]{:S(2)}, u32[]{:S(2)}) %collective-permute-start.10) | collective-permute-done | bytes 294944 | tf_op jit(solution)/shard_map/ppermute | solution.py:67
  21.3 1.7 %collective-permute-start.14 = (bf16[3,3,32,512]{3,2,1,0:T(8,128)(2,1)S(1)}, bf16[3,3,32,512]{3,2,1,0:T(8,128)(2,1)S(1)}, u32[]{:S(2)}, u32[]{:S(2)}) collective-permute-start(bf16[3,3,32,512]{3,2,1,0:T(8,128)(2,1)S(1)} %collective-permute-done.10.refs_2_), channel_id=1, source_target_pairs={{0,8},{2,6},{8,16},{10,2},{16,24},{18,10},{24,28},{26,18},{28,20},... | collective-permute-start | bytes 884744 | tf_op jit(solution)/shard_map/ppermute | solution.py:67
  23.0 0.3 join.2
  23.4 0.0 copy-start
  23.4 0.0 copy-start.7
  23.4 1.4 %early.2.acts0_ref = bf16[4,128,256]{2,1,0:T(8,128)(2,1)S(1)} custom-call(bf16[4,6,32,1536]{3,2,1,0:T(8,128)(2,1)S(1)} %get-tuple-element.17.wide_ref.wide0_ref, bf16[3,3,32,512]{3,2,1,0:T(8,128)(2,1)S(1)} %bitcast.6, bf16[3,3,32,512]{3,2,1,0:T(8,128)(2,1)S(1)} %collective-permute-done.1.refs_1_, bf16[3,3,32,512]{3,2,1,0:T(8,128)(2,1)S(1)} %collective-permute-done.2.refs_2_, ...), custom_call_target="tpu_custom_call" | custom-call | tf_op jit(solution)/shard_map/early/pallas_call | solution.py:359
  24.8 0.1 collective-permute-start.11
  24.9 0.0 collective-permute-done.12.refs_4_
  24.9 0.0 collective-permute-done.9.refs_1_
  24.9 3.1 %collective-permute-done.14.refs_6_ = bf16[3,3,32,512]{3,2,1,0:T(8,128)(2,1)S(1)} collective-permute-done((bf16[3,3,32,512]{3,2,1,0:T(8,128)(2,1)S(1)}, bf16[3,3,32,512]{3,2,1,0:T(8,128)(2,1)S(1)}, u32[]{:S(2)}, u32[]{:S(2)}) %collective-permute-start.14) | collective-permute-done | bytes 294944 | tf_op jit(solution)/shard_map/ppermute | solution.py:67
  28.0 0.0 collective-permute-start.15
  28.0 0.5 %collective-permute-start.13 = (bf16[3,3,32,512]{3,2,1,0:T(8,128)(2,1)S(1)}, bf16[3,3,32,512]{3,2,1,0:T(8,128)(2,1)S(1)}, u32[]{:S(2)}, u32[]{:S(2)}) collective-permute-start(bf16[3,3,32,512]{3,2,1,0:T(8,128)(2,1)S(1)} %collective-permute-done.12.refs_4_), channel_id=1, source_target_pairs={{0,2},{2,0},{4,6},{6,4},{8,10},{10,8},{12,14},{14,12},{16,18},{18,... | collective-permute-start | bytes 884744 | tf_op jit(solution)/shard_map/ppermute | solution.py:70
  28.5 0.0 copy-done
  28.5 0.0 copy-done.7
  28.5 1.9 %first.1 = (f32[8,128,512]{2,1,0:T(8,128)S(1)}, f32[3,128,512]{2,1,0:T(8,128)S(1)}) custom-call(bf16[4,4,32,512]{3,2,1,0:T(8,128)(2,1)S(1)} %get-tuple-element.19.lat0_ref, bf16[4,4,32,512]{3,2,1,0:T(8,128)(2,1)S(1)} %get-tuple-element.20.lat1_ref, bf16[4,128,256]{2,1,0:T(8,128)(2,1)S(1)} %early.2.acts0_ref, bf16[4,128,256]{2,1,0:T(8,128)(2,1)S(1)} %early.3.acts1_ref, ...), custom_call_target="tpu_custom_call" | custom-call | tf_op jit(solution)/shard_map/first/pallas_call | solution.py:374
  30.4 0.0 collective-permute-done.11.refs_3_
  30.5 0.0 collective-permute-done.15.refs_7_
  30.5 0.0 collective-permute-done.13.refs_5_
  30.5 3.6 %late.1 = (bf16[8,128,256]{2,1,0:T(8,128)(2,1)S(1)}, bf16[3,128,512]{2,1,0:T(8,128)(2,1)S(1)}) custom-call(bf16[4,6,32,1536]{3,2,1,0:T(8,128)(2,1)S(1)} %get-tuple-element.17.wide_ref.wide0_ref, bf16[4,6,32,1536]{3,2,1,0:T(8,128)(2,1)S(1)} %get-tuple-element.18.wide_ref.wide1_ref, s32[128]{0:T(128)S(1)} %copy-done.7, bf16[3,512,512]{2,1,0:T(8,128)(2,1)S(1)} %copy-done, ...), custom_call_target="tpu_custom_call" | custom-call | tf_op jit(solution)/shard_map/late/pallas_call | solution.py:400
  34.1 1.9 %collective-permute-start.16 = (bf16[3,128,512]{2,1,0:T(8,128)(2,1)S(1)}, bf16[3,128,512]{2,1,0:T(8,128)(2,1)S(1)}, u32[]{:S(2)}, u32[]{:S(2)}) collective-permute-start(bf16[3,128,512]{2,1,0:T(8,128)(2,1)S(1)} %get-tuple-element.28), channel_id=1, source_target_pairs={{0,2},{2,4},{4,6},{6,8},{8,10},{10,12},{12,14},{14,16},{16,18},{18... | collective-permute-start | bytes 1179656 | tf_op jit(solution)/shard_map/ppermute | solution.py:408
  36.0 0.0 copy-start.2
  36.0 0.0 copy-start.4
  36.0 0.0 copy-start.8
  36.0 1.7 %rest.1.base_ref = f32[8,128,512]{2,1,0:T(8,128)S(1)} custom-call(bf16[8,128,256]{2,1,0:T(8,128)(2,1)S(1)} %get-tuple-element.26.acts_ref, s32[128]{0:T(128)S(1)} %copy-done.7, bf16[3,512,512]{2,1,0:T(8,128)(2,1)S(1)} %copy-done, f32[8,128,512]{2,1,0:T(8,128)S(1)} %get-tuple-element.27.early_ref), custom_call_target="tpu_custom_call" | custom-call | tf_op jit(solution)/shard_map/rest/pallas_call | solution.py:409
  37.8 6.3 %collective-permute-done.16.packet_ref = bf16[3,128,512]{2,1,0:T(8,128)(2,1)S(1)} collective-permute-done((bf16[3,128,512]{2,1,0:T(8,128)(2,1)S(1)}, bf16[3,128,512]{2,1,0:T(8,128)(2,1)S(1)}, u32[]{:S(2)}, u32[]{:S(2)}) %collective-permute-start.16) | collective-permute-done | bytes 393248 | tf_op jit(solution)/shard_map/ppermute | solution.py:408
  44.1 0.0 copy-done.2
  44.1 0.0 copy-done.4
  44.1 0.0 copy-done.8
  44.1 5.1 %attend.1 = bf16[8,2,32,512]{3,2,1,0:T(8,128)(2,1)} custom-call(f32[8,128,512]{2,1,0:T(8,128)S(1)} %rest.1.base_ref, bf16[3,128,512]{2,1,0:T(8,128)(2,1)S(1)} %collective-permute-done.16.packet_ref, s32[128]{0:T(128)S(1)} %copy-done.7, f32[1,512]{1,0:T(1,128)S(1)} %bitcast.11, bf16[512,1536]{1,0:T(8,128)(2,1)S(1)} %copy-done.2, bf16[512,512]{1,0:T(8,128)(2,1)S(1)} %copy-done.4), custom_call_target="tpu_custom_call" | custom-call | tf_op jit(solution)/shard_map/attend/pallas_call | solution.py:417
Async XLA Ops:
  0.0 16.3 %copy-start.6 = (f32[512]{0:T(512)S(1)}, f32[512]{0:T(512)}, u32[]{:S(2)}) copy-start(f32[512]{0:T(512)} %param.10) | copy-start | bytes 6148
  0.0 3.1 %collective-permute-start.1 = (bf16[3,3,32,512]{3,2,1,0:T(8,128)(2,1)}, bf16[3,3,32,512]{3,2,1,0:T(8,128)(2,1)S(1)}, u32[]{:S(2)}, u32[]{:S(2)}) collective-permute-start(bf16[3,3,32,512]{3,2,1,0:T(8,128)(2,1)} %bitcast.3), channel_id=1, source_target_pairs={{0,2},{2,0},{4,6},{6,4},{8,10},{10,8},{12,14},{14,12},{16,18},{18,... | collective-permute-start | bytes 884744 | tf_op jit(solution)/shard_map/ppermute | solution.py:63
  0.0 7.0 %collective-permute-start.2 = (bf16[3,3,32,512]{3,2,1,0:T(8,128)(2,1)}, bf16[3,3,32,512]{3,2,1,0:T(8,128)(2,1)S(1)}, u32[]{:S(2)}, u32[]{:S(2)}) collective-permute-start(bf16[3,3,32,512]{3,2,1,0:T(8,128)(2,1)} %bitcast.4), channel_id=1, source_target_pairs={{0,8},{2,6},{8,16},{10,2},{16,24},{18,10},{24,28},{26,18},{28,20},... | collective-permute-start | bytes 884744 | tf_op jit(solution)/shard_map/ppermute | solution.py:67
  1.6 12.9 %collective-permute-start = (bf16[8,2,32,512]{3,2,1,0:T(8,128)(2,1)}, bf16[8,2,32,512]{3,2,1,0:T(8,128)(2,1)S(1)}, u32[]{:S(2)}, u32[]{:S(2)}) collective-permute-start(bf16[8,2,32,512]{3,2,1,0:T(8,128)(2,1)} %refs_1_.3), channel_id=1, source_target_pairs={{0,1},{1,0},{2,3},{3,2},{4,5},{5,4},{6,7},{7,6},{8,9},{9,8},{10,11... | collective-permute-start | bytes 1572872 | tf_op jit(solution)/shard_map/ppermute | solution.py:316
  3.1 7.8 %collective-permute-start.4 = (bf16[3,3,32,512]{3,2,1,0:T(8,128)(2,1)S(1)}, bf16[3,3,32,512]{3,2,1,0:T(8,128)(2,1)S(1)}, u32[]{:S(2)}, u32[]{:S(2)}) collective-permute-start(bf16[3,3,32,512]{3,2,1,0:T(8,128)(2,1)S(1)} %collective-permute-done.1.refs_1_), channel_id=1, source_target_pairs={{0,8},{2,6},{8,16},{10,2},{16,24},{18,10},{24,28},{26,18},{28,20},... | collective-permute-start | bytes 884744 | tf_op jit(solution)/shard_map/ppermute | solution.py:67
  7.0 6.7 %collective-permute-start.6 = (bf16[3,3,32,512]{3,2,1,0:T(8,128)(2,1)S(1)}, bf16[3,3,32,512]{3,2,1,0:T(8,128)(2,1)S(1)}, u32[]{:S(2)}, u32[]{:S(2)}) collective-permute-start(bf16[3,3,32,512]{3,2,1,0:T(8,128)(2,1)S(1)} %collective-permute-done.2.refs_2_), channel_id=1, source_target_pairs={{0,8},{2,6},{8,16},{10,2},{16,24},{18,10},{24,28},{26,18},{28,20},... | collective-permute-start | bytes 884744 | tf_op jit(solution)/shard_map/ppermute | solution.py:67
  8.6 1.0 %copy-start.1 = (bf16[8,2,32,512]{3,2,1,0:T(8,128)(2,1)S(1)}, bf16[8,2,32,512]{3,2,1,0:T(8,128)(2,1)}, u32[]{:S(2)}) copy-start(bf16[8,2,32,512]{3,2,1,0:T(8,128)(2,1)} %refs_1_.3) | copy-start | bytes 1572868
  9.6 0.7 %copy-start.5 = (f32[512]{0:T(512)S(1)}, f32[512]{0:T(512)}, u32[]{:S(2)}) copy-start(f32[512]{0:T(512)} %param.10) | copy-start | bytes 6148
  10.3 9.0 %copy-start.3 = (bf16[3,3,512,32]{2,3,1,0:T(8,128)(2,1)S(1)}, bf16[3,3,512,32]{2,3,1,0:T(8,128)(2,1)}, u32[]{:S(2)}) copy-start(bf16[3,3,512,32]{2,3,1,0:T(8,128)(2,1)} %param.11) | copy-start | bytes 884740
  10.8 8.4 %collective-permute-start.3 = (bf16[3,3,32,512]{3,2,1,0:T(8,128)(2,1)S(1)}, bf16[3,3,32,512]{3,2,1,0:T(8,128)(2,1)S(1)}, u32[]{:S(2)}, u32[]{:S(2)}) collective-permute-start(bf16[3,3,32,512]{3,2,1,0:T(8,128)(2,1)S(1)} %collective-permute-done.2.refs_2_), channel_id=1, source_target_pairs={{0,2},{2,0},{4,6},{6,4},{8,10},{10,8},{12,14},{14,12},{16,18},{18,... | collective-permute-start | bytes 884744 | tf_op jit(solution)/shard_map/ppermute | solution.py:70
  10.9 6.8 %collective-permute-start.8 = (bf16[3,3,32,512]{3,2,1,0:T(8,128)(2,1)S(1)}, bf16[3,3,32,512]{3,2,1,0:T(8,128)(2,1)S(1)}, u32[]{:S(2)}, u32[]{:S(2)}) collective-permute-start(bf16[3,3,32,512]{3,2,1,0:T(8,128)(2,1)S(1)} %collective-permute-done.4.refs_4_), channel_id=1, source_target_pairs={{0,8},{2,6},{8,16},{10,2},{16,24},{18,10},{24,28},{26,18},{28,20},... | collective-permute-start | bytes 884744 | tf_op jit(solution)/shard_map/ppermute | solution.py:67
  12.5 6.7 %collective-permute-start.5 = (bf16[3,3,32,512]{3,2,1,0:T(8,128)(2,1)S(1)}, bf16[3,3,32,512]{3,2,1,0:T(8,128)(2,1)S(1)}, u32[]{:S(2)}, u32[]{:S(2)}) collective-permute-start(bf16[3,3,32,512]{3,2,1,0:T(8,128)(2,1)S(1)} %collective-permute-done.4.refs_4_), channel_id=1, source_target_pairs={{0,2},{2,0},{4,6},{6,4},{8,10},{10,8},{12,14},{14,12},{16,18},{18,... | collective-permute-start | bytes 884744 | tf_op jit(solution)/shard_map/ppermute | solution.py:70
  13.7 5.6 %collective-permute-start.7 = (bf16[3,3,32,512]{3,2,1,0:T(8,128)(2,1)S(1)}, bf16[3,3,32,512]{3,2,1,0:T(8,128)(2,1)S(1)}, u32[]{:S(2)}, u32[]{:S(2)}) collective-permute-start(bf16[3,3,32,512]{3,2,1,0:T(8,128)(2,1)S(1)} %collective-permute-done.6.refs_6_), channel_id=1, source_target_pairs={{0,2},{2,0},{4,6},{6,4},{8,10},{10,8},{12,14},{14,12},{16,18},{18,... | collective-permute-start | bytes 884744 | tf_op jit(solution)/shard_map/ppermute | solution.py:70
  14.6 6.7 %collective-permute-start.10 = (bf16[3,3,32,512]{3,2,1,0:T(8,128)(2,1)S(1)}, bf16[3,3,32,512]{3,2,1,0:T(8,128)(2,1)S(1)}, u32[]{:S(2)}, u32[]{:S(2)}) collective-permute-start(bf16[3,3,32,512]{3,2,1,0:T(8,128)(2,1)S(1)} %collective-permute-done.6.refs_6_), channel_id=1, source_target_pairs={{0,8},{2,6},{8,16},{10,2},{16,24},{18,10},{24,28},{26,18},{28,20},... | collective-permute-start | bytes 884744 | tf_op jit(solution)/shard_map/ppermute | solution.py:67
  17.7 7.2 %collective-permute-start.12 = (bf16[3,3,32,512]{3,2,1,0:T(8,128)(2,1)S(1)}, bf16[3,3,32,512]{3,2,1,0:T(8,128)(2,1)S(1)}, u32[]{:S(2)}, u32[]{:S(2)}) collective-permute-start(bf16[3,3,32,512]{3,2,1,0:T(8,128)(2,1)S(1)} %collective-permute-done.8.refs_0_), channel_id=1, source_target_pairs={{0,8},{2,6},{8,16},{10,2},{16,24},{18,10},{24,28},{26,18},{28,20},... | collective-permute-start | bytes 884744 | tf_op jit(solution)/shard_map/ppermute | solution.py:67
  19.3 5.6 %collective-permute-start.9 = (bf16[3,3,32,512]{3,2,1,0:T(8,128)(2,1)S(1)}, bf16[3,3,32,512]{3,2,1,0:T(8,128)(2,1)S(1)}, u32[]{:S(2)}, u32[]{:S(2)}) collective-permute-start(bf16[3,3,32,512]{3,2,1,0:T(8,128)(2,1)S(1)} %collective-permute-done.8.refs_0_), channel_id=1, source_target_pairs={{0,2},{2,0},{4,6},{6,4},{8,10},{10,8},{12,14},{14,12},{16,18},{18,... | collective-permute-start | bytes 884744 | tf_op jit(solution)/shard_map/ppermute | solution.py:70
  21.3 6.7 %collective-permute-start.14 = (bf16[3,3,32,512]{3,2,1,0:T(8,128)(2,1)S(1)}, bf16[3,3,32,512]{3,2,1,0:T(8,128)(2,1)S(1)}, u32[]{:S(2)}, u32[]{:S(2)}) collective-permute-start(bf16[3,3,32,512]{3,2,1,0:T(8,128)(2,1)S(1)} %collective-permute-done.10.refs_2_), channel_id=1, source_target_pairs={{0,8},{2,6},{8,16},{10,2},{16,24},{18,10},{24,28},{26,18},{28,20},... | collective-permute-start | bytes 884744 | tf_op jit(solution)/shard_map/ppermute | solution.py:67
  23.4 5.2 %copy-start = (bf16[3,512,512]{2,1,0:T(8,128)(2,1)S(1)}, bf16[3,512,512]{2,1,0:T(8,128)(2,1)}, u32[]{:S(2)}) copy-start(bf16[3,512,512]{2,1,0:T(8,128)(2,1)} %time_ref.5) | copy-start | bytes 4718596
  23.4 5.2 %copy-start.7 = (s32[128]{0:T(128)S(1)}, s32[128]{0:T(128)}, u32[]{:S(2)}) copy-start(s32[128]{0:T(128)} %clips.7) | copy-start | bytes 1540
  24.8 5.6 %collective-permute-start.11 = (bf16[3,3,32,512]{3,2,1,0:T(8,128)(2,1)S(1)}, bf16[3,3,32,512]{3,2,1,0:T(8,128)(2,1)S(1)}, u32[]{:S(2)}, u32[]{:S(2)}) collective-permute-start(bf16[3,3,32,512]{3,2,1,0:T(8,128)(2,1)S(1)} %collective-permute-done.10.refs_2_), channel_id=1, source_target_pairs={{0,2},{2,0},{4,6},{6,4},{8,10},{10,8},{12,14},{14,12},{16,18},{18,... | collective-permute-start | bytes 884744 | tf_op jit(solution)/shard_map/ppermute | solution.py:70
  28.0 2.5 %collective-permute-start.15 = (bf16[3,3,32,512]{3,2,1,0:T(8,128)(2,1)S(1)}, bf16[3,3,32,512]{3,2,1,0:T(8,128)(2,1)S(1)}, u32[]{:S(2)}, u32[]{:S(2)}) collective-permute-start(bf16[3,3,32,512]{3,2,1,0:T(8,128)(2,1)S(1)} %collective-permute-done.14.refs_6_), channel_id=1, source_target_pairs={{0,2},{2,0},{4,6},{6,4},{8,10},{10,8},{12,14},{14,12},{16,18},{18,... | collective-permute-start | bytes 884744 | tf_op jit(solution)/shard_map/ppermute | solution.py:70
  28.0 2.5 %collective-permute-start.13 = (bf16[3,3,32,512]{3,2,1,0:T(8,128)(2,1)S(1)}, bf16[3,3,32,512]{3,2,1,0:T(8,128)(2,1)S(1)}, u32[]{:S(2)}, u32[]{:S(2)}) collective-permute-start(bf16[3,3,32,512]{3,2,1,0:T(8,128)(2,1)S(1)} %collective-permute-done.12.refs_4_), channel_id=1, source_target_pairs={{0,2},{2,0},{4,6},{6,4},{8,10},{10,8},{12,14},{14,12},{16,18},{18,... | collective-permute-start | bytes 884744 | tf_op jit(solution)/shard_map/ppermute | solution.py:70
  34.1 10.0 %collective-permute-start.16 = (bf16[3,128,512]{2,1,0:T(8,128)(2,1)S(1)}, bf16[3,128,512]{2,1,0:T(8,128)(2,1)S(1)}, u32[]{:S(2)}, u32[]{:S(2)}) collective-permute-start(bf16[3,128,512]{2,1,0:T(8,128)(2,1)S(1)} %get-tuple-element.28), channel_id=1, source_target_pairs={{0,2},{2,4},{4,6},{6,8},{8,10},{10,12},{12,14},{14,16},{16,18},{18... | collective-permute-start | bytes 1179656 | tf_op jit(solution)/shard_map/ppermute | solution.py:408
  36.0 8.1 %copy-start.2 = (bf16[512,1536]{1,0:T(8,128)(2,1)S(1)}, bf16[512,1536]{1,0:T(8,128)(2,1)}, u32[]{:S(2)}) copy-start(bf16[512,1536]{1,0:T(8,128)(2,1)} %qkv_ref.1) | copy-start | bytes 4718596
  36.0 8.1 %copy-start.4 = (bf16[512,512]{1,0:T(8,128)(2,1)S(1)}, bf16[512,512]{1,0:T(8,128)(2,1)}, u32[]{:S(2)}) copy-start(bf16[512,512]{1,0:T(8,128)(2,1)} %proj_ref.1) | copy-start | bytes 1572868
  36.0 8.0 %copy-start.8 = (f32[512]{0:T(512)S(1)}, f32[512]{0:T(512)}, u32[]{:S(2)}) copy-start(f32[512]{0:T(512)} %param.13) | copy-start | bytes 6148
